TPU v7x, 32 devices: a whole 2x2x4 slice. The times are simulated.
32 devices in a mesh: req: 8 (over z, y), tp: 4 (over x, core).
Axes of the slice: x: 2, y: 2, z: 4, core: 2. Of those that a mesh axis runs over, the one named last changes fastest.
Arguments:
- tokens: bfloat16 [4096, 2048], P('req', 'tp'), may hold values from -6 to 6
- owners: int32 [8], replicated, may hold values from 0 to 7, each once
- request_groups: int32 [8, 2], P('req'), may hold values from 0 to 3, all different within a row
- request_lengths: int32 [8, 2], P('req'), may hold values from 64 to 448, as said below
- prefix_cache: bfloat16 [8, 2, 768, 320], P('req'), may hold values from -25 to 25
- attn_gain: float32 [2048], replicated, may hold values from 0.5 to 1.5
- query_weight: bfloat16 [2048, 1280], P(None, 'tp'), may hold values from -0.125 to 0.125
- key_value_weight: bfloat16 [2048, 640], replicated, may hold values from -0.125 to 0.125
- query_gain: float32 [64], replicated, may hold values from 0.7 to 6
- key_gain: float32 [64], replicated, may hold values from 0.7 to 6
- w_out: bfloat16 [1280, 2048], P('tp'), may hold values from -0.15625 to 0.15625
- ffn_gain: float32 [2048], replicated, may hold values from 0.5 to 1.5
- w_gate_up: bfloat16 [2048, 2, 5120], P(None, None, 'tp'), may hold values from -0.125 to 0.125
- w_down: bfloat16 [5120, 2048], P('tp'), may hold values from -0.078125 to 0.078125
Outputs:
- hidden: bfloat16 [4096, 2048], P('req', 'tp')
- suffix_cache: bfloat16 [4096, 2, 320], P('req')
Inputs may be any that keep to these rules, and one draw needn't show every extreme that they name: `owners`: every req index holds exactly one half of one group's prefix. `request_groups`: the two groups of one device differ; every group has a request. `request_lengths`: a device's two lengths sum to 512.
All inputs are finite; a program needn't handle non-finite values.
Results may differ from a plain program's by a relative error of at most 0.012.
The roundings to bfloat16 on the way count: a program that leaves them out, or rounds other values in their place, can miss the bound.
Values may be sent and summed in bfloat16 or wider, within the bound.
No kernel may reach another device: no remote copies, remote signals or barrier semaphores. Data moves between devices by JAX's collectives and lax.ppermute only.
A program may use at most 192 MiB of HBM per device.

v0:
```python
import jax
import jax.numpy as jnp
from jax import lax
from jax.sharding import PartitionSpec as P

HEAD_SIZE = 64
PREFIX = 1536
MAXLEN = 448


eps_norm = 1e-06
rope_base = 10000.0
masked_score = -1e30


def rms_scale(values, gain_vec):
    mean_sq = jnp.mean(values * values, axis=-1, keepdims=True)
    return values * lax.rsqrt(mean_sq + eps_norm) * gain_vec


def rotate(values, positions):
    half_size = values.shape[-1] // 2
    frequency = rope_base ** (-jnp.arange(half_size, dtype=jnp.float32) * 2.0 / values.shape[-1])
    angles = positions.astype(jnp.float32)[:, None] * frequency[None, :]
    cos_part = jnp.cos(angles)[:, None, :]
    sin_part = jnp.sin(angles)[:, None, :]
    front_half = values[..., :half_size]
    back_half = values[..., half_size:]
    return jnp.concatenate(
        [
            front_half * cos_part - back_half * sin_part,
            back_half * cos_part + front_half * sin_part,
        ],
        axis=-1,
    )


def partial_attend(query_rows, key_rows, value_rows, allowed):
    score_scale = query_rows.shape[-1] ** (-0.5)
    scores = (
        jnp.einsum("rhd,shd->hrs", query_rows, key_rows, preferred_element_type=jnp.float32)
        * score_scale
    )
    if allowed is not None:
        scores = jnp.where(allowed[None], scores, masked_score)
    row_max = jnp.max(scores, axis=-1, keepdims=True)
    weights = jnp.exp(scores - row_max)
    row_total = jnp.sum(weights, axis=-1, keepdims=True)
    blended = jnp.einsum(
        "hrs,shd->rhd", weights.astype(jnp.bfloat16), value_rows, preferred_element_type=jnp.float32
    )
    blended = blended / jnp.transpose(row_total, (1, 0, 2))
    log_total = jnp.transpose(row_max + jnp.log(row_total), (1, 0, 2))[..., 0]
    return (blended, log_total)


def combine(out_parts, lse_parts):
    row_max = jnp.maximum(jnp.maximum(lse_parts[0], lse_parts[1]), lse_parts[2])
    factors = [jnp.exp(log_part - row_max) for log_part in lse_parts]
    row_total = factors[0] + factors[1] + factors[2]
    blended = factors[0][..., None] * out_parts[0].astype(jnp.float32)
    blended = blended + factors[1][..., None] * out_parts[1].astype(jnp.float32)
    blended = blended + factors[2][..., None] * out_parts[2]
    return blended / row_total[..., None]


def place(buffer, fresh_rows, first_row, request, padded_segment):
    count_rows = fresh_rows.shape[0]
    window = lax.dynamic_slice_in_dim(buffer, first_row, count_rows, 0)
    owned_rows = lax.dynamic_slice_in_dim(padded_segment, first_row, count_rows, 0) == request
    owned_rows = owned_rows.reshape(owned_rows.shape + (1,) * (fresh_rows.ndim - 1))
    return lax.dynamic_update_slice_in_dim(
        buffer, jnp.where(owned_rows, fresh_rows, window), first_row, 0
    )


def place_half(buffers, half_index, fresh_out, fresh_lse, first_row, request, padded_segment):
    out_buffer, lse_buffer = buffers
    half_out = lax.dynamic_index_in_dim(out_buffer, half_index, 0, keepdims=False)
    half_lse = lax.dynamic_index_in_dim(lse_buffer, half_index, 0, keepdims=False)
    half_out = place(half_out, fresh_out, first_row, request, padded_segment)
    half_lse = place(half_lse, fresh_lse, first_row, request, padded_segment)
    out_buffer = lax.dynamic_update_index_in_dim(out_buffer, half_out, half_index, 0)
    lse_buffer = lax.dynamic_update_index_in_dim(lse_buffer, half_lse, half_index, 0)
    return (out_buffer, lse_buffer)


def local(
    tokens,
    owners,
    request_groups,
    request_lengths,
    prefix_cache,
    attn_gain,
    query_weight,
    key_value_weight,
    query_gain,
    key_gain,
    w_out,
    ffn_gain,
    w_gate_up,
    w_down,
):
    row_count = tokens.shape[0]
    key_value_columns = query_weight.shape[1]
    head_count = key_value_columns // HEAD_SIZE
    full_rows = lax.all_gather(tokens, "tp", axis=1, tiled=True)
    row_index = jnp.arange(row_count, dtype=jnp.int32)
    first_len = request_lengths[0, 0]
    segment = (row_index >= first_len).astype(jnp.int32)
    position = row_index - segment * first_len + PREFIX
    residual_in = full_rows.astype(jnp.float32)
    normalized_input = rms_scale(residual_in, attn_gain).astype(jnp.bfloat16)
    query_rows = jnp.dot(
        normalized_input, query_weight, preferred_element_type=jnp.float32
    ).reshape(row_count, head_count, HEAD_SIZE)
    query_rows = rotate(rms_scale(query_rows, query_gain), position).astype(jnp.bfloat16)
    key_value_rows = jnp.dot(
        normalized_input, key_value_weight, preferred_element_type=jnp.float32
    ).reshape(row_count, 2, head_count, HEAD_SIZE)
    key_rows = rotate(rms_scale(key_value_rows[:, 0], key_gain), position).astype(jnp.bfloat16)
    value_rows = key_value_rows[:, 1].astype(jnp.bfloat16)
    cache_rows = jnp.stack(
        [
            key_rows.reshape(row_count, key_value_columns),
            value_rows.reshape(row_count, key_value_columns),
        ],
        axis=1,
    )
    allowed = (segment[:, None] == segment[None, :]) & (row_index[None, :] <= row_index[:, None])
    own_out, own_lse = partial_attend(query_rows, key_rows, value_rows, allowed)
    starts = jnp.stack([jnp.zeros((), jnp.int32), first_len])
    my_groups = request_groups[0]
    holder_ids = jnp.arange(owners.shape[0], dtype=jnp.int32)
    padded_segment = jnp.concatenate([segment, jnp.full((MAXLEN,), -1, jnp.int32)])
    padded_query = jnp.concatenate(
        [query_rows, jnp.zeros((MAXLEN, head_count, HEAD_SIZE), jnp.bfloat16)], axis=0
    )
    buffers = (
        jnp.zeros((2, row_count + MAXLEN, head_count, HEAD_SIZE), jnp.bfloat16),
        jnp.zeros((2, row_count + MAXLEN, head_count), jnp.float32),
    )

    def attend_into(running, request, half_index, slot_keys, slot_values):
        window = lax.dynamic_slice_in_dim(padded_query, starts[request], MAXLEN, 0)
        blended, log_total = partial_attend(window, slot_keys, slot_values, None)
        return place_half(
            running,
            half_index,
            blended.astype(jnp.bfloat16),
            log_total,
            starts[request],
            request,
            padded_segment,
        )

    def slot_place(holder):
        place_index = jnp.sum(jnp.where(owners == holder, holder_ids, 0))
        return (place_index // 2, place_index % 2)

    def make_attend(request, half_index, slot_keys, slot_values):

        def attend(running):
            return attend_into(running, request, half_index, slot_keys, slot_values)

        return attend

    def keep_state(running):
        return running

    shard_block = lax.all_gather(prefix_cache, "req", axis=0, tiled=True)

    def one_slot(step_index, inner):
        group_id, half_index = slot_place(step_index)
        stored_slot = lax.dynamic_index_in_dim(shard_block, step_index, 0, keepdims=False)
        slot_keys = stored_slot[0].reshape(-1, head_count, HEAD_SIZE)
        slot_values = stored_slot[1].reshape(-1, head_count, HEAD_SIZE)
        for request in range(2):
            inner = lax.cond(
                my_groups[request] == group_id,
                make_attend(request, half_index, slot_keys, slot_values),
                keep_state,
                inner,
            )
        return inner

    buffers = lax.fori_loop(0, shard_block.shape[0], one_slot, buffers)
    out_buffer, lse_buffer = buffers
    attention = combine(
        [out_buffer[0, :row_count], out_buffer[1, :row_count], own_out],
        [lse_buffer[0, :row_count], lse_buffer[1, :row_count], own_lse],
    )
    attention = attention.astype(jnp.bfloat16).reshape(row_count, key_value_columns)
    head_part = jnp.dot(attention, w_out, preferred_element_type=jnp.float32)
    head_total = lax.psum(head_part.astype(jnp.bfloat16), "tp").astype(jnp.float32)
    mixed = residual_in + head_total
    normed_ffn = rms_scale(mixed, ffn_gain).astype(jnp.bfloat16)
    gate_up = jnp.einsum("rd,dgf->rgf", normed_ffn, w_gate_up, preferred_element_type=jnp.float32)
    activated = (jax.nn.silu(gate_up[:, 0]) * gate_up[:, 1]).astype(jnp.bfloat16)
    down_part = jnp.dot(activated, w_down, preferred_element_type=jnp.float32)
    down_share = lax.psum_scatter(
        down_part.astype(jnp.bfloat16), "tp", scatter_dimension=1, tiled=True
    ).astype(jnp.float32)
    column_start = lax.axis_index("tp") * down_share.shape[1]
    own_mixed = lax.dynamic_slice_in_dim(mixed, column_start, down_share.shape[1], 1)
    return ((own_mixed + down_share).astype(jnp.bfloat16), cache_rows)


def solution(mesh):
    placed = (
        P("req", "tp"),
        P(),
        P("req", None),
        P("req", None),
        P("req", None, None, None),
        P(),
        P(None, "tp"),
        P(),
        P(),
        P(),
        P("tp", None),
        P(),
        P(None, None, "tp"),
        P("tp", None),
    )
    return jax.shard_map(
        local,
        mesh=mesh,
        in_specs=placed,
        out_specs=(P("req", "tp"), P("req", None, None)),
        check_vma=False,
    )
```

profile of v0, /device:TPU:0, one launch (start us, length us, event | category | flops | bytes accessed | tf_op | source)
XLA Modules:
  0.0 366.0 jit_solution(10930702406792488943)
XLA Ops:
  7.2 0.7 all-gather.3.cloned.1.call-update
  8.0 0.7 all-gather.5.cloned.1.call-update
  8.7 0.7 fusion.106
  9.4 0.7 add_convert_fusion.2
  10.6 24.3 %all-gather.3.cloned.1.call-done = bf16[512,2048]{1,0:T(8,128)(2,1)} async-done(((bf16[512,512]{1,0:T(8,128)(2,1)}), bf16[512,2048]{1,0:T(8,128)(2,1)}) %all-gather.3.cloned.1.call-update) | async-done | bytes 2097168 | tf_op jit(solution)/shard_map/all_gather | solution.py:107
  34.9 2.1 fusion.58
  37.0 2.9 fusion.96
  40.3 0.9 concatenate.15
  41.7 1.7 fusion.94
  43.8 0.7 copy-done.7
  44.5 1.0 fusion.57
  45.7 2.3 copy-done.5
  48.0 1.1 fusion.62
  49.1 106.0 %all-gather.5.cloned.1.call-done = bf16[8,2,768,320]{2,3,1,0:T(8,128)(2,1)} async-done(((bf16[1,2,768,320]{2,3,1,0:T(8,128)(2,1)}), bf16[8,2,768,320]{2,3,1,0:T(8,128)(2,1)}) %all-gather.5.cloned.1.call-update) | async-done | bytes 7864336 | tf_op jit(solution)/shard_map/all_gather | solution.py:171
  155.0 1.2 broadcast_in_dim.102
  156.3 94.2 %while.18 = (s32[]{:T(128)}, bf16[2,960,5,64]{1,3,2,0:T(8,128)(2,1)}, f32[2,960,5]{1,2,0:T(8,128)S(1)}, s32[2]{0:T(128)S(1)}, s32[8]{0:T(128)S(1)}, /*index=5*/b...) while((s32[]{:T(128)}, ...), condition=%wide.region_12.13_spmd.clone, body=%wide.region_2.12_spmd.clone.sunk | while | flops 909191104 | bytes 48375216 | solution.py:187
  156.5 0.6 fusion.126
  159.7 0.6 fusion.125
  161.6 1.3 constant_dynamic-slice_fusion.3
  163.0 0.6 fusion.126
  166.2 0.6 fusion.125
  168.1 1.3 constant_dynamic-slice_fusion.3
  169.4 11.1 %conditional.7 = ((bf16[2,960,5,64]{1,3,2,0:T(8,128)(2,1)}, f32[2,960,5]{1,2,0:T(8,128)S(1)})) conditional(s32[]{:T(128)} %convert_element_type.249, (bf16[2,960,5,64]{1,3,2,0:T(8,128)(2,1)}, f32[2,960,5]{1,2,0:T(8,128)S(1)}) %get-tuple-element.575, (s32[1,1]{1,0:T(1,128)S(1)}, s32[960]{0:T(1024)S(1)}, bf16[960,5,64]{0,2,1:T(8,128)(2,1)S(1)}, ...), branch_computations={%region_8.8_spmd, %region_9.11_spmd} | conditional | flops 454595008 | bytes 23203292 | solution.py:179
  169.6 1.5 multiply_reduce_fusion.1
  171.1 1.4 fusion.28
  172.5 2.7 fusion.46
  175.3 4.7 %dynamic_update_slice.24 = bf16[2,960,5,64]{1,3,2,0:T(8,128)(2,1)} dynamic-update-slice(bf16[2,960,5,64]{1,3,2,0:T(8,128)(2,1)} %get-tuple-element.330, bf16[1,448,5,64]{1,3,2,0:T(8,128)(2,1)S(1)} %fusion.46, s32[]{:T(128)S(6)} %select_n.93, s32[]{:T(128)S(6)} %select_n.95, s32[]{:T(128)} %constant.221.clone, s32[]{:T(128)} %constant.221.clone) | dynamic-update-slice | bytes 573444 | tf_op jit(solution)/shard_map/while/body/eval_jaxpr/cond/branch_1_fun/jit(dynamic_update_index_in_dim)/dynamic_update_slice | solution.py:83
  180.5 0.6 fusion.126
  185.7 1.3 constant_dynamic-slice_fusion.3
  187.0 0.6 fusion.126
  192.2 1.3 constant_dynamic-slice_fusion.3
  193.5 0.6 fusion.126
  198.7 1.3 constant_dynamic-slice_fusion.3
  199.9 9.9 %conditional.6 = ((bf16[2,960,5,64]{1,3,2,0:T(8,128)(2,1)}, f32[2,960,5]{1,2,0:T(8,128)S(1)})) conditional(s32[]{:T(128)} %convert_element_type.250, (bf16[2,960,5,64]{1,3,2,0:T(8,128)(2,1)}, f32[2,960,5]{1,2,0:T(8,128)S(1)}) %tuple.78, (s32[512]{0:T(512)S(1)}, bf16[512,5,64]{0,2,1:T(8,128)(2,1)S(1)}, bf16[768,5,64]{0,2,1:T(8,128)(2,1)S(1)}, ...), branch_computations={%region_4.4_spmd, %region_5.7_spmd} | conditional | flops 454595008 | bytes 23203210 | solution.py:179
  200.0 1.2 multiply_reduce_fusion
  201.2 1.4 fusion.4
  202.6 2.5 fusion.22
  205.5 4.4 %dynamic_update_slice.22 = bf16[2,960,5,64]{1,3,2,0:T(8,128)(2,1)} dynamic-update-slice(bf16[2,960,5,64]{1,3,2,0:T(8,128)(2,1)} %get-tuple-element.323, bf16[1,448,5,64]{1,3,2,0:T(8,128)(2,1)S(1)} %fusion.22, s32[]{:T(128)S(6)} %select_n.89, s32[]{:T(128)} %constant.216.clone, s32[]{:T(128)} %constant.216.clone, s32[]{:T(128)} %constant.216.clone) | dynamic-update-slice | bytes 573444 | tf_op jit(solution)/shard_map/while/body/eval_jaxpr/cond/branch_1_fun/jit(dynamic_update_index_in_dim)/dynamic_update_slice | solution.py:83
  209.9 0.6 fusion.126
  215.1 1.3 constant_dynamic-slice_fusion.3
  216.4 0.6 fusion.126
  221.6 1.3 constant_dynamic-slice_fusion.3
  222.8 9.9 %conditional.6 = ((bf16[2,960,5,64]{1,3,2,0:T(8,128)(2,1)}, f32[2,960,5]{1,2,0:T(8,128)S(1)})) conditional(s32[]{:T(128)} %convert_element_type.250, (bf16[2,960,5,64]{1,3,2,0:T(8,128)(2,1)}, f32[2,960,5]{1,2,0:T(8,128)S(1)}) %tuple.78, (s32[512]{0:T(512)S(1)}, bf16[512,5,64]{0,2,1:T(8,128)(2,1)S(1)}, bf16[768,5,64]{0,2,1:T(8,128)(2,1)S(1)}, ...), branch_computations={%region_4.4_spmd, %region_5.7_spmd} | conditional | flops 454595008 | bytes 23203210 | solution.py:179
  222.9 1.2 multiply_reduce_fusion
  224.1 1.4 fusion.4
  225.5 2.5 fusion.22
  228.4 4.4 %dynamic_update_slice.22 = bf16[2,960,5,64]{1,3,2,0:T(8,128)(2,1)} dynamic-update-slice(bf16[2,960,5,64]{1,3,2,0:T(8,128)(2,1)} %get-tuple-element.323, bf16[1,448,5,64]{1,3,2,0:T(8,128)(2,1)S(1)} %fusion.22, s32[]{:T(128)S(6)} %select_n.89, s32[]{:T(128)} %constant.216.clone, s32[]{:T(128)} %constant.216.clone, s32[]{:T(128)} %constant.216.clone) | dynamic-update-slice | bytes 573444 | tf_op jit(solution)/shard_map/while/body/eval_jaxpr/cond/branch_1_fun/jit(dynamic_update_index_in_dim)/dynamic_update_slice | solution.py:83
  232.7 0.6 fusion.126
  237.9 1.3 constant_dynamic-slice_fusion.3
  239.2 11.1 %conditional.7 = ((bf16[2,960,5,64]{1,3,2,0:T(8,128)(2,1)}, f32[2,960,5]{1,2,0:T(8,128)S(1)})) conditional(s32[]{:T(128)} %convert_element_type.249, (bf16[2,960,5,64]{1,3,2,0:T(8,128)(2,1)}, f32[2,960,5]{1,2,0:T(8,128)S(1)}) %get-tuple-element.575, (s32[1,1]{1,0:T(1,128)S(1)}, s32[960]{0:T(1024)S(1)}, bf16[960,5,64]{0,2,1:T(8,128)(2,1)S(1)}, ...), branch_computations={%region_8.8_spmd, %region_9.11_spmd} | conditional | flops 454595008 | bytes 23203292 | solution.py:179
  239.4 1.5 multiply_reduce_fusion.1
  240.9 1.4 fusion.28
  242.3 2.7 fusion.46
  245.1 4.7 %dynamic_update_slice.24 = bf16[2,960,5,64]{1,3,2,0:T(8,128)(2,1)} dynamic-update-slice(bf16[2,960,5,64]{1,3,2,0:T(8,128)(2,1)} %get-tuple-element.330, bf16[1,448,5,64]{1,3,2,0:T(8,128)(2,1)S(1)} %fusion.46, s32[]{:T(128)S(6)} %select_n.93, s32[]{:T(128)S(6)} %select_n.95, s32[]{:T(128)} %constant.221.clone, s32[]{:T(128)} %constant.221.clone) | dynamic-update-slice | bytes 573444 | tf_op jit(solution)/shard_map/while/body/eval_jaxpr/cond/branch_1_fun/jit(dynamic_update_index_in_dim)/dynamic_update_slice | solution.py:83
  250.6 4.5 %fusion.90 = bf16[512,5,64]{0,2,1:T(8,128)(2,1)S(1)} fusion(f32[5,512,512]{1,2,0:T(8,128)} %copy-done.5, f32[5,512]{1,0:T(8,128)S(1)} %get-tuple-element.434, pred[512,512]{0,1:T(8,128)(4,1)S(1)} %fusion.77, f32[512,5]{0,1:T(8,128)S(1)} %get-tuple-element.430, f32[512,5]{0,1:T(8,128)S(1)} %bitcast.212, f32[512,5]{0,1:T(8,128)S(1)} %get-tuple-element.431, ...), kind=kOutput, calls=%fused_computation.83 | convolution fusion | flops 174653440 | bytes 6877184 | tf_op jit(solution)/shard_map/hrs,shd->rhd/dot_general | solution.py:49
  255.1 2.6 convolution_convert_fusion.1
  257.8 49.9 %all-reduce.4.cloned.1.call-done = bf16[512,2048]{1,0:T(8,128)(2,1)} async-done(((bf16[512,2048]{1,0:T(8,128)(2,1)}), bf16[512,2048]{1,0:T(8,128)(2,1)}) %all-reduce.4.cloned.1.call-update) | async-done | bytes 2097168 | tf_op jit(solution)/shard_map/psum | solution.py:195
  307.7 4.4 %convert_add_fusion = (f32[512,2048]{1,0:T(8,128)}, f32[512]{0:T(512)S(1)}) fusion(bf16[512,2048]{1,0:T(8,128)(2,1)S(1)} %copy-done.3, bf16[512,2048]{1,0:T(8,128)(2,1)} %all-reduce.4.cloned.1.call-done), kind=kLoop, calls=%fused_computation.50 | loop fusion | flops 5242368 | bytes 8390656 | tf_op jit(solution)/shard_map/add | solution.py:196
  312.1 9.4 %fusion.55 = f32[512,2,1280]{2,0,1:T(8,128)S(1)} fusion(bf16[2048,2,1280]{2,1,0:T(2,128)(2,1)} %param.32, f32[2048]{0:T(1024)S(1)} %copy-done.18, f32[512]{0:T(512)S(1)} %add_rsqrt_fusion.2, bf16[512,2048]{1,0:T(8,128)(2,1)S(1)} %copy-done.3, bf16[512,2048]{1,0:T(8,128)(2,1)S(1)} %copy-done.6), kind=kOutput, calls=%fused_computation.48 | convolution fusion | flops 5375000576 | bytes 19933184 | tf_op jit(solution)/shard_map/rd,dgf->rgf/dot_general | solution.py:198
  321.5 4.2 %convolution_convert_fusion = bf16[512,2048]{1,0:T(8,128)(2,1)} fusion(bf16[1280,2048]{1,0:T(8,128)(2,1)S(1)} %bitcast.224, f32[512,2,1280]{2,0,1:T(8,128)S(1)} %fusion.55), kind=kOutput, calls=%fused_computation.63 | convolution fusion | flops 2689335296 | bytes 12582912 | tf_op jit(solution)/shard_map/dot_general | solution.py:200
  325.7 1.1 slice.146
  326.9 0.9 pad_maximum_fusion
  327.8 29.3 %reduce-scatter.2.cloned.1.call-done = bf16[512,512]{1,0:T(8,128)(2,1)} async-done(((bf16[512,2048]{1,0:T(8,128)(2,1)}), bf16[512,512]{1,0:T(8,128)(2,1)}) %reduce-scatter.2.cloned.1.call-update) | async-done | bytes 524304 | tf_op jit(solution)/shard_map/reduce_scatter | solution.py:201
  357.1 2.3 add_convert_fusion
  (106 shorter events, 7.8 us)
Async XLA Ops:
  7.2 34.1 %copy-start = (bf16[2048,640]{1,0:T(8,128)(2,1)S(1)}, bf16[2048,640]{1,0:T(8,128)(2,1)}, u32[]{:S(2)}) copy-start(bf16[2048,640]{1,0:T(8,128)(2,1)} %param.27) | copy-start | bytes 7864324
  7.2 27.7 %all-gather.3.cloned.1.call-start = ((), (), s32[]{:S(2)}) async-start(), calls=%async_computation.1 | async-start | bytes 2621440 | tf_op jit(solution)/shard_map/all_gather | solution.py:107
  7.9 147.1 %all-gather.5.cloned.1.call-start = ((), (), s32[]{:S(2)}) async-start(), calls=%async_computation.2 | async-start | bytes 8847360 | tf_op jit(solution)/shard_map/all_gather | solution.py:171
  8.7 299.0 %all-reduce.4.cloned.1.call-start = ((), (), s32[]{:S(2)}) async-start(), calls=%async_computation.3 | async-start | bytes 4194304 | tf_op jit(solution)/shard_map/psum | solution.py:195
  10.4 29.8 %copy-start.8 = (f32[512,32]{0,1:T(8,128)}, f32[512,32]{0,1:T(8,128)S(1)}, u32[]{:S(2)}) copy-start(f32[512,32]{0,1:T(8,128)S(1)} %get-tuple-element.432) | copy-start | bytes 196612
  10.4 29.8 %copy-start.10 = (f32[512,32]{0,1:T(8,128)}, f32[512,32]{0,1:T(8,128)S(1)}, u32[]{:S(2)}) copy-start(f32[512,32]{0,1:T(8,128)S(1)} %get-tuple-element.433) | copy-start | bytes 196612
  37.0 3.1 copy-start.14
  39.9 1.8 copy-start.2
  39.9 1.8 copy-start.17
  41.7 1.8 copy-start.15
  41.7 2.0 copy-start.9
  41.7 2.0 copy-start.11
  43.4 1.1 copy-start.7
  45.6 2.4 copy-start.5
  45.6 110.7 %copy-start.4 = (bf16[960,5,64]{0,2,1:T(8,128)(2,1)S(1)}, bf16[960,5,64]{0,2,1:T(8,128)(2,1)}, u32[]{:S(2)}) copy-start(bf16[960,5,64]{0,2,1:T(8,128)(2,1)} %concatenate.15) | copy-start | bytes 1843204
  45.6 110.6 %copy-start.12 = (s32[1,2]{1,0:T(1,128)S(1)}, s32[1,2]{1,0:T(1,128)}, u32[]{:S(2)}) copy-start(s32[1,2]{1,0:T(1,128)} %param.23) | copy-start | bytes 28
  45.6 110.6 %copy-start.13 = (s32[1,2]{1,0:T(1,128)S(1)}, s32[1,2]{1,0:T(1,128)}, u32[]{:S(2)}) copy-start(s32[1,2]{1,0:T(1,128)} %param.22) | copy-start | bytes 28
  45.6 110.6 %copy-start.19 = (s32[8]{0:T(128)S(1)}, s32[8]{0:T(128)}, u32[]{:S(2)}) copy-start(s32[8]{0:T(128)} %param.21) | copy-start | bytes 100
  250.6 4.5 %copy-start.16 = (bf16[320,2048]{1,0:T(8,128)(2,1)S(1)}, bf16[320,2048]{1,0:T(8,128)(2,1)}, u32[]{:S(2)}) copy-start(bf16[320,2048]{1,0:T(8,128)(2,1)} %param.30) | copy-start | bytes 3932164
  255.1 52.6 %copy-start.3 = (bf16[512,2048]{1,0:T(8,128)(2,1)S(1)}, bf16[512,2048]{1,0:T(8,128)(2,1)}, u32[]{:S(2)}) copy-start(bf16[512,2048]{1,0:T(8,128)(2,1)} %all-gather.3.cloned.1.call-done) | copy-start | bytes 6291460
  257.7 54.3 %copy-start.18 = (f32[2048]{0:T(1024)S(1)}, f32[2048]{0:T(1024)}, u32[]{:S(2)}) copy-start(f32[2048]{0:T(1024)} %param.31) | copy-start | bytes 24580
  257.7 99.3 %reduce-scatter.2.cloned.1.call-start = ((), (), s32[]{:S(2)}) async-start(), calls=%async_computation.4 | async-start | bytes 2621440 | tf_op jit(solution)/shard_map/reduce_scatter | solution.py:201
  307.7 4.4 %copy-start.6 = (bf16[512,2048]{1,0:T(8,128)(2,1)S(1)}, bf16[512,2048]{1,0:T(8,128)(2,1)}, u32[]{:S(2)}) copy-start(bf16[512,2048]{1,0:T(8,128)(2,1)} %all-reduce.4.cloned.1.call-done) | copy-start | bytes 6291460
  307.7 13.8 %slice-start = ((s8[5242880]{0:T(1024)(128)(4,1)}), s8[4194304]{0:T(1024)(128)(4,1)S(1)}, s32[]{:S(2)}) async-start(s8[5242880]{0:T(1024)(128)(4,1)} %bitcast.223), calls=%async_computation.5 | async-start | bytes 8388608
  312.1 9.4 %slice-start.1 = ((s8[5242880]{0:T(1024)(128)(4,1)}), s8[1048576]{0:T(1024)(128)(4,1)S(1)}, s32[]{:S(2)}) async-start(s8[5242880]{0:T(1024)(128)(4,1)} %bitcast.223), calls=%async_computation.6 | async-start | bytes 2097152
  321.5 38.0 %copy-start.1 = (bf16[2048,640]{1,0:T(8,128)(2,1)S(1)}, bf16[2048,640]{1,0:T(8,128)(2,1)}, u32[]{:S(2)}) copy-start(bf16[2048,640]{1,0:T(8,128)(2,1)} %param.27) | copy-start | bytes 7864324
Sparse Core Ops, SparseCore 0:
  9.5 25.2 all-gather.2
  37.1 117.9 all-gather.4
  257.8 49.7 all-reduce.3
  325.8 31.2 reduce-scatter.1
where the time goes:
time: 368 us; the launch traced here: 366 us
  waiting for transfers between devices  211 us (57%)
  matrix products  42.2 us (11%)
  local copies, waits for them, and re-layouts  41.3 us (11%)
  loops' own time  32.6 us (9%)
  other arithmetic  24.7 us (7%)
  between operations  14.2 us (4%)
    all_gather x1, waiting for transfers between devices, local(): shard_block = lax.all_gather(prefix_cache, 'req', axis=0, tiled=True)  106 us
    psum x1, waiting for transfers between devices, local(): lax.psum(head_part.astype(jnp.bfloat16), 'tp').astype(jnp.float32)  49.9 us
    another operation x1, loops' own time, local(): buffers = lax.fori_loop(0, shard_block.shape[0], one_slot, buffers)  32 us
    reduce_scatter x1, waiting for transfers between devices, local(): lax.psum_scatter(down_part.astype(jnp.bfloat16), 'tp', scatter_dimension=...  29.3 us
    all_gather x1, waiting for transfers between devices, local(): full_rows = lax.all_gather(tokens, 'tp', axis=1, tiled=True)  24.3 us
    dynamic_update_slice x4, local copies, waits for them, and re-layouts, place_half(): lax.dynamic_update_index_in_dim(out_buffer, half_out, half_index, 0)  18.2 us
    dot_general x5, matrix products, partial_attend(): jnp.einsum('hrs,shd->rhd', weights.astype(jnp.bfloat16), value_rows, pref...  14.9 us
    slice x8, local copies, waits for them, and re-layouts, one_slot(): slot_values = stored_slot[1].reshape(-1, head_count, HEAD_SIZE)  10 us
  transfers between devices with their start and end apart: 4, of which 4 were waited for; matrix products, arithmetic and copies ran while one was open for 4% of the time, Pallas kernels for 0%

commit v1 on v0

v1 whole, which is shorter than its diff:
```python
import functools

import jax
import jax.numpy as jnp
from jax import lax
from jax.experimental import pallas as pl
from jax.experimental.pallas import tpu as pltpu
from jax.sharding import PartitionSpec as P

HEAD_SIZE = 64
PREFIX = 1536

eps_norm = 1e-06
rope_base = 10000.0
masked_score = -1e30
VMEM_LIMIT = 60 * 1024 * 1024


def rms_scale(values, gain_vec):
    mean_sq = jnp.mean(values * values, axis=-1, keepdims=True)
    return values * lax.rsqrt(mean_sq + eps_norm) * gain_vec


def rotate(values, positions):
    half_size = values.shape[-1] // 2
    frequency = rope_base ** (-jnp.arange(half_size, dtype=jnp.float32) * 2.0 / values.shape[-1])
    angles = positions.astype(jnp.float32)[:, None] * frequency[None, :]
    cos_part = jnp.cos(angles)[:, None, :]
    sin_part = jnp.sin(angles)[:, None, :]
    front_half = values[..., :half_size]
    back_half = values[..., half_size:]
    return jnp.concatenate(
        [
            front_half * cos_part - back_half * sin_part,
            back_half * cos_part + front_half * sin_part,
        ],
        axis=-1,
    )


def tn_dot(lhs, rhs):
    return lax.dot_general(lhs, rhs, (((0,), (0,)), ((), ())), preferred_element_type=jnp.float32)


def nn_dot(lhs, rhs):
    return lax.dot_general(lhs, rhs, (((1,), (0,)), ((), ())), preferred_element_type=jnp.float32)


def norm_kernel(rank_ref, own_ref, core_ref, chip_ref, both_ref, gain_ref, full_ref, normed_ref):
    rank = rank_ref[0]
    width = own_ref.shape[1]
    pieces = [own_ref, core_ref, chip_ref, both_ref]
    values = [piece[...].astype(jnp.float32) for piece in pieces]
    total = sum(jnp.sum(v * v, axis=-1, keepdims=True) for v in values)
    scale = lax.rsqrt(total / full_ref.shape[1] + eps_norm)
    for flip, (piece, value) in enumerate(zip(pieces, values)):
        place = pl.multiple_of((rank ^ flip) * width, width)
        columns = pl.ds(place, width)
        full_ref[:, columns] = piece[...]
        normed_ref[:, columns] = (value * scale * gain_ref[:, columns]).astype(jnp.bfloat16)


def gather_norm(rank, pieces, gain):
    rows, width = pieces[0].shape
    block = 128
    full = width * len(pieces)
    piece_spec = pl.BlockSpec((block, width), lambda i, s: (i, 0))
    full_spec = pl.BlockSpec((block, full), lambda i, s: (i, 0))
    return pl.pallas_call(
        norm_kernel,
        out_shape=(
            jax.ShapeDtypeStruct((rows, full), jnp.bfloat16),
            jax.ShapeDtypeStruct((rows, full), jnp.bfloat16),
        ),
        grid_spec=pltpu.PrefetchScalarGridSpec(
            num_scalar_prefetch=1,
            grid=(rows // block,),
            in_specs=[piece_spec] * 4 + [pl.BlockSpec((1, full), lambda i, s: (0, 0))],
            out_specs=[full_spec, full_spec],
        ),
        name="gather_norm",
    )(rank.reshape(1), *pieces, gain.reshape(1, full))


def suffix_kernel(len_ref, q_ref, k_ref, v_ref, out_ref, lse_ref):
    first_len = len_ref[0]
    rows = q_ref.shape[1]
    block = 256
    heads = q_ref.shape[0] // HEAD_SIZE
    for start in range(0, rows, block):
        keys = start + block
        key_index = lax.broadcasted_iota(jnp.int32, (keys, block), 0)
        row_index = lax.broadcasted_iota(jnp.int32, (keys, block), 1) + start
        begin = jnp.where(row_index >= first_len, first_len, 0)
        allowed = (key_index <= row_index) & (key_index >= begin)
        for head in range(heads):
            band = pl.ds(head * HEAD_SIZE, HEAD_SIZE)
            scores = tn_dot(k_ref[band, :keys], q_ref[band, start : start + block]) * 0.125
            scores = jnp.where(allowed, scores, masked_score)
            row_max = jnp.max(scores, axis=0, keepdims=True)
            weights = jnp.exp(scores - row_max)
            total = jnp.sum(weights, axis=0, keepdims=True)
            blended = nn_dot(v_ref[band, :keys], weights.astype(jnp.bfloat16))
            out_ref[band, start : start + block] = blended / total
            lse_ref[head : head + 1, start : start + block] = row_max + jnp.log(total)


def suffix_attend(first_len, q_t, k_t, v_t):
    columns, rows = q_t.shape
    vmem = pl.BlockSpec(memory_space=pltpu.VMEM)
    return pl.pallas_call(
        suffix_kernel,
        out_shape=(
            jax.ShapeDtypeStruct((columns, rows), jnp.float32),
            jax.ShapeDtypeStruct((8, rows), jnp.float32),
        ),
        in_specs=[pl.BlockSpec(memory_space=pltpu.SMEM), vmem, vmem, vmem],
        out_specs=[vmem, vmem],
        cost_estimate=pl.CostEstimate(flops=4 * columns * rows * rows, bytes_accessed=3 << 20, transcendentals=5 * rows * rows),
        name="suffix_attend",
    )(first_len.reshape(1), q_t, k_t, v_t)


def prefix_kernel(n_units, meta_ref, own_q_ref, other_q_ref, *refs):
    units = refs[:n_units]
    own_out, own_lse, other_out, other_lse, buffer, sems = refs[n_units:]
    first_len = meta_ref[4]
    heads = own_q_ref.shape[0] // HEAD_SIZE
    block = 256
    blocks = own_q_ref.shape[1] // block
    for job in range(4):
        for unit in range(n_units):

            @pl.when(meta_ref[job] == unit)
            def _():
                pltpu.make_async_copy(units[unit], buffer.at[job], sems.at[job]).start()

    for request in range(2):
        for half in range(2):
            job = 2 * request + half
            pltpu.make_async_copy(units[0], buffer.at[job], sems.at[job]).wait()
        for part in range(blocks):
            start = part * block
            if request == 0:
                present = start < first_len
            else:
                present = start + block > first_len

            @pl.when(present)
            def _():
                lane = lax.broadcasted_iota(jnp.int32, (1, block), 1) + start
                mine = (lane < first_len) if request == 0 else (lane >= first_len)
                cols = pl.ds(start, block)

                for q_ref, out_ref, lse_ref in (
                    (own_q_ref, own_out, own_lse),
                    (other_q_ref, other_out, other_lse),
                ):

                    def one_head(head, carry, q_ref=q_ref, out_ref=out_ref, lse_ref=lse_ref):
                        band = pl.ds(pl.multiple_of(head * HEAD_SIZE, HEAD_SIZE), HEAD_SIZE)
                        query = q_ref[band, cols]
                        scores = [
                            tn_dot(buffer[2 * request + half, 0, band, :], query) * 0.125
                            for half in range(2)
                        ]
                        row_max = jnp.maximum(
                            jnp.max(scores[0], axis=0, keepdims=True),
                            jnp.max(scores[1], axis=0, keepdims=True),
                        )
                        weights = [jnp.exp(s - row_max) for s in scores]
                        total = jnp.sum(weights[0], axis=0, keepdims=True) + jnp.sum(
                            weights[1], axis=0, keepdims=True
                        )
                        blended = sum(
                            nn_dot(buffer[2 * request + half, 1, band, :], weights[half].astype(jnp.bfloat16))
                            for half in range(2)
                        )
                        out = (blended / total).astype(out_ref.dtype)
                        lse = row_max + jnp.log(total)
                        row = pl.ds(head, 1)
                        if request == 1:
                            out = jnp.where(mine, out, out_ref[band, cols])
                            lse = jnp.where(mine, lse, lse_ref[row, cols])
                        out_ref[band, cols] = out
                        lse_ref[row, cols] = lse
                        return carry

                    lax.fori_loop(0, heads, one_head, 0)


def prefix_attend(meta, own_q, other_q, units):
    columns, rows = own_q.shape
    vmem = pl.BlockSpec(memory_space=pltpu.VMEM)
    out = jax.ShapeDtypeStruct((columns, rows), jnp.float32)
    lse = jax.ShapeDtypeStruct((8, rows), jnp.float32)
    sent = jax.ShapeDtypeStruct((columns, rows), jnp.bfloat16)
    return pl.pallas_call(
        functools.partial(prefix_kernel, len(units)),
        out_shape=(out, lse, sent, lse),
        in_specs=[pl.BlockSpec(memory_space=pltpu.SMEM), vmem, vmem]
        + [pl.BlockSpec(memory_space=pl.ANY)] * len(units),
        out_specs=[vmem] * 4,
        scratch_shapes=[
            pltpu.VMEM((4,) + units[0].shape, jnp.bfloat16),
            pltpu.SemaphoreType.DMA((4,)),
        ],
        cost_estimate=pl.CostEstimate(flops=8 * columns * rows * 1536, bytes_accessed=6 << 20, transcendentals=10 * rows * 768),
        name="prefix_attend",
    )(meta, own_q, other_q, *units)


def local(
    n_req,
    tokens,
    owners,
    request_groups,
    request_lengths,
    prefix_cache,
    attn_gain,
    query_weight,
    key_value_weight,
    query_gain,
    key_gain,
    w_out,
    ffn_gain,
    w_gate_up,
    w_down,
):
    row_count, width = tokens.shape
    columns = query_weight.shape[1]
    head_count = columns // HEAD_SIZE
    rank = lax.axis_index("tp")
    my_req = lax.axis_index("req")
    core = rank % 2

    def across_chip(value):
        return lax.ppermute(value, "tp", [(i, i ^ 2) for i in range(4)])

    def across_core(value):
        return lax.ppermute(value, "tp", [(i, i ^ 1) for i in range(4)])

    length = n_req // 2
    share = prefix_cache.shape[2] // 2
    mine = lax.dynamic_slice_in_dim(jnp.transpose(prefix_cache[0], (0, 2, 1)), core * share, share, 2)

    def along(value, sources, step):
        pairs = [(2 * a + b, 2 * (a + step) + b) for a in sources for b in range(2)]
        return lax.ppermute(value, "req", pairs)

    def aside(value, members):
        return lax.ppermute(value, "req", [(2 * a + b, 2 * a + 1 - b) for a in members for b in range(2)])

    below, above = [mine], [mine]
    units = [mine, aside(mine, range(length))]
    for step in range(1, length):
        below.append(along(below[-1], range(step - 1, length - 1), 1))
        above.append(along(above[-1], range(1, length - step + 1), -1))
        units += [
            below[-1],
            aside(below[-1], range(step, length)),
            above[-1],
            aside(above[-1], range(0, length - step)),
        ]
    wanted = owners.reshape(-1, 2)[request_groups[0]].reshape(-1)
    distance = wanted // 2 - my_req // 2
    other_side = (wanted % 2 != my_req % 2).astype(jnp.int32)
    unit_index = jnp.where(
        distance == 0,
        0,
        jnp.where(distance < 0, -4 * distance - 2, 4 * distance),
    ) + other_side

    from_chip = across_chip(tokens)
    from_core = across_core(tokens)
    from_both = across_core(from_chip)
    full_rows, normalized_input = gather_norm(rank, (tokens, from_core, from_chip, from_both), attn_gain)

    w_out_held, _ = lax.optimization_barrier((w_out, from_chip))
    w_out_chip = across_chip(w_out_held)
    w_out_core = across_core(w_out_held)
    w_out_both = across_core(w_out_chip)
    w_out_all = jnp.concatenate([w_out, w_out_core, w_out_chip, w_out_both], axis=0)

    row_index = jnp.arange(row_count, dtype=jnp.int32)
    first_len = request_lengths[0, 0]
    segment = (row_index >= first_len).astype(jnp.int32)
    position = row_index - segment * first_len + PREFIX
    query_rows = jnp.dot(
        normalized_input, query_weight, preferred_element_type=jnp.float32
    ).reshape(row_count, head_count, HEAD_SIZE)
    query_rows = rotate(rms_scale(query_rows, query_gain), position).astype(jnp.bfloat16)
    key_value_rows = jnp.dot(
        normalized_input, key_value_weight, preferred_element_type=jnp.float32
    ).reshape(row_count, 2, head_count, HEAD_SIZE)
    key_rows = rotate(rms_scale(key_value_rows[:, 0], key_gain), position).astype(jnp.bfloat16)
    value_rows = key_value_rows[:, 1].astype(jnp.bfloat16)
    cache_rows = jnp.stack(
        [key_rows.reshape(row_count, columns), value_rows.reshape(row_count, columns)],
        axis=1,
    )
    own_q = query_rows.reshape(row_count, columns).T
    other_q = across_core(own_q)
    suffix_out, suffix_lse = suffix_attend(
        first_len, own_q, key_rows.reshape(row_count, columns).T, value_rows.reshape(row_count, columns).T
    )

    meta = jnp.concatenate([unit_index.astype(jnp.int32), first_len.reshape(1)])
    own_out, own_lse, sent_out, sent_lse = prefix_attend(meta, own_q, other_q, units)
    got_out = across_core(sent_out)
    got_lse = across_core(sent_lse)

    outs = [
        part.astype(jnp.float32).reshape(head_count, HEAD_SIZE, row_count)
        for part in (own_out, got_out, suffix_out)
    ]
    lses = [part[:head_count, None, :] for part in (own_lse, got_lse, suffix_lse)]
    top = jnp.maximum(jnp.maximum(lses[0], lses[1]), lses[2])
    factors = [jnp.exp(part - top) for part in lses]
    blended = sum(f * o for f, o in zip(factors, outs))
    attention = (blended / (factors[0] + factors[1] + factors[2])).astype(jnp.bfloat16)
    attention = attention.reshape(columns, row_count)

    att_chip = across_chip(attention)
    att_core = across_core(attention)
    att_both = across_core(att_chip)
    att_all = jnp.concatenate([attention, att_core, att_chip, att_both], axis=0)
    head_total = tn_dot(att_all, w_out_all)
    mixed = full_rows.astype(jnp.float32) + head_total

    normed_ffn = rms_scale(mixed, ffn_gain).astype(jnp.bfloat16)
    gate_up = jnp.einsum("rd,dgf->rgf", normed_ffn, w_gate_up, preferred_element_type=jnp.float32)
    activated = (jax.nn.silu(gate_up[:, 0]) * gate_up[:, 1]).astype(jnp.bfloat16)
    down_part = jnp.dot(activated, w_down, preferred_element_type=jnp.float32).astype(jnp.bfloat16)

    def block_of(value, flip):
        return lax.dynamic_slice_in_dim(value, (rank ^ flip) * width, width, 1)

    got_far = across_core(block_of(down_part, 3))
    got_near = across_core(block_of(down_part, 1))
    far_sum = (block_of(down_part, 2).astype(jnp.float32) + got_far.astype(jnp.float32)).astype(jnp.bfloat16)
    near_sum = block_of(mixed, 0) + block_of(down_part, 0).astype(jnp.float32) + got_near.astype(jnp.float32)
    hidden = near_sum + across_chip(far_sum).astype(jnp.float32)
    return (hidden.astype(jnp.bfloat16), cache_rows)


def solution(mesh):
    placed = (
        P("req", "tp"),
        P(),
        P("req", None),
        P("req", None),
        P("req", None, None, None),
        P(),
        P(None, "tp"),
        P(),
        P(),
        P(),
        P("tp", None),
        P(),
        P(None, None, "tp"),
        P("tp", None),
    )
    return jax.shard_map(
        functools.partial(local, mesh.shape["req"]),
        mesh=mesh,
        in_specs=placed,
        out_specs=(P("req", "tp"), P("req", None, None)),
        check_vma=False,
    )
```

time: 368 us -> 174 us (0.47)
  waiting for transfers between devices: 211 us -> 64.4 us
  Pallas kernels: 0 us -> 34.3 us
  local copies, waits for them, and re-layouts: 41.3 us -> 7.42 us
  loops' own time: 32.6 us -> 0 us
  starting transfers between devices: 0.16 us -> 29.3 us
  matrix products: 42.2 us -> 23.6 us
  between operations: 14.2 us -> 1.18 us
  other arithmetic: 24.7 us -> 12.9 us
    all_gather x2 -> x0, waiting for transfers between devices: 130 us -> none  [the longest x1 106 us: local(): shard_block = lax.all_gather(prefix_cache, 'req', axis=0, tiled=True)]
    ppermute x0 -> x28, waiting for transfers between devices: none -> 64.4 us  [the longest x4 32.1 us: across_chip(): return lax.ppermute(value, 'tp', [(i, i ^ 2) for i in range(4)])]
    psum x1 -> x0, waiting for transfers between devices: 49.9 us -> none  [local(): lax.psum(head_part.astype(jnp.bfloat16), 'tp').astype(jnp.float32)]
    pallas_call x0 -> x3, Pallas kernels: none -> 34.3 us  [the longest x1 23.8 us: prefix_attend(): pl.pallas_call(functools.partial(prefix_kernel, len(units)), out_shape=(o...]
    another operation x17 -> x0, loops' own time: 32.6 us -> none  [the longest x1 32 us: local(): buffers = lax.fori_loop(0, shard_block.shape[0], one_slot, buffers)]
    reduce_scatter x1 -> x0, waiting for transfers between devices: 29.3 us -> none  [local(): lax.psum_scatter(down_part.astype(jnp.bfloat16), 'tp', scatter_dimension=...]
    ppermute x0 -> x28, starting transfers between devices: none -> 29.3 us  [the longest x7 11.8 us: aside(): lax.ppermute(value, 'req', [(2 * a + b, 2 * a + 1 - b) for a in members f...]
    dynamic_update_slice x8 -> x0, local copies, waits for them, and re-layouts: 19.7 us -> none  [the longest x4 18.2 us: place_half(): lax.dynamic_update_index_in_dim(out_buffer, half_out, half_index, 0)]
  transfers between devices with their start and end apart: 4 -> 28, of which waited for: 4 -> 11; matrix products, arithmetic and copies ran while one was open for 4% -> 10% of each run, Pallas kernels for 0% -> 20%
where the time goes in v1:
time: 174 us; the launch traced here: 173 us
  waiting for transfers between devices  64.4 us (37%)
  Pallas kernels  34.3 us (20%)
  starting transfers between devices  29.3 us (17%)
  matrix products  23.6 us (14%)
  other arithmetic  12.9 us (7%)
  local copies, waits for them, and re-layouts  7.42 us (4%)
    ppermute x4, waiting for transfers between devices, across_chip(): return lax.ppermute(value, 'tp', [(i, i ^ 2) for i in range(4)])  32.1 us
    pallas_call x1, Pallas kernels, prefix_attend(): pl.pallas_call(functools.partial(prefix_kernel, len(units)), out_shape=(o...  23.8 us
    ppermute x7, waiting for transfers between devices, aside(): lax.ppermute(value, 'req', [(2 * a + b, 2 * a + 1 - b) for a in members f...  21.2 us
    ppermute x7, starting transfers between devices, aside(): lax.ppermute(value, 'req', [(2 * a + b, 2 * a + 1 - b) for a in members f...  11.8 us
    ppermute x6, starting transfers between devices, along(): return lax.ppermute(value, 'req', pairs)  11.7 us
    dot_general x1, matrix products, local(): jnp.einsum('rd,dgf->rgf', normed_ffn, w_gate_up, preferred_element_type=j...  10.5 us
    ppermute x6, waiting for transfers between devices, along(): return lax.ppermute(value, 'req', pairs)  6.07 us
    pallas_call x1, Pallas kernels, suffix_attend(): pl.pallas_call(suffix_kernel, out_shape=(jax.ShapeDtypeStruct((columns, r...  5.81 us
  transfers between devices with their start and end apart: 28, of which 11 were waited for; matrix products, arithmetic and copies ran while one was open for 10% of the time, Pallas kernels for 20%

profile of v1, /device:TPU:0, one launch (start us, length us, event | category | flops | bytes accessed | tf_op | source)
XLA Modules:
  0.0 173.0 jit_solution(11118068057044307386)
XLA Ops:
  0.7 1.2 dynamic-slice_bitcast_fusion.refs_0_
  1.9 5.7 %collective-permute-start.5 = (bf16[2,320,384]{2,1,0:T(8,128)(2,1)S(1)}, bf16[2,320,384]{2,1,0:T(8,128)(2,1)}, u32[]{:S(2)}, u32[]{:S(2)}) collective-permute-start(bf16[2,320,384]{2,1,0:T(8,128)(2,1)S(1)} %dynamic-slice_bitcast_fusion.refs_0_), channel_id=1, source_target_pairs={{0,8},{4,12},{8,16},{12,20},{16,24},{20,28},{1,9},{5,13},{9,17},{1... | collective-permute-start | bytes 1474568 | tf_op jit(solution)/shard_map/ppermute | solution.py:249
  7.7 1.3 collective-permute-start.7
  9.0 1.6 collective-permute-start.4
  10.5 1.5 collective-permute-start.1
  12.0 0.7 reshape.197
  12.8 0.7 fusion.33
  13.4 0.6 gather_fusion
  14.0 0.1 reshape.198
  14.1 9.9 %collective-permute-done.1.chip_ref = bf16[512,512]{1,0:T(8,128)(2,1)} collective-permute-done((bf16[512,512]{1,0:T(8,128)(2,1)}, bf16[512,512]{1,0:T(8,128)(2,1)}, u32[]{:S(2)}, u32[]{:S(2)}) %collective-permute-start.1) | collective-permute-done | bytes 524320 | tf_op jit(solution)/shard_map/ppermute | solution.py:238
  24.0 1.3 pad_add_fusion.meta_ref
  25.2 0.7 add_convert_fusion.3
  25.9 0.3 multiply_cosine_fusion
  26.2 1.4 collective-permute-start.9
  27.7 1.5 collective-permute-start.6
  29.2 1.3 collective-permute-start.11
  30.5 1.6 collective-permute-start.23
  32.0 4.7 %gather_norm.1 = (bf16[512,2048]{1,0:T(8,128)(2,1)}, bf16[512,2048]{1,0:T(8,128)(2,1)}) custom-call(s32[1]{0:T(128)} %bitcast.rank_ref, bf16[512,512]{1,0:T(8,128)(2,1)} %own_ref.1, bf16[512,512]{1,0:T(8,128)(2,1)} %collective-permute-done.core_ref, bf16[512,512]{1,0:T(8,128)(2,1)} %collective-permute-done.1.chip_ref, ...), custom_call_target="tpu_custom_call" | custom-call | tf_op jit(solution)/shard_map/gather_norm/pallas_call | solution.py:69
  36.7 3.3 %fusion.37 = f32[512,640]{0,1:T(8,128)S(1)} fusion(bf16[512,2048]{1,0:T(8,128)(2,1)} %get-tuple-element.12, bf16[2048,640]{1,0:T(8,128)(2,1)S(1)} %copy-done), kind=kOutput, calls=%fused_computation.84 | convolution fusion | flops 1342177280 | bytes 6029312 | tf_op jit(solution)/shard_map/dot_general | solution.py:293
  40.0 0.9 fusion.36
  40.9 0.1 multiply_reduce_fusion.2
  41.0 2.4 %collective-permute-start.8 = (bf16[2,320,384]{2,1,0:T(8,128)(2,1)}, bf16[2,320,384]{2,1,0:T(8,128)(2,1)S(1)}, u32[]{:S(2)}, u32[]{:S(2)}) collective-permute-start(bf16[2,320,384]{2,1,0:T(8,128)(2,1)} %collective-permute-done.7.refs_4_), channel_id=1, source_target_pairs={{0,4},{4,0},{8,12},{12,8},{16,20},{20,16},{1,5},{5,1},{9,13},{13,9... | collective-permute-start | bytes 1474568 | tf_op jit(solution)/shard_map/ppermute | solution.py:252
  43.5 0.1 multiply_multiply_fusion.1
  43.6 0.7 collective-permute-start.13
  44.3 3.8 %collective-permute-done.11.refs_8_ = bf16[2,320,384]{2,1,0:T(8,128)(2,1)} collective-permute-done((bf16[2,320,384]{2,1,0:T(8,128)(2,1)}, bf16[2,320,384]{2,1,0:T(8,128)(2,1)}, u32[]{:S(2)}, u32[]{:S(2)}) %collective-permute-start.11) | collective-permute-done | bytes 491552 | tf_op jit(solution)/shard_map/ppermute | solution.py:249
  48.1 1.3 collective-permute-start.15
  49.3 0.1 subtract_convert_fusion
  49.5 0.7 collective-permute-start.10
  50.2 6.3 %collective-permute-done.8.refs_5_ = bf16[2,320,384]{2,1,0:T(8,128)(2,1)S(1)} collective-permute-done((bf16[2,320,384]{2,1,0:T(8,128)(2,1)}, bf16[2,320,384]{2,1,0:T(8,128)(2,1)S(1)}, u32[]{:S(2)}, u32[]{:S(2)}) %collective-permute-start.8) | collective-permute-done | bytes 491552 | tf_op jit(solution)/shard_map/ppermute | solution.py:252
  56.6 1.5 collective-permute-done.3.other_q_ref
  58.1 2.4 %collective-permute-start.12 = (bf16[2,320,384]{2,1,0:T(8,128)(2,1)}, bf16[2,320,384]{2,1,0:T(8,128)(2,1)S(1)}, u32[]{:S(2)}, u32[]{:S(2)}) collective-permute-start(bf16[2,320,384]{2,1,0:T(8,128)(2,1)} %collective-permute-done.11.refs_8_), channel_id=1, source_target_pairs={{0,4},{4,0},{8,12},{12,8},{1,5},{5,1},{9,13},{13,9},{2,6},{6,2},{1... | collective-permute-start | bytes 1474568 | tf_op jit(solution)/shard_map/ppermute | solution.py:252
  60.6 0.7 collective-permute-start.14
  61.3 2.3 %collective-permute-done.15.refs_12_ = bf16[2,320,384]{2,1,0:T(8,128)(2,1)S(1)} collective-permute-done((bf16[2,320,384]{2,1,0:T(8,128)(2,1)}, bf16[2,320,384]{2,1,0:T(8,128)(2,1)S(1)}, u32[]{:S(2)}, u32[]{:S(2)}) %collective-permute-start.15) | collective-permute-done | bytes 491552 | tf_op jit(solution)/shard_map/ppermute | solution.py:249
  63.6 2.5 %collective-permute-start.16 = (bf16[2,320,384]{2,1,0:T(8,128)(2,1)S(1)}, bf16[2,320,384]{2,1,0:T(8,128)(2,1)}, u32[]{:S(2)}, u32[]{:S(2)}) collective-permute-start(bf16[2,320,384]{2,1,0:T(8,128)(2,1)S(1)} %collective-permute-done.15.refs_12_), channel_id=1, source_target_pairs={{0,4},{4,0},{1,5},{5,1},{2,6},{6,2},{3,7},{7,3}} | collective-permute-start | bytes 1474568 | tf_op jit(solution)/shard_map/ppermute | solution.py:252
  66.1 0.1 multiply_multiply_fusion
  66.3 0.5 collective-permute-start.24
  66.8 0.1 multiply_subtract_fusion
  66.9 0.8 slice.89
  67.7 6.6 %collective-permute-done.12.refs_9_ = bf16[2,320,384]{2,1,0:T(8,128)(2,1)S(1)} collective-permute-done((bf16[2,320,384]{2,1,0:T(8,128)(2,1)}, bf16[2,320,384]{2,1,0:T(8,128)(2,1)S(1)}, u32[]{:S(2)}, u32[]{:S(2)}) %collective-permute-start.12) | collective-permute-done | bytes 491552 | tf_op jit(solution)/shard_map/ppermute | solution.py:252
  74.3 0.8 copy-done.11
  75.1 0.8 copy-done.12
  75.9 8.3 %collective-permute-done.16.refs_13_ = bf16[2,320,384]{2,1,0:T(8,128)(2,1)} collective-permute-done((bf16[2,320,384]{2,1,0:T(8,128)(2,1)S(1)}, bf16[2,320,384]{2,1,0:T(8,128)(2,1)}, u32[]{:S(2)}, u32[]{:S(2)}) %collective-permute-start.16) | collective-permute-done | bytes 491552 | tf_op jit(solution)/shard_map/ppermute | solution.py:252
  84.1 23.8 %prefix_attend.1 = (f32[320,512]{1,0:T(8,128)}, f32[8,512]{1,0:T(8,128)}, bf16[320,512]{1,0:T(8,128)(2,1)}, f32[8,512]{1,0:T(8,128)}) custom-call(s32[5]{0:T(128)} %pad_add_fusion.meta_ref, bf16[320,512]{1,0:T(8,128)(2,1)} %bitcast.82, bf16[320,512]{1,0:T(8,128)(2,1)} %copy-done.13, bf16[2,320,384]{2,1,0:T(8,128)(2,1)} %copy-done.2, ...), custom_call_target="tpu_custom_call" | custom-call | flops 2013265920 | bytes 6291456 | tf_op jit(solution)/shard_map/prefix_attend/pallas_call | solution.py:198
  108.0 0.8 maximum_convert_fusion
  108.8 0.5 collective-permute-start.17
  109.3 5.8 %suffix_attend.1 = (f32[320,512]{1,0:T(8,128)}, f32[8,512]{1,0:T(8,128)}) custom-call(s32[1]{0:T(128)} %bitcast.87, bf16[320,512]{1,0:T(8,128)(2,1)} %bitcast.83, bf16[320,512]{1,0:T(8,128)(2,1)} %bitcast.79, bf16[320,512]{1,0:T(8,128)(2,1)} %bitcast.77), custom_call_target="tpu_custom_call" | custom-call | flops 335544320 | bytes 3145728 | tf_op jit(solution)/shard_map/suffix_attend/pallas_call | solution.py:111
  115.1 0.7 add_add_fusion
  115.9 2.1 %fusion.29 = bf16[320,512]{1,0:T(8,128)(2,1)} fusion(f32[320,512]{1,0:T(8,128)} %get-tuple-element.18, f32[320,512]{1,0:T(8,128)S(1)} %copy-done.6, bf16[320,512]{1,0:T(8,128)(2,1)} %collective-permute-done.18, f32[5,512]{1,0:T(8,128)S(1)} %get-tuple-element.20, f32[5,512]{1,0:T(8,128)S(1)} %get-tuple-element.23, f32[5,512]{1,0:T(8,128)S(1)} %get-tuple-element.21, ...), kind=kLoop, calls=%fused_computation.37 | loop fusion | flops 1310720 | bytes 2007040 | tf_op jit(solution)/shard_map/convert_element_type | solution.py:321
  118.0 0.5 collective-permute-start.20
  118.5 9.4 %collective-permute-done.20 = bf16[320,512]{1,0:T(8,128)(2,1)S(1)} collective-permute-done((bf16[320,512]{1,0:T(8,128)(2,1)}, bf16[320,512]{1,0:T(8,128)(2,1)S(1)}, u32[]{:S(2)}, u32[]{:S(2)}) %collective-permute-start.20) | collective-permute-done | bytes 327712 | tf_op jit(solution)/shard_map/ppermute | solution.py:238
  127.9 1.7 %collective-permute-done.21 = bf16[320,512]{1,0:T(8,128)(2,1)} collective-permute-done((bf16[320,512]{1,0:T(8,128)(2,1)S(1)}, bf16[320,512]{1,0:T(8,128)(2,1)}, u32[]{:S(2)}, u32[]{:S(2)}) %collective-permute-start.21) | collective-permute-done | bytes 327712 | tf_op jit(solution)/shard_map/ppermute | solution.py:241
  129.7 5.7 %multiply_reduce_fusion = (f32[512]{0:T(512)S(1)}, f32[512,2048]{1,0:T(8,128)S(1)}) fusion(bf16[320,2048]{1,0:T(8,128)(2,1)} %collective-permute-done.24, bf16[320,2048]{1,0:T(8,128)(2,1)} %collective-permute-done.23, bf16[320,2048]{1,0:T(8,128)(2,1)} %collective-permute-done.22, bf16[320,2048]{1,0:T(8,128)(2,1)} %param.24, ...), kind=kOutput, calls=%fused_computation.12 | convolution fusion | flops 2714762752 | bytes 12847104 | tf_op jit(solution)/shard_map/dot_general | solution.py:42
  135.4 10.5 %fusion = f32[512,2,1280]{2,0,1:T(8,128)S(1)} fusion(bf16[2048,2,1280]{2,1,0:T(2,128)(2,1)} %param.26, f32[512,2048]{1,0:T(8,128)S(1)} %get-tuple-element.33, f32[2048]{0:T(1024)S(1)} %copy-done.20, f32[512]{0:T(512)S(1)} %add_rsqrt_fusion.2), kind=kOutput, calls=%fused_computation.1 | convolution fusion | flops 5371854848 | bytes 19933184 | tf_op jit(solution)/shard_map/rd,dgf->rgf/dot_general | solution.py:332
  145.9 3.3 %convolution_convert_fusion = bf16[512,2048]{1,0:T(8,128)(2,1)S(1)} fusion(bf16[1280,2048]{1,0:T(8,128)(2,1)S(1)} %bitcast.89, f32[512,2,1280]{2,0,1:T(8,128)S(1)} %fusion), kind=kOutput, calls=%fused_computation.14 | convolution fusion | flops 2689335296 | bytes 12582912 | tf_op jit(solution)/shard_map/dot_general | solution.py:334
  149.2 1.4 copy-done.1
  150.6 1.1 constant_dynamic-slice_fusion.1
  151.6 0.1 collective-permute-start.26
  151.7 0.4 collective-permute-start.25
  152.1 1.7 %collective-permute-done.26 = bf16[512,512]{1,0:T(8,128)(2,1)} collective-permute-done((bf16[512,512]{1,0:T(8,128)(2,1)}, bf16[512,512]{1,0:T(8,128)(2,1)}, u32[]{:S(2)}, u32[]{:S(2)}) %collective-permute-start.26) | collective-permute-done | bytes 524320 | tf_op jit(solution)/shard_map/ppermute | solution.py:241
  153.9 2.1 %add_convert_fusion.1 = bf16[512,512]{1,0:T(8,128)(2,1)} fusion(bf16[512,512]{1,0:T(8,128)(2,1)} %collective-permute-done.26, bf16[512,2048]{1,0:T(8,128)(2,1)} %copy-done.1, s32[]{:T(128)S(6)} %select_n.70), kind=kLoop, calls=%fused_computation.31 | loop fusion | flops 1048576 | bytes 1572868 | tf_op jit(solution)/shard_map/convert_element_type | solution.py:341
  156.0 0.5 collective-permute-start.27
  156.6 0.9 pad_maximum_fusion
  157.4 12.8 %collective-permute-done.27 = bf16[512,512]{1,0:T(8,128)(2,1)} collective-permute-done((bf16[512,512]{1,0:T(8,128)(2,1)}, bf16[512,512]{1,0:T(8,128)(2,1)}, u32[]{:S(2)}, u32[]{:S(2)}) %collective-permute-start.27) | collective-permute-done | bytes 524320 | tf_op jit(solution)/shard_map/ppermute | solution.py:238
  170.3 2.8 %add_convert_fusion = bf16[512,512]{1,0:T(8,128)(2,1)} fusion(bf16[512,512]{1,0:T(8,128)(2,1)} %collective-permute-done.27, bf16[512,512]{1,0:T(8,128)(2,1)} %collective-permute-done.25, f32[512,2048]{1,0:T(8,128)} %copy-done.14, s32[]{:T(128)S(6)} %select_n.68, bf16[512,2048]{1,0:T(8,128)(2,1)} %copy-done.1), kind=kLoop, calls=%fused_computation.30 | loop fusion | flops 1835008 | bytes 3145732 | tf_op jit(solution)/shard_map/convert_element_type | solution.py:344
  (76 shorter events, 0.5 us)
Async XLA Ops:
  0.6 36.0 %copy-start = (bf16[2048,640]{1,0:T(8,128)(2,1)S(1)}, bf16[2048,640]{1,0:T(8,128)(2,1)}, u32[]{:S(2)}) copy-start(bf16[2048,640]{1,0:T(8,128)(2,1)} %param.21) | copy-start | bytes 7864324
  1.9 38.1 %copy-start.2 = (bf16[2,320,384]{2,1,0:T(8,128)(2,1)}, bf16[2,320,384]{2,1,0:T(8,128)(2,1)S(1)}, u32[]{:S(2)}) copy-start(bf16[2,320,384]{2,1,0:T(8,128)(2,1)S(1)} %dynamic-slice_bitcast_fusion.refs_0_) | copy-start | bytes 1474564
  1.9 24.3 %collective-permute-start.5 = (bf16[2,320,384]{2,1,0:T(8,128)(2,1)S(1)}, bf16[2,320,384]{2,1,0:T(8,128)(2,1)}, u32[]{:S(2)}, u32[]{:S(2)}) collective-permute-start(bf16[2,320,384]{2,1,0:T(8,128)(2,1)S(1)} %dynamic-slice_bitcast_fusion.refs_0_), channel_id=1, source_target_pairs={{0,8},{4,12},{8,16},{12,20},{16,24},{20,28},{1,9},{5,13},{9,17},{1... | collective-permute-start | bytes 1474568 | tf_op jit(solution)/shard_map/ppermute | solution.py:249
  7.7 20.0 %collective-permute-start.7 = (bf16[2,320,384]{2,1,0:T(8,128)(2,1)S(1)}, bf16[2,320,384]{2,1,0:T(8,128)(2,1)}, u32[]{:S(2)}, u32[]{:S(2)}) collective-permute-start(bf16[2,320,384]{2,1,0:T(8,128)(2,1)S(1)} %dynamic-slice_bitcast_fusion.refs_0_), channel_id=1, source_target_pairs={{8,0},{12,4},{16,8},{20,12},{24,16},{28,20},{9,1},{13,5},{17,9},{2... | collective-permute-start | bytes 1474568 | tf_op jit(solution)/shard_map/ppermute | solution.py:249
  9.0 32.1 %collective-permute-start.4 = (bf16[2,320,384]{2,1,0:T(8,128)(2,1)S(1)}, bf16[2,320,384]{2,1,0:T(8,128)(2,1)}, u32[]{:S(2)}, u32[]{:S(2)}) collective-permute-start(bf16[2,320,384]{2,1,0:T(8,128)(2,1)S(1)} %dynamic-slice_bitcast_fusion.refs_0_), channel_id=1, source_target_pairs={{0,4},{4,0},{8,12},{12,8},{16,20},{20,16},{24,28},{28,24},{1,5},{5... | collective-permute-start | bytes 1474568 | tf_op jit(solution)/shard_map/ppermute | solution.py:252
  10.5 13.4 %collective-permute-start.1 = (bf16[512,512]{1,0:T(8,128)(2,1)}, bf16[512,512]{1,0:T(8,128)(2,1)}, u32[]{:S(2)}, u32[]{:S(2)}) collective-permute-start(bf16[512,512]{1,0:T(8,128)(2,1)} %own_ref.1), channel_id=1, source_target_pairs={{0,2},{1,3},{2,0},{3,1},{4,6},{5,7},{6,4},{7,5},{8,10},{9,11},{10,... | collective-permute-start | bytes 1572872 | tf_op jit(solution)/shard_map/ppermute | solution.py:238
  12.0 17.1 %collective-permute-start = (bf16[512,512]{1,0:T(8,128)(2,1)}, bf16[512,512]{1,0:T(8,128)(2,1)}, u32[]{:S(2)}, u32[]{:S(2)}) collective-permute-start(bf16[512,512]{1,0:T(8,128)(2,1)} %own_ref.1), channel_id=1, source_target_pairs={{0,1},{1,0},{2,3},{3,2},{4,5},{5,4},{6,7},{7,6},{8,9},{9,8},{10,11... | collective-permute-start | bytes 1572872 | tf_op jit(solution)/shard_map/ppermute | solution.py:241
  24.0 6.5 %collective-permute-start.2 = (bf16[512,512]{1,0:T(8,128)(2,1)}, bf16[512,512]{1,0:T(8,128)(2,1)}, u32[]{:S(2)}, u32[]{:S(2)}) collective-permute-start(bf16[512,512]{1,0:T(8,128)(2,1)} %collective-permute-done.1.chip_ref), channel_id=1, source_target_pairs={{0,1},{1,0},{2,3},{3,2},{4,5},{5,4},{6,7},{7,6},{8,9},{9,8},{10,11... | collective-permute-start | bytes 1572872 | tf_op jit(solution)/shard_map/ppermute | solution.py:241
  26.2 17.4 %collective-permute-start.9 = (bf16[2,320,384]{2,1,0:T(8,128)(2,1)}, bf16[2,320,384]{2,1,0:T(8,128)(2,1)}, u32[]{:S(2)}, u32[]{:S(2)}) collective-permute-start(bf16[2,320,384]{2,1,0:T(8,128)(2,1)} %collective-permute-done.5.refs_2_), channel_id=1, source_target_pairs={{8,16},{12,20},{16,24},{20,28},{9,17},{13,21},{17,25},{21,29},{10,... | collective-permute-start | bytes 1474568 | tf_op jit(solution)/shard_map/ppermute | solution.py:249
  27.7 21.8 %collective-permute-start.6 = (bf16[2,320,384]{2,1,0:T(8,128)(2,1)}, bf16[2,320,384]{2,1,0:T(8,128)(2,1)}, u32[]{:S(2)}, u32[]{:S(2)}) collective-permute-start(bf16[2,320,384]{2,1,0:T(8,128)(2,1)} %collective-permute-done.5.refs_2_), channel_id=1, source_target_pairs={{8,12},{12,8},{16,20},{20,16},{24,28},{28,24},{9,13},{13,9},{17,21... | collective-permute-start | bytes 1474568 | tf_op jit(solution)/shard_map/ppermute | solution.py:252
  29.2 18.9 %collective-permute-start.11 = (bf16[2,320,384]{2,1,0:T(8,128)(2,1)}, bf16[2,320,384]{2,1,0:T(8,128)(2,1)}, u32[]{:S(2)}, u32[]{:S(2)}) collective-permute-start(bf16[2,320,384]{2,1,0:T(8,128)(2,1)} %collective-permute-done.7.refs_4_), channel_id=1, source_target_pairs={{8,0},{12,4},{16,8},{20,12},{9,1},{13,5},{17,9},{21,13},{10,2},{14... | collective-permute-start | bytes 1474568 | tf_op jit(solution)/shard_map/ppermute | solution.py:249
  30.5 35.9 %collective-permute-start.23 = (bf16[320,2048]{1,0:T(8,128)(2,1)}, bf16[320,2048]{1,0:T(8,128)(2,1)}, u32[]{:S(2)}, u32[]{:S(2)}) collective-permute-start(bf16[320,2048]{1,0:T(8,128)(2,1)} %param.24), channel_id=1, source_target_pairs={{0,2},{1,3},{2,0},{3,1},{4,6},{5,7},{6,4},{7,5},{8,10},{9,11},{10,... | collective-permute-start | bytes 3932168 | tf_op jit(solution)/shard_map/ppermute | solution.py:238
  36.7 3.3 %copy-start.18 = (bf16[512,2048]{1,0:T(8,128)(2,1)S(1)}, bf16[512,2048]{1,0:T(8,128)(2,1)}, u32[]{:S(2)}) copy-start(bf16[512,2048]{1,0:T(8,128)(2,1)} %get-tuple-element.12) | copy-start | bytes 6291460
  36.7 3.3 %copy-start.19 = (bf16[2048,320]{0,1:T(8,128)(2,1)S(1)}, bf16[2048,320]{0,1:T(8,128)(2,1)}, u32[]{:S(2)}) copy-start(bf16[2048,320]{0,1:T(8,128)(2,1)} %param.20) | copy-start | bytes 3932164
  40.0 3.4 %copy-start.16 = (f32[64]{0:T(128)S(1)}, f32[64]{0:T(128)}, u32[]{:S(2)}) copy-start(f32[64]{0:T(128)} %param.22) | copy-start | bytes 772
  40.9 25.2 %copy-start.17 = (f32[64]{0:T(128)S(1)}, f32[64]{0:T(128)}, u32[]{:S(2)}) copy-start(f32[64]{0:T(128)} %param.23) | copy-start | bytes 772
  41.0 15.5 %collective-permute-start.8 = (bf16[2,320,384]{2,1,0:T(8,128)(2,1)}, bf16[2,320,384]{2,1,0:T(8,128)(2,1)S(1)}, u32[]{:S(2)}, u32[]{:S(2)}) collective-permute-start(bf16[2,320,384]{2,1,0:T(8,128)(2,1)} %collective-permute-done.7.refs_4_), channel_id=1, source_target_pairs={{0,4},{4,0},{8,12},{12,8},{16,20},{20,16},{1,5},{5,1},{9,13},{13,9... | collective-permute-start | bytes 1474568 | tf_op jit(solution)/shard_map/ppermute | solution.py:252
  43.6 16.9 %collective-permute-start.13 = (bf16[2,320,384]{2,1,0:T(8,128)(2,1)}, bf16[2,320,384]{2,1,0:T(8,128)(2,1)S(1)}, u32[]{:S(2)}, u32[]{:S(2)}) collective-permute-start(bf16[2,320,384]{2,1,0:T(8,128)(2,1)} %collective-permute-done.9.refs_6_), channel_id=1, source_target_pairs={{16,24},{20,28},{17,25},{21,29},{18,26},{22,30},{19,27},{23,31}} | collective-permute-start | bytes 1474568 | tf_op jit(solution)/shard_map/ppermute | solution.py:249
  48.1 15.5 %collective-permute-start.15 = (bf16[2,320,384]{2,1,0:T(8,128)(2,1)}, bf16[2,320,384]{2,1,0:T(8,128)(2,1)S(1)}, u32[]{:S(2)}, u32[]{:S(2)}) collective-permute-start(bf16[2,320,384]{2,1,0:T(8,128)(2,1)} %collective-permute-done.11.refs_8_), channel_id=1, source_target_pairs={{8,0},{12,4},{9,1},{13,5},{10,2},{14,6},{11,3},{15,7}} | collective-permute-start | bytes 1474568 | tf_op jit(solution)/shard_map/ppermute | solution.py:249
  49.5 34.6 %copy-start.5 = (bf16[512,5,64]{0,2,1:T(8,128)(2,1)}, bf16[512,5,64]{0,2,1:T(8,128)(2,1)S(1)}, u32[]{:S(2)}) copy-start(bf16[512,5,64]{0,2,1:T(8,128)(2,1)S(1)} %pad_maximum_fusion.1) | copy-start | bytes 983044
  49.5 16.7 %collective-permute-start.10 = (bf16[2,320,384]{2,1,0:T(8,128)(2,1)}, bf16[2,320,384]{2,1,0:T(8,128)(2,1)S(1)}, u32[]{:S(2)}, u32[]{:S(2)}) collective-permute-start(bf16[2,320,384]{2,1,0:T(8,128)(2,1)} %collective-permute-done.9.refs_6_), channel_id=1, source_target_pairs={{16,20},{20,16},{24,28},{28,24},{17,21},{21,17},{25,29},{29,25},{1... | collective-permute-start | bytes 1474568 | tf_op jit(solution)/shard_map/ppermute | solution.py:252
  56.5 11.2 %copy-start.7 = (bf16[2,320,384]{2,1,0:T(8,128)(2,1)}, bf16[2,320,384]{2,1,0:T(8,128)(2,1)S(1)}, u32[]{:S(2)}) copy-start(bf16[2,320,384]{2,1,0:T(8,128)(2,1)S(1)} %collective-permute-done.8.refs_5_) | copy-start | bytes 1474564
  56.5 1.6 collective-permute-start.3
  58.1 5.4 %copy-start.13 = (bf16[320,512]{1,0:T(8,128)(2,1)}, bf16[320,512]{1,0:T(8,128)(2,1)S(1)}, u32[]{:S(2)}) copy-start(bf16[320,512]{1,0:T(8,128)(2,1)S(1)} %collective-permute-done.3.other_q_ref) | copy-start | bytes 983044
  58.1 16.2 %collective-permute-start.12 = (bf16[2,320,384]{2,1,0:T(8,128)(2,1)}, bf16[2,320,384]{2,1,0:T(8,128)(2,1)S(1)}, u32[]{:S(2)}, u32[]{:S(2)}) collective-permute-start(bf16[2,320,384]{2,1,0:T(8,128)(2,1)} %collective-permute-done.11.refs_8_), channel_id=1, source_target_pairs={{0,4},{4,0},{8,12},{12,8},{1,5},{5,1},{9,13},{13,9},{2,6},{6,2},{1... | collective-permute-start | bytes 1474568 | tf_op jit(solution)/shard_map/ppermute | solution.py:252
  60.6 13.8 %copy-start.8 = (bf16[2,320,384]{2,1,0:T(8,128)(2,1)}, bf16[2,320,384]{2,1,0:T(8,128)(2,1)S(1)}, u32[]{:S(2)}) copy-start(bf16[2,320,384]{2,1,0:T(8,128)(2,1)S(1)} %collective-permute-done.13.refs_10_) | copy-start | bytes 1474564
  60.6 13.8 %collective-permute-start.14 = (bf16[2,320,384]{2,1,0:T(8,128)(2,1)S(1)}, bf16[2,320,384]{2,1,0:T(8,128)(2,1)S(1)}, u32[]{:S(2)}, u32[]{:S(2)}) collective-permute-start(bf16[2,320,384]{2,1,0:T(8,128)(2,1)S(1)} %collective-permute-done.13.refs_10_), channel_id=1, source_target_pairs={{24,28},{28,24},{25,29},{29,25},{26,30},{30,26},{27,31},{31,27}} | collective-permute-start | bytes 1474568 | tf_op jit(solution)/shard_map/ppermute | solution.py:252
  63.6 10.8 %copy-start.9 = (bf16[2,320,384]{2,1,0:T(8,128)(2,1)}, bf16[2,320,384]{2,1,0:T(8,128)(2,1)S(1)}, u32[]{:S(2)}) copy-start(bf16[2,320,384]{2,1,0:T(8,128)(2,1)S(1)} %collective-permute-done.15.refs_12_) | copy-start | bytes 1474564
  63.6 20.5 %collective-permute-start.16 = (bf16[2,320,384]{2,1,0:T(8,128)(2,1)S(1)}, bf16[2,320,384]{2,1,0:T(8,128)(2,1)}, u32[]{:S(2)}, u32[]{:S(2)}) collective-permute-start(bf16[2,320,384]{2,1,0:T(8,128)(2,1)S(1)} %collective-permute-done.15.refs_12_), channel_id=1, source_target_pairs={{0,4},{4,0},{1,5},{5,1},{2,6},{6,2},{3,7},{7,3}} | collective-permute-start | bytes 1474568 | tf_op jit(solution)/shard_map/ppermute | solution.py:252
  66.2 8.1 %copy-start.10 = (bf16[2,320,384]{2,1,0:T(8,128)(2,1)}, bf16[2,320,384]{2,1,0:T(8,128)(2,1)S(1)}, u32[]{:S(2)}) copy-start(bf16[2,320,384]{2,1,0:T(8,128)(2,1)S(1)} %collective-permute-done.10.refs_7_) | copy-start | bytes 1474564
  66.2 61.7 %collective-permute-start.22 = (bf16[320,2048]{1,0:T(8,128)(2,1)}, bf16[320,2048]{1,0:T(8,128)(2,1)}, u32[]{:S(2)}, u32[]{:S(2)}) collective-permute-start(bf16[320,2048]{1,0:T(8,128)(2,1)} %param.24), channel_id=1, source_target_pairs={{0,1},{1,0},{2,3},{3,2},{4,5},{5,4},{6,7},{7,6},{8,9},{9,8},{10,11... | collective-permute-start | bytes 3932168 | tf_op jit(solution)/shard_map/ppermute | solution.py:241
  66.3 63.3 %collective-permute-start.24 = (bf16[320,2048]{1,0:T(8,128)(2,1)}, bf16[320,2048]{1,0:T(8,128)(2,1)}, u32[]{:S(2)}, u32[]{:S(2)}) collective-permute-start(bf16[320,2048]{1,0:T(8,128)(2,1)} %collective-permute-done.23), channel_id=1, source_target_pairs={{0,1},{1,0},{2,3},{3,2},{4,5},{5,4},{6,7},{7,6},{8,9},{9,8},{10,11... | collective-permute-start | bytes 3932168 | tf_op jit(solution)/shard_map/ppermute | solution.py:241
  74.3 0.8 copy-start.11
  75.1 0.8 copy-start.12
  107.9 7.2 %copy-start.15 = (f32[8,512]{1,0:T(8,128)S(1)}, f32[8,512]{1,0:T(8,128)}, u32[]{:S(2)}) copy-start(f32[8,512]{1,0:T(8,128)} %get-tuple-element.13) | copy-start | bytes 49156
  108.0 7.9 %collective-permute-start.18 = (bf16[320,512]{1,0:T(8,128)(2,1)}, bf16[320,512]{1,0:T(8,128)(2,1)}, u32[]{:S(2)}, u32[]{:S(2)}) collective-permute-start(bf16[320,512]{1,0:T(8,128)(2,1)} %get-tuple-element.17), channel_id=1, source_target_pairs={{0,1},{1,0},{2,3},{3,2},{4,5},{5,4},{6,7},{7,6},{8,9},{9,8},{10,11... | collective-permute-start | bytes 983048 | tf_op jit(solution)/shard_map/ppermute | solution.py:241
  108.8 7.1 %copy-start.6 = (f32[320,512]{1,0:T(8,128)S(1)}, f32[320,512]{1,0:T(8,128)}, u32[]{:S(2)}) copy-start(f32[320,512]{1,0:T(8,128)} %get-tuple-element.16) | copy-start | bytes 1966084
  108.8 6.3 %collective-permute-start.17 = (f32[8,512]{1,0:T(8,128)}, f32[8,512]{1,0:T(8,128)S(1)}, u32[]{:S(2)}, u32[]{:S(2)}) collective-permute-start(f32[8,512]{1,0:T(8,128)} %get-tuple-element.14), channel_id=1, source_target_pairs={{0,1},{1,0},{2,3},{3,2},{4,5},{5,4},{6,7},{7,6},{8,9},{9,8},{10,11... | collective-permute-start | bytes 49160 | tf_op jit(solution)/shard_map/ppermute | solution.py:241
  118.0 9.9 %collective-permute-start.20 = (bf16[320,512]{1,0:T(8,128)(2,1)}, bf16[320,512]{1,0:T(8,128)(2,1)S(1)}, u32[]{:S(2)}, u32[]{:S(2)}) collective-permute-start(bf16[320,512]{1,0:T(8,128)(2,1)} %fusion.29), channel_id=1, source_target_pairs={{0,2},{1,3},{2,0},{3,1},{4,6},{5,7},{6,4},{7,5},{8,10},{9,11},{10,... | collective-permute-start | bytes 983048 | tf_op jit(solution)/shard_map/ppermute | solution.py:238
  118.5 9.4 %collective-permute-start.19 = (bf16[320,512]{1,0:T(8,128)(2,1)}, bf16[320,512]{1,0:T(8,128)(2,1)S(1)}, u32[]{:S(2)}, u32[]{:S(2)}) collective-permute-start(bf16[320,512]{1,0:T(8,128)(2,1)} %fusion.29), channel_id=1, source_target_pairs={{0,1},{1,0},{2,3},{3,2},{4,5},{5,4},{6,7},{7,6},{8,9},{9,8},{10,11... | collective-permute-start | bytes 983048 | tf_op jit(solution)/shard_map/ppermute | solution.py:241
  127.9 1.8 %collective-permute-start.21 = (bf16[320,512]{1,0:T(8,128)(2,1)S(1)}, bf16[320,512]{1,0:T(8,128)(2,1)}, u32[]{:S(2)}, u32[]{:S(2)}) collective-permute-start(bf16[320,512]{1,0:T(8,128)(2,1)S(1)} %collective-permute-done.20), channel_id=1, source_target_pairs={{0,1},{1,0},{2,3},{3,2},{4,5},{5,4},{6,7},{7,6},{8,9},{9,8},{10,11... | collective-permute-start | bytes 983048 | tf_op jit(solution)/shard_map/ppermute | solution.py:241
  129.7 5.7 %copy-start.20 = (f32[2048]{0:T(1024)S(1)}, f32[2048]{0:T(1024)}, u32[]{:S(2)}) copy-start(f32[2048]{0:T(1024)} %param.25) | copy-start | bytes 24580
  129.7 16.2 %slice-start = ((s8[5242880]{0:T(1024)(128)(4,1)}), s8[4194304]{0:T(1024)(128)(4,1)S(1)}, s32[]{:S(2)}) async-start(s8[5242880]{0:T(1024)(128)(4,1)} %bitcast.88), calls=%async_computation | async-start | bytes 8388608
  135.3 10.6 %copy-start.14 = (f32[512,2048]{1,0:T(8,128)}, f32[512,2048]{1,0:T(8,128)S(1)}, u32[]{:S(2)}) copy-start(f32[512,2048]{1,0:T(8,128)S(1)} %get-tuple-element.33) | copy-start | bytes 12582916
  135.4 10.6 %slice-start.1 = ((s8[5242880]{0:T(1024)(128)(4,1)}), s8[1048576]{0:T(1024)(128)(4,1)S(1)}, s32[]{:S(2)}) async-start(s8[5242880]{0:T(1024)(128)(4,1)} %bitcast.88), calls=%async_computation.1 | async-start | bytes 2097152
  149.2 1.4 copy-start.1
  150.6 6.0 %copy-start.3 = (bf16[512,1,5,64]{0,3,2,1:T(8,128)(2,1)S(1)}, bf16[512,1,5,64]{0,3,2,1:T(8,128)(2,1)}, u32[]{:S(2)}) copy-start(bf16[512,1,5,64]{0,3,2,1:T(8,128)(2,1)} %slice.89) | copy-start | bytes 983044
  150.6 6.0 %copy-start.4 = (bf16[512,5,64]{0,2,1:T(8,128)(2,1)S(1)}, bf16[512,5,64]{0,2,1:T(8,128)(2,1)}, u32[]{:S(2)}) copy-start(bf16[512,5,64]{0,2,1:T(8,128)(2,1)} %maximum_convert_fusion) | copy-start | bytes 983044
  151.6 2.3 %collective-permute-start.26 = (bf16[512,512]{1,0:T(8,128)(2,1)}, bf16[512,512]{1,0:T(8,128)(2,1)}, u32[]{:S(2)}, u32[]{:S(2)}) collective-permute-start(bf16[512,512]{1,0:T(8,128)(2,1)} %get-tuple-element.25), channel_id=1, source_target_pairs={{0,1},{1,0},{2,3},{3,2},{4,5},{5,4},{6,7},{7,6},{8,9},{9,8},{10,11... | collective-permute-start | bytes 1572872 | tf_op jit(solution)/shard_map/ppermute | solution.py:241
  151.7 5.7 %collective-permute-start.25 = (bf16[512,512]{1,0:T(8,128)(2,1)}, bf16[512,512]{1,0:T(8,128)(2,1)}, u32[]{:S(2)}, u32[]{:S(2)}) collective-permute-start(bf16[512,512]{1,0:T(8,128)(2,1)} %get-tuple-element.24), channel_id=1, source_target_pairs={{0,1},{1,0},{2,3},{3,2},{4,5},{5,4},{6,7},{7,6},{8,9},{9,8},{10,11... | collective-permute-start | bytes 1572872 | tf_op jit(solution)/shard_map/ppermute | solution.py:241
  156.0 14.3 %collective-permute-start.27 = (bf16[512,512]{1,0:T(8,128)(2,1)}, bf16[512,512]{1,0:T(8,128)(2,1)}, u32[]{:S(2)}, u32[]{:S(2)}) collective-permute-start(bf16[512,512]{1,0:T(8,128)(2,1)} %add_convert_fusion.1), channel_id=1, source_target_pairs={{0,2},{1,3},{2,0},{3,1},{4,6},{5,7},{6,4},{7,5},{8,10},{9,11},{10,... | collective-permute-start | bytes 1572872 | tf_op jit(solution)/shard_map/ppermute | solution.py:238

commit v2 on v1

--- a/solution.py
+++ b/solution.py
@@ -95,7 +95,7 @@
         allowed = (key_index <= row_index) & (key_index >= begin)
         for head in range(heads):
             band = pl.ds(head * HEAD_SIZE, HEAD_SIZE)
-            scores = tn_dot(k_ref[band, :keys], q_ref[band, start : start + block]) * 0.125
+            scores = tn_dot(k_ref[band, :keys], q_ref[band, start : start + block])
             scores = jnp.where(allowed, scores, masked_score)
             row_max = jnp.max(scores, axis=0, keepdims=True)
             weights = jnp.exp(scores - row_max)
@@ -121,91 +121,121 @@
     )(first_len.reshape(1), q_t, k_t, v_t)
 
 
-def prefix_kernel(n_units, meta_ref, own_q_ref, other_q_ref, *refs):
+def fold(values, op):
+    return op(values.reshape(values.shape[0] // 8, 8, values.shape[1]), axis=0)
+
+
+def prefix_kernel(block, chunk, n_units, meta_ref, own_q_ref, other_q_ref, *refs):
     units = refs[:n_units]
-    own_out, own_lse, other_out, other_lse, buffer, sems = refs[n_units:]
+    (own_out, own_lse, other_out, other_lse), scratch = refs[n_units : n_units + 4], refs[n_units + 4 :]
+    kv, q_buf, o_buf, l_buf, s_a, s_b, m_a, m_b, sems = scratch
     first_len = meta_ref[4]
-    heads = own_q_ref.shape[0] // HEAD_SIZE
-    block = 256
-    blocks = own_q_ref.shape[1] // block
+    share = units[0].shape[2]
+
+    def landing(job):
+        return kv.at[job // 2, :, :, pl.ds((job % 2) * share, share)]
+
     for job in range(4):
         for unit in range(n_units):
 
             @pl.when(meta_ref[job] == unit)
             def _():
-                pltpu.make_async_copy(units[unit], buffer.at[job], sems.at[job]).start()
-
-    for request in range(2):
-        for half in range(2):
-            job = 2 * request + half
-            pltpu.make_async_copy(units[0], buffer.at[job], sems.at[job]).wait()
-        for part in range(blocks):
-            start = part * block
-            if request == 0:
-                present = start < first_len
-            else:
-                present = start + block > first_len
-
-            @pl.when(present)
-            def _():
-                lane = lax.broadcasted_iota(jnp.int32, (1, block), 1) + start
-                mine = (lane < first_len) if request == 0 else (lane >= first_len)
-                cols = pl.ds(start, block)
-
-                for q_ref, out_ref, lse_ref in (
-                    (own_q_ref, own_out, own_lse),
-                    (other_q_ref, other_out, other_lse),
-                ):
-
-                    def one_head(head, carry, q_ref=q_ref, out_ref=out_ref, lse_ref=lse_ref):
-                        band = pl.ds(pl.multiple_of(head * HEAD_SIZE, HEAD_SIZE), HEAD_SIZE)
-                        query = q_ref[band, cols]
-                        scores = [
-                            tn_dot(buffer[2 * request + half, 0, band, :], query) * 0.125
-                            for half in range(2)
-                        ]
-                        row_max = jnp.maximum(
-                            jnp.max(scores[0], axis=0, keepdims=True),
-                            jnp.max(scores[1], axis=0, keepdims=True),
-                        )
-                        weights = [jnp.exp(s - row_max) for s in scores]
-                        total = jnp.sum(weights[0], axis=0, keepdims=True) + jnp.sum(
-                            weights[1], axis=0, keepdims=True
-                        )
-                        blended = sum(
-                            nn_dot(buffer[2 * request + half, 1, band, :], weights[half].astype(jnp.bfloat16))
-                            for half in range(2)
-                        )
-                        out = (blended / total).astype(out_ref.dtype)
-                        lse = row_max + jnp.log(total)
-                        row = pl.ds(head, 1)
-                        if request == 1:
-                            out = jnp.where(mine, out, out_ref[band, cols])
-                            lse = jnp.where(mine, lse, lse_ref[row, cols])
-                        out_ref[band, cols] = out
-                        lse_ref[row, cols] = lse
-                        return carry
-
-                    lax.fori_loop(0, heads, one_head, 0)
+                pltpu.make_async_copy(units[unit], landing(job), sems.at[job]).start()
+
+    columns, rows = own_q_ref.shape
+    q_buf[:columns] = own_q_ref[...]
+    q_buf[columns:] = other_q_ref[...]
+    for job in range(4):
+        pltpu.make_async_copy(units[0], landing(job), sems.at[job]).wait()
+
+    heads = columns // HEAD_SIZE
+    per = 2 * heads
+    keys = 2 * share
+    n_first = (first_len + block - 1) // block
+    skipped = first_len // block
+    pairs = n_first + rows // block - skipped
+
+    def place(task):
+        pair = task // per
+        head = task % per
+        second = (pair >= n_first).astype(jnp.int32)
+        part = jnp.where(second == 1, pair - n_first + skipped, pair)
+        cols = pl.ds(pl.multiple_of(part * block, block), block)
+        q_band = pl.ds(pl.multiple_of(head * HEAD_SIZE, HEAD_SIZE), HEAD_SIZE)
+        k_band = pl.ds(pl.multiple_of((head % heads) * HEAD_SIZE, HEAD_SIZE), HEAD_SIZE)
+        return second, part, cols, q_band, k_band, head
+
+    def step(now, later, s_now, m_now, s_later, m_later):
+        if now is not None:
+            second, part, cols, q_band, k_band, head = place(now)
+            peak = m_now[...]
+        later_second, _, later_cols, later_q, later_k, _ = place(later)
+        query = q_buf[later_q, later_cols]
+        top = total = blended = None
+        for start in range(0, keys, chunk):
+            span = pl.ds(start, chunk)
+            scores = tn_dot(kv[later_second, 0, later_k, span], query)
+            s_later[span, :] = scores
+            folded = fold(scores, jnp.max)
+            top = folded if top is None else jnp.maximum(top, folded)
+            if now is not None:
+                weights = jnp.exp(s_now[span, :] - peak)
+                folded = fold(weights, jnp.sum)
+                total = folded if total is None else total + folded
+                out = nn_dot(kv[second, 1, k_band, span], weights.astype(jnp.bfloat16))
+                blended = out if blended is None else blended + out
+        m_later[...] = jnp.max(top, axis=0, keepdims=True)
+        if now is not None:
+            total = jnp.sum(total, axis=0, keepdims=True)
+            lane = lax.broadcasted_iota(jnp.int32, (1, block), 1) + part * block
+            mine = (lane >= first_len).astype(jnp.int32) == second
+            o_buf[q_band, cols] = jnp.where(mine, blended * (1.0 / total), o_buf[q_band, cols])
+            row = pl.ds(head, 1)
+            l_buf[row, cols] = jnp.where(mine, peak + jnp.log(total), l_buf[row, cols])
+
+    step(None, 0, None, None, s_a, m_a)
+
+    def two(index, carry):
+        task = 2 * index
+        step(task, task + 1, s_a, m_a, s_b, m_b)
+        step(task + 1, jnp.minimum(task + 2, pairs * per - 1), s_b, m_b, s_a, m_a)
+        return carry
+
+    lax.fori_loop(0, pairs * heads, two, 0)
+    own_out[...] = o_buf[:columns]
+    other_out[...] = o_buf[columns:].astype(jnp.bfloat16)
+    own_lse[:heads] = l_buf[:heads]
+    other_lse[:heads] = l_buf[heads:per]
 
 
 def prefix_attend(meta, own_q, other_q, units):
     columns, rows = own_q.shape
+    share = units[0].shape[2]
+    block = 256
     vmem = pl.BlockSpec(memory_space=pltpu.VMEM)
     out = jax.ShapeDtypeStruct((columns, rows), jnp.float32)
     lse = jax.ShapeDtypeStruct((8, rows), jnp.float32)
     sent = jax.ShapeDtypeStruct((columns, rows), jnp.bfloat16)
     return pl.pallas_call(
-        functools.partial(prefix_kernel, len(units)),
+        functools.partial(prefix_kernel, block, 256, len(units)),
         out_shape=(out, lse, sent, lse),
         in_specs=[pl.BlockSpec(memory_space=pltpu.SMEM), vmem, vmem]
         + [pl.BlockSpec(memory_space=pl.ANY)] * len(units),
         out_specs=[vmem] * 4,
         scratch_shapes=[
-            pltpu.VMEM((4,) + units[0].shape, jnp.bfloat16),
+            pltpu.VMEM((2, 2, columns, 2 * share), jnp.bfloat16),
+            pltpu.VMEM((2 * columns, rows), jnp.bfloat16),
+            pltpu.VMEM((2 * columns, rows), jnp.float32),
+            pltpu.VMEM((16, rows), jnp.float32),
+            pltpu.VMEM((2 * share, block), jnp.float32),
+            pltpu.VMEM((2 * share, block), jnp.float32),
+            pltpu.VMEM((1, block), jnp.float32),
+            pltpu.VMEM((1, block), jnp.float32),
             pltpu.SemaphoreType.DMA((4,)),
         ],
-        cost_estimate=pl.CostEstimate(flops=8 * columns * rows * 1536, bytes_accessed=6 << 20, transcendentals=10 * rows * 768),
+        cost_estimate=pl.CostEstimate(
+            flops=16 * columns * rows * share, bytes_accessed=6 << 20, transcendentals=20 * rows * share
+        ),
         name="prefix_attend",
     )(meta, own_q, other_q, *units)
 
@@ -244,32 +274,19 @@
     share = prefix_cache.shape[2] // 2
     mine = lax.dynamic_slice_in_dim(jnp.transpose(prefix_cache[0], (0, 2, 1)), core * share, share, 2)
 
-    def along(value, sources, step):
-        pairs = [(2 * a + b, 2 * (a + step) + b) for a in sources for b in range(2)]
-        return lax.ppermute(value, "req", pairs)
-
-    def aside(value, members):
-        return lax.ppermute(value, "req", [(2 * a + b, 2 * a + 1 - b) for a in members for b in range(2)])
-
-    below, above = [mine], [mine]
-    units = [mine, aside(mine, range(length))]
-    for step in range(1, length):
-        below.append(along(below[-1], range(step - 1, length - 1), 1))
-        above.append(along(above[-1], range(1, length - step + 1), -1))
-        units += [
-            below[-1],
-            aside(below[-1], range(step, length)),
-            above[-1],
-            aside(above[-1], range(0, length - step)),
-        ]
+    def ring(value):
+        return lax.ppermute(value, "req", [(r, (r + 2) % n_req) for r in range(n_req)])
+
+    def aside(value):
+        return lax.ppermute(value, "req", [(r, r ^ 1) for r in range(n_req)])
+
+    held = [mine]
+    for _ in range(length - 1):
+        held.append(ring(held[-1]))
+    units = [part for unit in held for part in (unit, aside(unit))]
     wanted = owners.reshape(-1, 2)[request_groups[0]].reshape(-1)
-    distance = wanted // 2 - my_req // 2
-    other_side = (wanted % 2 != my_req % 2).astype(jnp.int32)
-    unit_index = jnp.where(
-        distance == 0,
-        0,
-        jnp.where(distance < 0, -4 * distance - 2, 4 * distance),
-    ) + other_side
+    distance = (my_req // 2 - wanted // 2) % length
+    unit_index = 2 * distance + (wanted % 2 != my_req % 2).astype(jnp.int32)
 
     from_chip = across_chip(tokens)
     from_core = across_core(tokens)
@@ -299,12 +316,13 @@
         [key_rows.reshape(row_count, columns), value_rows.reshape(row_count, columns)],
         axis=1,
     )
-    own_q = query_rows.reshape(row_count, columns).T
+    own_q = (query_rows * HEAD_SIZE**-0.5).reshape(row_count, columns).T
     other_q = across_core(own_q)
     suffix_out, suffix_lse = suffix_attend(
         first_len, own_q, key_rows.reshape(row_count, columns).T, value_rows.reshape(row_count, columns).T
     )
 
+    own_q, suffix_out, suffix_lse = lax.optimization_barrier((own_q, suffix_out, suffix_lse))
     meta = jnp.concatenate([unit_index.astype(jnp.int32), first_len.reshape(1)])
     own_out, own_lse, sent_out, sent_lse = prefix_attend(meta, own_q, other_q, units)
     got_out = across_core(sent_out)

time: 174 us -> 140 us (0.80)
  starting transfers between devices: 29.3 us -> 14.2 us
  waiting for transfers between devices: 64.4 us -> 52.5 us
  Pallas kernels: 34.3 us -> 26 us
    ppermute x13 -> x7, starting transfers between devices: 23.5 us -> 7.72 us  [the longest x4 6.14 us: aside(): return lax.ppermute(value, 'req', [(r, r ^ 1) for r in range(n_req)])]
    pallas_call x1, Pallas kernels: 23.8 us -> 15.5 us  [prefix_attend(): pl.pallas_call(functools.partial(prefix_kernel, block, 256, len(units)),...]
    ppermute x4, waiting for transfers between devices: 32.1 us -> 25.7 us  [across_chip(): return lax.ppermute(value, 'tp', [(i, i ^ 2) for i in range(4)])]
    ppermute x13 -> x7, waiting for transfers between devices: 27.3 us -> 21.9 us  [the longest x3 21.9 us: ring(): lax.ppermute(value, 'req', [(r, (r + 2) % n_req) for r in range(n_req)])]
    dot_general x1, matrix products: 0.88 us -> 2.83 us  [local(): jnp.dot(normalized_input, query_weight, preferred_element_type=jnp.float32)]
  transfers between devices with their start and end apart: 28 -> 22, of which waited for: 11 -> 9; matrix products, arithmetic and copies ran while one was open for 10% -> 14% of each run, Pallas kernels for 20% -> 19%
where the time goes in v2:
time: 140 us
  waiting for transfers between devices  52.5 us (38%)
  Pallas kernels  26 us (19%)
  matrix products  23.8 us (17%)
  starting transfers between devices  14.2 us (10%)
  other arithmetic  13.6 us (10%)
  local copies, waits for them, and re-layouts  8.5 us (6%)
    ppermute x4, waiting for transfers between devices, across_chip(): return lax.ppermute(value, 'tp', [(i, i ^ 2) for i in range(4)])  25.7 us
    ppermute x3, waiting for transfers between devices, ring(): lax.ppermute(value, 'req', [(r, (r + 2) % n_req) for r in range(n_req)])  21.9 us
    pallas_call x1, Pallas kernels, prefix_attend(): pl.pallas_call(functools.partial(prefix_kernel, block, 256, len(units)),...  15.5 us
    dot_general x1, matrix products, local(): jnp.einsum('rd,dgf->rgf', normed_ffn, w_gate_up, preferred_element_type=j...  10.5 us
    ppermute x4, starting transfers between devices, aside(): return lax.ppermute(value, 'req', [(r, r ^ 1) for r in range(n_req)])  6.14 us
    pallas_call x1, Pallas kernels, suffix_attend(): pl.pallas_call(suffix_kernel, out_shape=(jax.ShapeDtypeStruct((columns, r...  5.77 us
    dot_general x1, matrix products, tn_dot(): lax.dot_general(lhs, rhs, (((0,), (0,)), ((), ())), preferred_element_typ...  5.66 us
    ppermute x11, waiting for transfers between devices, across_core(): return lax.ppermute(value, 'tp', [(i, i ^ 1) for i in range(4)])  4.92 us
  transfers between devices with their start and end apart: 22, of which 9 were waited for; matrix products, arithmetic and copies ran while one was open for 14% of the time, Pallas kernels for 19%

profile of v2, /device:TPU:0, one launch (start us, length us, event | category | flops | bytes accessed | tf_op | source)
XLA Modules:
  0.0 139.6 jit_solution(931052722246324787)
XLA Ops:
  0.6 0.0 copy-start
  0.6 3.0 %collective-permute-start.1 = (bf16[512,512]{1,0:T(8,128)(2,1)}, bf16[512,512]{1,0:T(8,128)(2,1)S(1)}, u32[]{:S(2)}, u32[]{:S(2)}) collective-permute-start(bf16[512,512]{1,0:T(8,128)(2,1)} %own_ref.1), channel_id=1, source_target_pairs={{0,2},{1,3},{2,0},{3,1},{4,6},{5,7},{6,4},{7,5},{8,10},{9,11},{10,... | collective-permute-start | bytes 1572872 | tf_op jit(solution)/shard_map/ppermute | solution.py:268
  3.7 1.9 %dynamic-slice_bitcast_fusion.refs_0_ = bf16[2,320,384]{2,1,0:T(8,128)(2,1)} fusion(bf16[1,2,768,320]{2,3,1,0:T(8,128)(2,1)} %param.18, s32[]{:T(128)S(6)} %select_n.63), kind=kLoop, calls=%fused_computation.47 | loop fusion | bytes 983044 | tf_op jit(solution)/shard_map/dynamic_slice | solution.py:275
  5.5 1.6 %collective-permute-start.5 = (bf16[2,320,384]{2,1,0:T(8,128)(2,1)}, bf16[2,320,384]{2,1,0:T(8,128)(2,1)}, u32[]{:S(2)}, u32[]{:S(2)}) collective-permute-start(bf16[2,320,384]{2,1,0:T(8,128)(2,1)} %dynamic-slice_bitcast_fusion.refs_0_), channel_id=1, source_target_pairs={{0,8},{4,12},{8,16},{12,20},{16,24},{20,28},{24,0},{28,4},{1,9},{5... | collective-permute-start | bytes 1474568 | tf_op jit(solution)/shard_map/ppermute | solution.py:278
  7.1 1.5 %collective-permute-start.4 = (bf16[2,320,384]{2,1,0:T(8,128)(2,1)}, bf16[2,320,384]{2,1,0:T(8,128)(2,1)}, u32[]{:S(2)}, u32[]{:S(2)}) collective-permute-start(bf16[2,320,384]{2,1,0:T(8,128)(2,1)} %dynamic-slice_bitcast_fusion.refs_0_), channel_id=1, source_target_pairs={{0,4},{4,0},{8,12},{12,8},{16,20},{20,16},{24,28},{28,24},{1,5},{5... | collective-permute-start | bytes 1474568 | tf_op jit(solution)/shard_map/ppermute | solution.py:281
  8.6 0.7 reshape.199
  9.4 0.7 fusion.35
  10.0 0.6 gather_fusion
  10.6 0.1 reshape.200
  10.7 10.6 %collective-permute-done.5.refs_2_ = bf16[2,320,384]{2,1,0:T(8,128)(2,1)} collective-permute-done((bf16[2,320,384]{2,1,0:T(8,128)(2,1)}, bf16[2,320,384]{2,1,0:T(8,128)(2,1)}, u32[]{:S(2)}, u32[]{:S(2)}) %collective-permute-start.5) | collective-permute-done | bytes 491552 | tf_op jit(solution)/shard_map/ppermute | solution.py:278
  21.4 0.1 collective-permute-start.2
  21.5 1.3 pad_add_fusion.meta_ref
  22.7 0.7 add_convert_fusion.3
  23.4 0.3 multiply_cosine_fusion
  23.7 1.6 %collective-permute-start.6 = (bf16[2,320,384]{2,1,0:T(8,128)(2,1)}, bf16[2,320,384]{2,1,0:T(8,128)(2,1)}, u32[]{:S(2)}, u32[]{:S(2)}) collective-permute-start(bf16[2,320,384]{2,1,0:T(8,128)(2,1)} %collective-permute-done.5.refs_2_), channel_id=1, source_target_pairs={{0,4},{4,0},{8,12},{12,8},{16,20},{20,16},{24,28},{28,24},{1,5},{5... | collective-permute-start | bytes 1474568 | tf_op jit(solution)/shard_map/ppermute | solution.py:281
  25.3 0.0 collective-permute-done.core_ref
  25.3 0.5 collective-permute-start.17
  25.8 10.5 %collective-permute-done.7.refs_4_ = bf16[2,320,384]{2,1,0:T(8,128)(2,1)} collective-permute-done((bf16[2,320,384]{2,1,0:T(8,128)(2,1)}, bf16[2,320,384]{2,1,0:T(8,128)(2,1)}, u32[]{:S(2)}, u32[]{:S(2)}) %collective-permute-start.7) | collective-permute-done | bytes 491552 | tf_op jit(solution)/shard_map/ppermute | solution.py:278
  36.3 0.8 copy-done.6
  37.1 1.5 %collective-permute-start.8 = (bf16[2,320,384]{2,1,0:T(8,128)(2,1)}, bf16[2,320,384]{2,1,0:T(8,128)(2,1)}, u32[]{:S(2)}, u32[]{:S(2)}) collective-permute-start(bf16[2,320,384]{2,1,0:T(8,128)(2,1)} %collective-permute-done.7.refs_4_), channel_id=1, source_target_pairs={{0,4},{4,0},{8,12},{12,8},{16,20},{20,16},{24,28},{28,24},{1,5},{5... | collective-permute-start | bytes 1474568 | tf_op jit(solution)/shard_map/ppermute | solution.py:281
  38.6 4.7 %gather_norm.1 = (bf16[512,2048]{1,0:T(8,128)(2,1)}, bf16[512,2048]{1,0:T(8,128)(2,1)}) custom-call(s32[1]{0:T(128)} %bitcast.rank_ref, bf16[512,512]{1,0:T(8,128)(2,1)} %own_ref.1, bf16[512,512]{1,0:T(8,128)(2,1)} %collective-permute-done.core_ref, bf16[512,512]{1,0:T(8,128)(2,1)} %copy-done.5, bf16[512,512]{1,0:T(8,128)(2,1)} %copy-done.6, f32[1,2048]{1,0:T(1,128)} %bitcast.81), custom_call_target="tpu_custom_call" | custom-call | tf_op jit(solution)/shard_map/gather_norm/pallas_call | solution.py:69
  43.4 2.8 %fusion.38 = f32[512,320]{0,1:T(8,128)S(1)} fusion(bf16[512,2048]{1,0:T(8,128)(2,1)} %get-tuple-element.15, bf16[2048,320]{0,1:T(8,128)(2,1)} %param.20), kind=kOutput, calls=%fused_computation.86 | convolution fusion | flops 671088640 | bytes 4063232 | tf_op jit(solution)/shard_map/dot_general | solution.py:306
  46.2 0.1 multiply_reduce_fusion.2
  46.3 0.1 multiply_multiply_fusion.1
  46.4 0.1 subtract_convert_fusion
  46.5 1.2 copy-done.11
  47.8 1.6 %fusion.39 = f32[512,640]{0,1:T(8,128)S(1)} fusion(bf16[512,2048]{1,0:T(8,128)(2,1)S(1)} %copy-done.11, bf16[2048,640]{1,0:T(8,128)(2,1)S(1)} %copy-done), kind=kOutput, calls=%fused_computation.87 | convolution fusion | flops 1342177280 | bytes 6029312 | tf_op jit(solution)/shard_map/dot_general | solution.py:310
  49.4 0.1 multiply_reduce_fusion.1
  49.5 0.1 multiply_multiply_fusion
  49.6 0.8 collective-permute-done.9.refs_6_
  50.4 1.5 %collective-permute-start.10 = (bf16[2,320,384]{2,1,0:T(8,128)(2,1)}, bf16[2,320,384]{2,1,0:T(8,128)(2,1)}, u32[]{:S(2)}, u32[]{:S(2)}) collective-permute-start(bf16[2,320,384]{2,1,0:T(8,128)(2,1)} %collective-permute-done.9.refs_6_), channel_id=1, source_target_pairs={{0,4},{4,0},{8,12},{12,8},{16,20},{20,16},{24,28},{28,24},{1,5},{5... | collective-permute-start | bytes 1474568 | tf_op jit(solution)/shard_map/ppermute | solution.py:281
  51.9 0.8 maximum_multiply_fusion
  52.7 0.0 collective-permute-done.4.refs_1_
  52.7 0.5 collective-permute-start.3
  53.2 3.2 %collective-permute-done.17 = bf16[320,2048]{1,0:T(8,128)(2,1)} collective-permute-done((bf16[320,2048]{1,0:T(8,128)(2,1)}, bf16[320,2048]{1,0:T(8,128)(2,1)}, u32[]{:S(2)}, u32[]{:S(2)}) %collective-permute-start.17) | collective-permute-done | bytes 1310752 | tf_op jit(solution)/shard_map/ppermute | solution.py:268
  56.5 0.0 collective-permute-start.18
  56.5 0.1 multiply_subtract_fusion
  56.6 0.8 slice.89
  57.3 0.7 maximum_convert_fusion
  58.1 5.8 %suffix_attend.1 = (f32[320,512]{1,0:T(8,128)}, f32[8,512]{1,0:T(8,128)}) custom-call(s32[1]{0:T(128)} %bitcast.84, bf16[320,512]{1,0:T(8,128)(2,1)} %bitcast.8.q_ref.own_q_ref, bf16[320,512]{1,0:T(8,128)(2,1)} %bitcast.79, bf16[320,512]{1,0:T(8,128)(2,1)} %bitcast.77), custom_call_target="tpu_custom_call" | custom-call | flops 335544320 | bytes 3145728 | tf_op jit(solution)/shard_map/suffix_attend/pallas_call | solution.py:111
  63.9 15.5 %prefix_attend.1 = (f32[320,512]{1,0:T(8,128)}, f32[8,512]{1,0:T(8,128)}, bf16[320,512]{1,0:T(8,128)(2,1)}, f32[8,512]{1,0:T(8,128)}) custom-call(s32[5]{0:T(128)} %pad_add_fusion.meta_ref, bf16[320,512]{1,0:T(8,128)(2,1)} %bitcast.8.q_ref.own_q_ref, bf16[320,512]{1,0:T(8,128)(2,1)} %collective-permute-done.3.other_q_ref, ...), custom_call_target="tpu_custom_call" | custom-call | flops 1006632960 | bytes 6291456 | tf_op jit(solution)/shard_map/prefix_attend/pallas_call | solution.py:219
  79.4 0.6 collective-permute-start.12
  80.0 0.1 collective-permute-start.11
  80.0 1.4 %collective-permute-done.11 = f32[8,512]{1,0:T(8,128)S(1)} collective-permute-done((f32[8,512]{1,0:T(8,128)}, f32[8,512]{1,0:T(8,128)S(1)}, u32[]{:S(2)}, u32[]{:S(2)}) %collective-permute-start.11) | collective-permute-done | bytes 16416 | tf_op jit(solution)/shard_map/ppermute | solution.py:271
  81.4 0.7 add_add_fusion
  82.2 2.0 %fusion.29 = bf16[320,512]{1,0:T(8,128)(2,1)} fusion(f32[320,512]{1,0:T(8,128)S(1)} %copy-done.4, f32[320,512]{1,0:T(8,128)} %get-tuple-element.22, bf16[320,512]{1,0:T(8,128)(2,1)S(1)} %collective-permute-done.12, f32[5,512]{1,0:T(8,128)S(1)} %get-tuple-element.26, f32[5,512]{1,0:T(8,128)S(1)} %get-tuple-element.29, f32[5,512]{1,0:T(8,128)S(1)} %get-tuple-element.27, ...), kind=kLoop, calls=%fused_computation.37 | loop fusion | flops 1310720 | bytes 2007040 | tf_op jit(solution)/shard_map/convert_element_type | solution.py:339
  84.2 0.5 collective-permute-start.14
  84.8 0.1 collective-permute-start.13
  84.9 9.6 %collective-permute-done.14 = bf16[320,512]{1,0:T(8,128)(2,1)S(1)} collective-permute-done((bf16[320,512]{1,0:T(8,128)(2,1)}, bf16[320,512]{1,0:T(8,128)(2,1)S(1)}, u32[]{:S(2)}, u32[]{:S(2)}) %collective-permute-start.14) | collective-permute-done | bytes 327712 | tf_op jit(solution)/shard_map/ppermute | solution.py:268
  94.4 1.7 %collective-permute-done.15 = bf16[320,512]{1,0:T(8,128)(2,1)} collective-permute-done((bf16[320,512]{1,0:T(8,128)(2,1)S(1)}, bf16[320,512]{1,0:T(8,128)(2,1)}, u32[]{:S(2)}, u32[]{:S(2)}) %collective-permute-start.15) | collective-permute-done | bytes 327712 | tf_op jit(solution)/shard_map/ppermute | solution.py:271
  96.2 5.7 %multiply_reduce_fusion = (f32[512]{0:T(512)S(1)}, f32[512,2048]{1,0:T(8,128)S(1)}) fusion(bf16[320,2048]{1,0:T(8,128)(2,1)} %collective-permute-done.18, bf16[320,2048]{1,0:T(8,128)(2,1)} %collective-permute-done.17, bf16[320,2048]{1,0:T(8,128)(2,1)} %collective-permute-done.16, bf16[320,2048]{1,0:T(8,128)(2,1)} %param.24, ...), kind=kOutput, calls=%fused_computation.12 | convolution fusion | flops 2714762752 | bytes 12847104 | tf_op jit(solution)/shard_map/dot_general | solution.py:42
  101.9 0.0 slice-start.1
  101.9 10.5 %fusion = f32[512,2,1280]{2,0,1:T(8,128)S(1)} fusion(bf16[2048,2,1280]{2,1,0:T(2,128)(2,1)} %param.26, f32[512,2048]{1,0:T(8,128)S(1)} %get-tuple-element.39, f32[2048]{0:T(1024)S(1)} %copy-done.12, f32[512]{0:T(512)S(1)} %add_rsqrt_fusion.2), kind=kOutput, calls=%fused_computation.1 | convolution fusion | flops 5371854848 | bytes 19933184 | tf_op jit(solution)/shard_map/rd,dgf->rgf/dot_general | solution.py:350
  112.5 3.3 %convolution_convert_fusion = bf16[512,2048]{1,0:T(8,128)(2,1)S(1)} fusion(bf16[1280,2048]{1,0:T(8,128)(2,1)S(1)} %bitcast.86, f32[512,2,1280]{2,0,1:T(8,128)S(1)} %fusion), kind=kOutput, calls=%fused_computation.14 | convolution fusion | flops 2689335296 | bytes 12582912 | tf_op jit(solution)/shard_map/dot_general | solution.py:352
  115.7 1.3 copy-done.1
  117.1 1.1 constant_dynamic-slice_fusion.1
  118.2 0.1 collective-permute-start.20
  118.3 0.4 collective-permute-start.19
  118.7 1.7 %collective-permute-done.20 = bf16[512,512]{1,0:T(8,128)(2,1)} collective-permute-done((bf16[512,512]{1,0:T(8,128)(2,1)}, bf16[512,512]{1,0:T(8,128)(2,1)}, u32[]{:S(2)}, u32[]{:S(2)}) %collective-permute-start.20) | collective-permute-done | bytes 524320 | tf_op jit(solution)/shard_map/ppermute | solution.py:271
  120.4 2.2 %add_convert_fusion.1 = bf16[512,512]{1,0:T(8,128)(2,1)} fusion(bf16[512,512]{1,0:T(8,128)(2,1)} %collective-permute-done.20, bf16[512,2048]{1,0:T(8,128)(2,1)} %copy-done.1, s32[]{:T(128)S(6)} %select_n.66), kind=kLoop, calls=%fused_computation.31 | loop fusion | flops 1048576 | bytes 1572868 | tf_op jit(solution)/shard_map/convert_element_type | solution.py:359
  122.6 0.5 collective-permute-start.21
  123.1 0.9 pad_maximum_fusion
  124.0 12.8 %collective-permute-done.21 = bf16[512,512]{1,0:T(8,128)(2,1)} collective-permute-done((bf16[512,512]{1,0:T(8,128)(2,1)}, bf16[512,512]{1,0:T(8,128)(2,1)}, u32[]{:S(2)}, u32[]{:S(2)}) %collective-permute-start.21) | collective-permute-done | bytes 524320 | tf_op jit(solution)/shard_map/ppermute | solution.py:268
  136.9 2.8 %add_convert_fusion = bf16[512,512]{1,0:T(8,128)(2,1)} fusion(bf16[512,512]{1,0:T(8,128)(2,1)} %collective-permute-done.21, bf16[512,512]{1,0:T(8,128)(2,1)} %collective-permute-done.19, f32[512,2048]{1,0:T(8,128)} %copy-done.7, s32[]{:T(128)S(6)} %select_n.64, bf16[512,2048]{1,0:T(8,128)(2,1)} %copy-done.1), kind=kLoop, calls=%fused_computation.30 | loop fusion | flops 1835008 | bytes 3145732 | tf_op jit(solution)/shard_map/convert_element_type | solution.py:362
  (48 shorter events, 0.2 us)
Async XLA Ops:
  0.6 45.9 %copy-start = (bf16[2048,640]{1,0:T(8,128)(2,1)S(1)}, bf16[2048,640]{1,0:T(8,128)(2,1)}, u32[]{:S(2)}) copy-start(bf16[2048,640]{1,0:T(8,128)(2,1)} %param.21) | copy-start | bytes 7864324
  0.6 20.7 %collective-permute-start.1 = (bf16[512,512]{1,0:T(8,128)(2,1)}, bf16[512,512]{1,0:T(8,128)(2,1)S(1)}, u32[]{:S(2)}, u32[]{:S(2)}) collective-permute-start(bf16[512,512]{1,0:T(8,128)(2,1)} %own_ref.1), channel_id=1, source_target_pairs={{0,2},{1,3},{2,0},{3,1},{4,6},{5,7},{6,4},{7,5},{8,10},{9,11},{10,... | collective-permute-start | bytes 1572872 | tf_op jit(solution)/shard_map/ppermute | solution.py:268
  3.7 21.6 %collective-permute-start = (bf16[512,512]{1,0:T(8,128)(2,1)}, bf16[512,512]{1,0:T(8,128)(2,1)}, u32[]{:S(2)}, u32[]{:S(2)}) collective-permute-start(bf16[512,512]{1,0:T(8,128)(2,1)} %own_ref.1), channel_id=1, source_target_pairs={{0,1},{1,0},{2,3},{3,2},{4,5},{5,4},{6,7},{7,6},{8,9},{9,8},{10,11... | collective-permute-start | bytes 1572872 | tf_op jit(solution)/shard_map/ppermute | solution.py:271
  5.5 15.8 %collective-permute-start.5 = (bf16[2,320,384]{2,1,0:T(8,128)(2,1)}, bf16[2,320,384]{2,1,0:T(8,128)(2,1)}, u32[]{:S(2)}, u32[]{:S(2)}) collective-permute-start(bf16[2,320,384]{2,1,0:T(8,128)(2,1)} %dynamic-slice_bitcast_fusion.refs_0_), channel_id=1, source_target_pairs={{0,8},{4,12},{8,16},{12,20},{16,24},{20,28},{24,0},{28,4},{1,9},{5... | collective-permute-start | bytes 1474568 | tf_op jit(solution)/shard_map/ppermute | solution.py:278
  7.1 45.6 %collective-permute-start.4 = (bf16[2,320,384]{2,1,0:T(8,128)(2,1)}, bf16[2,320,384]{2,1,0:T(8,128)(2,1)}, u32[]{:S(2)}, u32[]{:S(2)}) collective-permute-start(bf16[2,320,384]{2,1,0:T(8,128)(2,1)} %dynamic-slice_bitcast_fusion.refs_0_), channel_id=1, source_target_pairs={{0,4},{4,0},{8,12},{12,8},{16,20},{20,16},{24,28},{28,24},{1,5},{5... | collective-permute-start | bytes 1474568 | tf_op jit(solution)/shard_map/ppermute | solution.py:281
  21.4 14.9 %collective-permute-start.7 = (bf16[2,320,384]{2,1,0:T(8,128)(2,1)}, bf16[2,320,384]{2,1,0:T(8,128)(2,1)}, u32[]{:S(2)}, u32[]{:S(2)}) collective-permute-start(bf16[2,320,384]{2,1,0:T(8,128)(2,1)} %collective-permute-done.5.refs_2_), channel_id=1, source_target_pairs={{0,8},{4,12},{8,16},{12,20},{16,24},{20,28},{24,0},{28,4},{1,9},{5... | collective-permute-start | bytes 1474568 | tf_op jit(solution)/shard_map/ppermute | solution.py:278
  21.4 17.3 %copy-start.5 = (bf16[512,512]{1,0:T(8,128)(2,1)}, bf16[512,512]{1,0:T(8,128)(2,1)S(1)}, u32[]{:S(2)}) copy-start(bf16[512,512]{1,0:T(8,128)(2,1)S(1)} %collective-permute-done.1.chip_ref) | copy-start | bytes 1572868
  21.4 14.9 %collective-permute-start.2 = (bf16[512,512]{1,0:T(8,128)(2,1)S(1)}, bf16[512,512]{1,0:T(8,128)(2,1)S(1)}, u32[]{:S(2)}, u32[]{:S(2)}) collective-permute-start(bf16[512,512]{1,0:T(8,128)(2,1)S(1)} %collective-permute-done.1.chip_ref), channel_id=1, source_target_pairs={{0,1},{1,0},{2,3},{3,2},{4,5},{5,4},{6,7},{7,6},{8,9},{9,8},{10,11... | collective-permute-start | bytes 1572872 | tf_op jit(solution)/shard_map/ppermute | solution.py:271
  23.7 29.0 %collective-permute-start.6 = (bf16[2,320,384]{2,1,0:T(8,128)(2,1)}, bf16[2,320,384]{2,1,0:T(8,128)(2,1)}, u32[]{:S(2)}, u32[]{:S(2)}) collective-permute-start(bf16[2,320,384]{2,1,0:T(8,128)(2,1)} %collective-permute-done.5.refs_2_), channel_id=1, source_target_pairs={{0,4},{4,0},{8,12},{12,8},{16,20},{20,16},{24,28},{28,24},{1,5},{5... | collective-permute-start | bytes 1474568 | tf_op jit(solution)/shard_map/ppermute | solution.py:281
  25.3 31.2 %collective-permute-start.17 = (bf16[320,2048]{1,0:T(8,128)(2,1)}, bf16[320,2048]{1,0:T(8,128)(2,1)}, u32[]{:S(2)}, u32[]{:S(2)}) collective-permute-start(bf16[320,2048]{1,0:T(8,128)(2,1)} %param.24), channel_id=1, source_target_pairs={{0,2},{1,3},{2,0},{3,1},{4,6},{5,7},{6,4},{7,5},{8,10},{9,11},{10,... | collective-permute-start | bytes 3932168 | tf_op jit(solution)/shard_map/ppermute | solution.py:268
  36.3 14.1 %collective-permute-start.9 = (bf16[2,320,384]{2,1,0:T(8,128)(2,1)}, bf16[2,320,384]{2,1,0:T(8,128)(2,1)}, u32[]{:S(2)}, u32[]{:S(2)}) collective-permute-start(bf16[2,320,384]{2,1,0:T(8,128)(2,1)} %collective-permute-done.7.refs_4_), channel_id=1, source_target_pairs={{0,8},{4,12},{8,16},{12,20},{16,24},{20,28},{24,0},{28,4},{1,9},{5... | collective-permute-start | bytes 1474568 | tf_op jit(solution)/shard_map/ppermute | solution.py:278
  36.3 0.8 copy-start.6
  37.1 26.8 %collective-permute-start.8 = (bf16[2,320,384]{2,1,0:T(8,128)(2,1)}, bf16[2,320,384]{2,1,0:T(8,128)(2,1)}, u32[]{:S(2)}, u32[]{:S(2)}) collective-permute-start(bf16[2,320,384]{2,1,0:T(8,128)(2,1)} %collective-permute-done.7.refs_4_), channel_id=1, source_target_pairs={{0,4},{4,0},{8,12},{12,8},{16,20},{20,16},{24,28},{28,24},{1,5},{5... | collective-permute-start | bytes 1474568 | tf_op jit(solution)/shard_map/ppermute | solution.py:281
  43.3 3.0 %copy-start.9 = (f32[64]{0:T(128)S(1)}, f32[64]{0:T(128)}, u32[]{:S(2)}) copy-start(f32[64]{0:T(128)} %param.22) | copy-start | bytes 772
  46.2 1.6 %copy-start.11 = (bf16[512,2048]{1,0:T(8,128)(2,1)S(1)}, bf16[512,2048]{1,0:T(8,128)(2,1)}, u32[]{:S(2)}) copy-start(bf16[512,2048]{1,0:T(8,128)(2,1)} %get-tuple-element.15) | copy-start | bytes 6291460
  47.8 1.7 %copy-start.10 = (f32[64]{0:T(128)S(1)}, f32[64]{0:T(128)}, u32[]{:S(2)}) copy-start(f32[64]{0:T(128)} %param.23) | copy-start | bytes 772
  50.4 13.5 %collective-permute-start.10 = (bf16[2,320,384]{2,1,0:T(8,128)(2,1)}, bf16[2,320,384]{2,1,0:T(8,128)(2,1)}, u32[]{:S(2)}, u32[]{:S(2)}) collective-permute-start(bf16[2,320,384]{2,1,0:T(8,128)(2,1)} %collective-permute-done.9.refs_6_), channel_id=1, source_target_pairs={{0,4},{4,0},{8,12},{12,8},{16,20},{20,16},{24,28},{28,24},{1,5},{5... | collective-permute-start | bytes 1474568 | tf_op jit(solution)/shard_map/ppermute | solution.py:281
  52.7 41.7 %collective-permute-start.16 = (bf16[320,2048]{1,0:T(8,128)(2,1)}, bf16[320,2048]{1,0:T(8,128)(2,1)}, u32[]{:S(2)}, u32[]{:S(2)}) collective-permute-start(bf16[320,2048]{1,0:T(8,128)(2,1)} %param.24), channel_id=1, source_target_pairs={{0,1},{1,0},{2,3},{3,2},{4,5},{5,4},{6,7},{7,6},{8,9},{9,8},{10,11... | collective-permute-start | bytes 3932168 | tf_op jit(solution)/shard_map/ppermute | solution.py:271
  52.7 11.2 %collective-permute-start.3 = (bf16[320,512]{1,0:T(8,128)(2,1)}, bf16[320,512]{1,0:T(8,128)(2,1)}, u32[]{:S(2)}, u32[]{:S(2)}) collective-permute-start(bf16[320,512]{1,0:T(8,128)(2,1)} %bitcast.8.q_ref.own_q_ref), channel_id=1, source_target_pairs={{0,1},{1,0},{2,3},{3,2},{4,5},{5,4},{6,7},{7,6},{8,9},{9,8},{10,11... | collective-permute-start | bytes 983048 | tf_op jit(solution)/shard_map/ppermute | solution.py:271
  56.5 39.7 %collective-permute-start.18 = (bf16[320,2048]{1,0:T(8,128)(2,1)}, bf16[320,2048]{1,0:T(8,128)(2,1)}, u32[]{:S(2)}, u32[]{:S(2)}) collective-permute-start(bf16[320,2048]{1,0:T(8,128)(2,1)} %collective-permute-done.17), channel_id=1, source_target_pairs={{0,1},{1,0},{2,3},{3,2},{4,5},{5,4},{6,7},{7,6},{8,9},{9,8},{10,11... | collective-permute-start | bytes 3932168 | tf_op jit(solution)/shard_map/ppermute | solution.py:271
  63.9 17.6 %copy-start.8 = (f32[8,512]{1,0:T(8,128)S(1)}, f32[8,512]{1,0:T(8,128)}, u32[]{:S(2)}) copy-start(f32[8,512]{1,0:T(8,128)} %get-tuple-element.21) | copy-start | bytes 49156
  63.9 18.3 %copy-start.4 = (f32[320,512]{1,0:T(8,128)S(1)}, f32[320,512]{1,0:T(8,128)}, u32[]{:S(2)}) copy-start(f32[320,512]{1,0:T(8,128)} %get-tuple-element.24) | copy-start | bytes 1966084
  79.4 2.8 %collective-permute-start.12 = (bf16[320,512]{1,0:T(8,128)(2,1)}, bf16[320,512]{1,0:T(8,128)(2,1)S(1)}, u32[]{:S(2)}, u32[]{:S(2)}) collective-permute-start(bf16[320,512]{1,0:T(8,128)(2,1)} %get-tuple-element.23), channel_id=1, source_target_pairs={{0,1},{1,0},{2,3},{3,2},{4,5},{5,4},{6,7},{7,6},{8,9},{9,8},{10,11... | collective-permute-start | bytes 983048 | tf_op jit(solution)/shard_map/ppermute | solution.py:271
  80.0 1.5 %collective-permute-start.11 = (f32[8,512]{1,0:T(8,128)}, f32[8,512]{1,0:T(8,128)S(1)}, u32[]{:S(2)}, u32[]{:S(2)}) collective-permute-start(f32[8,512]{1,0:T(8,128)} %get-tuple-element.20), channel_id=1, source_target_pairs={{0,1},{1,0},{2,3},{3,2},{4,5},{5,4},{6,7},{7,6},{8,9},{9,8},{10,11... | collective-permute-start | bytes 49160 | tf_op jit(solution)/shard_map/ppermute | solution.py:271
  84.2 10.2 %collective-permute-start.14 = (bf16[320,512]{1,0:T(8,128)(2,1)}, bf16[320,512]{1,0:T(8,128)(2,1)S(1)}, u32[]{:S(2)}, u32[]{:S(2)}) collective-permute-start(bf16[320,512]{1,0:T(8,128)(2,1)} %fusion.29), channel_id=1, source_target_pairs={{0,2},{1,3},{2,0},{3,1},{4,6},{5,7},{6,4},{7,5},{8,10},{9,11},{10,... | collective-permute-start | bytes 983048 | tf_op jit(solution)/shard_map/ppermute | solution.py:268
  84.8 9.7 %collective-permute-start.13 = (bf16[320,512]{1,0:T(8,128)(2,1)}, bf16[320,512]{1,0:T(8,128)(2,1)S(1)}, u32[]{:S(2)}, u32[]{:S(2)}) collective-permute-start(bf16[320,512]{1,0:T(8,128)(2,1)} %fusion.29), channel_id=1, source_target_pairs={{0,1},{1,0},{2,3},{3,2},{4,5},{5,4},{6,7},{7,6},{8,9},{9,8},{10,11... | collective-permute-start | bytes 983048 | tf_op jit(solution)/shard_map/ppermute | solution.py:271
  94.4 1.8 %collective-permute-start.15 = (bf16[320,512]{1,0:T(8,128)(2,1)S(1)}, bf16[320,512]{1,0:T(8,128)(2,1)}, u32[]{:S(2)}, u32[]{:S(2)}) collective-permute-start(bf16[320,512]{1,0:T(8,128)(2,1)S(1)} %collective-permute-done.14), channel_id=1, source_target_pairs={{0,1},{1,0},{2,3},{3,2},{4,5},{5,4},{6,7},{7,6},{8,9},{9,8},{10,11... | collective-permute-start | bytes 983048 | tf_op jit(solution)/shard_map/ppermute | solution.py:271
  96.2 5.7 %copy-start.12 = (f32[2048]{0:T(1024)S(1)}, f32[2048]{0:T(1024)}, u32[]{:S(2)}) copy-start(f32[2048]{0:T(1024)} %param.25) | copy-start | bytes 24580
  96.2 16.2 %slice-start = ((s8[5242880]{0:T(1024)(128)(4,1)}), s8[4194304]{0:T(1024)(128)(4,1)S(1)}, s32[]{:S(2)}) async-start(s8[5242880]{0:T(1024)(128)(4,1)} %bitcast.85), calls=%async_computation | async-start | bytes 8388608
  101.9 10.6 %copy-start.7 = (f32[512,2048]{1,0:T(8,128)}, f32[512,2048]{1,0:T(8,128)S(1)}, u32[]{:S(2)}) copy-start(f32[512,2048]{1,0:T(8,128)S(1)} %get-tuple-element.39) | copy-start | bytes 12582916
  101.9 10.6 %slice-start.1 = ((s8[5242880]{0:T(1024)(128)(4,1)}), s8[1048576]{0:T(1024)(128)(4,1)S(1)}, s32[]{:S(2)}) async-start(s8[5242880]{0:T(1024)(128)(4,1)} %bitcast.85), calls=%async_computation.1 | async-start | bytes 2097152
  115.7 1.4 copy-start.1
  117.1 6.0 %copy-start.2 = (bf16[512,1,5,64]{0,3,2,1:T(8,128)(2,1)S(1)}, bf16[512,1,5,64]{0,3,2,1:T(8,128)(2,1)}, u32[]{:S(2)}) copy-start(bf16[512,1,5,64]{0,3,2,1:T(8,128)(2,1)} %slice.89) | copy-start | bytes 983044
  117.1 6.0 %copy-start.3 = (bf16[512,5,64]{0,2,1:T(8,128)(2,1)S(1)}, bf16[512,5,64]{0,2,1:T(8,128)(2,1)}, u32[]{:S(2)}) copy-start(bf16[512,5,64]{0,2,1:T(8,128)(2,1)} %maximum_convert_fusion) | copy-start | bytes 983044
  118.2 2.3 %collective-permute-start.20 = (bf16[512,512]{1,0:T(8,128)(2,1)}, bf16[512,512]{1,0:T(8,128)(2,1)}, u32[]{:S(2)}, u32[]{:S(2)}) collective-permute-start(bf16[512,512]{1,0:T(8,128)(2,1)} %get-tuple-element.31), channel_id=1, source_target_pairs={{0,1},{1,0},{2,3},{3,2},{4,5},{5,4},{6,7},{7,6},{8,9},{9,8},{10,11... | collective-permute-start | bytes 1572872 | tf_op jit(solution)/shard_map/ppermute | solution.py:271
  118.3 5.7 %collective-permute-start.19 = (bf16[512,512]{1,0:T(8,128)(2,1)}, bf16[512,512]{1,0:T(8,128)(2,1)}, u32[]{:S(2)}, u32[]{:S(2)}) collective-permute-start(bf16[512,512]{1,0:T(8,128)(2,1)} %get-tuple-element.30), channel_id=1, source_target_pairs={{0,1},{1,0},{2,3},{3,2},{4,5},{5,4},{6,7},{7,6},{8,9},{9,8},{10,11... | collective-permute-start | bytes 1572872 | tf_op jit(solution)/shard_map/ppermute | solution.py:271
  122.6 14.3 %collective-permute-start.21 = (bf16[512,512]{1,0:T(8,128)(2,1)}, bf16[512,512]{1,0:T(8,128)(2,1)}, u32[]{:S(2)}, u32[]{:S(2)}) collective-permute-start(bf16[512,512]{1,0:T(8,128)(2,1)} %add_convert_fusion.1), channel_id=1, source_target_pairs={{0,2},{1,3},{2,0},{3,1},{4,6},{5,7},{6,4},{7,5},{8,10},{9,11},{10,... | collective-permute-start | bytes 1572872 | tf_op jit(solution)/shard_map/ppermute | solution.py:268

commit v3 on v2

--- a/solution.py
+++ b/solution.py
@@ -125,11 +125,11 @@
     return op(values.reshape(values.shape[0] // 8, 8, values.shape[1]), axis=0)
 
 
-def prefix_kernel(block, chunk, n_units, meta_ref, own_q_ref, other_q_ref, *refs):
+def prefix_kernel(base, block, chunk, n_units, meta_ref, own_q_ref, other_q_ref, *refs):
     units = refs[:n_units]
-    (own_out, own_lse, other_out, other_lse), scratch = refs[n_units : n_units + 4], refs[n_units + 4 :]
+    (own_out, own_lse, other_out), scratch = refs[n_units : n_units + 3], refs[n_units + 3 :]
     kv, q_buf, o_buf, l_buf, s_a, s_b, m_a, m_b, sems = scratch
-    first_len = meta_ref[4]
+    first_len = meta_ref[4] - base
     share = units[0].shape[2]
 
     def landing(job):
@@ -142,18 +142,20 @@
             def _():
                 pltpu.make_async_copy(units[unit], landing(job), sems.at[job]).start()
 
-    columns, rows = own_q_ref.shape
-    q_buf[:columns] = own_q_ref[...]
-    q_buf[columns:] = other_q_ref[...]
+    columns, rows = own_out.shape
+    q_buf[:columns] = own_q_ref[:, base : base + rows]
+    q_buf[columns:] = other_q_ref[:, base : base + rows]
     for job in range(4):
         pltpu.make_async_copy(units[0], landing(job), sems.at[job]).wait()
 
     heads = columns // HEAD_SIZE
     per = 2 * heads
     keys = 2 * share
-    n_first = (first_len + block - 1) // block
-    skipped = first_len // block
-    pairs = n_first + rows // block - skipped
+    parts = rows // block
+    inside = jnp.clip(first_len, 0, rows)
+    n_first = (inside + block - 1) // block
+    skipped = inside // block
+    pairs = n_first + parts - skipped
 
     def place(task):
         pair = task // per
@@ -190,8 +192,7 @@
             lane = lax.broadcasted_iota(jnp.int32, (1, block), 1) + part * block
             mine = (lane >= first_len).astype(jnp.int32) == second
             o_buf[q_band, cols] = jnp.where(mine, blended * (1.0 / total), o_buf[q_band, cols])
-            row = pl.ds(head, 1)
-            l_buf[row, cols] = jnp.where(mine, peak + jnp.log(total), l_buf[row, cols])
+            l_buf[head, :, cols] = jnp.where(mine, peak + jnp.log(total), l_buf[head, :, cols])
 
     step(None, 0, None, None, s_a, m_a)
 
@@ -203,30 +204,37 @@
 
     lax.fori_loop(0, pairs * heads, two, 0)
     own_out[...] = o_buf[:columns]
-    other_out[...] = o_buf[columns:].astype(jnp.bfloat16)
-    own_lse[:heads] = l_buf[:heads]
-    other_lse[:heads] = l_buf[heads:per]
-
-
-def prefix_attend(meta, own_q, other_q, units):
-    columns, rows = own_q.shape
+    other_out[:columns] = o_buf[columns:].astype(jnp.bfloat16)
+    for head in range(heads):
+        own_lse[head : head + 1] = l_buf[head]
+    rest = jnp.concatenate([l_buf[heads + head] for head in range(heads)] + [jnp.zeros((8 - heads, rows), jnp.float32)])
+    terms = []
+    for _ in range(3):
+        terms.append(rest.astype(jnp.bfloat16).astype(jnp.float32))
+        rest = rest - terms[-1]
+    terms.append(jnp.zeros_like(rest))
+    other_out[columns:] = jnp.concatenate(terms).astype(jnp.bfloat16)
+
+
+def prefix_attend(meta, own_q, other_q, units, base, rows):
+    columns = own_q.shape[0]
     share = units[0].shape[2]
-    block = 256
+    block = 128
     vmem = pl.BlockSpec(memory_space=pltpu.VMEM)
     out = jax.ShapeDtypeStruct((columns, rows), jnp.float32)
     lse = jax.ShapeDtypeStruct((8, rows), jnp.float32)
-    sent = jax.ShapeDtypeStruct((columns, rows), jnp.bfloat16)
+    sent = jax.ShapeDtypeStruct((columns + 32, rows), jnp.bfloat16)
     return pl.pallas_call(
-        functools.partial(prefix_kernel, block, 256, len(units)),
-        out_shape=(out, lse, sent, lse),
+        functools.partial(prefix_kernel, base, block, 256, len(units)),
+        out_shape=(out, lse, sent),
         in_specs=[pl.BlockSpec(memory_space=pltpu.SMEM), vmem, vmem]
         + [pl.BlockSpec(memory_space=pl.ANY)] * len(units),
-        out_specs=[vmem] * 4,
+        out_specs=[vmem] * 3,
         scratch_shapes=[
             pltpu.VMEM((2, 2, columns, 2 * share), jnp.bfloat16),
             pltpu.VMEM((2 * columns, rows), jnp.bfloat16),
             pltpu.VMEM((2 * columns, rows), jnp.float32),
-            pltpu.VMEM((16, rows), jnp.float32),
+            pltpu.VMEM((16, 1, rows), jnp.float32),
             pltpu.VMEM((2 * share, block), jnp.float32),
             pltpu.VMEM((2 * share, block), jnp.float32),
             pltpu.VMEM((1, block), jnp.float32),
@@ -234,10 +242,47 @@
             pltpu.SemaphoreType.DMA((4,)),
         ],
         cost_estimate=pl.CostEstimate(
-            flops=16 * columns * rows * share, bytes_accessed=6 << 20, transcendentals=20 * rows * share
+            flops=32 * columns * rows * share, bytes_accessed=6 << 20, transcendentals=20 * rows * share
         ),
         name="prefix_attend",
     )(meta, own_q, other_q, *units)
+
+
+def merge_kernel(own_ref, own_lse_ref, got_ref, suffix_ref, suffix_lse_ref, out_ref):
+    columns = own_ref.shape[0]
+    packed = got_ref[columns:].astype(jnp.float32)
+    got_lse = packed[:8] + packed[8:16] + packed[16:24]
+    lses = [own_lse_ref[...], got_lse, suffix_lse_ref[...]]
+    for head in range(columns // HEAD_SIZE):
+        band = pl.ds(head * HEAD_SIZE, HEAD_SIZE)
+        parts = [lse[head : head + 1] for lse in lses]
+        top = jnp.maximum(jnp.maximum(parts[0], parts[1]), parts[2])
+        factors = [jnp.exp(part - top) for part in parts]
+        share = 1.0 / (factors[0] + factors[1] + factors[2])
+        out_ref[band] = (
+            own_ref[band] * (factors[0] * share)
+            + got_ref[band].astype(jnp.float32) * (factors[1] * share)
+            + suffix_ref[band] * (factors[2] * share)
+        ).astype(jnp.bfloat16)
+
+
+def merge(own, own_lse, got, suffix, suffix_lse, index):
+    columns, rows = own.shape
+    return pl.pallas_call(
+        merge_kernel,
+        out_shape=jax.ShapeDtypeStruct((columns, rows), jnp.bfloat16),
+        grid=(1,),
+        in_specs=[
+            pl.BlockSpec((columns, rows), lambda i: (0, 0)),
+            pl.BlockSpec((8, rows), lambda i: (0, 0)),
+            pl.BlockSpec((columns + 32, rows), lambda i: (0, 0)),
+            pl.BlockSpec((columns, rows), lambda i: (0, index)),
+            pl.BlockSpec((8, rows), lambda i: (0, index)),
+        ],
+        out_specs=pl.BlockSpec((columns, rows), lambda i: (0, 0)),
+        cost_estimate=pl.CostEstimate(flops=8 * columns * rows, bytes_accessed=1 << 20, transcendentals=15 * rows),
+        name="merge",
+    )(own, own_lse, got, suffix, suffix_lse)
 
 
 def local(
@@ -280,10 +325,8 @@
     def aside(value):
         return lax.ppermute(value, "req", [(r, r ^ 1) for r in range(n_req)])
 
-    held = [mine]
-    for _ in range(length - 1):
-        held.append(ring(held[-1]))
-    units = [part for unit in held for part in (unit, aside(unit))]
+    held = [mine, ring(mine)]
+    units = [mine, aside(mine)]
     wanted = owners.reshape(-1, 2)[request_groups[0]].reshape(-1)
     distance = (my_req // 2 - wanted // 2) % length
     unit_index = 2 * distance + (wanted % 2 != my_req % 2).astype(jnp.int32)
@@ -291,11 +334,15 @@
     from_chip = across_chip(tokens)
     from_core = across_core(tokens)
     from_both = across_core(from_chip)
-    full_rows, normalized_input = gather_norm(rank, (tokens, from_core, from_chip, from_both), attn_gain)
+    w_gate, w_up = w_gate_up[:, 0], w_gate_up[:, 1]
+    pieces, w_gate, w_up, _ = lax.optimization_barrier(
+        ((tokens, from_core, from_chip, from_both), w_gate, w_up, held[1])
+    )
+    full_rows, normalized_input = gather_norm(rank, pieces, attn_gain)
 
     w_out_held, _ = lax.optimization_barrier((w_out, from_chip))
     w_out_chip = across_chip(w_out_held)
-    w_out_core = across_core(w_out_held)
+    w_out_core = across_core(w_out)
     w_out_both = across_core(w_out_chip)
     w_out_all = jnp.concatenate([w_out, w_out_core, w_out_chip, w_out_both], axis=0)
 
@@ -306,10 +353,16 @@
     query_rows = jnp.dot(
         normalized_input, query_weight, preferred_element_type=jnp.float32
     ).reshape(row_count, head_count, HEAD_SIZE)
-    query_rows = rotate(rms_scale(query_rows, query_gain), position).astype(jnp.bfloat16)
     key_value_rows = jnp.dot(
         normalized_input, key_value_weight, preferred_element_type=jnp.float32
     ).reshape(row_count, 2, head_count, HEAD_SIZE)
+    query_rows, key_value_rows, second = lax.optimization_barrier((query_rows, key_value_rows, ring(held[1])))
+    units += [held[1], aside(held[1]), second, aside(second)]
+    held.append(second)
+    for _ in range(3, length):
+        held.append(ring(held[-1]))
+        units += [held[-1], aside(held[-1])]
+    query_rows = rotate(rms_scale(query_rows, query_gain), position).astype(jnp.bfloat16)
     key_rows = rotate(rms_scale(key_value_rows[:, 0], key_gain), position).astype(jnp.bfloat16)
     value_rows = key_value_rows[:, 1].astype(jnp.bfloat16)
     cache_rows = jnp.stack(
@@ -324,42 +377,39 @@
 
     own_q, suffix_out, suffix_lse = lax.optimization_barrier((own_q, suffix_out, suffix_lse))
     meta = jnp.concatenate([unit_index.astype(jnp.int32), first_len.reshape(1)])
-    own_out, own_lse, sent_out, sent_lse = prefix_attend(meta, own_q, other_q, units)
-    got_out = across_core(sent_out)
-    got_lse = across_core(sent_lse)
-
-    outs = [
-        part.astype(jnp.float32).reshape(head_count, HEAD_SIZE, row_count)
-        for part in (own_out, got_out, suffix_out)
-    ]
-    lses = [part[:head_count, None, :] for part in (own_lse, got_lse, suffix_lse)]
-    top = jnp.maximum(jnp.maximum(lses[0], lses[1]), lses[2])
-    factors = [jnp.exp(part - top) for part in lses]
-    blended = sum(f * o for f, o in zip(factors, outs))
-    attention = (blended / (factors[0] + factors[1] + factors[2])).astype(jnp.bfloat16)
-    attention = attention.reshape(columns, row_count)
-
-    att_chip = across_chip(attention)
-    att_core = across_core(attention)
-    att_both = across_core(att_chip)
-    att_all = jnp.concatenate([attention, att_core, att_chip, att_both], axis=0)
-    head_total = tn_dot(att_all, w_out_all)
-    mixed = full_rows.astype(jnp.float32) + head_total
-
-    normed_ffn = rms_scale(mixed, ffn_gain).astype(jnp.bfloat16)
-    gate_up = jnp.einsum("rd,dgf->rgf", normed_ffn, w_gate_up, preferred_element_type=jnp.float32)
-    activated = (jax.nn.silu(gate_up[:, 0]) * gate_up[:, 1]).astype(jnp.bfloat16)
-    down_part = jnp.dot(activated, w_down, preferred_element_type=jnp.float32).astype(jnp.bfloat16)
-
     def block_of(value, flip):
         return lax.dynamic_slice_in_dim(value, (rank ^ flip) * width, width, 1)
 
-    got_far = across_core(block_of(down_part, 3))
-    got_near = across_core(block_of(down_part, 1))
-    far_sum = (block_of(down_part, 2).astype(jnp.float32) + got_far.astype(jnp.float32)).astype(jnp.bfloat16)
-    near_sum = block_of(mixed, 0) + block_of(down_part, 0).astype(jnp.float32) + got_near.astype(jnp.float32)
-    hidden = near_sum + across_chip(far_sum).astype(jnp.float32)
-    return (hidden.astype(jnp.bfloat16), cache_rows)
+    chunk = row_count // 2
+    gathered = []
+    for base in range(0, row_count, chunk):
+        own_out, own_lse, sent = prefix_attend(meta, own_q, other_q, units, base, chunk)
+        attention = merge(own_out, own_lse, across_core(sent), suffix_out, suffix_lse, base // chunk)
+        att_chip = across_chip(attention)
+        gathered.append([attention, across_core(attention), att_chip, across_core(att_chip)])
+
+    hidden = []
+    far_sum = None
+    for index, parts in enumerate(gathered):
+        if far_sum is not None:
+            parts, far_sum = lax.optimization_barrier((parts, far_sum))
+            got_chip = across_chip(far_sum)
+        head_total = tn_dot(jnp.concatenate(parts, axis=0), w_out_all)
+        mixed = full_rows[index * chunk : (index + 1) * chunk].astype(jnp.float32) + head_total
+        normed_ffn = rms_scale(mixed, ffn_gain).astype(jnp.bfloat16)
+        gate = jnp.dot(normed_ffn, w_gate, preferred_element_type=jnp.float32)
+        up = jnp.dot(normed_ffn, w_up, preferred_element_type=jnp.float32)
+        activated = (jax.nn.silu(gate) * up).astype(jnp.bfloat16)
+        if far_sum is not None:
+            activated, got_chip = lax.optimization_barrier((activated, got_chip))
+            hidden.append((near_sum + got_chip.astype(jnp.float32)).astype(jnp.bfloat16))
+        down_part = jnp.dot(activated, w_down, preferred_element_type=jnp.float32).astype(jnp.bfloat16)
+        got_far = across_core(block_of(down_part, 3))
+        got_near = across_core(block_of(down_part, 1))
+        far_sum = (block_of(down_part, 2).astype(jnp.float32) + got_far.astype(jnp.float32)).astype(jnp.bfloat16)
+        near_sum = block_of(mixed, 0) + block_of(down_part, 0).astype(jnp.float32) + got_near.astype(jnp.float32)
+    hidden.append((near_sum + across_chip(far_sum).astype(jnp.float32)).astype(jnp.bfloat16))
+    return (jnp.concatenate(hidden, axis=0), cache_rows)
 
 
 def solution(mesh):

time: 140 us -> 197 us (1.41)
  local copies, waits for them, and re-layouts: 8.5 us -> 53.7 us
  Pallas kernels: 26 us -> 36.2 us
  other arithmetic: 13.6 us -> 7.05 us
  matrix products: 23.8 us -> 30.2 us
  starting transfers between devices: 14.2 us -> 18.2 us
  waiting for transfers between devices: 52.5 us -> 49.6 us
    slice x0 -> x1, local copies, waits for them, and re-layouts: none -> 20.9 us  [local(): w_gate, w_up = (w_gate_up[:, 0], w_gate_up[:, 1])]
    ppermute x3, waiting for transfers between devices: 21.9 us -> 3.51 us  [ring(): lax.ppermute(value, 'req', [(r, (r + 2) % n_req) for r in range(n_req)])]
    ppermute x4, waiting for transfers between devices: 0.01 us -> 15.5 us  [aside(): return lax.ppermute(value, 'req', [(r, r ^ 1) for r in range(n_req)])]
    squeeze x0 -> x1, local copies, waits for them, and re-layouts: none -> 15.4 us  [local(): w_gate, w_up = (w_gate_up[:, 0], w_gate_up[:, 1])]
    pallas_call x1 -> x4, Pallas kernels: 15.5 us -> 25.7 us  [the longest x2 21.9 us: prefix_attend(): pl.pallas_call(functools.partial(prefix_kernel, base, block, 256, len(uni...]
    unnamed x30 -> x65, local copies, waits for them, and re-layouts: 3.42 us -> 11.2 us
    dot_general x1 -> x2, matrix products: 3.26 us -> 9.67 us  [local(): jnp.dot(activated, w_down, preferred_element_type=jnp.float32)]
    ppermute x4 -> x6, starting transfers between devices: 4.63 us -> 8.54 us  [across_chip(): return lax.ppermute(value, 'tp', [(i, i ^ 2) for i in range(4)])]
  transfers between devices with their start and end apart: 22 -> 28, of which waited for: 9 -> 9; matrix products, arithmetic and copies ran while one was open for 14% -> 40% of each run, Pallas kernels for 19% -> 18%
where the time goes in v3:
time: 197 us; the launch traced here: 196 us
  local copies, waits for them, and re-layouts  53.7 us (27%)
  waiting for transfers between devices  49.6 us (25%)
  Pallas kernels  36.2 us (18%)
  matrix products  30.2 us (15%)
  starting transfers between devices  18.2 us (9%)
  other arithmetic  7.05 us (4%)
    ppermute x6, waiting for transfers between devices, across_chip(): return lax.ppermute(value, 'tp', [(i, i ^ 2) for i in range(4)])  28.2 us
    pallas_call x2, Pallas kernels, prefix_attend(): pl.pallas_call(functools.partial(prefix_kernel, base, block, 256, len(uni...  21.9 us
    slice x1, local copies, waits for them, and re-layouts, local(): w_gate, w_up = (w_gate_up[:, 0], w_gate_up[:, 1])  20.9 us
    ppermute x4, waiting for transfers between devices, aside(): return lax.ppermute(value, 'req', [(r, r ^ 1) for r in range(n_req)])  15.5 us
    squeeze x1, local copies, waits for them, and re-layouts, local(): w_gate, w_up = (w_gate_up[:, 0], w_gate_up[:, 1])  15.4 us
    unnamed x65, local copies, waits for them, and re-layouts  11.2 us
    dot_general x2, matrix products, local(): jnp.dot(activated, w_down, preferred_element_type=jnp.float32)  9.67 us
    dot_general x2, matrix products, tn_dot(): lax.dot_general(lhs, rhs, (((0,), (0,)), ((), ())), preferred_element_typ...  8.87 us
  transfers between devices with their start and end apart: 28, of which 9 were waited for; matrix products, arithmetic and copies ran while one was open for 40% of the time, Pallas kernels for 18%

profile of v3, /device:TPU:0, one launch (start us, length us, event | category | flops | bytes accessed | tf_op | source)
XLA Modules:
  0.0 196.1 jit_solution(13849175365553227903)
XLA Ops:
  0.6 3.0 %collective-permute-start.1 = (bf16[512,512]{1,0:T(8,128)(2,1)}, bf16[512,512]{1,0:T(8,128)(2,1)}, u32[]{:S(2)}, u32[]{:S(2)}) collective-permute-start(bf16[512,512]{1,0:T(8,128)(2,1)} %own_ref), channel_id=1, source_target_pairs={{0,2},{1,3},{2,0},{3,1},{4,6},{5,7},{6,4},{7,5},{8,10},{9,11},{10,... | collective-permute-start | bytes 1572872 | tf_op jit(solution)/shard_map/ppermute | solution.py:313
  3.7 1.1 dynamic-slice_bitcast_fusion.refs_0_
  4.8 1.6 collective-permute-start.3
  6.4 1.5 collective-permute-start.6
  7.9 20.9 %fusion.28 = (bf16[2048,1,1280]{2,1,0:T(2,128)(2,1)}, bf16[2048,1,1280]{2,1,0:T(2,128)(2,1)}) fusion(bf16[2048,2,1280]{2,1,0:T(2,128)(2,1)} %param.26), kind=kLoop, calls=%fused_computation.88 | loop fusion | bytes 20971520 | tf_op jit(solution)/shard_map/slice | solution.py:337
  29.0 15.4 %copy_bitcast_fusion = (bf16[2048,1280]{1,0:T(8,128)(2,1)}, bf16[2048,1280]{1,0:T(8,128)(2,1)}) fusion(bf16[2048,1,1280]{2,1,0:T(2,128)(2,1)} %get-tuple-element.62, bf16[2048,1,1280]{2,1,0:T(2,128)(2,1)} %get-tuple-element.63), kind=kLoop, calls=%fused_computation.1 | loop fusion | bytes 20971520 | tf_op jit(solution)/shard_map/squeeze | solution.py:337
  44.4 0.6 gather_fusion
  45.1 0.6 collective-permute-start.2
  45.7 0.6 pad_add_fusion.meta_ref
  46.3 0.3 multiply_cosine_fusion
  46.7 2.6 %constant_dynamic-update-slice_fusion.3 = bf16[1280,2048]{1,0:T(8,128)(2,1)} fusion(bf16[320,2048]{1,0:T(8,128)(2,1)} %param.24), kind=kLoop, calls=%fused_computation.55 | loop fusion | bytes 2621440
  49.2 1.6 collective-permute-start.4
  50.8 0.5 collective-permute-start.7
  51.3 0.7 collective-permute-start.16
  52.0 4.7 %gather_norm.1 = (bf16[512,2048]{1,0:T(8,128)(2,1)}, bf16[512,2048]{1,0:T(8,128)(2,1)}) custom-call(s32[1]{0:T(128)} %bitcast.rank_ref, bf16[512,512]{1,0:T(8,128)(2,1)} %own_ref, bf16[512,512]{1,0:T(8,128)(2,1)} %collective-permute-done.core_ref, bf16[512,512]{1,0:T(8,128)(2,1)} %collective-permute-done.1.chip_ref, ...), custom_call_target="tpu_custom_call" | custom-call | tf_op jit(solution)/shard_map/gather_norm/pallas_call | solution.py:69
  56.7 3.3 %fusion.30 = f32[512,640]{0,1:T(8,128)S(1)} fusion(bf16[512,2048]{1,0:T(8,128)(2,1)} %get-tuple-element.37, bf16[2048,640]{1,0:T(8,128)(2,1)S(1)} %copy-done), kind=kOutput, calls=%fused_computation.90 | convolution fusion | flops 1342177280 | bytes 6029312 | tf_op jit(solution)/shard_map/dot_general | solution.py:356
  60.1 0.9 fusion.29
  61.0 3.5 %collective-permute-done.4.refs_4_ = bf16[2,320,384]{2,1,0:T(8,128)(2,1)} collective-permute-done((bf16[2,320,384]{2,1,0:T(8,128)(2,1)}, bf16[2,320,384]{2,1,0:T(8,128)(2,1)}, u32[]{:S(2)}, u32[]{:S(2)}) %collective-permute-start.4) | collective-permute-done | bytes 491552 | tf_op jit(solution)/shard_map/ppermute | solution.py:323
  64.7 0.1 fusion.15
  64.9 16.8 %collective-permute-done.16 = bf16[320,2048]{1,0:T(8,128)(2,1)} collective-permute-done((bf16[320,2048]{1,0:T(8,128)(2,1)}, bf16[320,2048]{1,0:T(8,128)(2,1)}, u32[]{:S(2)}, u32[]{:S(2)}) %collective-permute-start.16) | collective-permute-done | bytes 1310752 | tf_op jit(solution)/shard_map/ppermute | solution.py:313
  81.9 0.8 slice.63
  82.7 1.5 collective-permute-start.8
  84.2 0.5 collective-permute-start.10
  85.0 0.8 maximum_convert_fusion
  85.7 5.8 %suffix_attend.1 = (f32[320,512]{1,0:T(8,128)}, f32[8,512]{1,0:T(8,128)}) custom-call(s32[1]{0:T(128)} %bitcast.68, bf16[320,512]{1,0:T(8,128)(2,1)} %bitcast.55, bf16[320,512]{1,0:T(8,128)(2,1)} %bitcast.65, bf16[320,512]{1,0:T(8,128)(2,1)} %bitcast.63), custom_call_target="tpu_custom_call" | custom-call | flops 335544320 | bytes 3145728 | tf_op jit(solution)/shard_map/suffix_attend/pallas_call | solution.py:111
  91.5 5.5 %collective-permute-done.8.refs_5_ = bf16[2,320,384]{2,1,0:T(8,128)(2,1)S(1)} collective-permute-done((bf16[2,320,384]{2,1,0:T(8,128)(2,1)}, bf16[2,320,384]{2,1,0:T(8,128)(2,1)S(1)}, u32[]{:S(2)}, u32[]{:S(2)}) %collective-permute-start.8) | collective-permute-done | bytes 491552 | tf_op jit(solution)/shard_map/ppermute | solution.py:326
  97.0 10.1 %collective-permute-done.10.refs_7_ = bf16[2,320,384]{2,1,0:T(8,128)(2,1)S(1)} collective-permute-done((bf16[2,320,384]{2,1,0:T(8,128)(2,1)}, bf16[2,320,384]{2,1,0:T(8,128)(2,1)S(1)}, u32[]{:S(2)}, u32[]{:S(2)}) %collective-permute-start.10) | collective-permute-done | bytes 491552 | tf_op jit(solution)/shard_map/ppermute | solution.py:326
  107.0 0.8 copy-done.5
  107.8 9.6 %prefix_attend.2 = (f32[320,256]{1,0:T(8,128)}, f32[8,256]{1,0:T(8,128)}, bf16[352,256]{1,0:T(8,128)(2,1)}) custom-call(s32[5]{0:T(128)} %pad_add_fusion.meta_ref, bf16[320,512]{1,0:T(8,128)(2,1)} %bitcast.56, bf16[320,512]{1,0:T(8,128)(2,1)} %copy-done.6, bf16[2,320,384]{2,1,0:T(8,128)(2,1)} %copy-done.2, ...), custom_call_target="tpu_custom_call" | custom-call | flops 1006632960 | bytes 6291456 | tf_op jit(solution)/shard_map/prefix_attend/pallas_call | solution.py:227
  117.5 2.5 %constant_dynamic-update-slice_fusion.2 = bf16[1280,2048]{1,0:T(8,128)(2,1)} fusion(bf16[1280,2048]{1,0:T(8,128)(2,1)} %constant_dynamic-update-slice_fusion.3, bf16[320,2048]{1,0:T(8,128)(2,1)} %collective-permute-done.15), kind=kLoop, calls=%fused_computation.54 | loop fusion | bytes 2621440
  120.0 0.7 copy-done.12
  120.7 1.9 merge.2
  122.6 0.7 collective-permute-start.13
  123.3 2.5 %constant_dynamic-update-slice_fusion.1 = bf16[1280,2048]{1,0:T(8,128)(2,1)} fusion(bf16[1280,2048]{1,0:T(8,128)(2,1)} %constant_dynamic-update-slice_fusion.2, bf16[320,2048]{1,0:T(8,128)(2,1)} %collective-permute-done.16), kind=kLoop, calls=%fused_computation.53 | loop fusion | bytes 2621440
  125.9 12.3 %prefix_attend.3 = (f32[320,256]{1,0:T(8,128)}, f32[8,256]{1,0:T(8,128)}, bf16[352,256]{1,0:T(8,128)(2,1)}) custom-call(s32[5]{0:T(128)} %pad_add_fusion.meta_ref, bf16[320,512]{1,0:T(8,128)(2,1)} %bitcast.57, bf16[320,512]{1,0:T(8,128)(2,1)} %copy-done.6, bf16[2,320,384]{2,1,0:T(8,128)(2,1)} %copy-done.2, ...), custom_call_target="tpu_custom_call" | custom-call | flops 1006632960 | bytes 6291456 | tf_op jit(solution)/shard_map/prefix_attend/pallas_call | solution.py:227
  138.2 0.3 collective-permute-start.19
  138.5 0.3 collective-permute-start.12
  138.8 0.2 collective-permute-start.14
  139.0 2.7 %constant_dynamic-update-slice_fusion = bf16[1280,2048]{1,0:T(8,128)(2,1)} fusion(bf16[1280,2048]{1,0:T(8,128)(2,1)} %constant_dynamic-update-slice_fusion.1, bf16[320,2048]{1,0:T(8,128)(2,1)} %collective-permute-done.17), kind=kLoop, calls=%fused_computation.52 | loop fusion | bytes 2621440 | tf_op jit(solution)/shard_map/concatenate | solution.py:347
  141.8 4.2 %multiply_reduce_fusion.1 = (f32[256]{0:T(256)S(1)}, f32[256,2048]{1,0:T(8,128)S(1)}) fusion(bf16[1280,2048]{1,0:T(8,128)(2,1)} %constant_dynamic-update-slice_fusion, bf16[320,256]{1,0:T(8,128)(2,1)S(1)} %collective-permute-done.14, bf16[320,256]{1,0:T(8,128)(2,1)S(1)} %collective-permute-done.13, bf16[320,256]{1,0:T(8,128)(2,1)S(1)} %collective-permute-done.12, ...), kind=kOutput, calls=%fused_computation.10 | convolution fusion | flops 1346895616 | bytes 9044992 | tf_op jit(solution)/shard_map/dot_general | solution.py:42
  146.0 1.4 copy-done.14
  147.4 1.6 fusion.24
  149.0 8.1 %convolution_convert_fusion.1 = bf16[256,2048]{1,0:T(8,128)(2,1)S(1)} fusion(bf16[1280,2048]{1,0:T(8,128)(2,1)} %param.27, f32[256,1280]{1,0:T(8,128)S(1)} %fusion.24, bf16[2048,1280]{1,0:T(8,128)(2,1)} %get-tuple-element.50, f32[256,2048]{1,0:T(8,128)} %copy-done.14, f32[2048]{0:T(1024)S(1)} %copy-done.23, f32[256]{0:T(256)S(1)} %add_rsqrt_fusion.3), kind=kOutput, calls=%fused_computation.6 | convolution fusion | flops 2688417792 | bytes 14951424 | tf_op jit(solution)/shard_map/dot_general | solution.py:406
  157.1 0.4 collective-permute-start.23
  157.5 0.7 copy-done.11
  158.2 1.9 merge.3
  160.1 1.3 collective-permute-start.21
  161.4 5.2 %collective-permute-done.21 = bf16[320,256]{1,0:T(8,128)(2,1)S(1)} collective-permute-done((bf16[320,256]{1,0:T(8,128)(2,1)}, bf16[320,256]{1,0:T(8,128)(2,1)S(1)}, u32[]{:S(2)}, u32[]{:S(2)}) %collective-permute-start.21) | collective-permute-done | bytes 163872 | tf_op jit(solution)/shard_map/ppermute | solution.py:313
  166.7 1.3 collective-permute-done.22
  168.0 4.6 %multiply_reduce_fusion = (f32[256]{0:T(256)S(1)}, f32[256,2048]{1,0:T(8,128)S(1)}) fusion(bf16[1280,2048]{1,0:T(8,128)(2,1)} %constant_dynamic-update-slice_fusion, bf16[320,256]{1,0:T(8,128)(2,1)S(1)} %collective-permute-done.22, bf16[320,256]{1,0:T(8,128)(2,1)S(1)} %collective-permute-done.21, bf16[320,256]{1,0:T(8,128)(2,1)S(1)} %collective-permute-done.20, ...), kind=kOutput, calls=%fused_computation.8 | convolution fusion | flops 1346895616 | bytes 9044992 | tf_op jit(solution)/shard_map/dot_general | solution.py:42
  172.7 1.4 collective-permute-start.24
  174.1 1.6 fusion.27
  175.7 4.2 %multiply_convert_fusion.2 = bf16[256,1280]{1,0:T(8,128)(2,1)S(1)} fusion(f32[256,1280]{1,0:T(8,128)S(1)} %fusion.27, bf16[2048,1280]{1,0:T(8,128)(2,1)} %get-tuple-element.51, f32[256,2048]{1,0:T(8,128)S(1)} %get-tuple-element.77, f32[256]{0:T(256)S(1)} %add_rsqrt_fusion.2, f32[2048]{0:T(1024)S(1)} %copy-done.23), kind=kOutput, calls=%fused_computation.11 | convolution fusion | flops 1345716224 | bytes 9315328 | tf_op jit(solution)/shard_map/dot_general | solution.py:401
  180.0 1.5 collective-permute-done.24
  181.5 1.6 convolution_convert_fusion
  183.1 0.8 constant_dynamic-slice_fusion.1
  183.9 0.5 collective-permute-start.18
  184.5 1.0 collective-permute-done.26
  185.6 1.4 collective-permute-start.27
  187.0 0.9 pad_maximum_fusion
  187.9 1.5 add_convert_fusion.2
  189.3 4.7 %collective-permute-done.27 = bf16[256,512]{1,0:T(8,128)(2,1)S(1)} collective-permute-done((bf16[256,512]{1,0:T(8,128)(2,1)S(1)}, bf16[256,512]{1,0:T(8,128)(2,1)S(1)}, u32[]{:S(2)}, u32[]{:S(2)}) %collective-permute-start.27) | collective-permute-done | bytes 262176 | tf_op jit(solution)/shard_map/ppermute | solution.py:313
  194.0 1.2 add_convert_fusion
  195.2 0.8 pad_maximum_fusion.1
  (110 shorter events, 1.4 us)
Async XLA Ops:
  0.6 56.1 %copy-start = (bf16[2048,640]{1,0:T(8,128)(2,1)S(1)}, bf16[2048,640]{1,0:T(8,128)(2,1)}, u32[]{:S(2)}) copy-start(bf16[2048,640]{1,0:T(8,128)(2,1)} %param.21) | copy-start | bytes 7864324
  0.6 44.5 %collective-permute-start.1 = (bf16[512,512]{1,0:T(8,128)(2,1)}, bf16[512,512]{1,0:T(8,128)(2,1)}, u32[]{:S(2)}, u32[]{:S(2)}) collective-permute-start(bf16[512,512]{1,0:T(8,128)(2,1)} %own_ref), channel_id=1, source_target_pairs={{0,2},{1,3},{2,0},{3,1},{4,6},{5,7},{6,4},{7,5},{8,10},{9,11},{10,... | collective-permute-start | bytes 1572872 | tf_op jit(solution)/shard_map/ppermute | solution.py:313
  3.7 47.1 %collective-permute-start = (bf16[512,512]{1,0:T(8,128)(2,1)}, bf16[512,512]{1,0:T(8,128)(2,1)}, u32[]{:S(2)}, u32[]{:S(2)}) collective-permute-start(bf16[512,512]{1,0:T(8,128)(2,1)} %own_ref), channel_id=1, source_target_pairs={{0,1},{1,0},{2,3},{3,2},{4,5},{5,4},{6,7},{7,6},{8,9},{9,8},{10,11... | collective-permute-start | bytes 1572872 | tf_op jit(solution)/shard_map/ppermute | solution.py:316
  4.8 24.1 %copy-start.2 = (bf16[2,320,384]{2,1,0:T(8,128)(2,1)}, bf16[2,320,384]{2,1,0:T(8,128)(2,1)S(1)}, u32[]{:S(2)}) copy-start(bf16[2,320,384]{2,1,0:T(8,128)(2,1)S(1)} %dynamic-slice_bitcast_fusion.refs_0_) | copy-start | bytes 1474564
  4.8 44.4 %collective-permute-start.3 = (bf16[2,320,384]{2,1,0:T(8,128)(2,1)S(1)}, bf16[2,320,384]{2,1,0:T(8,128)(2,1)}, u32[]{:S(2)}, u32[]{:S(2)}) collective-permute-start(bf16[2,320,384]{2,1,0:T(8,128)(2,1)S(1)} %dynamic-slice_bitcast_fusion.refs_0_), channel_id=1, source_target_pairs={{0,8},{4,12},{8,16},{12,20},{16,24},{20,28},{24,0},{28,4},{1,9},{5... | collective-permute-start | bytes 1474568 | tf_op jit(solution)/shard_map/ppermute | solution.py:323
  6.4 76.3 %collective-permute-start.6 = (bf16[2,320,384]{2,1,0:T(8,128)(2,1)S(1)}, bf16[2,320,384]{2,1,0:T(8,128)(2,1)}, u32[]{:S(2)}, u32[]{:S(2)}) collective-permute-start(bf16[2,320,384]{2,1,0:T(8,128)(2,1)S(1)} %dynamic-slice_bitcast_fusion.refs_0_), channel_id=1, source_target_pairs={{0,4},{4,0},{8,12},{12,8},{16,20},{20,16},{24,28},{28,24},{1,5},{5... | collective-permute-start | bytes 1474568 | tf_op jit(solution)/shard_map/ppermute | solution.py:326
  7.9 109.6 %collective-permute-start.15 = (bf16[320,2048]{1,0:T(8,128)(2,1)}, bf16[320,2048]{1,0:T(8,128)(2,1)}, u32[]{:S(2)}, u32[]{:S(2)}) collective-permute-start(bf16[320,2048]{1,0:T(8,128)(2,1)} %param.24), channel_id=1, source_target_pairs={{0,1},{1,0},{2,3},{3,2},{4,5},{5,4},{6,7},{7,6},{8,9},{9,8},{10,11... | collective-permute-start | bytes 3932168 | tf_op jit(solution)/shard_map/ppermute | solution.py:316
  7.9 21.0 %copy-start.24 = (s32[1,2]{1,0:T(1,128)S(1)}, s32[1,2]{1,0:T(1,128)}, u32[]{:S(2)}) copy-start(s32[1,2]{1,0:T(1,128)} %param.16) | copy-start | bytes 28
  7.9 21.0 %copy-start.18 = (s32[8]{0:T(128)S(1)}, s32[8]{0:T(128)}, u32[]{:S(2)}) copy-start(s32[8]{0:T(128)} %param.15) | copy-start | bytes 100
  29.0 16.0 %copy-start.19 = (s32[1,2]{1,0:T(1,128)S(1)}, s32[1,2]{1,0:T(1,128)}, u32[]{:S(2)}) copy-start(s32[1,2]{1,0:T(1,128)} %param.17) | copy-start | bytes 28
  45.1 6.2 %collective-permute-start.2 = (bf16[512,512]{1,0:T(8,128)(2,1)}, bf16[512,512]{1,0:T(8,128)(2,1)}, u32[]{:S(2)}, u32[]{:S(2)}) collective-permute-start(bf16[512,512]{1,0:T(8,128)(2,1)} %collective-permute-done.1.chip_ref), channel_id=1, source_target_pairs={{0,1},{1,0},{2,3},{3,2},{4,5},{5,4},{6,7},{7,6},{8,9},{9,8},{10,11... | collective-permute-start | bytes 1572872 | tf_op jit(solution)/shard_map/ppermute | solution.py:316
  49.2 15.3 %collective-permute-start.4 = (bf16[2,320,384]{2,1,0:T(8,128)(2,1)}, bf16[2,320,384]{2,1,0:T(8,128)(2,1)}, u32[]{:S(2)}, u32[]{:S(2)}) collective-permute-start(bf16[2,320,384]{2,1,0:T(8,128)(2,1)} %collective-permute-done.3.refs_2_), channel_id=1, source_target_pairs={{0,8},{4,12},{8,16},{12,20},{16,24},{20,28},{24,0},{28,4},{1,9},{5... | collective-permute-start | bytes 1474568 | tf_op jit(solution)/shard_map/ppermute | solution.py:323
  50.8 34.0 %collective-permute-start.7 = (bf16[2,320,384]{2,1,0:T(8,128)(2,1)}, bf16[2,320,384]{2,1,0:T(8,128)(2,1)}, u32[]{:S(2)}, u32[]{:S(2)}) collective-permute-start(bf16[2,320,384]{2,1,0:T(8,128)(2,1)} %collective-permute-done.3.refs_2_), channel_id=1, source_target_pairs={{0,4},{4,0},{8,12},{12,8},{16,20},{20,16},{24,28},{28,24},{1,5},{5... | collective-permute-start | bytes 1474568 | tf_op jit(solution)/shard_map/ppermute | solution.py:326
  51.3 30.5 %collective-permute-start.16 = (bf16[320,2048]{1,0:T(8,128)(2,1)}, bf16[320,2048]{1,0:T(8,128)(2,1)}, u32[]{:S(2)}, u32[]{:S(2)}) collective-permute-start(bf16[320,2048]{1,0:T(8,128)(2,1)} %param.24), channel_id=1, source_target_pairs={{0,2},{1,3},{2,0},{3,1},{4,6},{5,7},{6,4},{7,5},{8,10},{9,11},{10,... | collective-permute-start | bytes 3932168 | tf_op jit(solution)/shard_map/ppermute | solution.py:313
  56.7 3.3 %copy-start.21 = (bf16[512,2048]{1,0:T(8,128)(2,1)S(1)}, bf16[512,2048]{1,0:T(8,128)(2,1)}, u32[]{:S(2)}) copy-start(bf16[512,2048]{1,0:T(8,128)(2,1)} %get-tuple-element.37) | copy-start | bytes 6291460
  56.7 3.3 %copy-start.22 = (bf16[2048,320]{0,1:T(8,128)(2,1)S(1)}, bf16[2048,320]{0,1:T(8,128)(2,1)}, u32[]{:S(2)}) copy-start(bf16[2048,320]{0,1:T(8,128)(2,1)} %param.20) | copy-start | bytes 3932164
  60.1 4.6 %copy-start.16 = (f32[64]{0:T(128)S(1)}, f32[64]{0:T(128)}, u32[]{:S(2)}) copy-start(f32[64]{0:T(128)} %param.23) | copy-start | bytes 772
  61.0 3.8 %copy-start.17 = (f32[64]{0:T(128)S(1)}, f32[64]{0:T(128)}, u32[]{:S(2)}) copy-start(f32[64]{0:T(128)} %param.22) | copy-start | bytes 772
  64.5 19.7 %collective-permute-start.9 = (bf16[2,320,384]{2,1,0:T(8,128)(2,1)}, bf16[2,320,384]{2,1,0:T(8,128)(2,1)}, u32[]{:S(2)}, u32[]{:S(2)}) collective-permute-start(bf16[2,320,384]{2,1,0:T(8,128)(2,1)} %collective-permute-done.4.refs_4_), channel_id=1, source_target_pairs={{0,8},{4,12},{8,16},{12,20},{16,24},{20,28},{24,0},{28,4},{1,9},{5... | collective-permute-start | bytes 1474568 | tf_op jit(solution)/shard_map/ppermute | solution.py:323
  81.8 57.3 %collective-permute-start.17 = (bf16[320,2048]{1,0:T(8,128)(2,1)}, bf16[320,2048]{1,0:T(8,128)(2,1)}, u32[]{:S(2)}, u32[]{:S(2)}) collective-permute-start(bf16[320,2048]{1,0:T(8,128)(2,1)} %collective-permute-done.16), channel_id=1, source_target_pairs={{0,1},{1,0},{2,3},{3,2},{4,5},{5,4},{6,7},{7,6},{8,9},{9,8},{10,11... | collective-permute-start | bytes 3932168 | tf_op jit(solution)/shard_map/ppermute | solution.py:316
  82.7 14.3 %collective-permute-start.8 = (bf16[2,320,384]{2,1,0:T(8,128)(2,1)}, bf16[2,320,384]{2,1,0:T(8,128)(2,1)S(1)}, u32[]{:S(2)}, u32[]{:S(2)}) collective-permute-start(bf16[2,320,384]{2,1,0:T(8,128)(2,1)} %collective-permute-done.4.refs_4_), channel_id=1, source_target_pairs={{0,4},{4,0},{8,12},{12,8},{16,20},{20,16},{24,28},{28,24},{1,5},{5... | collective-permute-start | bytes 1474568 | tf_op jit(solution)/shard_map/ppermute | solution.py:326
  84.2 22.9 %collective-permute-start.10 = (bf16[2,320,384]{2,1,0:T(8,128)(2,1)}, bf16[2,320,384]{2,1,0:T(8,128)(2,1)S(1)}, u32[]{:S(2)}, u32[]{:S(2)}) collective-permute-start(bf16[2,320,384]{2,1,0:T(8,128)(2,1)} %collective-permute-done.9.refs_6_), channel_id=1, source_target_pairs={{0,4},{4,0},{8,12},{12,8},{16,20},{20,16},{24,28},{28,24},{1,5},{5... | collective-permute-start | bytes 1474568 | tf_op jit(solution)/shard_map/ppermute | solution.py:326
  84.7 1.0 copy-start.3
  84.8 6.7 %collective-permute-start.5 = (bf16[320,512]{1,0:T(8,128)(2,1)S(1)}, bf16[320,512]{1,0:T(8,128)(2,1)S(1)}, u32[]{:S(2)}, u32[]{:S(2)}) collective-permute-start(bf16[320,512]{1,0:T(8,128)(2,1)S(1)} %bitcast.54), channel_id=1, source_target_pairs={{0,1},{1,0},{2,3},{3,2},{4,5},{5,4},{6,7},{7,6},{8,9},{9,8},{10,11... | collective-permute-start | bytes 983048 | tf_op jit(solution)/shard_map/ppermute | solution.py:316
  91.5 15.5 %copy-start.6 = (bf16[320,512]{1,0:T(8,128)(2,1)}, bf16[320,512]{1,0:T(8,128)(2,1)S(1)}, u32[]{:S(2)}) copy-start(bf16[320,512]{1,0:T(8,128)(2,1)S(1)} %collective-permute-done.5.other_q_ref) | copy-start | bytes 983044
  97.0 10.1 %copy-start.4 = (bf16[2,320,384]{2,1,0:T(8,128)(2,1)}, bf16[2,320,384]{2,1,0:T(8,128)(2,1)S(1)}, u32[]{:S(2)}) copy-start(bf16[2,320,384]{2,1,0:T(8,128)(2,1)S(1)} %collective-permute-done.8.refs_5_) | copy-start | bytes 1474564
  107.0 0.8 copy-start.5
  117.4 2.6 %collective-permute-start.11 = (bf16[352,256]{1,0:T(8,128)(2,1)}, bf16[352,256]{1,0:T(8,128)(2,1)S(1)}, u32[]{:S(2)}, u32[]{:S(2)}) collective-permute-start(bf16[352,256]{1,0:T(8,128)(2,1)} %get-tuple-element.46), channel_id=1, source_target_pairs={{0,1},{1,0},{2,3},{3,2},{4,5},{5,4},{6,7},{7,6},{8,9},{9,8},{10,11... | collective-permute-start | bytes 540680 | tf_op jit(solution)/shard_map/ppermute | solution.py:316
  120.0 0.7 copy-start.12
  122.6 16.2 %collective-permute-start.13 = (bf16[320,256]{1,0:T(8,128)(2,1)}, bf16[320,256]{1,0:T(8,128)(2,1)S(1)}, u32[]{:S(2)}, u32[]{:S(2)}) collective-permute-start(bf16[320,256]{1,0:T(8,128)(2,1)} %merge.2), channel_id=1, source_target_pairs={{0,2},{1,3},{2,0},{3,1},{4,6},{5,7},{6,4},{7,5},{8,10},{9,11},{10,... | collective-permute-start | bytes 491528 | tf_op jit(solution)/shard_map/ppermute | solution.py:313
  125.9 12.6 %copy-start.13 = (bf16[320,256]{1,0:T(8,128)(2,1)S(1)}, bf16[320,256]{1,0:T(8,128)(2,1)}, u32[]{:S(2)}) copy-start(bf16[320,256]{1,0:T(8,128)(2,1)} %merge.2) | copy-start | bytes 491524
  138.2 3.5 %copy-start.20 = (bf16[512,2048]{1,0:T(8,128)(2,1)S(1)}, bf16[512,2048]{1,0:T(8,128)(2,1)}, u32[]{:S(2)}) copy-start(bf16[512,2048]{1,0:T(8,128)(2,1)} %get-tuple-element.36) | copy-start | bytes 6291460
  138.2 19.3 %collective-permute-start.19 = (bf16[352,256]{1,0:T(8,128)(2,1)}, bf16[352,256]{1,0:T(8,128)(2,1)S(1)}, u32[]{:S(2)}, u32[]{:S(2)}) collective-permute-start(bf16[352,256]{1,0:T(8,128)(2,1)} %get-tuple-element.54), channel_id=1, source_target_pairs={{0,1},{1,0},{2,3},{3,2},{4,5},{5,4},{6,7},{7,6},{8,9},{9,8},{10,11... | collective-permute-start | bytes 540680 | tf_op jit(solution)/shard_map/ppermute | solution.py:316
  138.5 3.2 %collective-permute-start.12 = (bf16[320,256]{1,0:T(8,128)(2,1)S(1)}, bf16[320,256]{1,0:T(8,128)(2,1)S(1)}, u32[]{:S(2)}, u32[]{:S(2)}) collective-permute-start(bf16[320,256]{1,0:T(8,128)(2,1)S(1)} %copy-done.13), channel_id=1, source_target_pairs={{0,1},{1,0},{2,3},{3,2},{4,5},{5,4},{6,7},{7,6},{8,9},{9,8},{10,11... | collective-permute-start | bytes 491528 | tf_op jit(solution)/shard_map/ppermute | solution.py:316
  138.8 2.9 %collective-permute-start.14 = (bf16[320,256]{1,0:T(8,128)(2,1)S(1)}, bf16[320,256]{1,0:T(8,128)(2,1)S(1)}, u32[]{:S(2)}, u32[]{:S(2)}) collective-permute-start(bf16[320,256]{1,0:T(8,128)(2,1)S(1)} %collective-permute-done.13), channel_id=1, source_target_pairs={{0,1},{1,0},{2,3},{3,2},{4,5},{5,4},{6,7},{7,6},{8,9},{9,8},{10,11... | collective-permute-start | bytes 491528 | tf_op jit(solution)/shard_map/ppermute | solution.py:316
  139.0 8.3 %slice-start = ((s8[5242880]{0:T(1024)(128)(4,1)}), s8[4194304]{0:T(1024)(128)(4,1)S(1)}, s32[]{:S(2)}) async-start(s8[5242880]{0:T(1024)(128)(4,1)} %bitcast.50), calls=%async_computation | async-start | bytes 8388608
  141.7 5.6 %slice-start.1 = ((s8[5242880]{0:T(1024)(128)(4,1)}), s8[1048576]{0:T(1024)(128)(4,1)S(1)}, s32[]{:S(2)}) async-start(s8[5242880]{0:T(1024)(128)(4,1)} %bitcast.50), calls=%async_computation.1 | async-start | bytes 2097152
  141.7 5.6 %copy-start.23 = (f32[2048]{0:T(1024)S(1)}, f32[2048]{0:T(1024)}, u32[]{:S(2)}) copy-start(f32[2048]{0:T(1024)} %param.25) | copy-start | bytes 24580
  146.0 1.4 copy-start.14
  157.1 15.6 %copy-start.9 = (bf16[256,2048]{1,0:T(8,128)(2,1)}, bf16[256,2048]{1,0:T(8,128)(2,1)S(1)}, u32[]{:S(2)}) copy-start(bf16[256,2048]{1,0:T(8,128)(2,1)S(1)} %convolution_convert_fusion.1) | copy-start | bytes 3145732
  157.1 9.5 %collective-permute-start.23 = (bf16[256,512]{1,0:T(8,128)(2,1)S(1)}, bf16[256,512]{1,0:T(8,128)(2,1)S(1)}, u32[]{:S(2)}, u32[]{:S(2)}) collective-permute-start(bf16[256,512]{1,0:T(8,128)(2,1)S(1)} %get-tuple-element.65), channel_id=1, source_target_pairs={{0,1},{1,0},{2,3},{3,2},{4,5},{5,4},{6,7},{7,6},{8,9},{9,8},{10,11... | collective-permute-start | bytes 786440 | tf_op jit(solution)/shard_map/ppermute | solution.py:316
  157.5 0.7 copy-start.11
  160.1 6.5 %collective-permute-start.21 = (bf16[320,256]{1,0:T(8,128)(2,1)}, bf16[320,256]{1,0:T(8,128)(2,1)S(1)}, u32[]{:S(2)}, u32[]{:S(2)}) collective-permute-start(bf16[320,256]{1,0:T(8,128)(2,1)} %merge.3), channel_id=1, source_target_pairs={{0,2},{1,3},{2,0},{3,1},{4,6},{5,7},{6,4},{7,5},{8,10},{9,11},{10,... | collective-permute-start | bytes 491528 | tf_op jit(solution)/shard_map/ppermute | solution.py:313
  161.4 5.3 %collective-permute-start.20 = (bf16[320,256]{1,0:T(8,128)(2,1)}, bf16[320,256]{1,0:T(8,128)(2,1)S(1)}, u32[]{:S(2)}, u32[]{:S(2)}) collective-permute-start(bf16[320,256]{1,0:T(8,128)(2,1)} %merge.3), channel_id=1, source_target_pairs={{0,1},{1,0},{2,3},{3,2},{4,5},{5,4},{6,7},{7,6},{8,9},{9,8},{10,11... | collective-permute-start | bytes 491528 | tf_op jit(solution)/shard_map/ppermute | solution.py:316
  166.6 1.4 collective-permute-start.22
  166.6 7.5 %slice-start.2 = ((s8[5242880]{0:T(1024)(128)(4,1)}), s8[4194304]{0:T(1024)(128)(4,1)S(1)}, s32[]{:S(2)}) async-start(s8[5242880]{0:T(1024)(128)(4,1)} %bitcast.52), calls=%async_computation.2 | async-start | bytes 8388608
  166.7 7.4 %slice-start.3 = ((s8[5242880]{0:T(1024)(128)(4,1)}), s8[1048576]{0:T(1024)(128)(4,1)S(1)}, s32[]{:S(2)}) async-start(s8[5242880]{0:T(1024)(128)(4,1)} %bitcast.52), calls=%async_computation.3 | async-start | bytes 2097152
  172.7 3.0 %copy-start.15 = (f32[256,2048]{1,0:T(8,128)}, f32[256,2048]{1,0:T(8,128)S(1)}, u32[]{:S(2)}) copy-start(f32[256,2048]{1,0:T(8,128)S(1)} %get-tuple-element.77) | copy-start | bytes 6291460
  172.7 8.8 %collective-permute-start.24 = (bf16[256,512]{1,0:T(8,128)(2,1)S(1)}, bf16[256,512]{1,0:T(8,128)(2,1)}, u32[]{:S(2)}, u32[]{:S(2)}) collective-permute-start(bf16[256,512]{1,0:T(8,128)(2,1)S(1)} %add_convert_fusion.3), channel_id=1, source_target_pairs={{0,2},{1,3},{2,0},{3,1},{4,6},{5,7},{6,4},{7,5},{8,10},{9,11},{10,... | collective-permute-start | bytes 786440 | tf_op jit(solution)/shard_map/ppermute | solution.py:313
  174.1 7.4 %slice-start.4 = ((s8[5242880]{0:T(1024)(128)(4,1)}), s8[4194304]{0:T(1024)(128)(4,1)S(1)}, s32[]{:S(2)}) async-start(s8[5242880]{0:T(1024)(128)(4,1)} %bitcast.71), calls=%async_computation.4 | async-start | bytes 8388608
  175.7 5.8 %slice-start.5 = ((s8[5242880]{0:T(1024)(128)(4,1)}), s8[1048576]{0:T(1024)(128)(4,1)S(1)}, s32[]{:S(2)}) async-start(s8[5242880]{0:T(1024)(128)(4,1)} %bitcast.71), calls=%async_computation.5 | async-start | bytes 2097152
  180.0 7.0 %copy-start.7 = (bf16[512,1,5,64]{0,3,2,1:T(8,128)(2,1)S(1)}, bf16[512,1,5,64]{0,3,2,1:T(8,128)(2,1)}, u32[]{:S(2)}) copy-start(bf16[512,1,5,64]{0,3,2,1:T(8,128)(2,1)} %slice.63) | copy-start | bytes 983044
  180.0 7.0 %copy-start.8 = (bf16[512,5,64]{0,2,1:T(8,128)(2,1)S(1)}, bf16[512,5,64]{0,2,1:T(8,128)(2,1)}, u32[]{:S(2)}) copy-start(bf16[512,5,64]{0,2,1:T(8,128)(2,1)} %maximum_convert_fusion) | copy-start | bytes 983044
  183.1 2.4 %copy-start.10 = (bf16[256,2048]{1,0:T(8,128)(2,1)}, bf16[256,2048]{1,0:T(8,128)(2,1)S(1)}, u32[]{:S(2)}) copy-start(bf16[256,2048]{1,0:T(8,128)(2,1)S(1)} %convolution_convert_fusion) | copy-start | bytes 3145732
  183.9 1.5 collective-permute-start.26
  183.9 3.9 %collective-permute-start.18 = (bf16[256,512]{1,0:T(8,128)(2,1)S(1)}, bf16[256,512]{1,0:T(8,128)(2,1)S(1)}, u32[]{:S(2)}, u32[]{:S(2)}) collective-permute-start(bf16[256,512]{1,0:T(8,128)(2,1)S(1)} %get-tuple-element.64), channel_id=1, source_target_pairs={{0,1},{1,0},{2,3},{3,2},{4,5},{5,4},{6,7},{7,6},{8,9},{9,8},{10,11... | collective-permute-start | bytes 786440 | tf_op jit(solution)/shard_map/ppermute | solution.py:316
  184.5 4.9 %collective-permute-start.25 = (bf16[256,512]{1,0:T(8,128)(2,1)}, bf16[256,512]{1,0:T(8,128)(2,1)S(1)}, u32[]{:S(2)}, u32[]{:S(2)}) collective-permute-start(bf16[256,512]{1,0:T(8,128)(2,1)} %get-tuple-element.66), channel_id=1, source_target_pairs={{0,1},{1,0},{2,3},{3,2},{4,5},{5,4},{6,7},{7,6},{8,9},{9,8},{10,11... | collective-permute-start | bytes 786440 | tf_op jit(solution)/shard_map/ppermute | solution.py:316
  185.6 8.4 %collective-permute-start.27 = (bf16[256,512]{1,0:T(8,128)(2,1)S(1)}, bf16[256,512]{1,0:T(8,128)(2,1)S(1)}, u32[]{:S(2)}, u32[]{:S(2)}) collective-permute-start(bf16[256,512]{1,0:T(8,128)(2,1)S(1)} %add_convert_fusion.1), channel_id=1, source_target_pairs={{0,2},{1,3},{2,0},{3,1},{4,6},{5,7},{6,4},{7,5},{8,10},{9,11},{10,... | collective-permute-start | bytes 786440 | tf_op jit(solution)/shard_map/ppermute | solution.py:313
  187.0 9.1 %copy-start.1 = (bf16[2048,640]{1,0:T(8,128)(2,1)S(1)}, bf16[2048,640]{1,0:T(8,128)(2,1)}, u32[]{:S(2)}) copy-start(bf16[2048,640]{1,0:T(8,128)(2,1)} %param.21) | copy-start | bytes 7864324

commit v4 on v3

--- a/solution.py
+++ b/solution.py
@@ -125,26 +125,31 @@
     return op(values.reshape(values.shape[0] // 8, 8, values.shape[1]), axis=0)
 
 
-def prefix_kernel(base, block, chunk, n_units, meta_ref, own_q_ref, other_q_ref, *refs):
-    units = refs[:n_units]
-    (own_out, own_lse, other_out), scratch = refs[n_units : n_units + 3], refs[n_units + 3 :]
+def prefix_kernel(block, chunk, n_units, meta_ref, own_q_ref, other_q_ref, *refs):
+    units, last_keys, last_values = refs[: n_units - 1], refs[n_units - 1], refs[n_units]
+    (own_out, own_lse, other_out), scratch = refs[n_units + 1 : n_units + 4], refs[n_units + 4 :]
     kv, q_buf, o_buf, l_buf, s_a, s_b, m_a, m_b, sems = scratch
-    first_len = meta_ref[4] - base
+    first_len = meta_ref[4]
     share = units[0].shape[2]
 
-    def landing(job):
-        return kv.at[job // 2, :, :, pl.ds((job % 2) * share, share)]
+    def landing(job, kind=slice(None)):
+        return kv.at[job // 2, kind, :, pl.ds((job % 2) * share, share)]
 
     for job in range(4):
-        for unit in range(n_units):
+        for unit in range(n_units - 1):
 
             @pl.when(meta_ref[job] == unit)
             def _():
                 pltpu.make_async_copy(units[unit], landing(job), sems.at[job]).start()
 
+        @pl.when(meta_ref[job] == n_units - 1)
+        def _():
+            pltpu.make_async_copy(last_keys, landing(job, pl.ds(0, 1)), sems.at[job]).start()
+            pltpu.make_async_copy(last_values, landing(job, pl.ds(1, 1)), sems.at[job]).start()
+
     columns, rows = own_out.shape
-    q_buf[:columns] = own_q_ref[:, base : base + rows]
-    q_buf[columns:] = other_q_ref[:, base : base + rows]
+    q_buf[:columns] = own_q_ref[...]
+    q_buf[columns:] = other_q_ref[...]
     for job in range(4):
         pltpu.make_async_copy(units[0], landing(job), sems.at[job]).wait()
 
@@ -216,16 +221,16 @@
     other_out[columns:] = jnp.concatenate(terms).astype(jnp.bfloat16)
 
 
-def prefix_attend(meta, own_q, other_q, units, base, rows):
-    columns = own_q.shape[0]
+def prefix_attend(meta, own_q, other_q, units):
+    columns, rows = own_q.shape
     share = units[0].shape[2]
-    block = 128
+    block = 256
     vmem = pl.BlockSpec(memory_space=pltpu.VMEM)
     out = jax.ShapeDtypeStruct((columns, rows), jnp.float32)
     lse = jax.ShapeDtypeStruct((8, rows), jnp.float32)
     sent = jax.ShapeDtypeStruct((columns + 32, rows), jnp.bfloat16)
     return pl.pallas_call(
-        functools.partial(prefix_kernel, base, block, 256, len(units)),
+        functools.partial(prefix_kernel, block, 256, len(units) - 1),
         out_shape=(out, lse, sent),
         in_specs=[pl.BlockSpec(memory_space=pltpu.SMEM), vmem, vmem]
         + [pl.BlockSpec(memory_space=pl.ANY)] * len(units),
@@ -266,20 +271,20 @@
         ).astype(jnp.bfloat16)
 
 
-def merge(own, own_lse, got, suffix, suffix_lse, index):
+def merge(own, own_lse, got, suffix, suffix_lse):
     columns, rows = own.shape
     return pl.pallas_call(
         merge_kernel,
         out_shape=jax.ShapeDtypeStruct((columns, rows), jnp.bfloat16),
-        grid=(1,),
+        grid=(rows // 256,),
         in_specs=[
-            pl.BlockSpec((columns, rows), lambda i: (0, 0)),
-            pl.BlockSpec((8, rows), lambda i: (0, 0)),
-            pl.BlockSpec((columns + 32, rows), lambda i: (0, 0)),
-            pl.BlockSpec((columns, rows), lambda i: (0, index)),
-            pl.BlockSpec((8, rows), lambda i: (0, index)),
+            pl.BlockSpec((columns, 256), lambda i: (0, i)),
+            pl.BlockSpec((8, 256), lambda i: (0, i)),
+            pl.BlockSpec((columns + 32, 256), lambda i: (0, i)),
+            pl.BlockSpec((columns, 256), lambda i: (0, i)),
+            pl.BlockSpec((8, 256), lambda i: (0, i)),
         ],
-        out_specs=pl.BlockSpec((columns, rows), lambda i: (0, 0)),
+        out_specs=pl.BlockSpec((columns, 256), lambda i: (0, i)),
         cost_estimate=pl.CostEstimate(flops=8 * columns * rows, bytes_accessed=1 << 20, transcendentals=15 * rows),
         name="merge",
     )(own, own_lse, got, suffix, suffix_lse)
@@ -334,9 +339,11 @@
     from_chip = across_chip(tokens)
     from_core = across_core(tokens)
     from_both = across_core(from_chip)
-    w_gate, w_up = w_gate_up[:, 0], w_gate_up[:, 1]
-    pieces, w_gate, w_up, _ = lax.optimization_barrier(
-        ((tokens, from_core, from_chip, from_both), w_gate, w_up, held[1])
+    down_blocks = [
+        lax.dynamic_slice_in_dim(w_down, (rank ^ flip) * width, width, 1) for flip in range(4)
+    ]
+    pieces, down_blocks, _ = lax.optimization_barrier(
+        ((tokens, from_core, from_chip, from_both), down_blocks, held[1])
     )
     full_rows, normalized_input = gather_norm(rank, pieces, attn_gain)
 
@@ -344,7 +351,6 @@
     w_out_chip = across_chip(w_out_held)
     w_out_core = across_core(w_out)
     w_out_both = across_core(w_out_chip)
-    w_out_all = jnp.concatenate([w_out, w_out_core, w_out_chip, w_out_both], axis=0)
 
     row_index = jnp.arange(row_count, dtype=jnp.int32)
     first_len = request_lengths[0, 0]
@@ -357,11 +363,12 @@
         normalized_input, key_value_weight, preferred_element_type=jnp.float32
     ).reshape(row_count, 2, head_count, HEAD_SIZE)
     query_rows, key_value_rows, second = lax.optimization_barrier((query_rows, key_value_rows, ring(held[1])))
-    units += [held[1], aside(held[1]), second, aside(second)]
+    units += [held[1], aside(held[1])]
     held.append(second)
     for _ in range(3, length):
+        units += [held[-1], aside(held[-1])]
         held.append(ring(held[-1]))
-        units += [held[-1], aside(held[-1])]
+    units += [held[-1], aside(held[-1][:1]), ring(units[-1][1:])]
     query_rows = rotate(rms_scale(query_rows, query_gain), position).astype(jnp.bfloat16)
     key_rows = rotate(rms_scale(key_value_rows[:, 0], key_gain), position).astype(jnp.bfloat16)
     value_rows = key_value_rows[:, 1].astype(jnp.bfloat16)
@@ -377,39 +384,29 @@
 
     own_q, suffix_out, suffix_lse = lax.optimization_barrier((own_q, suffix_out, suffix_lse))
     meta = jnp.concatenate([unit_index.astype(jnp.int32), first_len.reshape(1)])
-    def block_of(value, flip):
-        return lax.dynamic_slice_in_dim(value, (rank ^ flip) * width, width, 1)
-
-    chunk = row_count // 2
-    gathered = []
-    for base in range(0, row_count, chunk):
-        own_out, own_lse, sent = prefix_attend(meta, own_q, other_q, units, base, chunk)
-        attention = merge(own_out, own_lse, across_core(sent), suffix_out, suffix_lse, base // chunk)
-        att_chip = across_chip(attention)
-        gathered.append([attention, across_core(attention), att_chip, across_core(att_chip)])
-
-    hidden = []
-    far_sum = None
-    for index, parts in enumerate(gathered):
-        if far_sum is not None:
-            parts, far_sum = lax.optimization_barrier((parts, far_sum))
-            got_chip = across_chip(far_sum)
-        head_total = tn_dot(jnp.concatenate(parts, axis=0), w_out_all)
-        mixed = full_rows[index * chunk : (index + 1) * chunk].astype(jnp.float32) + head_total
-        normed_ffn = rms_scale(mixed, ffn_gain).astype(jnp.bfloat16)
-        gate = jnp.dot(normed_ffn, w_gate, preferred_element_type=jnp.float32)
-        up = jnp.dot(normed_ffn, w_up, preferred_element_type=jnp.float32)
-        activated = (jax.nn.silu(gate) * up).astype(jnp.bfloat16)
-        if far_sum is not None:
-            activated, got_chip = lax.optimization_barrier((activated, got_chip))
-            hidden.append((near_sum + got_chip.astype(jnp.float32)).astype(jnp.bfloat16))
-        down_part = jnp.dot(activated, w_down, preferred_element_type=jnp.float32).astype(jnp.bfloat16)
-        got_far = across_core(block_of(down_part, 3))
-        got_near = across_core(block_of(down_part, 1))
-        far_sum = (block_of(down_part, 2).astype(jnp.float32) + got_far.astype(jnp.float32)).astype(jnp.bfloat16)
-        near_sum = block_of(mixed, 0) + block_of(down_part, 0).astype(jnp.float32) + got_near.astype(jnp.float32)
-    hidden.append((near_sum + across_chip(far_sum).astype(jnp.float32)).astype(jnp.bfloat16))
-    return (jnp.concatenate(hidden, axis=0), cache_rows)
+    own_out, own_lse, sent = prefix_attend(meta, own_q, other_q, units)
+    attention = merge(own_out, own_lse, across_core(sent), suffix_out, suffix_lse)
+    att_chip = across_chip(attention)
+    att_core = across_core(attention)
+    near_total = full_rows.astype(jnp.float32) + tn_dot(attention, w_out) + tn_dot(att_core, w_out_core)
+    near_total, att_chip = lax.optimization_barrier((near_total, att_chip))
+    att_both = across_core(att_chip)
+    mixed = near_total + tn_dot(att_chip, w_out_chip) + tn_dot(att_both, w_out_both)
+    normed_ffn = rms_scale(mixed, ffn_gain).astype(jnp.bfloat16)
+    gate_up = jnp.einsum("rd,dgf->rgf", normed_ffn, w_gate_up, preferred_element_type=jnp.float32)
+    activated = (jax.nn.silu(gate_up[:, 0]) * gate_up[:, 1]).astype(jnp.bfloat16)
+
+    def down(flip):
+        return jnp.dot(activated, down_blocks[flip], preferred_element_type=jnp.float32).astype(jnp.bfloat16)
+
+    far = down(3)
+    far_sum = (down(2).astype(jnp.float32) + across_core(far).astype(jnp.float32)).astype(jnp.bfloat16)
+    from_far = across_chip(far_sum)
+    activated, far_sum = lax.optimization_barrier((activated, far_sum))
+    near = down(1)
+    own_mixed = lax.dynamic_slice_in_dim(mixed, rank * width, width, 1)
+    near_sum = own_mixed + down(0).astype(jnp.float32) + across_core(near).astype(jnp.float32)
+    return ((near_sum + from_far.astype(jnp.float32)).astype(jnp.bfloat16), cache_rows)
 
 
 def solution(mesh):

time: 197 us -> 129 us (0.65)
  local copies, waits for them, and re-layouts: 53.7 us -> 10.6 us
  waiting for transfers between devices: 49.6 us -> 37.5 us
  Pallas kernels: 36.2 us -> 28.1 us
  matrix products: 30.2 us -> 23.3 us
    slice x1 -> x2, local copies, waits for them, and re-layouts: 20.9 us -> 0.05 us  [local(): units += [held[-1], aside(held[-1][:1]), ring(units[-1][1:])]]
    ppermute x4, waiting for transfers between devices: 15.5 us -> 0.01 us  [aside(): return lax.ppermute(value, 'req', [(r, r ^ 1) for r in range(n_req)])]
    squeeze x1 -> x0, local copies, waits for them, and re-layouts: 15.4 us -> none  [local(): w_gate, w_up = (w_gate_up[:, 0], w_gate_up[:, 1])]
    ppermute x3 -> x4, waiting for transfers between devices: 3.51 us -> 16.8 us  [ring(): lax.ppermute(value, 'req', [(r, (r + 2) % n_req) for r in range(n_req)])]
    ppermute x6 -> x4, waiting for transfers between devices: 28.2 us -> 17.8 us  [across_chip(): return lax.ppermute(value, 'tp', [(i, i ^ 2) for i in range(4)])]
    unnamed x65 -> x44, local copies, waits for them, and re-layouts: 11.2 us -> 1.64 us
    dot_general x5, matrix products: 17.1 us -> 8.99 us  [the longest x1 5.64 us: local(): jnp.einsum('rd,dgf->rgf', normed_ffn, w_gate_up, preferred_element_type=j...]
    pallas_call x2 -> x1, Pallas kernels: 21.9 us -> 15.3 us  [prefix_attend(): pl.pallas_call(functools.partial(prefix_kernel, block, 256, len(units) -...]
  transfers between devices with their start and end apart: 28 -> 22, of which waited for: 9 -> 8; matrix products, arithmetic and copies ran while one was open for 40% -> 22% of each run, Pallas kernels for 18% -> 22%
where the time goes in v4:
time: 129 us; the launch traced here: 128 us
  waiting for transfers between devices  37.5 us (29%)
  Pallas kernels  28.1 us (22%)
  matrix products  23.3 us (18%)
  starting transfers between devices  19.2 us (15%)
  local copies, waits for them, and re-layouts  10.6 us (8%)
  other arithmetic  8.7 us (7%)
    ppermute x4, waiting for transfers between devices, across_chip(): return lax.ppermute(value, 'tp', [(i, i ^ 2) for i in range(4)])  17.8 us
    ppermute x4, waiting for transfers between devices, ring(): lax.ppermute(value, 'req', [(r, (r + 2) % n_req) for r in range(n_req)])  16.8 us
    pallas_call x1, Pallas kernels, prefix_attend(): pl.pallas_call(functools.partial(prefix_kernel, block, 256, len(units) -...  15.3 us
    dot_general x4, matrix products, tn_dot(): lax.dot_general(lhs, rhs, (((0,), (0,)), ((), ())), preferred_element_typ...  9.8 us
    ppermute x4, starting transfers between devices, across_chip(): return lax.ppermute(value, 'tp', [(i, i ^ 2) for i in range(4)])  7.51 us
    ppermute x4, starting transfers between devices, aside(): return lax.ppermute(value, 'req', [(r, r ^ 1) for r in range(n_req)])  5.93 us
    pallas_call x1, Pallas kernels, suffix_attend(): pl.pallas_call(suffix_kernel, out_shape=(jax.ShapeDtypeStruct((columns, r...  5.81 us
    dot_general x1, matrix products, local(): jnp.einsum('rd,dgf->rgf', normed_ffn, w_gate_up, preferred_element_type=j...  5.64 us
  transfers between devices with their start and end apart: 22, of which 8 were waited for; matrix products, arithmetic and copies ran while one was open for 22% of the time, Pallas kernels for 22%

profile of v4, /device:TPU:0, one launch (start us, length us, event | category | flops | bytes accessed | tf_op | source)
XLA Modules:
  0.0 128.4 jit_solution(62704863547290739)
XLA Ops:
  0.6 0.0 copy-start
  0.6 3.0 %collective-permute-start.1 = (bf16[512,512]{1,0:T(8,128)(2,1)}, bf16[512,512]{1,0:T(8,128)(2,1)S(1)}, u32[]{:S(2)}, u32[]{:S(2)}) collective-permute-start(bf16[512,512]{1,0:T(8,128)(2,1)} %own_ref), channel_id=1, source_target_pairs={{0,2},{1,3},{2,0},{3,1},{4,6},{5,7},{6,4},{7,5},{8,10},{9,11},{10,... | collective-permute-start | bytes 1572872 | tf_op jit(solution)/shard_map/ppermute | solution.py:318
  3.7 1.8 %dynamic-slice_bitcast_fusion.refs_0_ = bf16[2,320,384]{2,1,0:T(8,128)(2,1)} fusion(bf16[1,2,768,320]{2,3,1,0:T(8,128)(2,1)} %param.18, s32[]{:T(128)S(6)} %select_n.61), kind=kLoop, calls=%fused_computation.32 | loop fusion | bytes 983044 | tf_op jit(solution)/shard_map/dynamic_slice | solution.py:325
  5.5 1.6 %collective-permute-start.3 = (bf16[2,320,384]{2,1,0:T(8,128)(2,1)}, bf16[2,320,384]{2,1,0:T(8,128)(2,1)}, u32[]{:S(2)}, u32[]{:S(2)}) collective-permute-start(bf16[2,320,384]{2,1,0:T(8,128)(2,1)} %dynamic-slice_bitcast_fusion.refs_0_), channel_id=1, source_target_pairs={{0,8},{4,12},{8,16},{12,20},{16,24},{20,28},{24,0},{28,4},{1,9},{5... | collective-permute-start | bytes 1474568 | tf_op jit(solution)/shard_map/ppermute | solution.py:328
  7.1 1.5 %collective-permute-start.6 = (bf16[2,320,384]{2,1,0:T(8,128)(2,1)}, bf16[2,320,384]{2,1,0:T(8,128)(2,1)}, u32[]{:S(2)}, u32[]{:S(2)}) collective-permute-start(bf16[2,320,384]{2,1,0:T(8,128)(2,1)} %dynamic-slice_bitcast_fusion.refs_0_), channel_id=1, source_target_pairs={{0,4},{4,0},{8,12},{12,8},{16,20},{20,16},{24,28},{28,24},{1,5},{5... | collective-permute-start | bytes 1474568 | tf_op jit(solution)/shard_map/ppermute | solution.py:331
  8.6 0.7 add_convert_fusion.2
  9.3 0.7 fusion.17
  10.0 0.7 reshape.178
  10.7 0.6 gather_fusion
  11.3 0.1 reshape.179
  11.4 0.3 multiply_cosine_fusion
  11.7 4.1 %collective-permute-done.1.chip_ref = bf16[512,512]{1,0:T(8,128)(2,1)S(1)} collective-permute-done((bf16[512,512]{1,0:T(8,128)(2,1)}, bf16[512,512]{1,0:T(8,128)(2,1)S(1)}, u32[]{:S(2)}, u32[]{:S(2)}) %collective-permute-start.1) | collective-permute-done | bytes 524320 | tf_op jit(solution)/shard_map/ppermute | solution.py:318
  15.8 1.3 pad_add_fusion.meta_ref
  17.1 4.9 %constant_dynamic-slice_fusion = (bf16[1280,512]{1,0:T(8,128)(2,1)}, bf16[1280,512]{1,0:T(8,128)(2,1)}, bf16[1280,512]{1,0:T(8,128)(2,1)}, bf16[1280,512]{1,0:T(8,128)(2,1)}) fusion(bf16[1280,2048]{1,0:T(8,128)(2,1)} %param.27, s32[]{:T(128)S(6)} %select_n.59, s32[]{:T(128)S(6)} %select_n.57, s32[]{:T(128)S(6)} %select_n.56, s32[]{:T(128)S(6)} %select_n.58), kind=kLoop, calls=%fused_computation.53 | loop fusion | bytes 10485776 | tf_op jit(solution)/shard_map/dynamic_slice | solution.py:343
  22.0 1.9 %collective-permute-start.4 = (bf16[2,320,384]{2,1,0:T(8,128)(2,1)}, bf16[2,320,384]{2,1,0:T(8,128)(2,1)}, u32[]{:S(2)}, u32[]{:S(2)}) collective-permute-start(bf16[2,320,384]{2,1,0:T(8,128)(2,1)} %collective-permute-done.3.refs_2_), channel_id=1, source_target_pairs={{0,8},{4,12},{8,16},{12,20},{16,24},{20,28},{24,0},{28,4},{1,9},{5... | collective-permute-start | bytes 1474568 | tf_op jit(solution)/shard_map/ppermute | solution.py:328
  23.9 1.5 %collective-permute-start.7 = (bf16[2,320,384]{2,1,0:T(8,128)(2,1)}, bf16[2,320,384]{2,1,0:T(8,128)(2,1)}, u32[]{:S(2)}, u32[]{:S(2)}) collective-permute-start(bf16[2,320,384]{2,1,0:T(8,128)(2,1)} %collective-permute-done.3.refs_2_), channel_id=1, source_target_pairs={{0,4},{4,0},{8,12},{12,8},{16,20},{20,16},{24,28},{28,24},{1,5},{5... | collective-permute-start | bytes 1474568 | tf_op jit(solution)/shard_map/ppermute | solution.py:331
  25.4 1.5 %collective-permute-start.16 = (bf16[320,2048]{1,0:T(8,128)(2,1)}, bf16[320,2048]{1,0:T(8,128)(2,1)}, u32[]{:S(2)}, u32[]{:S(2)}) collective-permute-start(bf16[320,2048]{1,0:T(8,128)(2,1)} %param.24), channel_id=1, source_target_pairs={{0,2},{1,3},{2,0},{3,1},{4,6},{5,7},{6,4},{7,5},{8,10},{9,11},{10,... | collective-permute-start | bytes 3932168 | tf_op jit(solution)/shard_map/ppermute | solution.py:318
  26.9 4.7 %gather_norm.1 = (bf16[512,2048]{1,0:T(8,128)(2,1)}, bf16[512,2048]{1,0:T(8,128)(2,1)}) custom-call(s32[1]{0:T(128)} %bitcast.rank_ref, bf16[512,512]{1,0:T(8,128)(2,1)} %own_ref, bf16[512,512]{1,0:T(8,128)(2,1)} %collective-permute-done.core_ref, bf16[512,512]{1,0:T(8,128)(2,1)} %copy-done.9, bf16[512,512]{1,0:T(8,128)(2,1)} %collective-permute-done.2.both_ref, ...), custom_call_target="tpu_custom_call" | custom-call | tf_op jit(solution)/shard_map/gather_norm/pallas_call | solution.py:69
  31.7 3.0 %fusion.18 = f32[512,320]{0,1:T(8,128)S(1)} fusion(bf16[512,2048]{1,0:T(8,128)(2,1)} %get-tuple-element.32, bf16[2048,320]{0,1:T(8,128)(2,1)} %param.20), kind=kOutput, calls=%fused_computation.66 | convolution fusion | flops 671088640 | bytes 4063232 | tf_op jit(solution)/shard_map/dot_general | solution.py:359
  34.7 1.6 %fusion.19 = f32[512,640]{0,1:T(8,128)S(1)} fusion(bf16[512,2048]{1,0:T(8,128)(2,1)S(1)} %copy-done.16, bf16[2048,640]{1,0:T(8,128)(2,1)S(1)} %copy-done), kind=kOutput, calls=%fused_computation.67 | convolution fusion | flops 1342177280 | bytes 6029312 | tf_op jit(solution)/shard_map/dot_general | solution.py:362
  36.3 1.9 %collective-permute-done.4.refs_4_ = bf16[2,320,384]{2,1,0:T(8,128)(2,1)} collective-permute-done((bf16[2,320,384]{2,1,0:T(8,128)(2,1)}, bf16[2,320,384]{2,1,0:T(8,128)(2,1)}, u32[]{:S(2)}, u32[]{:S(2)}) %collective-permute-start.4) | collective-permute-done | bytes 491552 | tf_op jit(solution)/shard_map/ppermute | solution.py:328
  38.1 1.5 %collective-permute-start.8 = (bf16[2,320,384]{2,1,0:T(8,128)(2,1)}, bf16[2,320,384]{2,1,0:T(8,128)(2,1)S(1)}, u32[]{:S(2)}, u32[]{:S(2)}) collective-permute-start(bf16[2,320,384]{2,1,0:T(8,128)(2,1)} %collective-permute-done.4.refs_4_), channel_id=1, source_target_pairs={{0,4},{4,0},{8,12},{12,8},{16,20},{20,16},{24,28},{28,24},{1,5},{5... | collective-permute-start | bytes 1474568 | tf_op jit(solution)/shard_map/ppermute | solution.py:331
  39.7 0.1 multiply_reduce_fusion.1
  39.8 0.2 fusion.12
  40.0 0.1 subtract_convert_fusion
  40.1 0.1 maximum_multiply_fusion
  40.2 0.1 fusion.13
  40.3 12.8 %collective-permute-done.9.refs_6_ = bf16[2,320,384]{2,1,0:T(8,128)(2,1)S(1)} collective-permute-done((bf16[2,320,384]{2,1,0:T(8,128)(2,1)}, bf16[2,320,384]{2,1,0:T(8,128)(2,1)S(1)}, u32[]{:S(2)}, u32[]{:S(2)}) %collective-permute-start.9) | collective-permute-done | bytes 491552 | tf_op jit(solution)/shard_map/ppermute | solution.py:328
  53.3 0.6 collective-permute-start.5
  53.9 1.4 %collective-permute-start.10 = (bf16[1,320,384]{2,1,0:T(8,128)(2,1)S(1)}, bf16[1,320,384]{2,1,0:T(8,128)(2,1)S(1)}, u32[]{:S(2)}, u32[]{:S(2)}) collective-permute-start(bf16[1,320,384]{2,1,0:T(8,128)(2,1)S(1)} %slice.50), channel_id=1, source_target_pairs={{0,4},{4,0},{8,12},{12,8},{16,20},{20,16},{24,28},{28,24},{1,5},{5... | collective-permute-start | bytes 737288 | tf_op jit(solution)/shard_map/ppermute | solution.py:331
  55.2 0.1 multiply_subtract_fusion
  55.3 0.8 slice.73
  56.1 0.7 maximum_convert_fusion
  56.9 5.8 %suffix_attend.1 = (f32[320,512]{1,0:T(8,128)}, f32[8,512]{1,0:T(8,128)}) custom-call(s32[1]{0:T(128)} %bitcast.81, bf16[320,512]{1,0:T(8,128)(2,1)} %bitcast.76, bf16[320,512]{1,0:T(8,128)(2,1)} %bitcast.73, bf16[320,512]{1,0:T(8,128)(2,1)} %bitcast.71), custom_call_target="tpu_custom_call" | custom-call | flops 335544320 | bytes 3145728 | tf_op jit(solution)/shard_map/suffix_attend/pallas_call | solution.py:111
  62.7 2.0 %collective-permute-done.11.refs_8_ = bf16[1,320,384]{2,1,0:T(8,128)(2,1)} collective-permute-done((bf16[1,320,384]{2,1,0:T(8,128)(2,1)S(1)}, bf16[1,320,384]{2,1,0:T(8,128)(2,1)}, u32[]{:S(2)}, u32[]{:S(2)}) %collective-permute-start.11) | collective-permute-done | bytes 245792 | tf_op jit(solution)/shard_map/ppermute | solution.py:328
  64.7 15.3 %prefix_attend.1 = (f32[320,512]{1,0:T(8,128)}, f32[8,512]{1,0:T(8,128)}, bf16[352,512]{1,0:T(8,128)(2,1)}) custom-call(s32[5]{0:T(128)} %pad_add_fusion.meta_ref, bf16[320,512]{1,0:T(8,128)(2,1)} %bitcast.77, bf16[320,512]{1,0:T(8,128)(2,1)} %collective-permute-done.5.other_q_ref, bf16[2,320,384]{2,1,0:T(8,128)(2,1)} %dynamic-slice_bitcast_fusion.refs_0_, ...), custom_call_target="tpu_custom_call" | custom-call | flops 2013265920 | bytes 6291456 | tf_op jit(solution)/shard_map/prefix_attend/pallas_call | solution.py:232
  80.0 0.1 collective-permute-start.12
  80.1 0.5 collective-permute-start.18
  80.6 1.4 %collective-permute-done.12.got_ref = bf16[352,512]{1,0:T(8,128)(2,1)S(1)} collective-permute-done((bf16[352,512]{1,0:T(8,128)(2,1)}, bf16[352,512]{1,0:T(8,128)(2,1)S(1)}, u32[]{:S(2)}, u32[]{:S(2)}) %collective-permute-start.12) | collective-permute-done | bytes 360480 | tf_op jit(solution)/shard_map/ppermute | solution.py:321
  82.0 0.7 copy-done.10
  82.7 2.2 %merge.1 = bf16[320,512]{1,0:T(8,128)(2,1)} custom-call(f32[320,512]{1,0:T(8,128)} %get-tuple-element.39.own_ref, f32[8,512]{1,0:T(8,128)} %get-tuple-element.40.own_lse_ref, bf16[352,512]{1,0:T(8,128)(2,1)} %copy-done.10, f32[320,512]{1,0:T(8,128)} %get-tuple-element.42.suffix_ref, f32[8,512]{1,0:T(8,128)} %get-tuple-element.43.suffix_lse_ref), custom_call_target="tpu_custom_call" | custom-call | flops 1310720 | bytes 1048576 | tf_op jit(solution)/shard_map/merge/pallas_call | solution.py:276
  84.9 0.1 collective-permute-start.13
  85.1 1.5 %collective-permute-start.15 = (bf16[320,512]{1,0:T(8,128)(2,1)}, bf16[320,512]{1,0:T(8,128)(2,1)S(1)}, u32[]{:S(2)}, u32[]{:S(2)}) collective-permute-start(bf16[320,512]{1,0:T(8,128)(2,1)} %merge.1), channel_id=1, source_target_pairs={{0,2},{1,3},{2,0},{3,1},{4,6},{5,7},{6,4},{7,5},{8,10},{9,11},{10,... | collective-permute-start | bytes 983048 | tf_op jit(solution)/shard_map/ppermute | solution.py:318
  86.6 2.7 %fusion.20 = f32[512,2048]{1,0:T(8,128)S(1)} fusion(bf16[320,512]{1,0:T(8,128)(2,1)} %merge.1, bf16[320,2048]{1,0:T(8,128)(2,1)} %param.24), kind=kOutput, calls=%fused_computation.68 | convolution fusion | flops 671088640 | bytes 5832704 | tf_op jit(solution)/shard_map/dot_general | solution.py:42
  89.3 1.3 fusion.21
  90.6 0.3 copy-done.2
  90.9 1.5 %add_add_fusion.1 = f32[512,2048]{1,0:T(8,128)S(1)} fusion(f32[512,2048]{1,0:T(8,128)S(1)} %fusion.21, f32[512,2048]{1,0:T(8,128)S(1)} %fusion.20, bf16[512,2048]{1,0:T(8,128)(2,1)S(1)} %copy-done.2), kind=kLoop, calls=%fused_computation.6 | loop fusion | flops 3145728 | bytes 14680064 | tf_op jit(solution)/shard_map/add | solution.py:391
  92.4 2.9 %collective-permute-done.15 = bf16[320,512]{1,0:T(8,128)(2,1)S(1)} collective-permute-done((bf16[320,512]{1,0:T(8,128)(2,1)}, bf16[320,512]{1,0:T(8,128)(2,1)S(1)}, u32[]{:S(2)}, u32[]{:S(2)}) %collective-permute-start.15) | collective-permute-done | bytes 327712 | tf_op jit(solution)/shard_map/ppermute | solution.py:318
  95.3 2.6 %fusion.22 = f32[512,2048]{1,0:T(8,128)S(1)} fusion(bf16[320,512]{1,0:T(8,128)(2,1)S(1)} %collective-permute-done.15, bf16[320,2048]{1,0:T(8,128)(2,1)} %collective-permute-done.16), kind=kOutput, calls=%fused_computation.70 | convolution fusion | flops 671088640 | bytes 5832704 | tf_op jit(solution)/shard_map/dot_general | solution.py:42
  97.9 3.2 %multiply_reduce_fusion = (f32[512]{0:T(512)S(1)}, f32[512,2048]{1,0:T(8,128)S(1)}) fusion(bf16[320,512]{1,0:T(8,128)(2,1)S(1)} %collective-permute-done.17, bf16[320,2048]{1,0:T(8,128)(2,1)} %collective-permute-done.18, f32[512,2048]{1,0:T(8,128)S(1)} %add_add_fusion.1, f32[512,2048]{1,0:T(8,128)S(1)} %fusion.22), kind=kOutput, calls=%fused_computation.4 | convolution fusion | flops 675282432 | bytes 14223360 | tf_op jit(solution)/shard_map/dot_general | solution.py:42
  101.2 5.6 %fusion = f32[512,2,1280]{2,0,1:T(8,128)S(1)} fusion(bf16[2048,2,1280]{2,1,0:T(2,128)(2,1)S(1)} %bitcast.83, f32[512,2048]{1,0:T(8,128)S(1)} %get-tuple-element.63, f32[2048]{0:T(1024)S(1)} %copy-done.18, f32[512]{0:T(512)S(1)} %add_rsqrt_fusion.2), kind=kOutput, calls=%fused_computation.1 | convolution fusion | flops 5371854848 | bytes 19933184 | tf_op jit(solution)/shard_map/rd,dgf->rgf/dot_general | solution.py:396
  106.9 0.8 fusion.3
  107.7 0.5 copy-done.8
  108.2 0.8 convolution_convert_fusion.2
  109.0 0.6 collective-permute-start.19
  109.6 1.5 %collective-permute-done.19 = bf16[512,512]{1,0:T(8,128)(2,1)S(1)} collective-permute-done((bf16[512,512]{1,0:T(8,128)(2,1)S(1)}, bf16[512,512]{1,0:T(8,128)(2,1)S(1)}, u32[]{:S(2)}, u32[]{:S(2)}) %collective-permute-start.19) | collective-permute-done | bytes 524320 | tf_op jit(solution)/shard_map/ppermute | solution.py:321
  111.2 0.8 fusion.10
  112.0 0.8 convolution_convert_fusion
  112.9 0.4 collective-permute-start.20
  113.3 1.5 %collective-permute-start.21 = (bf16[512,512]{1,0:T(8,128)(2,1)S(1)}, bf16[512,512]{1,0:T(8,128)(2,1)S(1)}, u32[]{:S(2)}, u32[]{:S(2)}) collective-permute-start(bf16[512,512]{1,0:T(8,128)(2,1)S(1)} %fusion.10), channel_id=1, source_target_pairs={{0,2},{1,3},{2,0},{3,1},{4,6},{5,7},{6,4},{7,5},{8,10},{9,11},{10,... | collective-permute-start | bytes 1572872 | tf_op jit(solution)/shard_map/ppermute | solution.py:318
  114.8 0.9 pad_maximum_fusion
  115.7 0.8 fusion.11
  116.6 10.7 %collective-permute-done.21 = bf16[512,512]{1,0:T(8,128)(2,1)S(1)} collective-permute-done((bf16[512,512]{1,0:T(8,128)(2,1)S(1)}, bf16[512,512]{1,0:T(8,128)(2,1)S(1)}, u32[]{:S(2)}, u32[]{:S(2)}) %collective-permute-start.21) | collective-permute-done | bytes 524320 | tf_op jit(solution)/shard_map/ppermute | solution.py:318
  127.3 1.1 add_convert_fusion
  (69 shorter events, 0.3 us)
Async XLA Ops:
  0.6 34.0 %copy-start = (bf16[2048,640]{1,0:T(8,128)(2,1)S(1)}, bf16[2048,640]{1,0:T(8,128)(2,1)}, u32[]{:S(2)}) copy-start(bf16[2048,640]{1,0:T(8,128)(2,1)} %param.21) | copy-start | bytes 7864324
  0.6 15.2 %collective-permute-start.1 = (bf16[512,512]{1,0:T(8,128)(2,1)}, bf16[512,512]{1,0:T(8,128)(2,1)S(1)}, u32[]{:S(2)}, u32[]{:S(2)}) collective-permute-start(bf16[512,512]{1,0:T(8,128)(2,1)} %own_ref), channel_id=1, source_target_pairs={{0,2},{1,3},{2,0},{3,1},{4,6},{5,7},{6,4},{7,5},{8,10},{9,11},{10,... | collective-permute-start | bytes 1572872 | tf_op jit(solution)/shard_map/ppermute | solution.py:318
  3.7 21.7 %collective-permute-start = (bf16[512,512]{1,0:T(8,128)(2,1)}, bf16[512,512]{1,0:T(8,128)(2,1)}, u32[]{:S(2)}, u32[]{:S(2)}) collective-permute-start(bf16[512,512]{1,0:T(8,128)(2,1)} %own_ref), channel_id=1, source_target_pairs={{0,1},{1,0},{2,3},{3,2},{4,5},{5,4},{6,7},{7,6},{8,9},{9,8},{10,11... | collective-permute-start | bytes 1572872 | tf_op jit(solution)/shard_map/ppermute | solution.py:321
  5.5 16.5 %collective-permute-start.3 = (bf16[2,320,384]{2,1,0:T(8,128)(2,1)}, bf16[2,320,384]{2,1,0:T(8,128)(2,1)}, u32[]{:S(2)}, u32[]{:S(2)}) collective-permute-start(bf16[2,320,384]{2,1,0:T(8,128)(2,1)} %dynamic-slice_bitcast_fusion.refs_0_), channel_id=1, source_target_pairs={{0,8},{4,12},{8,16},{12,20},{16,24},{20,28},{24,0},{28,4},{1,9},{5... | collective-permute-start | bytes 1474568 | tf_op jit(solution)/shard_map/ppermute | solution.py:328
  7.1 46.7 %collective-permute-start.6 = (bf16[2,320,384]{2,1,0:T(8,128)(2,1)}, bf16[2,320,384]{2,1,0:T(8,128)(2,1)}, u32[]{:S(2)}, u32[]{:S(2)}) collective-permute-start(bf16[2,320,384]{2,1,0:T(8,128)(2,1)} %dynamic-slice_bitcast_fusion.refs_0_), channel_id=1, source_target_pairs={{0,4},{4,0},{8,12},{12,8},{16,20},{20,16},{24,28},{28,24},{1,5},{5... | collective-permute-start | bytes 1474568 | tf_op jit(solution)/shard_map/ppermute | solution.py:331
  15.8 6.2 %copy-start.9 = (bf16[512,512]{1,0:T(8,128)(2,1)}, bf16[512,512]{1,0:T(8,128)(2,1)S(1)}, u32[]{:S(2)}) copy-start(bf16[512,512]{1,0:T(8,128)(2,1)S(1)} %collective-permute-done.1.chip_ref) | copy-start | bytes 1572868
  15.8 11.1 %collective-permute-start.2 = (bf16[512,512]{1,0:T(8,128)(2,1)S(1)}, bf16[512,512]{1,0:T(8,128)(2,1)}, u32[]{:S(2)}, u32[]{:S(2)}) collective-permute-start(bf16[512,512]{1,0:T(8,128)(2,1)S(1)} %collective-permute-done.1.chip_ref), channel_id=1, source_target_pairs={{0,1},{1,0},{2,3},{3,2},{4,5},{5,4},{6,7},{7,6},{8,9},{9,8},{10,11... | collective-permute-start | bytes 1572872 | tf_op jit(solution)/shard_map/ppermute | solution.py:321
  22.0 16.1 %collective-permute-start.4 = (bf16[2,320,384]{2,1,0:T(8,128)(2,1)}, bf16[2,320,384]{2,1,0:T(8,128)(2,1)}, u32[]{:S(2)}, u32[]{:S(2)}) collective-permute-start(bf16[2,320,384]{2,1,0:T(8,128)(2,1)} %collective-permute-done.3.refs_2_), channel_id=1, source_target_pairs={{0,8},{4,12},{8,16},{12,20},{16,24},{20,28},{24,0},{28,4},{1,9},{5... | collective-permute-start | bytes 1474568 | tf_op jit(solution)/shard_map/ppermute | solution.py:328
  23.9 31.3 %collective-permute-start.7 = (bf16[2,320,384]{2,1,0:T(8,128)(2,1)}, bf16[2,320,384]{2,1,0:T(8,128)(2,1)}, u32[]{:S(2)}, u32[]{:S(2)}) collective-permute-start(bf16[2,320,384]{2,1,0:T(8,128)(2,1)} %collective-permute-done.3.refs_2_), channel_id=1, source_target_pairs={{0,4},{4,0},{8,12},{12,8},{16,20},{20,16},{24,28},{28,24},{1,5},{5... | collective-permute-start | bytes 1474568 | tf_op jit(solution)/shard_map/ppermute | solution.py:331
  25.4 54.7 %collective-permute-start.16 = (bf16[320,2048]{1,0:T(8,128)(2,1)}, bf16[320,2048]{1,0:T(8,128)(2,1)}, u32[]{:S(2)}, u32[]{:S(2)}) collective-permute-start(bf16[320,2048]{1,0:T(8,128)(2,1)} %param.24), channel_id=1, source_target_pairs={{0,2},{1,3},{2,0},{3,1},{4,6},{5,7},{6,4},{7,5},{8,10},{9,11},{10,... | collective-permute-start | bytes 3932168 | tf_op jit(solution)/shard_map/ppermute | solution.py:318
  31.7 3.0 %copy-start.16 = (bf16[512,2048]{1,0:T(8,128)(2,1)S(1)}, bf16[512,2048]{1,0:T(8,128)(2,1)}, u32[]{:S(2)}) copy-start(bf16[512,2048]{1,0:T(8,128)(2,1)} %get-tuple-element.32) | copy-start | bytes 6291460
  34.7 5.1 %copy-start.15 = (f32[64]{0:T(128)S(1)}, f32[64]{0:T(128)}, u32[]{:S(2)}) copy-start(f32[64]{0:T(128)} %param.22) | copy-start | bytes 772
  38.1 2.1 %copy-start.14 = (f32[64]{0:T(128)S(1)}, f32[64]{0:T(128)}, u32[]{:S(2)}) copy-start(f32[64]{0:T(128)} %param.23) | copy-start | bytes 772
  38.1 15.1 %collective-permute-start.9 = (bf16[2,320,384]{2,1,0:T(8,128)(2,1)}, bf16[2,320,384]{2,1,0:T(8,128)(2,1)S(1)}, u32[]{:S(2)}, u32[]{:S(2)}) collective-permute-start(bf16[2,320,384]{2,1,0:T(8,128)(2,1)} %collective-permute-done.4.refs_4_), channel_id=1, source_target_pairs={{0,8},{4,12},{8,16},{12,20},{16,24},{20,28},{24,0},{28,4},{1,9},{5... | collective-permute-start | bytes 1474568 | tf_op jit(solution)/shard_map/ppermute | solution.py:328
  38.1 15.1 %collective-permute-start.8 = (bf16[2,320,384]{2,1,0:T(8,128)(2,1)}, bf16[2,320,384]{2,1,0:T(8,128)(2,1)S(1)}, u32[]{:S(2)}, u32[]{:S(2)}) collective-permute-start(bf16[2,320,384]{2,1,0:T(8,128)(2,1)} %collective-permute-done.4.refs_4_), channel_id=1, source_target_pairs={{0,4},{4,0},{8,12},{12,8},{16,20},{20,16},{24,28},{28,24},{1,5},{5... | collective-permute-start | bytes 1474568 | tf_op jit(solution)/shard_map/ppermute | solution.py:331
  40.2 16.6 %copy-start.11 = (bf16[512,5,64]{0,2,1:T(8,128)(2,1)}, bf16[512,5,64]{0,2,1:T(8,128)(2,1)S(1)}, u32[]{:S(2)}) copy-start(bf16[512,5,64]{0,2,1:T(8,128)(2,1)S(1)} %maximum_multiply_fusion) | copy-start | bytes 983044
  53.2 3.7 %copy-start.12 = (bf16[2,320,384]{2,1,0:T(8,128)(2,1)}, bf16[2,320,384]{2,1,0:T(8,128)(2,1)S(1)}, u32[]{:S(2)}) copy-start(bf16[2,320,384]{2,1,0:T(8,128)(2,1)S(1)} %collective-permute-done.9.refs_6_) | copy-start | bytes 1474564
  53.2 36.1 %collective-permute-start.14 = (bf16[320,2048]{1,0:T(8,128)(2,1)}, bf16[320,2048]{1,0:T(8,128)(2,1)S(1)}, u32[]{:S(2)}, u32[]{:S(2)}) collective-permute-start(bf16[320,2048]{1,0:T(8,128)(2,1)} %param.24), channel_id=1, source_target_pairs={{0,1},{1,0},{2,3},{3,2},{4,5},{5,4},{6,7},{7,6},{8,9},{9,8},{10,11... | collective-permute-start | bytes 3932168 | tf_op jit(solution)/shard_map/ppermute | solution.py:321
  53.2 3.6 %copy-start.13 = (bf16[2,320,384]{2,1,0:T(8,128)(2,1)}, bf16[2,320,384]{2,1,0:T(8,128)(2,1)S(1)}, u32[]{:S(2)}) copy-start(bf16[2,320,384]{2,1,0:T(8,128)(2,1)S(1)} %collective-permute-done.8.refs_5_) | copy-start | bytes 1474564
  53.3 9.4 %collective-permute-start.5 = (bf16[320,512]{1,0:T(8,128)(2,1)S(1)}, bf16[320,512]{1,0:T(8,128)(2,1)}, u32[]{:S(2)}, u32[]{:S(2)}) collective-permute-start(bf16[320,512]{1,0:T(8,128)(2,1)S(1)} %bitcast.75), channel_id=1, source_target_pairs={{0,1},{1,0},{2,3},{3,2},{4,5},{5,4},{6,7},{7,6},{8,9},{9,8},{10,11... | collective-permute-start | bytes 983048 | tf_op jit(solution)/shard_map/ppermute | solution.py:321
  53.9 8.8 %collective-permute-start.10 = (bf16[1,320,384]{2,1,0:T(8,128)(2,1)S(1)}, bf16[1,320,384]{2,1,0:T(8,128)(2,1)S(1)}, u32[]{:S(2)}, u32[]{:S(2)}) collective-permute-start(bf16[1,320,384]{2,1,0:T(8,128)(2,1)S(1)} %slice.50), channel_id=1, source_target_pairs={{0,4},{4,0},{8,12},{12,8},{16,20},{20,16},{24,28},{28,24},{1,5},{5... | collective-permute-start | bytes 737288 | tf_op jit(solution)/shard_map/ppermute | solution.py:331
  55.2 9.5 %collective-permute-start.11 = (bf16[1,320,384]{2,1,0:T(8,128)(2,1)S(1)}, bf16[1,320,384]{2,1,0:T(8,128)(2,1)}, u32[]{:S(2)}, u32[]{:S(2)}) collective-permute-start(bf16[1,320,384]{2,1,0:T(8,128)(2,1)S(1)} %slice.51), channel_id=1, source_target_pairs={{0,8},{4,12},{8,16},{12,20},{16,24},{20,28},{24,0},{28,4},{1,9},{5... | collective-permute-start | bytes 737288 | tf_op jit(solution)/shard_map/ppermute | solution.py:328
  62.7 2.1 %copy-start.17 = (bf16[1,320,384]{2,1,0:T(8,128)(2,1)}, bf16[1,320,384]{2,1,0:T(8,128)(2,1)S(1)}, u32[]{:S(2)}) copy-start(bf16[1,320,384]{2,1,0:T(8,128)(2,1)S(1)} %collective-permute-done.10.refs_7_) | copy-start | bytes 737284
  80.0 2.0 %collective-permute-start.12 = (bf16[352,512]{1,0:T(8,128)(2,1)}, bf16[352,512]{1,0:T(8,128)(2,1)S(1)}, u32[]{:S(2)}, u32[]{:S(2)}) collective-permute-start(bf16[352,512]{1,0:T(8,128)(2,1)} %get-tuple-element.41), channel_id=1, source_target_pairs={{0,1},{1,0},{2,3},{3,2},{4,5},{5,4},{6,7},{7,6},{8,9},{9,8},{10,11... | collective-permute-start | bytes 1081352 | tf_op jit(solution)/shard_map/ppermute | solution.py:321
  80.1 17.8 %collective-permute-start.18 = (bf16[320,2048]{1,0:T(8,128)(2,1)}, bf16[320,2048]{1,0:T(8,128)(2,1)}, u32[]{:S(2)}, u32[]{:S(2)}) collective-permute-start(bf16[320,2048]{1,0:T(8,128)(2,1)} %collective-permute-done.16), channel_id=1, source_target_pairs={{0,1},{1,0},{2,3},{3,2},{4,5},{5,4},{6,7},{7,6},{8,9},{9,8},{10,11... | collective-permute-start | bytes 3932168 | tf_op jit(solution)/shard_map/ppermute | solution.py:321
  82.0 0.7 copy-start.10
  84.9 4.3 %collective-permute-start.13 = (bf16[320,512]{1,0:T(8,128)(2,1)}, bf16[320,512]{1,0:T(8,128)(2,1)S(1)}, u32[]{:S(2)}, u32[]{:S(2)}) collective-permute-start(bf16[320,512]{1,0:T(8,128)(2,1)} %merge.1), channel_id=1, source_target_pairs={{0,1},{1,0},{2,3},{3,2},{4,5},{5,4},{6,7},{7,6},{8,9},{9,8},{10,11... | collective-permute-start | bytes 983048 | tf_op jit(solution)/shard_map/ppermute | solution.py:321
  85.1 10.2 %collective-permute-start.15 = (bf16[320,512]{1,0:T(8,128)(2,1)}, bf16[320,512]{1,0:T(8,128)(2,1)S(1)}, u32[]{:S(2)}, u32[]{:S(2)}) collective-permute-start(bf16[320,512]{1,0:T(8,128)(2,1)} %merge.1), channel_id=1, source_target_pairs={{0,2},{1,3},{2,0},{3,1},{4,6},{5,7},{6,4},{7,5},{8,10},{9,11},{10,... | collective-permute-start | bytes 983048 | tf_op jit(solution)/shard_map/ppermute | solution.py:318
  89.3 1.6 %copy-start.2 = (bf16[512,2048]{1,0:T(8,128)(2,1)S(1)}, bf16[512,2048]{1,0:T(8,128)(2,1)}, u32[]{:S(2)}) copy-start(bf16[512,2048]{1,0:T(8,128)(2,1)} %get-tuple-element.31) | copy-start | bytes 6291460
  90.9 10.3 %slice-start = ((s8[10485760]{0:T(1024)(128)(4,1)}), s8[4194304]{0:T(1024)(128)(4,1)S(1)}, s32[]{:S(2)}) async-start(s8[10485760]{0:T(1024)(128)(4,1)} %bitcast.82), calls=%async_computation | async-start | bytes 8388608
  90.9 10.3 %slice-start.1 = ((s8[10485760]{0:T(1024)(128)(4,1)}), s8[2097152]{0:T(1024)(128)(4,1)S(1)}, s32[]{:S(2)}) async-start(s8[10485760]{0:T(1024)(128)(4,1)} %bitcast.82), calls=%async_computation.1 | async-start | bytes 4194304
  95.3 2.6 %collective-permute-start.17 = (bf16[320,512]{1,0:T(8,128)(2,1)S(1)}, bf16[320,512]{1,0:T(8,128)(2,1)S(1)}, u32[]{:S(2)}, u32[]{:S(2)}) collective-permute-start(bf16[320,512]{1,0:T(8,128)(2,1)S(1)} %collective-permute-done.15), channel_id=1, source_target_pairs={{0,1},{1,0},{2,3},{3,2},{4,5},{5,4},{6,7},{7,6},{8,9},{9,8},{10,11... | collective-permute-start | bytes 983048 | tf_op jit(solution)/shard_map/ppermute | solution.py:321
  97.9 3.3 %slice-start.2 = ((s8[10485760]{0:T(1024)(128)(4,1)}), s8[4194304]{0:T(1024)(128)(4,1)S(1)}, s32[]{:S(2)}) async-start(s8[10485760]{0:T(1024)(128)(4,1)} %bitcast.82), calls=%async_computation.2 | async-start | bytes 8388608
  97.9 3.3 %copy-start.18 = (f32[2048]{0:T(1024)S(1)}, f32[2048]{0:T(1024)}, u32[]{:S(2)}) copy-start(f32[2048]{0:T(1024)} %param.25) | copy-start | bytes 24580
  106.9 1.3 %copy-start.8 = (bf16[1280,512]{1,0:T(8,128)(2,1)S(1)}, bf16[1280,512]{1,0:T(8,128)(2,1)}, u32[]{:S(2)}) copy-start(bf16[1280,512]{1,0:T(8,128)(2,1)} %get-tuple-element.48) | copy-start | bytes 3932164
  108.2 3.0 %copy-start.7 = (bf16[1280,512]{1,0:T(8,128)(2,1)S(1)}, bf16[1280,512]{1,0:T(8,128)(2,1)}, u32[]{:S(2)}) copy-start(bf16[1280,512]{1,0:T(8,128)(2,1)} %get-tuple-element.47) | copy-start | bytes 3932164
  109.0 3.0 %copy-start.6 = (bf16[1280,512]{1,0:T(8,128)(2,1)S(1)}, bf16[1280,512]{1,0:T(8,128)(2,1)}, u32[]{:S(2)}) copy-start(bf16[1280,512]{1,0:T(8,128)(2,1)} %get-tuple-element.51) | copy-start | bytes 3932164
  109.0 2.1 %collective-permute-start.19 = (bf16[512,512]{1,0:T(8,128)(2,1)S(1)}, bf16[512,512]{1,0:T(8,128)(2,1)S(1)}, u32[]{:S(2)}, u32[]{:S(2)}) collective-permute-start(bf16[512,512]{1,0:T(8,128)(2,1)S(1)} %convolution_convert_fusion.2), channel_id=1, source_target_pairs={{0,1},{1,0},{2,3},{3,2},{4,5},{5,4},{6,7},{7,6},{8,9},{9,8},{10,11... | collective-permute-start | bytes 1572872 | tf_op jit(solution)/shard_map/ppermute | solution.py:321
  112.0 2.8 %copy-start.3 = (bf16[512,1,5,64]{0,3,2,1:T(8,128)(2,1)S(1)}, bf16[512,1,5,64]{0,3,2,1:T(8,128)(2,1)}, u32[]{:S(2)}) copy-start(bf16[512,1,5,64]{0,3,2,1:T(8,128)(2,1)} %slice.73) | copy-start | bytes 983044
  112.0 2.8 %copy-start.4 = (bf16[512,5,64]{0,2,1:T(8,128)(2,1)S(1)}, bf16[512,5,64]{0,2,1:T(8,128)(2,1)}, u32[]{:S(2)}) copy-start(bf16[512,5,64]{0,2,1:T(8,128)(2,1)} %maximum_convert_fusion) | copy-start | bytes 983044
  112.0 3.7 %copy-start.5 = (bf16[1280,512]{1,0:T(8,128)(2,1)S(1)}, bf16[1280,512]{1,0:T(8,128)(2,1)}, u32[]{:S(2)}) copy-start(bf16[1280,512]{1,0:T(8,128)(2,1)} %get-tuple-element.50) | copy-start | bytes 3932164
  112.9 3.7 %collective-permute-start.20 = (bf16[512,512]{1,0:T(8,128)(2,1)S(1)}, bf16[512,512]{1,0:T(8,128)(2,1)S(1)}, u32[]{:S(2)}, u32[]{:S(2)}) collective-permute-start(bf16[512,512]{1,0:T(8,128)(2,1)S(1)} %convolution_convert_fusion), channel_id=1, source_target_pairs={{0,1},{1,0},{2,3},{3,2},{4,5},{5,4},{6,7},{7,6},{8,9},{9,8},{10,11... | collective-permute-start | bytes 1572872 | tf_op jit(solution)/shard_map/ppermute | solution.py:321
  113.3 14.0 %collective-permute-start.21 = (bf16[512,512]{1,0:T(8,128)(2,1)S(1)}, bf16[512,512]{1,0:T(8,128)(2,1)S(1)}, u32[]{:S(2)}, u32[]{:S(2)}) collective-permute-start(bf16[512,512]{1,0:T(8,128)(2,1)S(1)} %fusion.10), channel_id=1, source_target_pairs={{0,2},{1,3},{2,0},{3,1},{4,6},{5,7},{6,4},{7,5},{8,10},{9,11},{10,... | collective-permute-start | bytes 1572872 | tf_op jit(solution)/shard_map/ppermute | solution.py:318
  115.7 12.7 %copy-start.1 = (bf16[2048,640]{1,0:T(8,128)(2,1)S(1)}, bf16[2048,640]{1,0:T(8,128)(2,1)}, u32[]{:S(2)}) copy-start(bf16[2048,640]{1,0:T(8,128)(2,1)} %param.21) | copy-start | bytes 7864324

commit v5 on v4

--- a/solution.py
+++ b/solution.py
@@ -21,12 +21,16 @@
     return values * lax.rsqrt(mean_sq + eps_norm) * gain_vec
 
 
-def rotate(values, positions):
+def turns(positions, half_size):
+    frequency = rope_base ** (-jnp.arange(half_size, dtype=jnp.float32) * 2.0 / (2 * half_size))
+    angles = positions.astype(jnp.float32)[:, None] * frequency[None, :]
+    return jnp.cos(angles), jnp.sin(angles)
+
+
+def rotate(values, cos_part, sin_part):
     half_size = values.shape[-1] // 2
-    frequency = rope_base ** (-jnp.arange(half_size, dtype=jnp.float32) * 2.0 / values.shape[-1])
-    angles = positions.astype(jnp.float32)[:, None] * frequency[None, :]
-    cos_part = jnp.cos(angles)[:, None, :]
-    sin_part = jnp.sin(angles)[:, None, :]
+    cos_part = cos_part[:, None, :]
+    sin_part = sin_part[:, None, :]
     front_half = values[..., :half_size]
     back_half = values[..., half_size:]
     return jnp.concatenate(
@@ -83,7 +87,7 @@
 
 
 def suffix_kernel(len_ref, q_ref, k_ref, v_ref, out_ref, lse_ref):
-    first_len = len_ref[0]
+    first_len = len_ref[0, 0]
     rows = q_ref.shape[1]
     block = 256
     heads = q_ref.shape[0] // HEAD_SIZE
@@ -105,7 +109,7 @@
             lse_ref[head : head + 1, start : start + block] = row_max + jnp.log(total)
 
 
-def suffix_attend(first_len, q_t, k_t, v_t):
+def suffix_attend(lengths, q_t, k_t, v_t):
     columns, rows = q_t.shape
     vmem = pl.BlockSpec(memory_space=pltpu.VMEM)
     return pl.pallas_call(
@@ -118,31 +122,41 @@
         out_specs=[vmem, vmem],
         cost_estimate=pl.CostEstimate(flops=4 * columns * rows * rows, bytes_accessed=3 << 20, transcendentals=5 * rows * rows),
         name="suffix_attend",
-    )(first_len.reshape(1), q_t, k_t, v_t)
+    )(lengths, q_t, k_t, v_t)
 
 
 def fold(values, op):
     return op(values.reshape(values.shape[0] // 8, 8, values.shape[1]), axis=0)
 
 
-def prefix_kernel(block, chunk, n_units, meta_ref, own_q_ref, other_q_ref, *refs):
+def turn(place, length):
+    return jnp.where(place % 2 == 0, place // 2, length - (place + 1) // 2)
+
+
+def prefix_kernel(block, chunk, n_units, owners_ref, groups_ref, lengths_ref, me_ref, own_q_ref, other_q_ref, *refs):
     units, last_keys, last_values = refs[: n_units - 1], refs[n_units - 1], refs[n_units]
     (own_out, own_lse, other_out), scratch = refs[n_units + 1 : n_units + 4], refs[n_units + 4 :]
     kv, q_buf, o_buf, l_buf, s_a, s_b, m_a, m_b, sems = scratch
-    first_len = meta_ref[4]
+    first_len = lengths_ref[0, 0]
+    me = me_ref[0]
+    length = n_units // 2
     share = units[0].shape[2]
 
     def landing(job, kind=slice(None)):
         return kv.at[job // 2, kind, :, pl.ds((job % 2) * share, share)]
 
     for job in range(4):
+        holder = owners_ref[2 * groups_ref[0, job // 2] + job % 2]
+        away = turn(me // 2, length) - turn(holder // 2, length)
+        away = jnp.where(away < 0, away + length, away)
+        wanted = 2 * away + jnp.where(holder % 2 == me % 2, 0, 1)
         for unit in range(n_units - 1):
 
-            @pl.when(meta_ref[job] == unit)
+            @pl.when(wanted == unit)
             def _():
                 pltpu.make_async_copy(units[unit], landing(job), sems.at[job]).start()
 
-        @pl.when(meta_ref[job] == n_units - 1)
+        @pl.when(wanted == n_units - 1)
         def _():
             pltpu.make_async_copy(last_keys, landing(job, pl.ds(0, 1)), sems.at[job]).start()
             pltpu.make_async_copy(last_values, landing(job, pl.ds(1, 1)), sems.at[job]).start()
@@ -221,7 +235,7 @@
     other_out[columns:] = jnp.concatenate(terms).astype(jnp.bfloat16)
 
 
-def prefix_attend(meta, own_q, other_q, units):
+def prefix_attend(owners, groups, lengths, me, own_q, other_q, units):
     columns, rows = own_q.shape
     share = units[0].shape[2]
     block = 256
@@ -232,7 +246,8 @@
     return pl.pallas_call(
         functools.partial(prefix_kernel, block, 256, len(units) - 1),
         out_shape=(out, lse, sent),
-        in_specs=[pl.BlockSpec(memory_space=pltpu.SMEM), vmem, vmem]
+        in_specs=[pl.BlockSpec(memory_space=pltpu.SMEM)] * 4
+        + [vmem] * 2
         + [pl.BlockSpec(memory_space=pl.ANY)] * len(units),
         out_specs=[vmem] * 3,
         scratch_shapes=[
@@ -250,7 +265,7 @@
             flops=32 * columns * rows * share, bytes_accessed=6 << 20, transcendentals=20 * rows * share
         ),
         name="prefix_attend",
-    )(meta, own_q, other_q, *units)
+    )(owners, groups, lengths, me, own_q, other_q, *units)
 
 
 def merge_kernel(own_ref, own_lse_ref, got_ref, suffix_ref, suffix_lse_ref, out_ref):
@@ -320,42 +335,43 @@
     def across_core(value):
         return lax.ppermute(value, "tp", [(i, i ^ 1) for i in range(4)])
 
+    row_index = jnp.arange(row_count, dtype=jnp.int32)
+    first_len = request_lengths[0, 0]
+    segment = (row_index >= first_len).astype(jnp.int32)
+    position = row_index - segment * first_len + PREFIX
+    cos_part, sin_part = turns(position, HEAD_SIZE // 2)
+
     length = n_req // 2
     share = prefix_cache.shape[2] // 2
-    mine = lax.dynamic_slice_in_dim(jnp.transpose(prefix_cache[0], (0, 2, 1)), core * share, share, 2)
+    mine = lax.dynamic_slice(jnp.transpose(prefix_cache[0], (0, 2, 1)), (0, 0, core * share), (2, columns, share))
 
     def ring(value):
-        return lax.ppermute(value, "req", [(r, (r + 2) % n_req) for r in range(n_req)])
+        order = [*range(0, length, 2), *range(length - 1 - length % 2, 0, -2)]
+        steps = zip(order, order[1:] + order[:1])
+        return lax.ppermute(value, "req", [(2 * a + b, 2 * c + b) for a, c in steps for b in range(2)])
 
     def aside(value):
         return lax.ppermute(value, "req", [(r, r ^ 1) for r in range(n_req)])
 
     held = [mine, ring(mine)]
     units = [mine, aside(mine)]
-    wanted = owners.reshape(-1, 2)[request_groups[0]].reshape(-1)
-    distance = (my_req // 2 - wanted // 2) % length
-    unit_index = 2 * distance + (wanted % 2 != my_req % 2).astype(jnp.int32)
-
     from_chip = across_chip(tokens)
     from_core = across_core(tokens)
-    from_both = across_core(from_chip)
     down_blocks = [
         lax.dynamic_slice_in_dim(w_down, (rank ^ flip) * width, width, 1) for flip in range(4)
     ]
-    pieces, down_blocks, _ = lax.optimization_barrier(
-        ((tokens, from_core, from_chip, from_both), down_blocks, held[1])
-    )
-    full_rows, normalized_input = gather_norm(rank, pieces, attn_gain)
+    held[1], units[1], down_blocks, cos_part, sin_part = lax.optimization_barrier(
+        (held[1], units[1], down_blocks, cos_part, sin_part)
+    )
+    from_chip, _ = lax.optimization_barrier((from_chip, held[1]))
+    from_both = across_core(from_chip)
+    full_rows, normalized_input = gather_norm(rank, (tokens, from_core, from_chip, from_both), attn_gain)
 
     w_out_held, _ = lax.optimization_barrier((w_out, from_chip))
     w_out_chip = across_chip(w_out_held)
     w_out_core = across_core(w_out)
     w_out_both = across_core(w_out_chip)
 
-    row_index = jnp.arange(row_count, dtype=jnp.int32)
-    first_len = request_lengths[0, 0]
-    segment = (row_index >= first_len).astype(jnp.int32)
-    position = row_index - segment * first_len + PREFIX
     query_rows = jnp.dot(
         normalized_input, query_weight, preferred_element_type=jnp.float32
     ).reshape(row_count, head_count, HEAD_SIZE)
@@ -369,8 +385,8 @@
         units += [held[-1], aside(held[-1])]
         held.append(ring(held[-1]))
     units += [held[-1], aside(held[-1][:1]), ring(units[-1][1:])]
-    query_rows = rotate(rms_scale(query_rows, query_gain), position).astype(jnp.bfloat16)
-    key_rows = rotate(rms_scale(key_value_rows[:, 0], key_gain), position).astype(jnp.bfloat16)
+    query_rows = rotate(rms_scale(query_rows, query_gain), cos_part, sin_part).astype(jnp.bfloat16)
+    key_rows = rotate(rms_scale(key_value_rows[:, 0], key_gain), cos_part, sin_part).astype(jnp.bfloat16)
     value_rows = key_value_rows[:, 1].astype(jnp.bfloat16)
     cache_rows = jnp.stack(
         [key_rows.reshape(row_count, columns), value_rows.reshape(row_count, columns)],
@@ -379,12 +395,13 @@
     own_q = (query_rows * HEAD_SIZE**-0.5).reshape(row_count, columns).T
     other_q = across_core(own_q)
     suffix_out, suffix_lse = suffix_attend(
-        first_len, own_q, key_rows.reshape(row_count, columns).T, value_rows.reshape(row_count, columns).T
+        request_lengths, own_q, key_rows.reshape(row_count, columns).T, value_rows.reshape(row_count, columns).T
     )
 
     own_q, suffix_out, suffix_lse = lax.optimization_barrier((own_q, suffix_out, suffix_lse))
-    meta = jnp.concatenate([unit_index.astype(jnp.int32), first_len.reshape(1)])
-    own_out, own_lse, sent = prefix_attend(meta, own_q, other_q, units)
+    own_out, own_lse, sent = prefix_attend(
+        owners, request_groups, request_lengths, my_req.reshape(1), own_q, other_q, units
+    )
     attention = merge(own_out, own_lse, across_core(sent), suffix_out, suffix_lse)
     att_chip = across_chip(attention)
     att_core = across_core(attention)

time: 129 us -> 124 us (0.961)
  other arithmetic: 8.7 us -> 5.27 us
  waiting for transfers between devices: 37.5 us -> 34.1 us
  matrix products: 23.3 us -> 24.9 us
  starting transfers between devices: 19.2 us -> 20.7 us
    ppermute x4, starting transfers between devices: 3.46 us -> 9.47 us  [ring(): lax.ppermute(value, 'req', [(2 * a + b, 2 * c + b) for a, c in steps for...]
    ppermute x4, waiting for transfers between devices: 16.8 us -> 11.3 us  [ring(): lax.ppermute(value, 'req', [(2 * a + b, 2 * c + b) for a, c in steps for...]
    ppermute x4, waiting for transfers between devices: 0.01 us -> 4.27 us  [aside(): return lax.ppermute(value, 'req', [(r, r ^ 1) for r in range(n_req)])]
    ppermute x4, starting transfers between devices: 5.93 us -> 3.04 us  [aside(): return lax.ppermute(value, 'req', [(r, r ^ 1) for r in range(n_req)])]
    ppermute x4, waiting for transfers between devices: 17.8 us -> 15.7 us  [across_chip(): return lax.ppermute(value, 'tp', [(i, i ^ 2) for i in range(4)])]
    dot_general x4, matrix products: 9.8 us -> 11.4 us  [tn_dot(): lax.dot_general(lhs, rhs, (((0,), (0,)), ((), ())), preferred_element_typ...]
    ppermute x4, starting transfers between devices: 7.51 us -> 5.96 us  [across_chip(): return lax.ppermute(value, 'tp', [(i, i ^ 2) for i in range(4)])]
    add x2 -> x0, other arithmetic: 1.52 us -> none  [the longest x1 1.5 us: local(): full_rows.astype(jnp.float32) + tn_dot(attention, w_out)]
  transfers between devices with their start and end apart: 22 -> 22, of which waited for: 8 -> 10; matrix products, arithmetic and copies ran while one was open for 22% -> 18% of each run, Pallas kernels for 22% -> 22%
where the time goes in v5:
time: 124 us
  waiting for transfers between devices  34.1 us (28%)
  Pallas kernels  27.6 us (22%)
  matrix products  24.9 us (20%)
  starting transfers between devices  20.7 us (17%)
  local copies, waits for them, and re-layouts  9.97 us (8%)
  other arithmetic  5.27 us (4%)
    ppermute x4, waiting for transfers between devices, across_chip(): return lax.ppermute(value, 'tp', [(i, i ^ 2) for i in range(4)])  15.7 us
    pallas_call x1, Pallas kernels, prefix_attend(): pl.pallas_call(functools.partial(prefix_kernel, block, 256, len(units) -...  15.5 us
    dot_general x4, matrix products, tn_dot(): lax.dot_general(lhs, rhs, (((0,), (0,)), ((), ())), preferred_element_typ...  11.4 us
    ppermute x4, waiting for transfers between devices, ring(): lax.ppermute(value, 'req', [(2 * a + b, 2 * c + b) for a, c in steps for...  11.3 us
    ppermute x4, starting transfers between devices, ring(): lax.ppermute(value, 'req', [(2 * a + b, 2 * c + b) for a, c in steps for...  9.47 us
    ppermute x4, starting transfers between devices, across_chip(): return lax.ppermute(value, 'tp', [(i, i ^ 2) for i in range(4)])  5.96 us
    dot_general x1, matrix products, local(): jnp.einsum('rd,dgf->rgf', normed_ffn, w_gate_up, preferred_element_type=j...  5.64 us
    pallas_call x1, Pallas kernels, suffix_attend(): pl.pallas_call(suffix_kernel, out_shape=(jax.ShapeDtypeStruct((columns, r...  5.17 us
  transfers between devices with their start and end apart: 22, of which 10 were waited for; matrix products, arithmetic and copies ran while one was open for 18% of the time, Pallas kernels for 22%

profile of v5, /device:TPU:0, one launch (start us, length us, event | category | flops | bytes accessed | tf_op | source)
XLA Modules:
  0.0 123.7 jit_solution(8256162125288774897)
XLA Ops:
  0.6 0.0 copy-start
  0.7 2.0 %dynamic-slice_bitcast_fusion.refs_0_ = bf16[2,320,384]{2,1,0:T(8,128)(2,1)} fusion(bf16[1,2,768,320]{2,3,1,0:T(8,128)(2,1)} %param.18, s32[]{:T(128)S(6)} %select_n.24), kind=kLoop, calls=%fused_computation.31 | loop fusion | bytes 983044 | tf_op jit(solution)/shard_map/dynamic_slice | solution.py:346
  2.7 4.1 %collective-permute-start.2 = (bf16[2,320,384]{2,1,0:T(8,128)(2,1)}, bf16[2,320,384]{2,1,0:T(8,128)(2,1)}, u32[]{:S(2)}, u32[]{:S(2)}) collective-permute-start(bf16[2,320,384]{2,1,0:T(8,128)(2,1)} %dynamic-slice_bitcast_fusion.refs_0_), channel_id=1, source_target_pairs={{0,16},{4,20},{16,24},{20,28},{24,8},{28,12},{8,0},{12,4},{1,17},{... | collective-permute-start | bytes 1474568 | tf_op jit(solution)/shard_map/ppermute | solution.py:351
  6.8 1.5 %collective-permute-start.3 = (bf16[2,320,384]{2,1,0:T(8,128)(2,1)}, bf16[2,320,384]{2,1,0:T(8,128)(2,1)}, u32[]{:S(2)}, u32[]{:S(2)}) collective-permute-start(bf16[2,320,384]{2,1,0:T(8,128)(2,1)} %dynamic-slice_bitcast_fusion.refs_0_), channel_id=1, source_target_pairs={{0,4},{4,0},{8,12},{12,8},{16,20},{20,16},{24,28},{28,24},{1,5},{5... | collective-permute-start | bytes 1474568 | tf_op jit(solution)/shard_map/ppermute | solution.py:354
  8.3 1.5 %collective-permute-start.1 = (bf16[512,512]{1,0:T(8,128)(2,1)}, bf16[512,512]{1,0:T(8,128)(2,1)S(1)}, u32[]{:S(2)}, u32[]{:S(2)}) collective-permute-start(bf16[512,512]{1,0:T(8,128)(2,1)} %own_ref.1), channel_id=1, source_target_pairs={{0,2},{1,3},{2,0},{3,1},{4,6},{5,7},{6,4},{7,5},{8,10},{9,11},{10,... | collective-permute-start | bytes 1572872 | tf_op jit(solution)/shard_map/ppermute | solution.py:333
  9.8 0.7 add_convert_fusion.2
  10.4 0.3 multiply_sine_fusion
  10.8 4.9 %constant_dynamic-slice_fusion = (bf16[1280,512]{1,0:T(8,128)(2,1)}, bf16[1280,512]{1,0:T(8,128)(2,1)}, bf16[1280,512]{1,0:T(8,128)(2,1)}, bf16[1280,512]{1,0:T(8,128)(2,1)}) fusion(bf16[1280,2048]{1,0:T(8,128)(2,1)} %param.27, s32[]{:T(128)S(6)} %select_n.28, s32[]{:T(128)S(6)} %select_n.26, s32[]{:T(128)S(6)} %select_n.25, s32[]{:T(128)S(6)} %select_n.27), kind=kLoop, calls=%fused_computation.44 | loop fusion | bytes 10485776 | tf_op jit(solution)/shard_map/dynamic_slice | solution.py:361
  15.7 1.8 %collective-permute-done.2.refs_2_ = bf16[2,320,384]{2,1,0:T(8,128)(2,1)} collective-permute-done((bf16[2,320,384]{2,1,0:T(8,128)(2,1)}, bf16[2,320,384]{2,1,0:T(8,128)(2,1)}, u32[]{:S(2)}, u32[]{:S(2)}) %collective-permute-start.2) | collective-permute-done | bytes 491552 | tf_op jit(solution)/shard_map/ppermute | solution.py:351
  17.6 2.2 %collective-permute-done.3.refs_1_ = bf16[2,320,384]{2,1,0:T(8,128)(2,1)} collective-permute-done((bf16[2,320,384]{2,1,0:T(8,128)(2,1)}, bf16[2,320,384]{2,1,0:T(8,128)(2,1)}, u32[]{:S(2)}, u32[]{:S(2)}) %collective-permute-start.3) | collective-permute-done | bytes 491552 | tf_op jit(solution)/shard_map/ppermute | solution.py:354
  19.8 1.8 %collective-permute-done.1.chip_ref = bf16[512,512]{1,0:T(8,128)(2,1)S(1)} collective-permute-done((bf16[512,512]{1,0:T(8,128)(2,1)}, bf16[512,512]{1,0:T(8,128)(2,1)S(1)}, u32[]{:S(2)}, u32[]{:S(2)}) %collective-permute-start.1) | collective-permute-done | bytes 524320 | tf_op jit(solution)/shard_map/ppermute | solution.py:333
  21.6 0.5 collective-permute-start.14
  22.1 1.6 %collective-permute-start.5 = (bf16[2,320,384]{2,1,0:T(8,128)(2,1)}, bf16[2,320,384]{2,1,0:T(8,128)(2,1)}, u32[]{:S(2)}, u32[]{:S(2)}) collective-permute-start(bf16[2,320,384]{2,1,0:T(8,128)(2,1)} %collective-permute-done.2.refs_2_), channel_id=1, source_target_pairs={{0,16},{4,20},{16,24},{20,28},{24,8},{28,12},{8,0},{12,4},{1,17},{... | collective-permute-start | bytes 1474568 | tf_op jit(solution)/shard_map/ppermute | solution.py:351
  23.7 0.5 collective-permute-start.7
  24.2 1.5 %collective-permute-start.16 = (bf16[320,2048]{1,0:T(8,128)(2,1)}, bf16[320,2048]{1,0:T(8,128)(2,1)}, u32[]{:S(2)}, u32[]{:S(2)}) collective-permute-start(bf16[320,2048]{1,0:T(8,128)(2,1)} %param.24), channel_id=1, source_target_pairs={{0,2},{1,3},{2,0},{3,1},{4,6},{5,7},{6,4},{7,5},{8,10},{9,11},{10,... | collective-permute-start | bytes 3932168 | tf_op jit(solution)/shard_map/ppermute | solution.py:333
  25.7 4.7 %gather_norm.1 = (bf16[512,2048]{1,0:T(8,128)(2,1)}, bf16[512,2048]{1,0:T(8,128)(2,1)}) custom-call(s32[1]{0:T(128)} %bitcast.rank_ref, bf16[512,512]{1,0:T(8,128)(2,1)} %own_ref.1, bf16[512,512]{1,0:T(8,128)(2,1)} %collective-permute-done.core_ref, bf16[512,512]{1,0:T(8,128)(2,1)} %copy-done.9, bf16[512,512]{1,0:T(8,128)(2,1)} %collective-permute-done.4.both_ref, ...), custom_call_target="tpu_custom_call" | custom-call | tf_op jit(solution)/shard_map/gather_norm/pallas_call | solution.py:73
  30.4 3.0 %fusion.14 = f32[512,320]{0,1:T(8,128)S(1)} fusion(bf16[512,2048]{1,0:T(8,128)(2,1)} %get-tuple-element.31, bf16[2048,320]{0,1:T(8,128)(2,1)} %param.20), kind=kOutput, calls=%fused_computation.49 | convolution fusion | flops 671088640 | bytes 4063232 | tf_op jit(solution)/shard_map/dot_general | solution.py:375
  33.4 1.6 %fusion.15 = f32[512,640]{0,1:T(8,128)S(1)} fusion(bf16[512,2048]{1,0:T(8,128)(2,1)S(1)} %copy-done.16, bf16[2048,640]{1,0:T(8,128)(2,1)S(1)} %copy-done), kind=kOutput, calls=%fused_computation.50 | convolution fusion | flops 1342177280 | bytes 6029312 | tf_op jit(solution)/shard_map/dot_general | solution.py:378
  35.0 0.5 collective-permute-done.5.refs_4_
  35.6 2.5 %collective-permute-start.9 = (bf16[2,320,384]{2,1,0:T(8,128)(2,1)}, bf16[2,320,384]{2,1,0:T(8,128)(2,1)S(1)}, u32[]{:S(2)}, u32[]{:S(2)}) collective-permute-start(bf16[2,320,384]{2,1,0:T(8,128)(2,1)} %collective-permute-done.5.refs_4_), channel_id=1, source_target_pairs={{0,16},{4,20},{16,24},{20,28},{24,8},{28,12},{8,0},{12,4},{1,17},{... | collective-permute-start | bytes 1474568 | tf_op jit(solution)/shard_map/ppermute | solution.py:351
  38.0 0.5 collective-permute-start.8
  38.5 0.1 multiply_reduce_fusion.1
  38.6 0.2 fusion.12
  38.9 0.1 subtract_convert_fusion
  39.0 0.1 maximum_multiply_fusion
  39.1 0.1 fusion.13
  39.2 8.9 %collective-permute-done.9.refs_6_ = bf16[2,320,384]{2,1,0:T(8,128)(2,1)S(1)} collective-permute-done((bf16[2,320,384]{2,1,0:T(8,128)(2,1)}, bf16[2,320,384]{2,1,0:T(8,128)(2,1)S(1)}, u32[]{:S(2)}, u32[]{:S(2)}) %collective-permute-start.9) | collective-permute-done | bytes 491552 | tf_op jit(solution)/shard_map/ppermute | solution.py:351
  48.2 2.1 %collective-permute-done.8.refs_5_ = bf16[2,320,384]{2,1,0:T(8,128)(2,1)S(1)} collective-permute-done((bf16[2,320,384]{2,1,0:T(8,128)(2,1)}, bf16[2,320,384]{2,1,0:T(8,128)(2,1)S(1)}, u32[]{:S(2)}, u32[]{:S(2)}) %collective-permute-start.8) | collective-permute-done | bytes 491552 | tf_op jit(solution)/shard_map/ppermute | solution.py:354
  50.2 0.5 collective-permute-start.10
  50.8 1.4 %collective-permute-start.11 = (bf16[1,320,384]{2,1,0:T(8,128)(2,1)S(1)}, bf16[1,320,384]{2,1,0:T(8,128)(2,1)}, u32[]{:S(2)}, u32[]{:S(2)}) collective-permute-start(bf16[1,320,384]{2,1,0:T(8,128)(2,1)S(1)} %slice.49), channel_id=1, source_target_pairs={{0,16},{4,20},{16,24},{20,28},{24,8},{28,12},{8,0},{12,4},{1,17},{... | collective-permute-start | bytes 737288 | tf_op jit(solution)/shard_map/ppermute | solution.py:351
  52.1 0.1 multiply_subtract_fusion
  52.2 0.8 slice.71
  53.0 0.8 maximum_convert_fusion
  53.8 5.2 %suffix_attend.1 = (f32[320,512]{1,0:T(8,128)}, f32[8,512]{1,0:T(8,128)}) custom-call(s32[1,2]{1,0:T(1,128)} %lengths_ref.1, bf16[320,512]{1,0:T(8,128)(2,1)} %bitcast.72, bf16[320,512]{1,0:T(8,128)(2,1)} %bitcast.69, bf16[320,512]{1,0:T(8,128)(2,1)} %bitcast.67), custom_call_target="tpu_custom_call" | custom-call | flops 335544320 | bytes 3145728 | tf_op jit(solution)/shard_map/suffix_attend/pallas_call | solution.py:115
  59.0 0.7 copy-done.17
  59.7 0.1 copy-done.18
  59.8 15.5 %prefix_attend.1 = (f32[320,512]{1,0:T(8,128)}, f32[8,512]{1,0:T(8,128)}, bf16[352,512]{1,0:T(8,128)(2,1)}) custom-call(s32[8]{0:T(128)} %owners_ref.1, s32[1,2]{1,0:T(1,128)} %groups_ref.1, s32[1,2]{1,0:T(1,128)} %lengths_ref.1, s32[1]{0:T(128)} %bitcast.6.me_ref, bf16[320,512]{1,0:T(8,128)(2,1)} %bitcast.73, bf16[320,512]{1,0:T(8,128)(2,1)} %copy-done.17, ...), custom_call_target="tpu_custom_call" | custom-call | flops 2013265920 | bytes 6291456 | tf_op jit(solution)/shard_map/prefix_attend/pallas_call | solution.py:246
  75.3 0.1 collective-permute-start.12
  75.4 0.5 collective-permute-start.18
  75.9 1.4 %collective-permute-done.12.got_ref = bf16[352,512]{1,0:T(8,128)(2,1)S(1)} collective-permute-done((bf16[352,512]{1,0:T(8,128)(2,1)}, bf16[352,512]{1,0:T(8,128)(2,1)S(1)}, u32[]{:S(2)}, u32[]{:S(2)}) %collective-permute-start.12) | collective-permute-done | bytes 360480 | tf_op jit(solution)/shard_map/ppermute | solution.py:336
  77.3 0.7 copy-done.10
  78.0 2.2 %merge.1 = bf16[320,512]{1,0:T(8,128)(2,1)} custom-call(f32[320,512]{1,0:T(8,128)} %get-tuple-element.41.own_ref, f32[8,512]{1,0:T(8,128)} %get-tuple-element.42.own_lse_ref, bf16[352,512]{1,0:T(8,128)(2,1)} %copy-done.10, f32[320,512]{1,0:T(8,128)} %get-tuple-element.44.suffix_ref, f32[8,512]{1,0:T(8,128)} %get-tuple-element.45.suffix_lse_ref), custom_call_target="tpu_custom_call" | custom-call | flops 1310720 | bytes 1048576 | tf_op jit(solution)/shard_map/merge/pallas_call | solution.py:291
  80.2 0.1 collective-permute-start.13
  80.4 1.5 %collective-permute-start.15 = (bf16[320,512]{1,0:T(8,128)(2,1)}, bf16[320,512]{1,0:T(8,128)(2,1)S(1)}, u32[]{:S(2)}, u32[]{:S(2)}) collective-permute-start(bf16[320,512]{1,0:T(8,128)(2,1)} %merge.1), channel_id=1, source_target_pairs={{0,2},{1,3},{2,0},{3,1},{4,6},{5,7},{6,4},{7,5},{8,10},{9,11},{10,... | collective-permute-start | bytes 983048 | tf_op jit(solution)/shard_map/ppermute | solution.py:333
  81.9 2.7 %fusion.16 = f32[512,2048]{1,0:T(8,128)S(1)} fusion(bf16[320,512]{1,0:T(8,128)(2,1)} %merge.1, bf16[320,2048]{1,0:T(8,128)(2,1)} %param.24), kind=kOutput, calls=%fused_computation.51 | convolution fusion | flops 671088640 | bytes 5832704 | tf_op jit(solution)/shard_map/dot_general | solution.py:46
  84.6 2.8 %add_add_fusion.1 = f32[512,2048]{1,0:T(8,128)S(1)} fusion(f32[512,2048]{1,0:T(8,128)S(1)} %fusion.16, bf16[512,2048]{1,0:T(8,128)(2,1)S(1)} %copy-done.2, bf16[320,512]{1,0:T(8,128)(2,1)S(1)} %collective-permute-done.13, bf16[320,2048]{1,0:T(8,128)(2,1)} %collective-permute-done.14), kind=kOutput, calls=%fused_computation.5 | convolution fusion | flops 674234368 | bytes 12124160 | tf_op jit(solution)/shard_map/dot_general | solution.py:46
  87.5 3.1 %collective-permute-done.15 = bf16[320,512]{1,0:T(8,128)(2,1)S(1)} collective-permute-done((bf16[320,512]{1,0:T(8,128)(2,1)}, bf16[320,512]{1,0:T(8,128)(2,1)S(1)}, u32[]{:S(2)}, u32[]{:S(2)}) %collective-permute-start.15) | collective-permute-done | bytes 327712 | tf_op jit(solution)/shard_map/ppermute | solution.py:333
  90.6 2.6 %fusion.17 = f32[512,2048]{1,0:T(8,128)S(1)} fusion(bf16[320,512]{1,0:T(8,128)(2,1)S(1)} %collective-permute-done.15, bf16[320,2048]{1,0:T(8,128)(2,1)} %collective-permute-done.16), kind=kOutput, calls=%fused_computation.52 | convolution fusion | flops 671088640 | bytes 5832704 | tf_op jit(solution)/shard_map/dot_general | solution.py:46
  93.2 0.0 slice-start.2
  93.2 3.2 %multiply_reduce_fusion = (f32[512]{0:T(512)S(1)}, f32[512,2048]{1,0:T(8,128)S(1)}) fusion(bf16[320,512]{1,0:T(8,128)(2,1)S(1)} %collective-permute-done.17, bf16[320,2048]{1,0:T(8,128)(2,1)} %collective-permute-done.18, f32[512,2048]{1,0:T(8,128)S(1)} %add_add_fusion.1, f32[512,2048]{1,0:T(8,128)S(1)} %fusion.17), kind=kOutput, calls=%fused_computation.3 | convolution fusion | flops 675282432 | bytes 14223360 | tf_op jit(solution)/shard_map/dot_general | solution.py:46
  96.5 5.6 %fusion = f32[512,2,1280]{2,0,1:T(8,128)S(1)} fusion(bf16[2048,2,1280]{2,1,0:T(2,128)(2,1)S(1)} %bitcast.77, f32[512,2048]{1,0:T(8,128)S(1)} %get-tuple-element.65, f32[2048]{0:T(1024)S(1)} %copy-done.19, f32[512]{0:T(512)S(1)} %add_rsqrt_fusion.2), kind=kOutput, calls=%fused_computation | convolution fusion | flops 5371854848 | bytes 19933184 | tf_op jit(solution)/shard_map/rd,dgf->rgf/dot_general | solution.py:413
  102.1 0.8 fusion.3
  102.9 0.5 copy-done.8
  103.5 0.8 convolution_convert_fusion.2
  104.3 0.6 collective-permute-start.19
  104.9 1.5 %collective-permute-done.19 = bf16[512,512]{1,0:T(8,128)(2,1)S(1)} collective-permute-done((bf16[512,512]{1,0:T(8,128)(2,1)S(1)}, bf16[512,512]{1,0:T(8,128)(2,1)S(1)}, u32[]{:S(2)}, u32[]{:S(2)}) %collective-permute-start.19) | collective-permute-done | bytes 524320 | tf_op jit(solution)/shard_map/ppermute | solution.py:336
  106.4 0.8 fusion.10
  107.3 0.8 convolution_convert_fusion
  108.2 0.4 collective-permute-start.20
  108.6 1.5 %collective-permute-start.21 = (bf16[512,512]{1,0:T(8,128)(2,1)S(1)}, bf16[512,512]{1,0:T(8,128)(2,1)S(1)}, u32[]{:S(2)}, u32[]{:S(2)}) collective-permute-start(bf16[512,512]{1,0:T(8,128)(2,1)S(1)} %fusion.10), channel_id=1, source_target_pairs={{0,2},{1,3},{2,0},{3,1},{4,6},{5,7},{6,4},{7,5},{8,10},{9,11},{10,... | collective-permute-start | bytes 1572872 | tf_op jit(solution)/shard_map/ppermute | solution.py:333
  110.1 0.9 pad_maximum_fusion
  111.0 0.8 fusion.11
  111.8 10.7 %collective-permute-done.21 = bf16[512,512]{1,0:T(8,128)(2,1)S(1)} collective-permute-done((bf16[512,512]{1,0:T(8,128)(2,1)S(1)}, bf16[512,512]{1,0:T(8,128)(2,1)S(1)}, u32[]{:S(2)}, u32[]{:S(2)}) %collective-permute-start.21) | collective-permute-done | bytes 524320 | tf_op jit(solution)/shard_map/ppermute | solution.py:333
  122.6 1.1 add_convert_fusion
  (63 shorter events, 0.2 us)
Async XLA Ops:
  0.6 32.8 %copy-start = (bf16[2048,640]{1,0:T(8,128)(2,1)S(1)}, bf16[2048,640]{1,0:T(8,128)(2,1)}, u32[]{:S(2)}) copy-start(bf16[2048,640]{1,0:T(8,128)(2,1)} %param.21) | copy-start | bytes 7864324
  2.7 14.9 %collective-permute-start.2 = (bf16[2,320,384]{2,1,0:T(8,128)(2,1)}, bf16[2,320,384]{2,1,0:T(8,128)(2,1)}, u32[]{:S(2)}, u32[]{:S(2)}) collective-permute-start(bf16[2,320,384]{2,1,0:T(8,128)(2,1)} %dynamic-slice_bitcast_fusion.refs_0_), channel_id=1, source_target_pairs={{0,16},{4,20},{16,24},{20,28},{24,8},{28,12},{8,0},{12,4},{1,17},{... | collective-permute-start | bytes 1474568 | tf_op jit(solution)/shard_map/ppermute | solution.py:351
  6.8 13.0 %collective-permute-start.3 = (bf16[2,320,384]{2,1,0:T(8,128)(2,1)}, bf16[2,320,384]{2,1,0:T(8,128)(2,1)}, u32[]{:S(2)}, u32[]{:S(2)}) collective-permute-start(bf16[2,320,384]{2,1,0:T(8,128)(2,1)} %dynamic-slice_bitcast_fusion.refs_0_), channel_id=1, source_target_pairs={{0,4},{4,0},{8,12},{12,8},{16,20},{20,16},{24,28},{28,24},{1,5},{5... | collective-permute-start | bytes 1474568 | tf_op jit(solution)/shard_map/ppermute | solution.py:354
  8.3 13.3 %collective-permute-start.1 = (bf16[512,512]{1,0:T(8,128)(2,1)}, bf16[512,512]{1,0:T(8,128)(2,1)S(1)}, u32[]{:S(2)}, u32[]{:S(2)}) collective-permute-start(bf16[512,512]{1,0:T(8,128)(2,1)} %own_ref.1), channel_id=1, source_target_pairs={{0,2},{1,3},{2,0},{3,1},{4,6},{5,7},{6,4},{7,5},{8,10},{9,11},{10,... | collective-permute-start | bytes 1572872 | tf_op jit(solution)/shard_map/ppermute | solution.py:333
  9.8 14.4 %collective-permute-start = (bf16[512,512]{1,0:T(8,128)(2,1)}, bf16[512,512]{1,0:T(8,128)(2,1)}, u32[]{:S(2)}, u32[]{:S(2)}) collective-permute-start(bf16[512,512]{1,0:T(8,128)(2,1)} %own_ref.1), channel_id=1, source_target_pairs={{0,1},{1,0},{2,3},{3,2},{4,5},{5,4},{6,7},{7,6},{8,9},{9,8},{10,11... | collective-permute-start | bytes 1572872 | tf_op jit(solution)/shard_map/ppermute | solution.py:336
  21.6 4.1 %copy-start.9 = (bf16[512,512]{1,0:T(8,128)(2,1)}, bf16[512,512]{1,0:T(8,128)(2,1)S(1)}, u32[]{:S(2)}) copy-start(bf16[512,512]{1,0:T(8,128)(2,1)S(1)} %collective-permute-done.1.chip_ref) | copy-start | bytes 1572868
  21.6 4.1 %collective-permute-start.4 = (bf16[512,512]{1,0:T(8,128)(2,1)S(1)}, bf16[512,512]{1,0:T(8,128)(2,1)}, u32[]{:S(2)}, u32[]{:S(2)}) collective-permute-start(bf16[512,512]{1,0:T(8,128)(2,1)S(1)} %collective-permute-done.1.chip_ref), channel_id=1, source_target_pairs={{0,1},{1,0},{2,3},{3,2},{4,5},{5,4},{6,7},{7,6},{8,9},{9,8},{10,11... | collective-permute-start | bytes 1572872 | tf_op jit(solution)/shard_map/ppermute | solution.py:336
  21.6 63.0 %collective-permute-start.14 = (bf16[320,2048]{1,0:T(8,128)(2,1)}, bf16[320,2048]{1,0:T(8,128)(2,1)}, u32[]{:S(2)}, u32[]{:S(2)}) collective-permute-start(bf16[320,2048]{1,0:T(8,128)(2,1)} %param.24), channel_id=1, source_target_pairs={{0,1},{1,0},{2,3},{3,2},{4,5},{5,4},{6,7},{7,6},{8,9},{9,8},{10,11... | collective-permute-start | bytes 3932168 | tf_op jit(solution)/shard_map/ppermute | solution.py:336
  22.1 13.4 %collective-permute-start.5 = (bf16[2,320,384]{2,1,0:T(8,128)(2,1)}, bf16[2,320,384]{2,1,0:T(8,128)(2,1)}, u32[]{:S(2)}, u32[]{:S(2)}) collective-permute-start(bf16[2,320,384]{2,1,0:T(8,128)(2,1)} %collective-permute-done.2.refs_2_), channel_id=1, source_target_pairs={{0,16},{4,20},{16,24},{20,28},{24,8},{28,12},{8,0},{12,4},{1,17},{... | collective-permute-start | bytes 1474568 | tf_op jit(solution)/shard_map/ppermute | solution.py:351
  23.7 27.1 %collective-permute-start.7 = (bf16[2,320,384]{2,1,0:T(8,128)(2,1)}, bf16[2,320,384]{2,1,0:T(8,128)(2,1)}, u32[]{:S(2)}, u32[]{:S(2)}) collective-permute-start(bf16[2,320,384]{2,1,0:T(8,128)(2,1)} %collective-permute-done.2.refs_2_), channel_id=1, source_target_pairs={{0,4},{4,0},{8,12},{12,8},{16,20},{20,16},{24,28},{28,24},{1,5},{5... | collective-permute-start | bytes 1474568 | tf_op jit(solution)/shard_map/ppermute | solution.py:354
  24.2 51.2 %collective-permute-start.16 = (bf16[320,2048]{1,0:T(8,128)(2,1)}, bf16[320,2048]{1,0:T(8,128)(2,1)}, u32[]{:S(2)}, u32[]{:S(2)}) collective-permute-start(bf16[320,2048]{1,0:T(8,128)(2,1)} %param.24), channel_id=1, source_target_pairs={{0,2},{1,3},{2,0},{3,1},{4,6},{5,7},{6,4},{7,5},{8,10},{9,11},{10,... | collective-permute-start | bytes 3932168 | tf_op jit(solution)/shard_map/ppermute | solution.py:333
  30.4 3.0 %copy-start.16 = (bf16[512,2048]{1,0:T(8,128)(2,1)S(1)}, bf16[512,2048]{1,0:T(8,128)(2,1)}, u32[]{:S(2)}) copy-start(bf16[512,2048]{1,0:T(8,128)(2,1)} %get-tuple-element.31) | copy-start | bytes 6291460
  33.4 5.2 %copy-start.15 = (f32[64]{0:T(128)S(1)}, f32[64]{0:T(128)}, u32[]{:S(2)}) copy-start(f32[64]{0:T(128)} %param.22) | copy-start | bytes 772
  35.5 3.5 %copy-start.14 = (f32[64]{0:T(128)S(1)}, f32[64]{0:T(128)}, u32[]{:S(2)}) copy-start(f32[64]{0:T(128)} %param.23) | copy-start | bytes 772
  35.6 12.6 %collective-permute-start.9 = (bf16[2,320,384]{2,1,0:T(8,128)(2,1)}, bf16[2,320,384]{2,1,0:T(8,128)(2,1)S(1)}, u32[]{:S(2)}, u32[]{:S(2)}) collective-permute-start(bf16[2,320,384]{2,1,0:T(8,128)(2,1)} %collective-permute-done.5.refs_4_), channel_id=1, source_target_pairs={{0,16},{4,20},{16,24},{20,28},{24,8},{28,12},{8,0},{12,4},{1,17},{... | collective-permute-start | bytes 1474568 | tf_op jit(solution)/shard_map/ppermute | solution.py:351
  38.0 12.2 %collective-permute-start.8 = (bf16[2,320,384]{2,1,0:T(8,128)(2,1)}, bf16[2,320,384]{2,1,0:T(8,128)(2,1)S(1)}, u32[]{:S(2)}, u32[]{:S(2)}) collective-permute-start(bf16[2,320,384]{2,1,0:T(8,128)(2,1)} %collective-permute-done.5.refs_4_), channel_id=1, source_target_pairs={{0,4},{4,0},{8,12},{12,8},{16,20},{20,16},{24,28},{28,24},{1,5},{5... | collective-permute-start | bytes 1474568 | tf_op jit(solution)/shard_map/ppermute | solution.py:354
  39.1 14.7 %copy-start.11 = (bf16[512,5,64]{0,2,1:T(8,128)(2,1)}, bf16[512,5,64]{0,2,1:T(8,128)(2,1)S(1)}, u32[]{:S(2)}) copy-start(bf16[512,5,64]{0,2,1:T(8,128)(2,1)S(1)} %maximum_multiply_fusion) | copy-start | bytes 983044
  48.1 10.8 %copy-start.12 = (bf16[2,320,384]{2,1,0:T(8,128)(2,1)}, bf16[2,320,384]{2,1,0:T(8,128)(2,1)S(1)}, u32[]{:S(2)}) copy-start(bf16[2,320,384]{2,1,0:T(8,128)(2,1)S(1)} %collective-permute-done.9.refs_6_) | copy-start | bytes 1474564
  48.1 10.8 %collective-permute-start.6 = (bf16[320,512]{1,0:T(8,128)(2,1)S(1)}, bf16[320,512]{1,0:T(8,128)(2,1)S(1)}, u32[]{:S(2)}, u32[]{:S(2)}) collective-permute-start(bf16[320,512]{1,0:T(8,128)(2,1)S(1)} %bitcast.71), channel_id=1, source_target_pairs={{0,1},{1,0},{2,3},{3,2},{4,5},{5,4},{6,7},{7,6},{8,9},{9,8},{10,11... | collective-permute-start | bytes 983048 | tf_op jit(solution)/shard_map/ppermute | solution.py:336
  50.2 8.7 %copy-start.13 = (bf16[2,320,384]{2,1,0:T(8,128)(2,1)}, bf16[2,320,384]{2,1,0:T(8,128)(2,1)S(1)}, u32[]{:S(2)}) copy-start(bf16[2,320,384]{2,1,0:T(8,128)(2,1)S(1)} %collective-permute-done.8.refs_5_) | copy-start | bytes 1474564
  50.2 8.8 %collective-permute-start.10 = (bf16[1,320,384]{2,1,0:T(8,128)(2,1)S(1)}, bf16[1,320,384]{2,1,0:T(8,128)(2,1)S(1)}, u32[]{:S(2)}, u32[]{:S(2)}) collective-permute-start(bf16[1,320,384]{2,1,0:T(8,128)(2,1)S(1)} %slice.48), channel_id=1, source_target_pairs={{0,4},{4,0},{8,12},{12,8},{16,20},{20,16},{24,28},{28,24},{1,5},{5... | collective-permute-start | bytes 737288 | tf_op jit(solution)/shard_map/ppermute | solution.py:354
  50.8 8.2 %collective-permute-start.11 = (bf16[1,320,384]{2,1,0:T(8,128)(2,1)S(1)}, bf16[1,320,384]{2,1,0:T(8,128)(2,1)}, u32[]{:S(2)}, u32[]{:S(2)}) collective-permute-start(bf16[1,320,384]{2,1,0:T(8,128)(2,1)S(1)} %slice.49), channel_id=1, source_target_pairs={{0,16},{4,20},{16,24},{20,28},{24,8},{28,12},{8,0},{12,4},{1,17},{... | collective-permute-start | bytes 737288 | tf_op jit(solution)/shard_map/ppermute | solution.py:351
  59.0 0.7 copy-start.17
  59.0 0.8 copy-start.18
  75.3 2.0 %collective-permute-start.12 = (bf16[352,512]{1,0:T(8,128)(2,1)}, bf16[352,512]{1,0:T(8,128)(2,1)S(1)}, u32[]{:S(2)}, u32[]{:S(2)}) collective-permute-start(bf16[352,512]{1,0:T(8,128)(2,1)} %get-tuple-element.43), channel_id=1, source_target_pairs={{0,1},{1,0},{2,3},{3,2},{4,5},{5,4},{6,7},{7,6},{8,9},{9,8},{10,11... | collective-permute-start | bytes 1081352 | tf_op jit(solution)/shard_map/ppermute | solution.py:336
  75.4 17.8 %collective-permute-start.18 = (bf16[320,2048]{1,0:T(8,128)(2,1)}, bf16[320,2048]{1,0:T(8,128)(2,1)}, u32[]{:S(2)}, u32[]{:S(2)}) collective-permute-start(bf16[320,2048]{1,0:T(8,128)(2,1)} %collective-permute-done.16), channel_id=1, source_target_pairs={{0,1},{1,0},{2,3},{3,2},{4,5},{5,4},{6,7},{7,6},{8,9},{9,8},{10,11... | collective-permute-start | bytes 3932168 | tf_op jit(solution)/shard_map/ppermute | solution.py:336
  77.3 0.7 copy-start.10
  80.2 4.4 %copy-start.2 = (bf16[512,2048]{1,0:T(8,128)(2,1)S(1)}, bf16[512,2048]{1,0:T(8,128)(2,1)}, u32[]{:S(2)}) copy-start(bf16[512,2048]{1,0:T(8,128)(2,1)} %get-tuple-element.30) | copy-start | bytes 6291460
  80.2 4.3 %collective-permute-start.13 = (bf16[320,512]{1,0:T(8,128)(2,1)}, bf16[320,512]{1,0:T(8,128)(2,1)S(1)}, u32[]{:S(2)}, u32[]{:S(2)}) collective-permute-start(bf16[320,512]{1,0:T(8,128)(2,1)} %merge.1), channel_id=1, source_target_pairs={{0,1},{1,0},{2,3},{3,2},{4,5},{5,4},{6,7},{7,6},{8,9},{9,8},{10,11... | collective-permute-start | bytes 983048 | tf_op jit(solution)/shard_map/ppermute | solution.py:336
  80.4 10.2 %collective-permute-start.15 = (bf16[320,512]{1,0:T(8,128)(2,1)}, bf16[320,512]{1,0:T(8,128)(2,1)S(1)}, u32[]{:S(2)}, u32[]{:S(2)}) collective-permute-start(bf16[320,512]{1,0:T(8,128)(2,1)} %merge.1), channel_id=1, source_target_pairs={{0,2},{1,3},{2,0},{3,1},{4,6},{5,7},{6,4},{7,5},{8,10},{9,11},{10,... | collective-permute-start | bytes 983048 | tf_op jit(solution)/shard_map/ppermute | solution.py:333
  84.6 11.9 %slice-start = ((s8[10485760]{0:T(1024)(128)(4,1)}), s8[4194304]{0:T(1024)(128)(4,1)S(1)}, s32[]{:S(2)}) async-start(s8[10485760]{0:T(1024)(128)(4,1)} %bitcast.76), calls=%async_computation | async-start | bytes 8388608
  84.6 11.9 %slice-start.1 = ((s8[10485760]{0:T(1024)(128)(4,1)}), s8[4194304]{0:T(1024)(128)(4,1)S(1)}, s32[]{:S(2)}) async-start(s8[10485760]{0:T(1024)(128)(4,1)} %bitcast.76), calls=%async_computation.1 | async-start | bytes 8388608
  90.6 2.6 %collective-permute-start.17 = (bf16[320,512]{1,0:T(8,128)(2,1)S(1)}, bf16[320,512]{1,0:T(8,128)(2,1)S(1)}, u32[]{:S(2)}, u32[]{:S(2)}) collective-permute-start(bf16[320,512]{1,0:T(8,128)(2,1)S(1)} %collective-permute-done.15), channel_id=1, source_target_pairs={{0,1},{1,0},{2,3},{3,2},{4,5},{5,4},{6,7},{7,6},{8,9},{9,8},{10,11... | collective-permute-start | bytes 983048 | tf_op jit(solution)/shard_map/ppermute | solution.py:336
  93.2 3.3 %slice-start.2 = ((s8[10485760]{0:T(1024)(128)(4,1)}), s8[2097152]{0:T(1024)(128)(4,1)S(1)}, s32[]{:S(2)}) async-start(s8[10485760]{0:T(1024)(128)(4,1)} %bitcast.76), calls=%async_computation.2 | async-start | bytes 4194304
  93.2 3.3 %copy-start.19 = (f32[2048]{0:T(1024)S(1)}, f32[2048]{0:T(1024)}, u32[]{:S(2)}) copy-start(f32[2048]{0:T(1024)} %param.25) | copy-start | bytes 24580
  102.1 1.3 %copy-start.8 = (bf16[1280,512]{1,0:T(8,128)(2,1)S(1)}, bf16[1280,512]{1,0:T(8,128)(2,1)}, u32[]{:S(2)}) copy-start(bf16[1280,512]{1,0:T(8,128)(2,1)} %get-tuple-element.50) | copy-start | bytes 3932164
  103.5 3.0 %copy-start.7 = (bf16[1280,512]{1,0:T(8,128)(2,1)S(1)}, bf16[1280,512]{1,0:T(8,128)(2,1)}, u32[]{:S(2)}) copy-start(bf16[1280,512]{1,0:T(8,128)(2,1)} %get-tuple-element.49) | copy-start | bytes 3932164
  104.3 3.0 %copy-start.6 = (bf16[1280,512]{1,0:T(8,128)(2,1)S(1)}, bf16[1280,512]{1,0:T(8,128)(2,1)}, u32[]{:S(2)}) copy-start(bf16[1280,512]{1,0:T(8,128)(2,1)} %get-tuple-element.53) | copy-start | bytes 3932164
  104.3 2.1 %collective-permute-start.19 = (bf16[512,512]{1,0:T(8,128)(2,1)S(1)}, bf16[512,512]{1,0:T(8,128)(2,1)S(1)}, u32[]{:S(2)}, u32[]{:S(2)}) collective-permute-start(bf16[512,512]{1,0:T(8,128)(2,1)S(1)} %convolution_convert_fusion.2), channel_id=1, source_target_pairs={{0,1},{1,0},{2,3},{3,2},{4,5},{5,4},{6,7},{7,6},{8,9},{9,8},{10,11... | collective-permute-start | bytes 1572872 | tf_op jit(solution)/shard_map/ppermute | solution.py:336
  107.3 2.8 %copy-start.3 = (bf16[512,1,5,64]{0,3,2,1:T(8,128)(2,1)S(1)}, bf16[512,1,5,64]{0,3,2,1:T(8,128)(2,1)}, u32[]{:S(2)}) copy-start(bf16[512,1,5,64]{0,3,2,1:T(8,128)(2,1)} %slice.71) | copy-start | bytes 983044
  107.3 2.8 %copy-start.4 = (bf16[512,5,64]{0,2,1:T(8,128)(2,1)S(1)}, bf16[512,5,64]{0,2,1:T(8,128)(2,1)}, u32[]{:S(2)}) copy-start(bf16[512,5,64]{0,2,1:T(8,128)(2,1)} %maximum_convert_fusion) | copy-start | bytes 983044
  107.3 3.7 %copy-start.5 = (bf16[1280,512]{1,0:T(8,128)(2,1)S(1)}, bf16[1280,512]{1,0:T(8,128)(2,1)}, u32[]{:S(2)}) copy-start(bf16[1280,512]{1,0:T(8,128)(2,1)} %get-tuple-element.52) | copy-start | bytes 3932164
  108.2 3.7 %collective-permute-start.20 = (bf16[512,512]{1,0:T(8,128)(2,1)S(1)}, bf16[512,512]{1,0:T(8,128)(2,1)S(1)}, u32[]{:S(2)}, u32[]{:S(2)}) collective-permute-start(bf16[512,512]{1,0:T(8,128)(2,1)S(1)} %convolution_convert_fusion), channel_id=1, source_target_pairs={{0,1},{1,0},{2,3},{3,2},{4,5},{5,4},{6,7},{7,6},{8,9},{9,8},{10,11... | collective-permute-start | bytes 1572872 | tf_op jit(solution)/shard_map/ppermute | solution.py:336
  108.6 14.0 %collective-permute-start.21 = (bf16[512,512]{1,0:T(8,128)(2,1)S(1)}, bf16[512,512]{1,0:T(8,128)(2,1)S(1)}, u32[]{:S(2)}, u32[]{:S(2)}) collective-permute-start(bf16[512,512]{1,0:T(8,128)(2,1)S(1)} %fusion.10), channel_id=1, source_target_pairs={{0,2},{1,3},{2,0},{3,1},{4,6},{5,7},{6,4},{7,5},{8,10},{9,11},{10,... | collective-permute-start | bytes 1572872 | tf_op jit(solution)/shard_map/ppermute | solution.py:333
  111.0 12.7 %copy-start.1 = (bf16[2048,640]{1,0:T(8,128)(2,1)S(1)}, bf16[2048,640]{1,0:T(8,128)(2,1)}, u32[]{:S(2)}) copy-start(bf16[2048,640]{1,0:T(8,128)(2,1)} %param.21) | copy-start | bytes 7864324

commit v6 on v5

--- a/solution.py
+++ b/solution.py
@@ -360,12 +360,15 @@
     down_blocks = [
         lax.dynamic_slice_in_dim(w_down, (rank ^ flip) * width, width, 1) for flip in range(4)
     ]
-    held[1], units[1], down_blocks, cos_part, sin_part = lax.optimization_barrier(
-        (held[1], units[1], down_blocks, cos_part, sin_part)
-    )
-    from_chip, _ = lax.optimization_barrier((from_chip, held[1]))
+    from_chip, down_blocks, cos_part, sin_part = lax.optimization_barrier(
+        (from_chip, down_blocks, cos_part, sin_part)
+    )
     from_both = across_core(from_chip)
-    full_rows, normalized_input = gather_norm(rank, (tokens, from_core, from_chip, from_both), attn_gain)
+    held[1], _ = lax.optimization_barrier((held[1], from_chip))
+    pieces, units[1], _ = lax.optimization_barrier(
+        ((tokens, from_core, from_chip, from_both), units[1], held[1])
+    )
+    full_rows, normalized_input = gather_norm(rank, pieces, attn_gain)
 
     w_out_held, _ = lax.optimization_barrier((w_out, from_chip))
     w_out_chip = across_chip(w_out_held)
@@ -384,7 +387,6 @@
     for _ in range(3, length):
         units += [held[-1], aside(held[-1])]
         held.append(ring(held[-1]))
-    units += [held[-1], aside(held[-1][:1]), ring(units[-1][1:])]
     query_rows = rotate(rms_scale(query_rows, query_gain), cos_part, sin_part).astype(jnp.bfloat16)
     key_rows = rotate(rms_scale(key_value_rows[:, 0], key_gain), cos_part, sin_part).astype(jnp.bfloat16)
     value_rows = key_value_rows[:, 1].astype(jnp.bfloat16)
@@ -398,7 +400,8 @@
         request_lengths, own_q, key_rows.reshape(row_count, columns).T, value_rows.reshape(row_count, columns).T
     )
 
-    own_q, suffix_out, suffix_lse = lax.optimization_barrier((own_q, suffix_out, suffix_lse))
+    held[-1], suffix_out, suffix_lse = lax.optimization_barrier((held[-1], suffix_out, suffix_lse))
+    units += [held[-1], aside(held[-1][:1]), ring(units[-1][1:])]
     own_out, own_lse, sent = prefix_attend(
         owners, request_groups, request_lengths, my_req.reshape(1), own_q, other_q, units
     )
@@ -416,11 +419,10 @@
     def down(flip):
         return jnp.dot(activated, down_blocks[flip], preferred_element_type=jnp.float32).astype(jnp.bfloat16)
 
-    far = down(3)
-    far_sum = (down(2).astype(jnp.float32) + across_core(far).astype(jnp.float32)).astype(jnp.bfloat16)
+    got_far, near = lax.optimization_barrier((across_core(down(3)), down(1)))
+    far_sum = (down(2).astype(jnp.float32) + got_far.astype(jnp.float32)).astype(jnp.bfloat16)
     from_far = across_chip(far_sum)
     activated, far_sum = lax.optimization_barrier((activated, far_sum))
-    near = down(1)
     own_mixed = lax.dynamic_slice_in_dim(mixed, rank * width, width, 1)
     near_sum = own_mixed + down(0).astype(jnp.float32) + across_core(near).astype(jnp.float32)
     return ((near_sum + from_far.astype(jnp.float32)).astype(jnp.bfloat16), cache_rows)

time: 124 us -> 138 us (1.11)
  waiting for transfers between devices: 34.1 us -> 46.3 us
  starting transfers between devices: 20.7 us -> 24 us
    ppermute x4, waiting for transfers between devices: 11.3 us -> 19.2 us  [ring(): lax.ppermute(value, 'req', [(2 * a + b, 2 * c + b) for a, c in steps for...]
    ppermute x4, waiting for transfers between devices: 15.7 us -> 20 us  [across_chip(): return lax.ppermute(value, 'tp', [(i, i ^ 2) for i in range(4)])]
    ppermute x4, starting transfers between devices: 3.04 us -> 5.13 us  [aside(): return lax.ppermute(value, 'req', [(r, r ^ 1) for r in range(n_req)])]
    dynamic_slice x1, local copies, waits for them, and re-layouts: 2.03 us -> 0.06 us  [local(): lax.dynamic_slice(jnp.transpose(prefix_cache[0], (0, 2, 1)), (0, 0, core...]
    ppermute x4, starting transfers between devices: 5.96 us -> 7.58 us  [across_chip(): return lax.ppermute(value, 'tp', [(i, i ^ 2) for i in range(4)])]
    unnamed x46 -> x56, local copies, waits for them, and re-layouts: 2.15 us -> 2.85 us
  transfers between devices with their start and end apart: 22 -> 22, of which waited for: 10 -> 9; matrix products, arithmetic and copies ran while one was open for 18% -> 17% of each run, Pallas kernels for 22% -> 20%
where the time goes in v6:
time: 138 us
  waiting for transfers between devices  46.3 us (34%)
  Pallas kernels  27.5 us (20%)
  matrix products  24.9 us (18%)
  starting transfers between devices  24 us (17%)
  local copies, waits for them, and re-layouts  8.79 us (6%)
  other arithmetic  5.34 us (4%)
    ppermute x4, waiting for transfers between devices, across_chip(): return lax.ppermute(value, 'tp', [(i, i ^ 2) for i in range(4)])  20 us
    ppermute x4, waiting for transfers between devices, ring(): lax.ppermute(value, 'req', [(2 * a + b, 2 * c + b) for a, c in steps for...  19.2 us
    pallas_call x1, Pallas kernels, prefix_attend(): pl.pallas_call(functools.partial(prefix_kernel, block, 256, len(units) -...  15.5 us
    dot_general x4, matrix products, tn_dot(): lax.dot_general(lhs, rhs, (((0,), (0,)), ((), ())), preferred_element_typ...  11.4 us
    ppermute x4, starting transfers between devices, ring(): lax.ppermute(value, 'req', [(2 * a + b, 2 * c + b) for a, c in steps for...  9.95 us
    ppermute x4, starting transfers between devices, across_chip(): return lax.ppermute(value, 'tp', [(i, i ^ 2) for i in range(4)])  7.58 us
    dot_general x1, matrix products, local(): jnp.einsum('rd,dgf->rgf', normed_ffn, w_gate_up, preferred_element_type=j...  5.64 us
    pallas_call x1, Pallas kernels, suffix_attend(): pl.pallas_call(suffix_kernel, out_shape=(jax.ShapeDtypeStruct((columns, r...  5.15 us
  transfers between devices with their start and end apart: 22, of which 9 were waited for; matrix products, arithmetic and copies ran while one was open for 17% of the time, Pallas kernels for 20%

profile of v6, /device:TPU:0, one launch (start us, length us, event | category | flops | bytes accessed | tf_op | source)
XLA Modules:
  0.0 138.0 jit_solution(12381980836611800951)
XLA Ops:
  0.6 0.0 copy-start
  0.6 3.0 %collective-permute-start.1 = (bf16[512,512]{1,0:T(8,128)(2,1)}, bf16[512,512]{1,0:T(8,128)(2,1)S(1)}, u32[]{:S(2)}, u32[]{:S(2)}) collective-permute-start(bf16[512,512]{1,0:T(8,128)(2,1)} %own_ref), channel_id=1, source_target_pairs={{0,2},{1,3},{2,0},{3,1},{4,6},{5,7},{6,4},{7,5},{8,10},{9,11},{10,... | collective-permute-start | bytes 1572872 | tf_op jit(solution)/shard_map/ppermute | solution.py:333
  3.7 0.7 add_convert_fusion.2
  4.4 0.3 multiply_sine_fusion
  4.7 5.0 %constant_dynamic-slice_fusion = (bf16[1280,512]{1,0:T(8,128)(2,1)}, bf16[1280,512]{1,0:T(8,128)(2,1)}, bf16[1280,512]{1,0:T(8,128)(2,1)}, bf16[1280,512]{1,0:T(8,128)(2,1)}) fusion(bf16[1280,2048]{1,0:T(8,128)(2,1)} %param.27, s32[]{:T(128)S(6)} %select_n.26, s32[]{:T(128)S(6)} %select_n.24, s32[]{:T(128)S(6)} %select_n.23, s32[]{:T(128)S(6)} %select_n.25), kind=kLoop, calls=%fused_computation.44 | loop fusion | bytes 10485776 | tf_op jit(solution)/shard_map/dynamic_slice | solution.py:361
  9.7 6.1 %collective-permute-done.1.chip_ref = bf16[512,512]{1,0:T(8,128)(2,1)S(1)} collective-permute-done((bf16[512,512]{1,0:T(8,128)(2,1)}, bf16[512,512]{1,0:T(8,128)(2,1)S(1)}, u32[]{:S(2)}, u32[]{:S(2)}) %collective-permute-start.1) | collective-permute-done | bytes 524320 | tf_op jit(solution)/shard_map/ppermute | solution.py:333
  15.8 0.1 dynamic-slice_bitcast_fusion.refs_0_
  15.9 2.9 %collective-permute-start.4 = (bf16[2,320,384]{2,1,0:T(8,128)(2,1)S(1)}, bf16[2,320,384]{2,1,0:T(8,128)(2,1)}, u32[]{:S(2)}, u32[]{:S(2)}) collective-permute-start(bf16[2,320,384]{2,1,0:T(8,128)(2,1)S(1)} %dynamic-slice_bitcast_fusion.refs_0_), channel_id=1, source_target_pairs={{0,16},{4,20},{16,24},{20,28},{24,8},{28,12},{8,0},{12,4},{1,17},{... | collective-permute-start | bytes 1474568 | tf_op jit(solution)/shard_map/ppermute | solution.py:351
  18.8 1.5 %collective-permute-start.3 = (bf16[2,320,384]{2,1,0:T(8,128)(2,1)S(1)}, bf16[2,320,384]{2,1,0:T(8,128)(2,1)S(1)}, u32[]{:S(2)}, u32[]{:S(2)}) collective-permute-start(bf16[2,320,384]{2,1,0:T(8,128)(2,1)S(1)} %dynamic-slice_bitcast_fusion.refs_0_), channel_id=1, source_target_pairs={{0,4},{4,0},{8,12},{12,8},{16,20},{20,16},{24,28},{28,24},{1,5},{5... | collective-permute-start | bytes 1474568 | tf_op jit(solution)/shard_map/ppermute | solution.py:354
  20.3 9.6 %collective-permute-done.4.refs_2_ = bf16[2,320,384]{2,1,0:T(8,128)(2,1)} collective-permute-done((bf16[2,320,384]{2,1,0:T(8,128)(2,1)S(1)}, bf16[2,320,384]{2,1,0:T(8,128)(2,1)}, u32[]{:S(2)}, u32[]{:S(2)}) %collective-permute-start.4) | collective-permute-done | bytes 491552 | tf_op jit(solution)/shard_map/ppermute | solution.py:351
  29.9 3.5 %collective-permute-start.5 = (bf16[2,320,384]{2,1,0:T(8,128)(2,1)}, bf16[2,320,384]{2,1,0:T(8,128)(2,1)}, u32[]{:S(2)}, u32[]{:S(2)}) collective-permute-start(bf16[2,320,384]{2,1,0:T(8,128)(2,1)} %collective-permute-done.4.refs_2_), channel_id=1, source_target_pairs={{0,16},{4,20},{16,24},{20,28},{24,8},{28,12},{8,0},{12,4},{1,17},{... | collective-permute-start | bytes 1474568 | tf_op jit(solution)/shard_map/ppermute | solution.py:351
  33.4 1.5 %collective-permute-start.7 = (bf16[2,320,384]{2,1,0:T(8,128)(2,1)}, bf16[2,320,384]{2,1,0:T(8,128)(2,1)}, u32[]{:S(2)}, u32[]{:S(2)}) collective-permute-start(bf16[2,320,384]{2,1,0:T(8,128)(2,1)} %collective-permute-done.4.refs_2_), channel_id=1, source_target_pairs={{0,4},{4,0},{8,12},{12,8},{16,20},{20,16},{24,28},{28,24},{1,5},{5... | collective-permute-start | bytes 1474568 | tf_op jit(solution)/shard_map/ppermute | solution.py:354
  34.9 1.5 %collective-permute-start.16 = (bf16[320,2048]{1,0:T(8,128)(2,1)}, bf16[320,2048]{1,0:T(8,128)(2,1)}, u32[]{:S(2)}, u32[]{:S(2)}) collective-permute-start(bf16[320,2048]{1,0:T(8,128)(2,1)} %param.24), channel_id=1, source_target_pairs={{0,2},{1,3},{2,0},{3,1},{4,6},{5,7},{6,4},{7,5},{8,10},{9,11},{10,... | collective-permute-start | bytes 3932168 | tf_op jit(solution)/shard_map/ppermute | solution.py:333
  36.4 0.8 copy-done.10
  37.2 4.7 %gather_norm.1 = (bf16[512,2048]{1,0:T(8,128)(2,1)}, bf16[512,2048]{1,0:T(8,128)(2,1)}) custom-call(s32[1]{0:T(128)} %bitcast.rank_ref, bf16[512,512]{1,0:T(8,128)(2,1)} %own_ref, bf16[512,512]{1,0:T(8,128)(2,1)} %collective-permute-done.core_ref, bf16[512,512]{1,0:T(8,128)(2,1)} %copy-done.9, bf16[512,512]{1,0:T(8,128)(2,1)} %copy-done.10, f32[1,2048]{1,0:T(1,128)} %bitcast.74), custom_call_target="tpu_custom_call" | custom-call | tf_op jit(solution)/shard_map/gather_norm/pallas_call | solution.py:73
  41.9 3.0 %fusion.14 = f32[512,320]{0,1:T(8,128)S(1)} fusion(bf16[512,2048]{1,0:T(8,128)(2,1)} %get-tuple-element.41, bf16[2048,320]{0,1:T(8,128)(2,1)} %param.20), kind=kOutput, calls=%fused_computation.49 | convolution fusion | flops 671088640 | bytes 4063232 | tf_op jit(solution)/shard_map/dot_general | solution.py:378
  44.9 1.6 %fusion.15 = f32[512,640]{0,1:T(8,128)S(1)} fusion(bf16[512,2048]{1,0:T(8,128)(2,1)S(1)} %copy-done.19, bf16[2048,640]{1,0:T(8,128)(2,1)S(1)} %copy-done), kind=kOutput, calls=%fused_computation.50 | convolution fusion | flops 1342177280 | bytes 6029312 | tf_op jit(solution)/shard_map/dot_general | solution.py:381
  46.5 0.8 collective-permute-start.9
  47.4 1.5 %collective-permute-start.8 = (bf16[2,320,384]{2,1,0:T(8,128)(2,1)}, bf16[2,320,384]{2,1,0:T(8,128)(2,1)S(1)}, u32[]{:S(2)}, u32[]{:S(2)}) collective-permute-start(bf16[2,320,384]{2,1,0:T(8,128)(2,1)} %collective-permute-done.5.refs_4_), channel_id=1, source_target_pairs={{0,4},{4,0},{8,12},{12,8},{16,20},{20,16},{24,28},{28,24},{1,5},{5... | collective-permute-start | bytes 1474568 | tf_op jit(solution)/shard_map/ppermute | solution.py:354
  48.9 0.1 multiply_reduce_fusion.1
  49.0 0.2 fusion.12
  49.3 0.1 fusion.13
  49.4 0.1 subtract_convert_fusion
  49.5 0.1 maximum_multiply_fusion
  49.6 0.1 multiply_subtract_fusion
  49.7 9.0 %collective-permute-done.9.refs_6_ = bf16[2,320,384]{2,1,0:T(8,128)(2,1)S(1)} collective-permute-done((bf16[2,320,384]{2,1,0:T(8,128)(2,1)}, bf16[2,320,384]{2,1,0:T(8,128)(2,1)S(1)}, u32[]{:S(2)}, u32[]{:S(2)}) %collective-permute-start.9) | collective-permute-done | bytes 491552 | tf_op jit(solution)/shard_map/ppermute | solution.py:351
  58.7 0.8 maximum_convert_fusion
  59.6 0.8 slice.70
  60.4 5.2 %suffix_attend.1 = (f32[320,512]{1,0:T(8,128)}, f32[8,512]{1,0:T(8,128)}) custom-call(s32[1,2]{1,0:T(1,128)} %lengths_ref.1, bf16[320,512]{1,0:T(8,128)(2,1)} %bitcast.72, bf16[320,512]{1,0:T(8,128)(2,1)} %bitcast.67, bf16[320,512]{1,0:T(8,128)(2,1)} %bitcast.69), custom_call_target="tpu_custom_call" | custom-call | flops 335544320 | bytes 3145728 | tf_op jit(solution)/shard_map/suffix_attend/pallas_call | solution.py:115
  65.6 0.6 collective-permute-start.10
  66.2 2.7 %collective-permute-start.11 = (bf16[1,320,384]{2,1,0:T(8,128)(2,1)S(1)}, bf16[1,320,384]{2,1,0:T(8,128)(2,1)S(1)}, u32[]{:S(2)}, u32[]{:S(2)}) collective-permute-start(bf16[1,320,384]{2,1,0:T(8,128)(2,1)S(1)} %slice.48), channel_id=1, source_target_pairs={{0,16},{4,20},{16,24},{20,28},{24,8},{28,12},{8,0},{12,4},{1,17},{... | collective-permute-start | bytes 737288 | tf_op jit(solution)/shard_map/ppermute | solution.py:351
  69.0 5.0 %collective-permute-done.10.refs_7_ = bf16[1,320,384]{2,1,0:T(8,128)(2,1)S(1)} collective-permute-done((bf16[1,320,384]{2,1,0:T(8,128)(2,1)S(1)}, bf16[1,320,384]{2,1,0:T(8,128)(2,1)S(1)}, u32[]{:S(2)}, u32[]{:S(2)}) %collective-permute-start.10) | collective-permute-done | bytes 245792 | tf_op jit(solution)/shard_map/ppermute | solution.py:354
  74.0 0.5 collective-permute-done.11.refs_8_
  74.5 0.1 copy-done.22
  74.6 0.5 copy-done.23
  75.2 15.5 %prefix_attend.1 = (f32[320,512]{1,0:T(8,128)}, f32[8,512]{1,0:T(8,128)}, bf16[352,512]{1,0:T(8,128)(2,1)}) custom-call(s32[8]{0:T(128)} %owners_ref.1, s32[1,2]{1,0:T(1,128)} %groups_ref.1, s32[1,2]{1,0:T(1,128)} %lengths_ref.1, s32[1]{0:T(128)} %bitcast.6.me_ref, bf16[320,512]{1,0:T(8,128)(2,1)} %bitcast.73, bf16[320,512]{1,0:T(8,128)(2,1)} %copy-done.21, ...), custom_call_target="tpu_custom_call" | custom-call | flops 2013265920 | bytes 6291456 | tf_op jit(solution)/shard_map/prefix_attend/pallas_call | solution.py:246
  90.7 0.1 collective-permute-start.12
  90.8 0.5 collective-permute-start.18
  91.3 1.4 collective-permute-done.12.got_ref
  92.6 0.7 copy-done.12
  93.4 2.2 %merge.1 = bf16[320,512]{1,0:T(8,128)(2,1)} custom-call(f32[320,512]{1,0:T(8,128)} %get-tuple-element.51.own_ref, f32[8,512]{1,0:T(8,128)} %get-tuple-element.52.own_lse_ref, bf16[352,512]{1,0:T(8,128)(2,1)} %copy-done.12, f32[320,512]{1,0:T(8,128)} %get-tuple-element.54.suffix_ref, f32[8,512]{1,0:T(8,128)} %get-tuple-element.55.suffix_lse_ref), custom_call_target="tpu_custom_call" | custom-call | flops 1310720 | bytes 1048576 | tf_op jit(solution)/shard_map/merge/pallas_call | solution.py:291
  95.6 0.1 collective-permute-start.13
  95.7 1.5 %collective-permute-start.15 = (bf16[320,512]{1,0:T(8,128)(2,1)}, bf16[320,512]{1,0:T(8,128)(2,1)S(1)}, u32[]{:S(2)}, u32[]{:S(2)}) collective-permute-start(bf16[320,512]{1,0:T(8,128)(2,1)} %merge.1), channel_id=1, source_target_pairs={{0,2},{1,3},{2,0},{3,1},{4,6},{5,7},{6,4},{7,5},{8,10},{9,11},{10,... | collective-permute-start | bytes 983048 | tf_op jit(solution)/shard_map/ppermute | solution.py:333
  97.2 2.7 %fusion.16 = f32[512,2048]{1,0:T(8,128)S(1)} fusion(bf16[320,512]{1,0:T(8,128)(2,1)} %merge.1, bf16[320,2048]{1,0:T(8,128)(2,1)} %param.24), kind=kOutput, calls=%fused_computation.51 | convolution fusion | flops 671088640 | bytes 5832704 | tf_op jit(solution)/shard_map/dot_general | solution.py:46
  99.9 0.0 slice-start
  99.9 2.8 %add_add_fusion.1 = f32[512,2048]{1,0:T(8,128)S(1)} fusion(f32[512,2048]{1,0:T(8,128)S(1)} %fusion.16, bf16[512,2048]{1,0:T(8,128)(2,1)S(1)} %copy-done.2, bf16[320,512]{1,0:T(8,128)(2,1)S(1)} %collective-permute-done.13, bf16[320,2048]{1,0:T(8,128)(2,1)} %collective-permute-done.14), kind=kOutput, calls=%fused_computation.5 | convolution fusion | flops 674234368 | bytes 12124160 | tf_op jit(solution)/shard_map/dot_general | solution.py:46
  102.8 3.1 %collective-permute-done.15 = bf16[320,512]{1,0:T(8,128)(2,1)S(1)} collective-permute-done((bf16[320,512]{1,0:T(8,128)(2,1)}, bf16[320,512]{1,0:T(8,128)(2,1)S(1)}, u32[]{:S(2)}, u32[]{:S(2)}) %collective-permute-start.15) | collective-permute-done | bytes 327712 | tf_op jit(solution)/shard_map/ppermute | solution.py:333
  105.9 2.6 %fusion.17 = f32[512,2048]{1,0:T(8,128)S(1)} fusion(bf16[320,512]{1,0:T(8,128)(2,1)S(1)} %collective-permute-done.15, bf16[320,2048]{1,0:T(8,128)(2,1)} %collective-permute-done.16), kind=kOutput, calls=%fused_computation.52 | convolution fusion | flops 671088640 | bytes 5832704 | tf_op jit(solution)/shard_map/dot_general | solution.py:46
  108.5 0.0 slice-start.2
  108.5 3.2 %multiply_reduce_fusion = (f32[512]{0:T(512)S(1)}, f32[512,2048]{1,0:T(8,128)S(1)}) fusion(bf16[320,512]{1,0:T(8,128)(2,1)S(1)} %collective-permute-done.17, bf16[320,2048]{1,0:T(8,128)(2,1)} %collective-permute-done.18, f32[512,2048]{1,0:T(8,128)S(1)} %add_add_fusion.1, f32[512,2048]{1,0:T(8,128)S(1)} %fusion.17), kind=kOutput, calls=%fused_computation.3 | convolution fusion | flops 675282432 | bytes 14223360 | tf_op jit(solution)/shard_map/dot_general | solution.py:46
  111.8 5.6 %fusion = f32[512,2,1280]{2,0,1:T(8,128)S(1)} fusion(bf16[2048,2,1280]{2,1,0:T(2,128)(2,1)S(1)} %bitcast.77, f32[512,2048]{1,0:T(8,128)S(1)} %get-tuple-element.77, f32[2048]{0:T(1024)S(1)} %copy-done.24, f32[512]{0:T(512)S(1)} %add_rsqrt_fusion.2), kind=kOutput, calls=%fused_computation | convolution fusion | flops 5371854848 | bytes 19933184 | tf_op jit(solution)/shard_map/rd,dgf->rgf/dot_general | solution.py:416
  117.5 0.8 fusion.3
  118.3 0.5 copy-done.8
  118.8 0.8 convolution_convert_fusion.2
  119.7 0.6 collective-permute-start.19
  120.2 0.8 convolution_convert_fusion.1
  121.1 0.7 collective-permute-done.19
  121.8 0.8 fusion.10
  122.6 1.6 %collective-permute-start.21 = (bf16[512,512]{1,0:T(8,128)(2,1)S(1)}, bf16[512,512]{1,0:T(8,128)(2,1)S(1)}, u32[]{:S(2)}, u32[]{:S(2)}) collective-permute-start(bf16[512,512]{1,0:T(8,128)(2,1)S(1)} %fusion.10), channel_id=1, source_target_pairs={{0,2},{1,3},{2,0},{3,1},{4,6},{5,7},{6,4},{7,5},{8,10},{9,11},{10,... | collective-permute-start | bytes 1572872 | tf_op jit(solution)/shard_map/ppermute | solution.py:333
  124.2 0.1 collective-permute-start.20
  124.3 0.9 pad_maximum_fusion
  125.2 0.8 fusion.11
  126.0 10.9 %collective-permute-done.21 = bf16[512,512]{1,0:T(8,128)(2,1)S(1)} collective-permute-done((bf16[512,512]{1,0:T(8,128)(2,1)S(1)}, bf16[512,512]{1,0:T(8,128)(2,1)S(1)}, u32[]{:S(2)}, u32[]{:S(2)}) %collective-permute-start.21) | collective-permute-done | bytes 524320 | tf_op jit(solution)/shard_map/ppermute | solution.py:333
  136.9 1.1 add_convert_fusion
  (73 shorter events, 0.2 us)
Async XLA Ops:
  0.6 44.3 %copy-start = (bf16[2048,640]{1,0:T(8,128)(2,1)S(1)}, bf16[2048,640]{1,0:T(8,128)(2,1)}, u32[]{:S(2)}) copy-start(bf16[2048,640]{1,0:T(8,128)(2,1)} %param.21) | copy-start | bytes 7864324
  0.6 15.2 %collective-permute-start.1 = (bf16[512,512]{1,0:T(8,128)(2,1)}, bf16[512,512]{1,0:T(8,128)(2,1)S(1)}, u32[]{:S(2)}, u32[]{:S(2)}) collective-permute-start(bf16[512,512]{1,0:T(8,128)(2,1)} %own_ref), channel_id=1, source_target_pairs={{0,2},{1,3},{2,0},{3,1},{4,6},{5,7},{6,4},{7,5},{8,10},{9,11},{10,... | collective-permute-start | bytes 1572872 | tf_op jit(solution)/shard_map/ppermute | solution.py:333
  3.7 31.3 %collective-permute-start = (bf16[512,512]{1,0:T(8,128)(2,1)}, bf16[512,512]{1,0:T(8,128)(2,1)}, u32[]{:S(2)}, u32[]{:S(2)}) collective-permute-start(bf16[512,512]{1,0:T(8,128)(2,1)} %own_ref), channel_id=1, source_target_pairs={{0,1},{1,0},{2,3},{3,2},{4,5},{5,4},{6,7},{7,6},{8,9},{9,8},{10,11... | collective-permute-start | bytes 1572872 | tf_op jit(solution)/shard_map/ppermute | solution.py:336
  4.7 11.1 %copy-start.14 = (bf16[1,2,768,320]{2,3,1,0:T(8,128)(2,1)S(1)}, bf16[1,2,768,320]{2,3,1,0:T(8,128)(2,1)}, u32[]{:S(2)}) copy-start(bf16[1,2,768,320]{2,3,1,0:T(8,128)(2,1)} %param.18) | copy-start | bytes 2949124
  15.8 21.4 %copy-start.9 = (bf16[512,512]{1,0:T(8,128)(2,1)}, bf16[512,512]{1,0:T(8,128)(2,1)S(1)}, u32[]{:S(2)}) copy-start(bf16[512,512]{1,0:T(8,128)(2,1)S(1)} %collective-permute-done.1.chip_ref) | copy-start | bytes 1572868
  15.8 20.6 %collective-permute-start.2 = (bf16[512,512]{1,0:T(8,128)(2,1)S(1)}, bf16[512,512]{1,0:T(8,128)(2,1)S(1)}, u32[]{:S(2)}, u32[]{:S(2)}) collective-permute-start(bf16[512,512]{1,0:T(8,128)(2,1)S(1)} %collective-permute-done.1.chip_ref), channel_id=1, source_target_pairs={{0,1},{1,0},{2,3},{3,2},{4,5},{5,4},{6,7},{7,6},{8,9},{9,8},{10,11... | collective-permute-start | bytes 1572872 | tf_op jit(solution)/shard_map/ppermute | solution.py:336
  15.9 21.3 %copy-start.11 = (bf16[2,320,384]{2,1,0:T(8,128)(2,1)}, bf16[2,320,384]{2,1,0:T(8,128)(2,1)S(1)}, u32[]{:S(2)}) copy-start(bf16[2,320,384]{2,1,0:T(8,128)(2,1)S(1)} %dynamic-slice_bitcast_fusion.refs_0_) | copy-start | bytes 1474564
  15.9 14.0 %collective-permute-start.4 = (bf16[2,320,384]{2,1,0:T(8,128)(2,1)S(1)}, bf16[2,320,384]{2,1,0:T(8,128)(2,1)}, u32[]{:S(2)}, u32[]{:S(2)}) collective-permute-start(bf16[2,320,384]{2,1,0:T(8,128)(2,1)S(1)} %dynamic-slice_bitcast_fusion.refs_0_), channel_id=1, source_target_pairs={{0,16},{4,20},{16,24},{20,28},{24,8},{28,12},{8,0},{12,4},{1,17},{... | collective-permute-start | bytes 1474568 | tf_op jit(solution)/shard_map/ppermute | solution.py:351
  18.8 14.6 %collective-permute-start.3 = (bf16[2,320,384]{2,1,0:T(8,128)(2,1)S(1)}, bf16[2,320,384]{2,1,0:T(8,128)(2,1)S(1)}, u32[]{:S(2)}, u32[]{:S(2)}) collective-permute-start(bf16[2,320,384]{2,1,0:T(8,128)(2,1)S(1)} %dynamic-slice_bitcast_fusion.refs_0_), channel_id=1, source_target_pairs={{0,4},{4,0},{8,12},{12,8},{16,20},{20,16},{24,28},{28,24},{1,5},{5... | collective-permute-start | bytes 1474568 | tf_op jit(solution)/shard_map/ppermute | solution.py:354
  20.3 79.6 %collective-permute-start.14 = (bf16[320,2048]{1,0:T(8,128)(2,1)}, bf16[320,2048]{1,0:T(8,128)(2,1)}, u32[]{:S(2)}, u32[]{:S(2)}) collective-permute-start(bf16[320,2048]{1,0:T(8,128)(2,1)} %param.24), channel_id=1, source_target_pairs={{0,1},{1,0},{2,3},{3,2},{4,5},{5,4},{6,7},{7,6},{8,9},{9,8},{10,11... | collective-permute-start | bytes 3932168 | tf_op jit(solution)/shard_map/ppermute | solution.py:336
  29.9 16.6 %collective-permute-start.5 = (bf16[2,320,384]{2,1,0:T(8,128)(2,1)}, bf16[2,320,384]{2,1,0:T(8,128)(2,1)}, u32[]{:S(2)}, u32[]{:S(2)}) collective-permute-start(bf16[2,320,384]{2,1,0:T(8,128)(2,1)} %collective-permute-done.4.refs_2_), channel_id=1, source_target_pairs={{0,16},{4,20},{16,24},{20,28},{24,8},{28,12},{8,0},{12,4},{1,17},{... | collective-permute-start | bytes 1474568 | tf_op jit(solution)/shard_map/ppermute | solution.py:351
  33.4 3.8 %copy-start.20 = (bf16[2,320,384]{2,1,0:T(8,128)(2,1)}, bf16[2,320,384]{2,1,0:T(8,128)(2,1)S(1)}, u32[]{:S(2)}) copy-start(bf16[2,320,384]{2,1,0:T(8,128)(2,1)S(1)} %collective-permute-done.3.refs_1_) | copy-start | bytes 1474564
  33.4 32.8 %collective-permute-start.7 = (bf16[2,320,384]{2,1,0:T(8,128)(2,1)}, bf16[2,320,384]{2,1,0:T(8,128)(2,1)}, u32[]{:S(2)}, u32[]{:S(2)}) collective-permute-start(bf16[2,320,384]{2,1,0:T(8,128)(2,1)} %collective-permute-done.4.refs_2_), channel_id=1, source_target_pairs={{0,4},{4,0},{8,12},{12,8},{16,20},{20,16},{24,28},{28,24},{1,5},{5... | collective-permute-start | bytes 1474568 | tf_op jit(solution)/shard_map/ppermute | solution.py:354
  34.9 55.8 %collective-permute-start.16 = (bf16[320,2048]{1,0:T(8,128)(2,1)}, bf16[320,2048]{1,0:T(8,128)(2,1)}, u32[]{:S(2)}, u32[]{:S(2)}) collective-permute-start(bf16[320,2048]{1,0:T(8,128)(2,1)} %param.24), channel_id=1, source_target_pairs={{0,2},{1,3},{2,0},{3,1},{4,6},{5,7},{6,4},{7,5},{8,10},{9,11},{10,... | collective-permute-start | bytes 3932168 | tf_op jit(solution)/shard_map/ppermute | solution.py:333
  36.4 0.8 copy-start.10
  41.9 3.0 %copy-start.19 = (bf16[512,2048]{1,0:T(8,128)(2,1)S(1)}, bf16[512,2048]{1,0:T(8,128)(2,1)}, u32[]{:S(2)}) copy-start(bf16[512,2048]{1,0:T(8,128)(2,1)} %get-tuple-element.41) | copy-start | bytes 6291460
  44.9 4.1 %copy-start.18 = (f32[64]{0:T(128)S(1)}, f32[64]{0:T(128)}, u32[]{:S(2)}) copy-start(f32[64]{0:T(128)} %param.22) | copy-start | bytes 772
  46.5 2.8 %copy-start.17 = (f32[64]{0:T(128)S(1)}, f32[64]{0:T(128)}, u32[]{:S(2)}) copy-start(f32[64]{0:T(128)} %param.23) | copy-start | bytes 772
  46.5 12.2 %collective-permute-start.9 = (bf16[2,320,384]{2,1,0:T(8,128)(2,1)}, bf16[2,320,384]{2,1,0:T(8,128)(2,1)S(1)}, u32[]{:S(2)}, u32[]{:S(2)}) collective-permute-start(bf16[2,320,384]{2,1,0:T(8,128)(2,1)} %collective-permute-done.5.refs_4_), channel_id=1, source_target_pairs={{0,16},{4,20},{16,24},{20,28},{24,8},{28,12},{8,0},{12,4},{1,17},{... | collective-permute-start | bytes 1474568 | tf_op jit(solution)/shard_map/ppermute | solution.py:351
  47.4 18.2 %collective-permute-start.8 = (bf16[2,320,384]{2,1,0:T(8,128)(2,1)}, bf16[2,320,384]{2,1,0:T(8,128)(2,1)S(1)}, u32[]{:S(2)}, u32[]{:S(2)}) collective-permute-start(bf16[2,320,384]{2,1,0:T(8,128)(2,1)} %collective-permute-done.5.refs_4_), channel_id=1, source_target_pairs={{0,4},{4,0},{8,12},{12,8},{16,20},{20,16},{24,28},{28,24},{1,5},{5... | collective-permute-start | bytes 1474568 | tf_op jit(solution)/shard_map/ppermute | solution.py:354
  49.6 10.8 %copy-start.13 = (bf16[512,5,64]{0,2,1:T(8,128)(2,1)}, bf16[512,5,64]{0,2,1:T(8,128)(2,1)S(1)}, u32[]{:S(2)}) copy-start(bf16[512,5,64]{0,2,1:T(8,128)(2,1)S(1)} %maximum_multiply_fusion) | copy-start | bytes 983044
  58.7 6.8 %copy-start.15 = (bf16[2,320,384]{2,1,0:T(8,128)(2,1)}, bf16[2,320,384]{2,1,0:T(8,128)(2,1)S(1)}, u32[]{:S(2)}) copy-start(bf16[2,320,384]{2,1,0:T(8,128)(2,1)S(1)} %collective-permute-done.9.refs_6_) | copy-start | bytes 1474564
  58.7 10.2 %collective-permute-start.6 = (bf16[320,512]{1,0:T(8,128)(2,1)S(1)}, bf16[320,512]{1,0:T(8,128)(2,1)S(1)}, u32[]{:S(2)}, u32[]{:S(2)}) collective-permute-start(bf16[320,512]{1,0:T(8,128)(2,1)S(1)} %bitcast.71), channel_id=1, source_target_pairs={{0,1},{1,0},{2,3},{3,2},{4,5},{5,4},{6,7},{7,6},{8,9},{9,8},{10,11... | collective-permute-start | bytes 983048 | tf_op jit(solution)/shard_map/ppermute | solution.py:336
  65.6 8.9 %copy-start.16 = (bf16[2,320,384]{2,1,0:T(8,128)(2,1)}, bf16[2,320,384]{2,1,0:T(8,128)(2,1)S(1)}, u32[]{:S(2)}) copy-start(bf16[2,320,384]{2,1,0:T(8,128)(2,1)S(1)} %collective-permute-done.8.refs_5_) | copy-start | bytes 1474564
  65.6 8.4 %collective-permute-start.10 = (bf16[1,320,384]{2,1,0:T(8,128)(2,1)S(1)}, bf16[1,320,384]{2,1,0:T(8,128)(2,1)S(1)}, u32[]{:S(2)}, u32[]{:S(2)}) collective-permute-start(bf16[1,320,384]{2,1,0:T(8,128)(2,1)S(1)} %slice.40), channel_id=1, source_target_pairs={{0,4},{4,0},{8,12},{12,8},{16,20},{20,16},{24,28},{28,24},{1,5},{5... | collective-permute-start | bytes 737288 | tf_op jit(solution)/shard_map/ppermute | solution.py:354
  66.2 8.3 %collective-permute-start.11 = (bf16[1,320,384]{2,1,0:T(8,128)(2,1)S(1)}, bf16[1,320,384]{2,1,0:T(8,128)(2,1)S(1)}, u32[]{:S(2)}, u32[]{:S(2)}) collective-permute-start(bf16[1,320,384]{2,1,0:T(8,128)(2,1)S(1)} %slice.48), channel_id=1, source_target_pairs={{0,16},{4,20},{16,24},{20,28},{24,8},{28,12},{8,0},{12,4},{1,17},{... | collective-permute-start | bytes 737288 | tf_op jit(solution)/shard_map/ppermute | solution.py:351
  69.0 5.5 %copy-start.21 = (bf16[320,512]{1,0:T(8,128)(2,1)}, bf16[320,512]{1,0:T(8,128)(2,1)S(1)}, u32[]{:S(2)}) copy-start(bf16[320,512]{1,0:T(8,128)(2,1)S(1)} %collective-permute-done.6.other_q_ref) | copy-start | bytes 983044
  74.0 0.7 copy-start.22
  74.5 0.7 copy-start.23
  90.7 2.0 %collective-permute-start.12 = (bf16[352,512]{1,0:T(8,128)(2,1)}, bf16[352,512]{1,0:T(8,128)(2,1)S(1)}, u32[]{:S(2)}, u32[]{:S(2)}) collective-permute-start(bf16[352,512]{1,0:T(8,128)(2,1)} %get-tuple-element.53), channel_id=1, source_target_pairs={{0,1},{1,0},{2,3},{3,2},{4,5},{5,4},{6,7},{7,6},{8,9},{9,8},{10,11... | collective-permute-start | bytes 1081352 | tf_op jit(solution)/shard_map/ppermute | solution.py:336
  90.8 17.8 %collective-permute-start.18 = (bf16[320,2048]{1,0:T(8,128)(2,1)}, bf16[320,2048]{1,0:T(8,128)(2,1)}, u32[]{:S(2)}, u32[]{:S(2)}) collective-permute-start(bf16[320,2048]{1,0:T(8,128)(2,1)} %collective-permute-done.16), channel_id=1, source_target_pairs={{0,1},{1,0},{2,3},{3,2},{4,5},{5,4},{6,7},{7,6},{8,9},{9,8},{10,11... | collective-permute-start | bytes 3932168 | tf_op jit(solution)/shard_map/ppermute | solution.py:336
  92.6 0.7 copy-start.12
  95.6 4.3 %copy-start.2 = (bf16[512,2048]{1,0:T(8,128)(2,1)S(1)}, bf16[512,2048]{1,0:T(8,128)(2,1)}, u32[]{:S(2)}) copy-start(bf16[512,2048]{1,0:T(8,128)(2,1)} %get-tuple-element.40) | copy-start | bytes 6291460
  95.6 4.3 %collective-permute-start.13 = (bf16[320,512]{1,0:T(8,128)(2,1)}, bf16[320,512]{1,0:T(8,128)(2,1)S(1)}, u32[]{:S(2)}, u32[]{:S(2)}) collective-permute-start(bf16[320,512]{1,0:T(8,128)(2,1)} %merge.1), channel_id=1, source_target_pairs={{0,1},{1,0},{2,3},{3,2},{4,5},{5,4},{6,7},{7,6},{8,9},{9,8},{10,11... | collective-permute-start | bytes 983048 | tf_op jit(solution)/shard_map/ppermute | solution.py:336
  95.7 10.2 %collective-permute-start.15 = (bf16[320,512]{1,0:T(8,128)(2,1)}, bf16[320,512]{1,0:T(8,128)(2,1)S(1)}, u32[]{:S(2)}, u32[]{:S(2)}) collective-permute-start(bf16[320,512]{1,0:T(8,128)(2,1)} %merge.1), channel_id=1, source_target_pairs={{0,2},{1,3},{2,0},{3,1},{4,6},{5,7},{6,4},{7,5},{8,10},{9,11},{10,... | collective-permute-start | bytes 983048 | tf_op jit(solution)/shard_map/ppermute | solution.py:333
  99.9 11.9 %slice-start = ((s8[10485760]{0:T(1024)(128)(4,1)}), s8[4194304]{0:T(1024)(128)(4,1)S(1)}, s32[]{:S(2)}) async-start(s8[10485760]{0:T(1024)(128)(4,1)} %bitcast.76), calls=%async_computation | async-start | bytes 8388608
  99.9 11.9 %slice-start.1 = ((s8[10485760]{0:T(1024)(128)(4,1)}), s8[4194304]{0:T(1024)(128)(4,1)S(1)}, s32[]{:S(2)}) async-start(s8[10485760]{0:T(1024)(128)(4,1)} %bitcast.76), calls=%async_computation.1 | async-start | bytes 8388608
  105.9 2.6 %collective-permute-start.17 = (bf16[320,512]{1,0:T(8,128)(2,1)S(1)}, bf16[320,512]{1,0:T(8,128)(2,1)S(1)}, u32[]{:S(2)}, u32[]{:S(2)}) collective-permute-start(bf16[320,512]{1,0:T(8,128)(2,1)S(1)} %collective-permute-done.15), channel_id=1, source_target_pairs={{0,1},{1,0},{2,3},{3,2},{4,5},{5,4},{6,7},{7,6},{8,9},{9,8},{10,11... | collective-permute-start | bytes 983048 | tf_op jit(solution)/shard_map/ppermute | solution.py:336
  108.5 3.3 %slice-start.2 = ((s8[10485760]{0:T(1024)(128)(4,1)}), s8[2097152]{0:T(1024)(128)(4,1)S(1)}, s32[]{:S(2)}) async-start(s8[10485760]{0:T(1024)(128)(4,1)} %bitcast.76), calls=%async_computation.2 | async-start | bytes 4194304
  108.5 3.3 %copy-start.24 = (f32[2048]{0:T(1024)S(1)}, f32[2048]{0:T(1024)}, u32[]{:S(2)}) copy-start(f32[2048]{0:T(1024)} %param.25) | copy-start | bytes 24580
  117.5 1.3 copy-start.8
  118.8 1.4 %copy-start.7 = (bf16[1280,512]{1,0:T(8,128)(2,1)S(1)}, bf16[1280,512]{1,0:T(8,128)(2,1)}, u32[]{:S(2)}) copy-start(bf16[1280,512]{1,0:T(8,128)(2,1)} %get-tuple-element.61) | copy-start | bytes 3932164
  119.6 2.1 %copy-start.6 = (bf16[1280,512]{1,0:T(8,128)(2,1)S(1)}, bf16[1280,512]{1,0:T(8,128)(2,1)}, u32[]{:S(2)}) copy-start(bf16[1280,512]{1,0:T(8,128)(2,1)} %get-tuple-element.59) | copy-start | bytes 3932164
  119.7 2.1 %collective-permute-start.19 = (bf16[512,512]{1,0:T(8,128)(2,1)S(1)}, bf16[512,512]{1,0:T(8,128)(2,1)S(1)}, u32[]{:S(2)}, u32[]{:S(2)}) collective-permute-start(bf16[512,512]{1,0:T(8,128)(2,1)S(1)} %convolution_convert_fusion.2), channel_id=1, source_target_pairs={{0,1},{1,0},{2,3},{3,2},{4,5},{5,4},{6,7},{7,6},{8,9},{9,8},{10,11... | collective-permute-start | bytes 1572872 | tf_op jit(solution)/shard_map/ppermute | solution.py:336
  121.1 3.2 %copy-start.3 = (bf16[512,5,64]{0,2,1:T(8,128)(2,1)S(1)}, bf16[512,5,64]{0,2,1:T(8,128)(2,1)}, u32[]{:S(2)}) copy-start(bf16[512,5,64]{0,2,1:T(8,128)(2,1)} %maximum_convert_fusion) | copy-start | bytes 983044
  121.1 3.2 %copy-start.4 = (bf16[512,1,5,64]{0,3,2,1:T(8,128)(2,1)S(1)}, bf16[512,1,5,64]{0,3,2,1:T(8,128)(2,1)}, u32[]{:S(2)}) copy-start(bf16[512,1,5,64]{0,3,2,1:T(8,128)(2,1)} %slice.70) | copy-start | bytes 983044
  121.1 4.1 %copy-start.5 = (bf16[1280,512]{1,0:T(8,128)(2,1)S(1)}, bf16[1280,512]{1,0:T(8,128)(2,1)}, u32[]{:S(2)}) copy-start(bf16[1280,512]{1,0:T(8,128)(2,1)} %get-tuple-element.64) | copy-start | bytes 3932164
  122.6 14.3 %collective-permute-start.21 = (bf16[512,512]{1,0:T(8,128)(2,1)S(1)}, bf16[512,512]{1,0:T(8,128)(2,1)S(1)}, u32[]{:S(2)}, u32[]{:S(2)}) collective-permute-start(bf16[512,512]{1,0:T(8,128)(2,1)S(1)} %fusion.10), channel_id=1, source_target_pairs={{0,2},{1,3},{2,0},{3,1},{4,6},{5,7},{6,4},{7,5},{8,10},{9,11},{10,... | collective-permute-start | bytes 1572872 | tf_op jit(solution)/shard_map/ppermute | solution.py:333
  124.2 12.7 %collective-permute-start.20 = (bf16[512,512]{1,0:T(8,128)(2,1)S(1)}, bf16[512,512]{1,0:T(8,128)(2,1)S(1)}, u32[]{:S(2)}, u32[]{:S(2)}) collective-permute-start(bf16[512,512]{1,0:T(8,128)(2,1)S(1)} %convolution_convert_fusion.1), channel_id=1, source_target_pairs={{0,1},{1,0},{2,3},{3,2},{4,5},{5,4},{6,7},{7,6},{8,9},{9,8},{10,11... | collective-permute-start | bytes 1572872 | tf_op jit(solution)/shard_map/ppermute | solution.py:336
  125.2 12.8 %copy-start.1 = (bf16[2048,640]{1,0:T(8,128)(2,1)S(1)}, bf16[2048,640]{1,0:T(8,128)(2,1)}, u32[]{:S(2)}) copy-start(bf16[2048,640]{1,0:T(8,128)(2,1)} %param.21) | copy-start | bytes 7864324

commit v7 on v6

--- a/solution.py
+++ b/solution.py
@@ -357,22 +357,13 @@
     units = [mine, aside(mine)]
     from_chip = across_chip(tokens)
     from_core = across_core(tokens)
-    down_blocks = [
-        lax.dynamic_slice_in_dim(w_down, (rank ^ flip) * width, width, 1) for flip in range(4)
-    ]
-    from_chip, down_blocks, cos_part, sin_part = lax.optimization_barrier(
-        (from_chip, down_blocks, cos_part, sin_part)
-    )
+    held[1], cos_part, sin_part = lax.optimization_barrier((held[1], cos_part, sin_part))
+    from_chip, units[1], _ = lax.optimization_barrier((from_chip, units[1], held[1]))
     from_both = across_core(from_chip)
-    held[1], _ = lax.optimization_barrier((held[1], from_chip))
-    pieces, units[1], _ = lax.optimization_barrier(
-        ((tokens, from_core, from_chip, from_both), units[1], held[1])
-    )
-    full_rows, normalized_input = gather_norm(rank, pieces, attn_gain)
+    full_rows, normalized_input = gather_norm(rank, (tokens, from_core, from_chip, from_both), attn_gain)
 
     w_out_held, _ = lax.optimization_barrier((w_out, from_chip))
     w_out_chip = across_chip(w_out_held)
-    w_out_core = across_core(w_out)
     w_out_both = across_core(w_out_chip)
 
     query_rows = jnp.dot(
@@ -384,6 +375,8 @@
     query_rows, key_value_rows, second = lax.optimization_barrier((query_rows, key_value_rows, ring(held[1])))
     units += [held[1], aside(held[1])]
     held.append(second)
+    w_out_held, _ = lax.optimization_barrier((w_out, second))
+    w_out_core = across_core(w_out_held)
     for _ in range(3, length):
         units += [held[-1], aside(held[-1])]
         held.append(ring(held[-1]))
@@ -402,6 +395,11 @@
 
     held[-1], suffix_out, suffix_lse = lax.optimization_barrier((held[-1], suffix_out, suffix_lse))
     units += [held[-1], aside(held[-1][:1]), ring(units[-1][1:])]
+    w_down_held, _ = lax.optimization_barrier((w_down, held[-1]))
+    down_blocks = [
+        lax.dynamic_slice_in_dim(w_down_held, (rank ^ flip) * width, width, 1) for flip in range(4)
+    ]
+    own_q, down_blocks = lax.optimization_barrier((own_q, down_blocks))
     own_out, own_lse, sent = prefix_attend(
         owners, request_groups, request_lengths, my_req.reshape(1), own_q, other_q, units
     )

time: 138 us -> 122 us (0.88)
  waiting for transfers between devices: 46.3 us -> 31.9 us
  starting transfers between devices: 24 us -> 20.9 us
    ppermute x4, waiting for transfers between devices: 19.2 us -> 10.6 us  [ring(): lax.ppermute(value, 'req', [(2 * a + b, 2 * c + b) for a, c in steps for...]
    ppermute x4, waiting for transfers between devices: 20 us -> 15.6 us  [across_chip(): return lax.ppermute(value, 'tp', [(i, i ^ 2) for i in range(4)])]
    ppermute x4, starting transfers between devices: 7.58 us -> 5.19 us  [across_chip(): return lax.ppermute(value, 'tp', [(i, i ^ 2) for i in range(4)])]
    ppermute x4, starting transfers between devices: 9.95 us -> 8.04 us  [ring(): lax.ppermute(value, 'req', [(2 * a + b, 2 * c + b) for a, c in steps for...]
    unnamed x56 -> x54, local copies, waits for them, and re-layouts: 2.85 us -> 2.84 us
  transfers between devices with their start and end apart: 22 -> 22, of which waited for: 9 -> 9; matrix products, arithmetic and copies ran while one was open for 17% -> 21% of each run, Pallas kernels for 20% -> 23%
where the time goes in v7:
time: 122 us; the launch traced here: 121 us
  waiting for transfers between devices  31.9 us (26%)
  Pallas kernels  27.4 us (22%)
  matrix products  24.9 us (20%)
  starting transfers between devices  20.9 us (17%)
  local copies, waits for them, and re-layouts  9.72 us (8%)
  other arithmetic  5.41 us (4%)
    ppermute x4, waiting for transfers between devices, across_chip(): return lax.ppermute(value, 'tp', [(i, i ^ 2) for i in range(4)])  15.6 us
    pallas_call x1, Pallas kernels, prefix_attend(): pl.pallas_call(functools.partial(prefix_kernel, block, 256, len(units) -...  15.3 us
    dot_general x4, matrix products, tn_dot(): lax.dot_general(lhs, rhs, (((0,), (0,)), ((), ())), preferred_element_typ...  11.4 us
    ppermute x4, waiting for transfers between devices, ring(): lax.ppermute(value, 'req', [(2 * a + b, 2 * c + b) for a, c in steps for...  10.6 us
    ppermute x4, starting transfers between devices, ring(): lax.ppermute(value, 'req', [(2 * a + b, 2 * c + b) for a, c in steps for...  8.04 us
    ppermute x4, starting transfers between devices, aside(): return lax.ppermute(value, 'req', [(r, r ^ 1) for r in range(n_req)])  6.08 us
    dot_general x1, matrix products, local(): jnp.einsum('rd,dgf->rgf', normed_ffn, w_gate_up, preferred_element_type=j...  5.64 us
    ppermute x4, starting transfers between devices, across_chip(): return lax.ppermute(value, 'tp', [(i, i ^ 2) for i in range(4)])  5.19 us
  transfers between devices with their start and end apart: 22, of which 9 were waited for; matrix products, arithmetic and copies ran while one was open for 21% of the time, Pallas kernels for 23%

profile of v7, /device:TPU:0, one launch (start us, length us, event | category | flops | bytes accessed | tf_op | source)
XLA Modules:
  0.0 121.3 jit_solution(3132382961996201170)
XLA Ops:
  0.6 3.0 %collective-permute-start.1 = (bf16[512,512]{1,0:T(8,128)(2,1)}, bf16[512,512]{1,0:T(8,128)(2,1)S(1)}, u32[]{:S(2)}, u32[]{:S(2)}) collective-permute-start(bf16[512,512]{1,0:T(8,128)(2,1)} %own_ref.1), channel_id=1, source_target_pairs={{0,2},{1,3},{2,0},{3,1},{4,6},{5,7},{6,4},{7,5},{8,10},{9,11},{10,... | collective-permute-start | bytes 1572872 | tf_op jit(solution)/shard_map/ppermute | solution.py:333
  3.7 1.1 dynamic-slice_bitcast_fusion.refs_0_
  4.8 2.6 %collective-permute-start.3 = (bf16[2,320,384]{2,1,0:T(8,128)(2,1)S(1)}, bf16[2,320,384]{2,1,0:T(8,128)(2,1)S(1)}, u32[]{:S(2)}, u32[]{:S(2)}) collective-permute-start(bf16[2,320,384]{2,1,0:T(8,128)(2,1)S(1)} %dynamic-slice_bitcast_fusion.refs_0_), channel_id=1, source_target_pairs={{0,16},{4,20},{16,24},{20,28},{24,8},{28,12},{8,0},{12,4},{1,17},{... | collective-permute-start | bytes 1474568 | tf_op jit(solution)/shard_map/ppermute | solution.py:351
  7.4 1.5 %collective-permute-start.2 = (bf16[2,320,384]{2,1,0:T(8,128)(2,1)S(1)}, bf16[2,320,384]{2,1,0:T(8,128)(2,1)S(1)}, u32[]{:S(2)}, u32[]{:S(2)}) collective-permute-start(bf16[2,320,384]{2,1,0:T(8,128)(2,1)S(1)} %dynamic-slice_bitcast_fusion.refs_0_), channel_id=1, source_target_pairs={{0,4},{4,0},{8,12},{12,8},{16,20},{20,16},{24,28},{28,24},{1,5},{5... | collective-permute-start | bytes 1474568 | tf_op jit(solution)/shard_map/ppermute | solution.py:354
  8.9 0.7 add_convert_fusion.3
  9.6 0.3 multiply_sine_fusion
  9.9 7.7 %collective-permute-done.3.refs_2_ = bf16[2,320,384]{2,1,0:T(8,128)(2,1)S(1)} collective-permute-done((bf16[2,320,384]{2,1,0:T(8,128)(2,1)S(1)}, bf16[2,320,384]{2,1,0:T(8,128)(2,1)S(1)}, u32[]{:S(2)}, u32[]{:S(2)}) %collective-permute-start.3) | collective-permute-done | bytes 491552 | tf_op jit(solution)/shard_map/ppermute | solution.py:351
  17.6 2.2 %collective-permute-done.2.refs_1_ = bf16[2,320,384]{2,1,0:T(8,128)(2,1)S(1)} collective-permute-done((bf16[2,320,384]{2,1,0:T(8,128)(2,1)S(1)}, bf16[2,320,384]{2,1,0:T(8,128)(2,1)S(1)}, u32[]{:S(2)}, u32[]{:S(2)}) %collective-permute-start.2) | collective-permute-done | bytes 491552 | tf_op jit(solution)/shard_map/ppermute | solution.py:354
  19.8 0.8 copy-done.19
  20.6 1.6 %collective-permute-start.5 = (bf16[2,320,384]{2,1,0:T(8,128)(2,1)}, bf16[2,320,384]{2,1,0:T(8,128)(2,1)}, u32[]{:S(2)}, u32[]{:S(2)}) collective-permute-start(bf16[2,320,384]{2,1,0:T(8,128)(2,1)} %copy-done.18), channel_id=1, source_target_pairs={{0,16},{4,20},{16,24},{20,28},{24,8},{28,12},{8,0},{12,4},{1,17},{... | collective-permute-start | bytes 1474568 | tf_op jit(solution)/shard_map/ppermute | solution.py:351
  22.2 1.5 %collective-permute-start.8 = (bf16[2,320,384]{2,1,0:T(8,128)(2,1)}, bf16[2,320,384]{2,1,0:T(8,128)(2,1)}, u32[]{:S(2)}, u32[]{:S(2)}) collective-permute-start(bf16[2,320,384]{2,1,0:T(8,128)(2,1)} %copy-done.18), channel_id=1, source_target_pairs={{0,4},{4,0},{8,12},{12,8},{16,20},{20,16},{24,28},{28,24},{1,5},{5... | collective-permute-start | bytes 1474568 | tf_op jit(solution)/shard_map/ppermute | solution.py:354
  23.7 0.7 collective-permute-start.16
  24.4 4.7 %gather_norm.1 = (bf16[512,2048]{1,0:T(8,128)(2,1)}, bf16[512,2048]{1,0:T(8,128)(2,1)}) custom-call(s32[1]{0:T(128)} %bitcast.rank_ref, bf16[512,512]{1,0:T(8,128)(2,1)} %own_ref.1, bf16[512,512]{1,0:T(8,128)(2,1)} %collective-permute-done.core_ref, bf16[512,512]{1,0:T(8,128)(2,1)} %copy-done.9, bf16[512,512]{1,0:T(8,128)(2,1)} %collective-permute-done.4.both_ref, ...), custom_call_target="tpu_custom_call" | custom-call | tf_op jit(solution)/shard_map/gather_norm/pallas_call | solution.py:73
  29.2 3.0 %fusion.12 = f32[512,320]{0,1:T(8,128)S(1)} fusion(bf16[512,2048]{1,0:T(8,128)(2,1)} %get-tuple-element.36, bf16[2048,320]{0,1:T(8,128)(2,1)} %param.20), kind=kOutput, calls=%fused_computation.48 | convolution fusion | flops 671088640 | bytes 4063232 | tf_op jit(solution)/shard_map/dot_general | solution.py:369
  32.2 1.6 %fusion.13 = f32[512,640]{0,1:T(8,128)S(1)} fusion(bf16[512,2048]{1,0:T(8,128)(2,1)S(1)} %copy-done.17, bf16[2048,640]{1,0:T(8,128)(2,1)S(1)} %copy-done), kind=kOutput, calls=%fused_computation.49 | convolution fusion | flops 1342177280 | bytes 6029312 | tf_op jit(solution)/shard_map/dot_general | solution.py:372
  33.8 0.8 collective-permute-done.5.refs_4_
  34.6 2.5 %collective-permute-start.6 = (bf16[2,320,384]{2,1,0:T(8,128)(2,1)}, bf16[2,320,384]{2,1,0:T(8,128)(2,1)S(1)}, u32[]{:S(2)}, u32[]{:S(2)}) collective-permute-start(bf16[2,320,384]{2,1,0:T(8,128)(2,1)} %collective-permute-done.5.refs_4_), channel_id=1, source_target_pairs={{0,16},{4,20},{16,24},{20,28},{24,8},{28,12},{8,0},{12,4},{1,17},{... | collective-permute-start | bytes 1474568 | tf_op jit(solution)/shard_map/ppermute | solution.py:351
  37.1 1.5 %collective-permute-start.9 = (bf16[2,320,384]{2,1,0:T(8,128)(2,1)}, bf16[2,320,384]{2,1,0:T(8,128)(2,1)S(1)}, u32[]{:S(2)}, u32[]{:S(2)}) collective-permute-start(bf16[2,320,384]{2,1,0:T(8,128)(2,1)} %collective-permute-done.5.refs_4_), channel_id=1, source_target_pairs={{0,4},{4,0},{8,12},{12,8},{16,20},{20,16},{24,28},{28,24},{1,5},{5... | collective-permute-start | bytes 1474568 | tf_op jit(solution)/shard_map/ppermute | solution.py:354
  38.6 0.1 multiply_reduce_fusion.1
  38.7 0.2 fusion.10
  39.0 0.1 subtract_convert_fusion
  39.1 0.1 maximum_multiply_fusion
  39.1 0.1 collective-permute-start.7
  39.2 0.1 fusion.11
  39.3 0.8 slice.70
  40.1 0.1 multiply_subtract_fusion
  40.2 0.8 maximum_convert_fusion
  41.0 5.2 %suffix_attend.1 = (f32[320,512]{1,0:T(8,128)}, f32[8,512]{1,0:T(8,128)}) custom-call(s32[1,2]{1,0:T(1,128)} %lengths_ref.1, bf16[320,512]{1,0:T(8,128)(2,1)} %bitcast.72, bf16[320,512]{1,0:T(8,128)(2,1)} %bitcast.69, bf16[320,512]{1,0:T(8,128)(2,1)} %bitcast.67), custom_call_target="tpu_custom_call" | custom-call | flops 335544320 | bytes 3145728 | tf_op jit(solution)/shard_map/suffix_attend/pallas_call | solution.py:115
  46.1 1.6 %collective-permute-done.6.refs_6_ = bf16[2,320,384]{2,1,0:T(8,128)(2,1)S(1)} collective-permute-done((bf16[2,320,384]{2,1,0:T(8,128)(2,1)}, bf16[2,320,384]{2,1,0:T(8,128)(2,1)S(1)}, u32[]{:S(2)}, u32[]{:S(2)}) %collective-permute-start.6) | collective-permute-done | bytes 491552 | tf_op jit(solution)/shard_map/ppermute | solution.py:351
  47.7 2.1 %collective-permute-done.9.refs_5_ = bf16[2,320,384]{2,1,0:T(8,128)(2,1)S(1)} collective-permute-done((bf16[2,320,384]{2,1,0:T(8,128)(2,1)}, bf16[2,320,384]{2,1,0:T(8,128)(2,1)S(1)}, u32[]{:S(2)}, u32[]{:S(2)}) %collective-permute-start.9) | collective-permute-done | bytes 491552 | tf_op jit(solution)/shard_map/ppermute | solution.py:354
  49.8 1.5 %collective-permute-start.10 = (bf16[1,320,384]{2,1,0:T(8,128)(2,1)S(1)}, bf16[1,320,384]{2,1,0:T(8,128)(2,1)S(1)}, u32[]{:S(2)}, u32[]{:S(2)}) collective-permute-start(bf16[1,320,384]{2,1,0:T(8,128)(2,1)S(1)} %slice.40), channel_id=1, source_target_pairs={{0,4},{4,0},{8,12},{12,8},{16,20},{20,16},{24,28},{28,24},{1,5},{5... | collective-permute-start | bytes 737288 | tf_op jit(solution)/shard_map/ppermute | solution.py:354
  51.3 1.4 %collective-permute-start.11 = (bf16[1,320,384]{2,1,0:T(8,128)(2,1)S(1)}, bf16[1,320,384]{2,1,0:T(8,128)(2,1)S(1)}, u32[]{:S(2)}, u32[]{:S(2)}) collective-permute-start(bf16[1,320,384]{2,1,0:T(8,128)(2,1)S(1)} %slice.48), channel_id=1, source_target_pairs={{0,16},{4,20},{16,24},{20,28},{24,8},{28,12},{8,0},{12,4},{1,17},{... | collective-permute-start | bytes 737288 | tf_op jit(solution)/shard_map/ppermute | solution.py:351
  52.7 5.0 %constant_dynamic-slice_fusion = (bf16[1280,512]{1,0:T(8,128)(2,1)}, bf16[1280,512]{1,0:T(8,128)(2,1)}, bf16[1280,512]{1,0:T(8,128)(2,1)}, bf16[1280,512]{1,0:T(8,128)(2,1)}) fusion(bf16[1280,2048]{1,0:T(8,128)(2,1)} %param.27, s32[]{:T(128)S(6)} %select_n.28, s32[]{:T(128)S(6)} %select_n.27, s32[]{:T(128)S(6)} %select_n.26, s32[]{:T(128)S(6)} %select_n.25), kind=kLoop, calls=%fused_computation.43 | loop fusion | bytes 10485776 | tf_op jit(solution)/shard_map/dynamic_slice | solution.py:400
  57.7 0.6 collective-permute-done.11.refs_8_
  58.3 0.1 copy-done.20
  58.4 0.1 copy-done.21
  58.5 0.5 copy-done.22
  59.0 15.3 %prefix_attend.1 = (f32[320,512]{1,0:T(8,128)}, f32[8,512]{1,0:T(8,128)}, bf16[352,512]{1,0:T(8,128)(2,1)}) custom-call(s32[8]{0:T(128)} %owners_ref.1, s32[1,2]{1,0:T(1,128)} %groups_ref.1, s32[1,2]{1,0:T(1,128)} %lengths_ref.1, s32[1]{0:T(128)} %bitcast.6.me_ref, bf16[320,512]{1,0:T(8,128)(2,1)} %bitcast.73, bf16[320,512]{1,0:T(8,128)(2,1)} %copy-done.20, ...), custom_call_target="tpu_custom_call" | custom-call | flops 2013265920 | bytes 6291456 | tf_op jit(solution)/shard_map/prefix_attend/pallas_call | solution.py:246
  74.3 0.1 collective-permute-start.12
  74.4 0.5 collective-permute-start.18
  74.9 1.4 %collective-permute-done.12.got_ref = bf16[352,512]{1,0:T(8,128)(2,1)S(1)} collective-permute-done((bf16[352,512]{1,0:T(8,128)(2,1)}, bf16[352,512]{1,0:T(8,128)(2,1)S(1)}, u32[]{:S(2)}, u32[]{:S(2)}) %collective-permute-start.12) | collective-permute-done | bytes 360480 | tf_op jit(solution)/shard_map/ppermute | solution.py:336
  76.3 0.7 copy-done.11
  77.0 2.2 %merge.1 = bf16[320,512]{1,0:T(8,128)(2,1)} custom-call(f32[320,512]{1,0:T(8,128)} %get-tuple-element.48.own_ref, f32[8,512]{1,0:T(8,128)} %get-tuple-element.49.own_lse_ref, bf16[352,512]{1,0:T(8,128)(2,1)} %copy-done.11, f32[320,512]{1,0:T(8,128)} %get-tuple-element.51.suffix_ref, f32[8,512]{1,0:T(8,128)} %get-tuple-element.52.suffix_lse_ref), custom_call_target="tpu_custom_call" | custom-call | flops 1310720 | bytes 1048576 | tf_op jit(solution)/shard_map/merge/pallas_call | solution.py:291
  79.2 0.1 collective-permute-start.13
  79.3 0.7 collective-permute-start.15
  80.0 2.7 %fusion.14 = f32[512,2048]{1,0:T(8,128)S(1)} fusion(bf16[320,512]{1,0:T(8,128)(2,1)} %merge.1, bf16[320,2048]{1,0:T(8,128)(2,1)} %param.24), kind=kOutput, calls=%fused_computation.50 | convolution fusion | flops 671088640 | bytes 5832704 | tf_op jit(solution)/shard_map/dot_general | solution.py:46
  82.8 2.8 %add_add_fusion.1 = f32[512,2048]{1,0:T(8,128)S(1)} fusion(f32[512,2048]{1,0:T(8,128)S(1)} %fusion.14, bf16[512,2048]{1,0:T(8,128)(2,1)S(1)} %copy-done.2, bf16[320,512]{1,0:T(8,128)(2,1)S(1)} %collective-permute-done.13, bf16[320,2048]{1,0:T(8,128)(2,1)} %collective-permute-done.14), kind=kOutput, calls=%fused_computation.5 | convolution fusion | flops 674234368 | bytes 12124160 | tf_op jit(solution)/shard_map/dot_general | solution.py:46
  85.6 3.9 %collective-permute-done.15 = bf16[320,512]{1,0:T(8,128)(2,1)S(1)} collective-permute-done((bf16[320,512]{1,0:T(8,128)(2,1)}, bf16[320,512]{1,0:T(8,128)(2,1)S(1)}, u32[]{:S(2)}, u32[]{:S(2)}) %collective-permute-start.15) | collective-permute-done | bytes 327712 | tf_op jit(solution)/shard_map/ppermute | solution.py:333
  89.5 2.6 %fusion.15 = f32[512,2048]{1,0:T(8,128)S(1)} fusion(bf16[320,512]{1,0:T(8,128)(2,1)S(1)} %collective-permute-done.15, bf16[320,2048]{1,0:T(8,128)(2,1)} %collective-permute-done.16), kind=kOutput, calls=%fused_computation.51 | convolution fusion | flops 671088640 | bytes 5832704 | tf_op jit(solution)/shard_map/dot_general | solution.py:46
  92.2 3.2 %multiply_reduce_fusion = (f32[512]{0:T(512)S(1)}, f32[512,2048]{1,0:T(8,128)S(1)}) fusion(bf16[320,512]{1,0:T(8,128)(2,1)S(1)} %collective-permute-done.17, bf16[320,2048]{1,0:T(8,128)(2,1)} %collective-permute-done.18, f32[512,2048]{1,0:T(8,128)S(1)} %add_add_fusion.1, f32[512,2048]{1,0:T(8,128)S(1)} %fusion.15), kind=kOutput, calls=%fused_computation.3 | convolution fusion | flops 675282432 | bytes 14223360 | tf_op jit(solution)/shard_map/dot_general | solution.py:46
  95.5 5.6 %fusion = f32[512,2,1280]{2,0,1:T(8,128)S(1)} fusion(bf16[2048,2,1280]{2,1,0:T(2,128)(2,1)S(1)} %bitcast.77, f32[512,2048]{1,0:T(8,128)S(1)} %get-tuple-element.75, f32[2048]{0:T(1024)S(1)} %copy-done.23, f32[512]{0:T(512)S(1)} %add_rsqrt_fusion.2), kind=kOutput, calls=%fused_computation | convolution fusion | flops 5371854848 | bytes 19933184 | tf_op jit(solution)/shard_map/rd,dgf->rgf/dot_general | solution.py:414
  101.1 0.8 fusion.3
  101.9 0.5 copy-done.8
  102.4 0.8 convolution_convert_fusion.2
  103.3 0.6 collective-permute-start.19
  103.9 0.8 convolution_convert_fusion.1
  104.7 0.8 fusion.8
  105.6 0.2 add_convert_fusion.1
  105.8 0.8 collective-permute-start.21
  106.5 0.2 collective-permute-start.20
  106.7 0.9 pad_maximum_fusion
  107.6 0.8 fusion.9
  108.5 11.7 %collective-permute-done.21 = bf16[512,512]{1,0:T(8,128)(2,1)S(1)} collective-permute-done((bf16[512,512]{1,0:T(8,128)(2,1)S(1)}, bf16[512,512]{1,0:T(8,128)(2,1)S(1)}, u32[]{:S(2)}, u32[]{:S(2)}) %collective-permute-start.21) | collective-permute-done | bytes 524320 | tf_op jit(solution)/shard_map/ppermute | solution.py:333
  120.2 1.1 add_convert_fusion
  (72 shorter events, 0.2 us)
Async XLA Ops:
  0.6 31.5 %copy-start = (bf16[2048,640]{1,0:T(8,128)(2,1)S(1)}, bf16[2048,640]{1,0:T(8,128)(2,1)}, u32[]{:S(2)}) copy-start(bf16[2048,640]{1,0:T(8,128)(2,1)} %param.21) | copy-start | bytes 7864324
  0.6 19.2 %collective-permute-start.1 = (bf16[512,512]{1,0:T(8,128)(2,1)}, bf16[512,512]{1,0:T(8,128)(2,1)S(1)}, u32[]{:S(2)}, u32[]{:S(2)}) collective-permute-start(bf16[512,512]{1,0:T(8,128)(2,1)} %own_ref.1), channel_id=1, source_target_pairs={{0,2},{1,3},{2,0},{3,1},{4,6},{5,7},{6,4},{7,5},{8,10},{9,11},{10,... | collective-permute-start | bytes 1572872 | tf_op jit(solution)/shard_map/ppermute | solution.py:333
  4.8 15.1 %copy-start.10 = (bf16[2,320,384]{2,1,0:T(8,128)(2,1)}, bf16[2,320,384]{2,1,0:T(8,128)(2,1)S(1)}, u32[]{:S(2)}) copy-start(bf16[2,320,384]{2,1,0:T(8,128)(2,1)S(1)} %dynamic-slice_bitcast_fusion.refs_0_) | copy-start | bytes 1474564
  4.8 12.8 %collective-permute-start.3 = (bf16[2,320,384]{2,1,0:T(8,128)(2,1)S(1)}, bf16[2,320,384]{2,1,0:T(8,128)(2,1)S(1)}, u32[]{:S(2)}, u32[]{:S(2)}) collective-permute-start(bf16[2,320,384]{2,1,0:T(8,128)(2,1)S(1)} %dynamic-slice_bitcast_fusion.refs_0_), channel_id=1, source_target_pairs={{0,16},{4,20},{16,24},{20,28},{24,8},{28,12},{8,0},{12,4},{1,17},{... | collective-permute-start | bytes 1474568 | tf_op jit(solution)/shard_map/ppermute | solution.py:351
  7.4 12.4 %collective-permute-start.2 = (bf16[2,320,384]{2,1,0:T(8,128)(2,1)S(1)}, bf16[2,320,384]{2,1,0:T(8,128)(2,1)S(1)}, u32[]{:S(2)}, u32[]{:S(2)}) collective-permute-start(bf16[2,320,384]{2,1,0:T(8,128)(2,1)S(1)} %dynamic-slice_bitcast_fusion.refs_0_), channel_id=1, source_target_pairs={{0,4},{4,0},{8,12},{12,8},{16,20},{20,16},{24,28},{28,24},{1,5},{5... | collective-permute-start | bytes 1474568 | tf_op jit(solution)/shard_map/ppermute | solution.py:354
  8.9 15.5 %collective-permute-start = (bf16[512,512]{1,0:T(8,128)(2,1)}, bf16[512,512]{1,0:T(8,128)(2,1)}, u32[]{:S(2)}, u32[]{:S(2)}) collective-permute-start(bf16[512,512]{1,0:T(8,128)(2,1)} %own_ref.1), channel_id=1, source_target_pairs={{0,1},{1,0},{2,3},{3,2},{4,5},{5,4},{6,7},{7,6},{8,9},{9,8},{10,11... | collective-permute-start | bytes 1572872 | tf_op jit(solution)/shard_map/ppermute | solution.py:336
  17.6 2.2 %copy-start.18 = (bf16[2,320,384]{2,1,0:T(8,128)(2,1)}, bf16[2,320,384]{2,1,0:T(8,128)(2,1)S(1)}, u32[]{:S(2)}) copy-start(bf16[2,320,384]{2,1,0:T(8,128)(2,1)S(1)} %collective-permute-done.3.refs_2_) | copy-start | bytes 1474564
  19.8 0.8 copy-start.19
  20.6 3.8 %copy-start.9 = (bf16[512,512]{1,0:T(8,128)(2,1)}, bf16[512,512]{1,0:T(8,128)(2,1)S(1)}, u32[]{:S(2)}) copy-start(bf16[512,512]{1,0:T(8,128)(2,1)S(1)} %collective-permute-done.1.chip_ref) | copy-start | bytes 1572868
  20.6 3.8 %collective-permute-start.4 = (bf16[512,512]{1,0:T(8,128)(2,1)S(1)}, bf16[512,512]{1,0:T(8,128)(2,1)}, u32[]{:S(2)}, u32[]{:S(2)}) collective-permute-start(bf16[512,512]{1,0:T(8,128)(2,1)S(1)} %collective-permute-done.1.chip_ref), channel_id=1, source_target_pairs={{0,1},{1,0},{2,3},{3,2},{4,5},{5,4},{6,7},{7,6},{8,9},{9,8},{10,11... | collective-permute-start | bytes 1572872 | tf_op jit(solution)/shard_map/ppermute | solution.py:336
  20.6 13.9 %collective-permute-start.5 = (bf16[2,320,384]{2,1,0:T(8,128)(2,1)}, bf16[2,320,384]{2,1,0:T(8,128)(2,1)}, u32[]{:S(2)}, u32[]{:S(2)}) collective-permute-start(bf16[2,320,384]{2,1,0:T(8,128)(2,1)} %copy-done.18), channel_id=1, source_target_pairs={{0,16},{4,20},{16,24},{20,28},{24,8},{28,12},{8,0},{12,4},{1,17},{... | collective-permute-start | bytes 1474568 | tf_op jit(solution)/shard_map/ppermute | solution.py:351
  22.2 29.1 %collective-permute-start.8 = (bf16[2,320,384]{2,1,0:T(8,128)(2,1)}, bf16[2,320,384]{2,1,0:T(8,128)(2,1)}, u32[]{:S(2)}, u32[]{:S(2)}) collective-permute-start(bf16[2,320,384]{2,1,0:T(8,128)(2,1)} %copy-done.18), channel_id=1, source_target_pairs={{0,4},{4,0},{8,12},{12,8},{16,20},{20,16},{24,28},{28,24},{1,5},{5... | collective-permute-start | bytes 1474568 | tf_op jit(solution)/shard_map/ppermute | solution.py:354
  23.7 50.7 %collective-permute-start.16 = (bf16[320,2048]{1,0:T(8,128)(2,1)}, bf16[320,2048]{1,0:T(8,128)(2,1)}, u32[]{:S(2)}, u32[]{:S(2)}) collective-permute-start(bf16[320,2048]{1,0:T(8,128)(2,1)} %param.24), channel_id=1, source_target_pairs={{0,2},{1,3},{2,0},{3,1},{4,6},{5,7},{6,4},{7,5},{8,10},{9,11},{10,... | collective-permute-start | bytes 3932168 | tf_op jit(solution)/shard_map/ppermute | solution.py:333
  29.2 3.0 %copy-start.17 = (bf16[512,2048]{1,0:T(8,128)(2,1)S(1)}, bf16[512,2048]{1,0:T(8,128)(2,1)}, u32[]{:S(2)}) copy-start(bf16[512,2048]{1,0:T(8,128)(2,1)} %get-tuple-element.36) | copy-start | bytes 6291460
  32.2 6.5 %copy-start.16 = (f32[64]{0:T(128)S(1)}, f32[64]{0:T(128)}, u32[]{:S(2)}) copy-start(f32[64]{0:T(128)} %param.22) | copy-start | bytes 772
  34.6 4.6 %copy-start.15 = (f32[64]{0:T(128)S(1)}, f32[64]{0:T(128)}, u32[]{:S(2)}) copy-start(f32[64]{0:T(128)} %param.23) | copy-start | bytes 772
  34.6 13.1 %collective-permute-start.6 = (bf16[2,320,384]{2,1,0:T(8,128)(2,1)}, bf16[2,320,384]{2,1,0:T(8,128)(2,1)S(1)}, u32[]{:S(2)}, u32[]{:S(2)}) collective-permute-start(bf16[2,320,384]{2,1,0:T(8,128)(2,1)} %collective-permute-done.5.refs_4_), channel_id=1, source_target_pairs={{0,16},{4,20},{16,24},{20,28},{24,8},{28,12},{8,0},{12,4},{1,17},{... | collective-permute-start | bytes 1474568 | tf_op jit(solution)/shard_map/ppermute | solution.py:351
  37.1 12.7 %collective-permute-start.9 = (bf16[2,320,384]{2,1,0:T(8,128)(2,1)}, bf16[2,320,384]{2,1,0:T(8,128)(2,1)S(1)}, u32[]{:S(2)}, u32[]{:S(2)}) collective-permute-start(bf16[2,320,384]{2,1,0:T(8,128)(2,1)} %collective-permute-done.5.refs_4_), channel_id=1, source_target_pairs={{0,4},{4,0},{8,12},{12,8},{16,20},{20,16},{24,28},{28,24},{1,5},{5... | collective-permute-start | bytes 1474568 | tf_op jit(solution)/shard_map/ppermute | solution.py:354
  39.1 1.8 %copy-start.12 = (bf16[512,5,64]{0,2,1:T(8,128)(2,1)}, bf16[512,5,64]{0,2,1:T(8,128)(2,1)S(1)}, u32[]{:S(2)}) copy-start(bf16[512,5,64]{0,2,1:T(8,128)(2,1)S(1)} %maximum_multiply_fusion) | copy-start | bytes 983044
  39.1 18.5 %collective-permute-start.7 = (bf16[320,512]{1,0:T(8,128)(2,1)S(1)}, bf16[320,512]{1,0:T(8,128)(2,1)S(1)}, u32[]{:S(2)}, u32[]{:S(2)}) collective-permute-start(bf16[320,512]{1,0:T(8,128)(2,1)S(1)} %bitcast.71), channel_id=1, source_target_pairs={{0,1},{1,0},{2,3},{3,2},{4,5},{5,4},{6,7},{7,6},{8,9},{9,8},{10,11... | collective-permute-start | bytes 983048 | tf_op jit(solution)/shard_map/ppermute | solution.py:336
  47.7 10.0 %copy-start.13 = (bf16[2,320,384]{2,1,0:T(8,128)(2,1)}, bf16[2,320,384]{2,1,0:T(8,128)(2,1)S(1)}, u32[]{:S(2)}) copy-start(bf16[2,320,384]{2,1,0:T(8,128)(2,1)S(1)} %collective-permute-done.6.refs_6_) | copy-start | bytes 1474564
  47.7 35.1 %collective-permute-start.14 = (bf16[320,2048]{1,0:T(8,128)(2,1)}, bf16[320,2048]{1,0:T(8,128)(2,1)}, u32[]{:S(2)}, u32[]{:S(2)}) collective-permute-start(bf16[320,2048]{1,0:T(8,128)(2,1)} %param.24), channel_id=1, source_target_pairs={{0,1},{1,0},{2,3},{3,2},{4,5},{5,4},{6,7},{7,6},{8,9},{9,8},{10,11... | collective-permute-start | bytes 3932168 | tf_op jit(solution)/shard_map/ppermute | solution.py:336
  49.8 7.9 %copy-start.14 = (bf16[2,320,384]{2,1,0:T(8,128)(2,1)}, bf16[2,320,384]{2,1,0:T(8,128)(2,1)S(1)}, u32[]{:S(2)}) copy-start(bf16[2,320,384]{2,1,0:T(8,128)(2,1)S(1)} %collective-permute-done.9.refs_5_) | copy-start | bytes 1474564
  49.8 7.9 %collective-permute-start.10 = (bf16[1,320,384]{2,1,0:T(8,128)(2,1)S(1)}, bf16[1,320,384]{2,1,0:T(8,128)(2,1)S(1)}, u32[]{:S(2)}, u32[]{:S(2)}) collective-permute-start(bf16[1,320,384]{2,1,0:T(8,128)(2,1)S(1)} %slice.40), channel_id=1, source_target_pairs={{0,4},{4,0},{8,12},{12,8},{16,20},{20,16},{24,28},{28,24},{1,5},{5... | collective-permute-start | bytes 737288 | tf_op jit(solution)/shard_map/ppermute | solution.py:354
  51.3 7.0 %collective-permute-start.11 = (bf16[1,320,384]{2,1,0:T(8,128)(2,1)S(1)}, bf16[1,320,384]{2,1,0:T(8,128)(2,1)S(1)}, u32[]{:S(2)}, u32[]{:S(2)}) collective-permute-start(bf16[1,320,384]{2,1,0:T(8,128)(2,1)S(1)} %slice.48), channel_id=1, source_target_pairs={{0,16},{4,20},{16,24},{20,28},{24,8},{28,12},{8,0},{12,4},{1,17},{... | collective-permute-start | bytes 737288 | tf_op jit(solution)/shard_map/ppermute | solution.py:351
  57.7 0.7 copy-start.20
  57.7 0.8 copy-start.21
  58.3 0.7 copy-start.22
  74.3 2.0 %collective-permute-start.12 = (bf16[352,512]{1,0:T(8,128)(2,1)}, bf16[352,512]{1,0:T(8,128)(2,1)S(1)}, u32[]{:S(2)}, u32[]{:S(2)}) collective-permute-start(bf16[352,512]{1,0:T(8,128)(2,1)} %get-tuple-element.50), channel_id=1, source_target_pairs={{0,1},{1,0},{2,3},{3,2},{4,5},{5,4},{6,7},{7,6},{8,9},{9,8},{10,11... | collective-permute-start | bytes 1081352 | tf_op jit(solution)/shard_map/ppermute | solution.py:336
  74.4 17.8 %collective-permute-start.18 = (bf16[320,2048]{1,0:T(8,128)(2,1)}, bf16[320,2048]{1,0:T(8,128)(2,1)}, u32[]{:S(2)}, u32[]{:S(2)}) collective-permute-start(bf16[320,2048]{1,0:T(8,128)(2,1)} %collective-permute-done.16), channel_id=1, source_target_pairs={{0,1},{1,0},{2,3},{3,2},{4,5},{5,4},{6,7},{7,6},{8,9},{9,8},{10,11... | collective-permute-start | bytes 3932168 | tf_op jit(solution)/shard_map/ppermute | solution.py:336
  76.3 0.7 copy-start.11
  79.2 3.6 %copy-start.2 = (bf16[512,2048]{1,0:T(8,128)(2,1)S(1)}, bf16[512,2048]{1,0:T(8,128)(2,1)}, u32[]{:S(2)}) copy-start(bf16[512,2048]{1,0:T(8,128)(2,1)} %get-tuple-element.35) | copy-start | bytes 6291460
  79.2 3.5 %collective-permute-start.13 = (bf16[320,512]{1,0:T(8,128)(2,1)}, bf16[320,512]{1,0:T(8,128)(2,1)S(1)}, u32[]{:S(2)}, u32[]{:S(2)}) collective-permute-start(bf16[320,512]{1,0:T(8,128)(2,1)} %merge.1), channel_id=1, source_target_pairs={{0,1},{1,0},{2,3},{3,2},{4,5},{5,4},{6,7},{7,6},{8,9},{9,8},{10,11... | collective-permute-start | bytes 983048 | tf_op jit(solution)/shard_map/ppermute | solution.py:336
  79.3 10.2 %collective-permute-start.15 = (bf16[320,512]{1,0:T(8,128)(2,1)}, bf16[320,512]{1,0:T(8,128)(2,1)S(1)}, u32[]{:S(2)}, u32[]{:S(2)}) collective-permute-start(bf16[320,512]{1,0:T(8,128)(2,1)} %merge.1), channel_id=1, source_target_pairs={{0,2},{1,3},{2,0},{3,1},{4,6},{5,7},{6,4},{7,5},{8,10},{9,11},{10,... | collective-permute-start | bytes 983048 | tf_op jit(solution)/shard_map/ppermute | solution.py:333
  82.8 12.7 %slice-start = ((s8[10485760]{0:T(1024)(128)(4,1)}), s8[4194304]{0:T(1024)(128)(4,1)S(1)}, s32[]{:S(2)}) async-start(s8[10485760]{0:T(1024)(128)(4,1)} %bitcast.76), calls=%async_computation | async-start | bytes 8388608
  82.8 12.7 %slice-start.1 = ((s8[10485760]{0:T(1024)(128)(4,1)}), s8[4194304]{0:T(1024)(128)(4,1)S(1)}, s32[]{:S(2)}) async-start(s8[10485760]{0:T(1024)(128)(4,1)} %bitcast.76), calls=%async_computation.1 | async-start | bytes 8388608
  89.5 2.6 %collective-permute-start.17 = (bf16[320,512]{1,0:T(8,128)(2,1)S(1)}, bf16[320,512]{1,0:T(8,128)(2,1)S(1)}, u32[]{:S(2)}, u32[]{:S(2)}) collective-permute-start(bf16[320,512]{1,0:T(8,128)(2,1)S(1)} %collective-permute-done.15), channel_id=1, source_target_pairs={{0,1},{1,0},{2,3},{3,2},{4,5},{5,4},{6,7},{7,6},{8,9},{9,8},{10,11... | collective-permute-start | bytes 983048 | tf_op jit(solution)/shard_map/ppermute | solution.py:336
  92.1 3.3 %slice-start.2 = ((s8[10485760]{0:T(1024)(128)(4,1)}), s8[2097152]{0:T(1024)(128)(4,1)S(1)}, s32[]{:S(2)}) async-start(s8[10485760]{0:T(1024)(128)(4,1)} %bitcast.76), calls=%async_computation.2 | async-start | bytes 4194304
  92.1 3.3 %copy-start.23 = (f32[2048]{0:T(1024)S(1)}, f32[2048]{0:T(1024)}, u32[]{:S(2)}) copy-start(f32[2048]{0:T(1024)} %param.25) | copy-start | bytes 24580
  101.1 1.3 %copy-start.8 = (bf16[1280,512]{1,0:T(8,128)(2,1)S(1)}, bf16[1280,512]{1,0:T(8,128)(2,1)}, u32[]{:S(2)}) copy-start(bf16[1280,512]{1,0:T(8,128)(2,1)} %get-tuple-element.58) | copy-start | bytes 3932164
  102.4 1.4 %copy-start.7 = (bf16[1280,512]{1,0:T(8,128)(2,1)S(1)}, bf16[1280,512]{1,0:T(8,128)(2,1)}, u32[]{:S(2)}) copy-start(bf16[1280,512]{1,0:T(8,128)(2,1)} %get-tuple-element.59) | copy-start | bytes 3932164
  103.3 1.4 %copy-start.6 = (bf16[1280,512]{1,0:T(8,128)(2,1)S(1)}, bf16[1280,512]{1,0:T(8,128)(2,1)}, u32[]{:S(2)}) copy-start(bf16[1280,512]{1,0:T(8,128)(2,1)} %get-tuple-element.57) | copy-start | bytes 3932164
  103.3 2.3 %collective-permute-start.19 = (bf16[512,512]{1,0:T(8,128)(2,1)S(1)}, bf16[512,512]{1,0:T(8,128)(2,1)S(1)}, u32[]{:S(2)}, u32[]{:S(2)}) collective-permute-start(bf16[512,512]{1,0:T(8,128)(2,1)S(1)} %convolution_convert_fusion.2), channel_id=1, source_target_pairs={{0,1},{1,0},{2,3},{3,2},{4,5},{5,4},{6,7},{7,6},{8,9},{9,8},{10,11... | collective-permute-start | bytes 1572872 | tf_op jit(solution)/shard_map/ppermute | solution.py:336
  105.6 1.2 copy-start.3
  105.6 1.2 copy-start.4
  105.6 2.1 %copy-start.5 = (bf16[1280,512]{1,0:T(8,128)(2,1)S(1)}, bf16[1280,512]{1,0:T(8,128)(2,1)}, u32[]{:S(2)}) copy-start(bf16[1280,512]{1,0:T(8,128)(2,1)} %get-tuple-element.62) | copy-start | bytes 3932164
  105.8 14.4 %collective-permute-start.21 = (bf16[512,512]{1,0:T(8,128)(2,1)S(1)}, bf16[512,512]{1,0:T(8,128)(2,1)S(1)}, u32[]{:S(2)}, u32[]{:S(2)}) collective-permute-start(bf16[512,512]{1,0:T(8,128)(2,1)S(1)} %add_convert_fusion.1), channel_id=1, source_target_pairs={{0,2},{1,3},{2,0},{3,1},{4,6},{5,7},{6,4},{7,5},{8,10},{9,11},{10,... | collective-permute-start | bytes 1572872 | tf_op jit(solution)/shard_map/ppermute | solution.py:333
  106.5 13.6 %collective-permute-start.20 = (bf16[512,512]{1,0:T(8,128)(2,1)S(1)}, bf16[512,512]{1,0:T(8,128)(2,1)S(1)}, u32[]{:S(2)}, u32[]{:S(2)}) collective-permute-start(bf16[512,512]{1,0:T(8,128)(2,1)S(1)} %convolution_convert_fusion.1), channel_id=1, source_target_pairs={{0,1},{1,0},{2,3},{3,2},{4,5},{5,4},{6,7},{7,6},{8,9},{9,8},{10,11... | collective-permute-start | bytes 1572872 | tf_op jit(solution)/shard_map/ppermute | solution.py:336
  107.6 13.6 %copy-start.1 = (bf16[2048,640]{1,0:T(8,128)(2,1)S(1)}, bf16[2048,640]{1,0:T(8,128)(2,1)}, u32[]{:S(2)}) copy-start(bf16[2048,640]{1,0:T(8,128)(2,1)} %param.21) | copy-start | bytes 7864324

commit v8 on v7

--- a/solution.py
+++ b/solution.py
@@ -176,9 +176,9 @@
     skipped = inside // block
     pairs = n_first + parts - skipped
 
-    def place(task):
+    def place(task, head=None):
         pair = task // per
-        head = task % per
+        head = task % per if head is None else head
         second = (pair >= n_first).astype(jnp.int32)
         part = jnp.where(second == 1, pair - n_first + skipped, pair)
         cols = pl.ds(pl.multiple_of(part * block, block), block)
@@ -213,7 +213,28 @@
             o_buf[q_band, cols] = jnp.where(mine, blended * (1.0 / total), o_buf[q_band, cols])
             l_buf[head, :, cols] = jnp.where(mine, peak + jnp.log(total), l_buf[head, :, cols])
 
-    step(None, 0, None, None, s_a, m_a)
+    def group(pair, outside):
+        for head in range(per):
+            second, part, cols, q_band, k_band, _ = place(pair * per + head, head)
+            query = q_buf[q_band, cols]
+            total = blended = None
+            for start in range(0, keys, chunk):
+                span = pl.ds(start, chunk)
+                weights = jnp.exp(tn_dot(kv[second, 0, k_band, span], query))
+                folded = fold(weights, jnp.sum)
+                total = folded if total is None else total + folded
+                out = nn_dot(kv[second, 1, k_band, span], weights.astype(jnp.bfloat16))
+                blended = out if blended is None else blended + out
+            total = jnp.sum(total, axis=0, keepdims=True)
+            lane = lax.broadcasted_iota(jnp.int32, (1, block), 1) + part * block
+            mine = (lane >= first_len).astype(jnp.int32) == second
+            o_buf[q_band, cols] = jnp.where(mine, blended * (1.0 / total), o_buf[q_band, cols])
+            l_buf[head, :, cols] = jnp.where(mine, jnp.log(total), l_buf[head, :, cols])
+            inside_range = (total > 1e-20) & (total < 1e20)
+            outside = jnp.maximum(outside, jnp.where(inside_range | ~mine, 0.0, 1.0))
+        return outside
+
+    outside = lax.fori_loop(0, pairs, group, jnp.zeros((1, block), jnp.float32))
 
     def two(index, carry):
         task = 2 * index
@@ -221,7 +242,11 @@
         step(task + 1, jnp.minimum(task + 2, pairs * per - 1), s_b, m_b, s_a, m_a)
         return carry
 
-    lax.fori_loop(0, pairs * heads, two, 0)
+    @pl.when(jnp.max(outside) > 0.0)
+    def _():
+        step(None, 0, None, None, s_a, m_a)
+        lax.fori_loop(0, pairs * heads, two, 0)
+
     own_out[...] = o_buf[:columns]
     other_out[:columns] = o_buf[columns:].astype(jnp.bfloat16)
     for head in range(heads):

time: 122 us -> 131 us (1.074)
  Pallas kernels: 27.4 us -> 36.9 us
    pallas_call x1, Pallas kernels: 15.3 us -> 24.8 us  [prefix_attend(): pl.pallas_call(functools.partial(prefix_kernel, block, 256, len(units) -...]
  transfers between devices with their start and end apart: 22 -> 22, of which waited for: 9 -> 9; matrix products, arithmetic and copies ran while one was open for 21% -> 19% of each run, Pallas kernels for 23% -> 28%
where the time goes in v8:
time: 131 us
  Pallas kernels  36.9 us (28%)
  waiting for transfers between devices  31.9 us (24%)
  matrix products  24.9 us (19%)
  starting transfers between devices  20.9 us (16%)
  local copies, waits for them, and re-layouts  9.72 us (7%)
  other arithmetic  5.41 us (4%)
    pallas_call x1, Pallas kernels, prefix_attend(): pl.pallas_call(functools.partial(prefix_kernel, block, 256, len(units) -...  24.8 us
    ppermute x4, waiting for transfers between devices, across_chip(): return lax.ppermute(value, 'tp', [(i, i ^ 2) for i in range(4)])  15.6 us
    dot_general x4, matrix products, tn_dot(): lax.dot_general(lhs, rhs, (((0,), (0,)), ((), ())), preferred_element_typ...  11.4 us
    ppermute x4, waiting for transfers between devices, ring(): lax.ppermute(value, 'req', [(2 * a + b, 2 * c + b) for a, c in steps for...  10.6 us
    ppermute x4, starting transfers between devices, ring(): lax.ppermute(value, 'req', [(2 * a + b, 2 * c + b) for a, c in steps for...  8.04 us
    ppermute x4, starting transfers between devices, aside(): return lax.ppermute(value, 'req', [(r, r ^ 1) for r in range(n_req)])  6.08 us
    dot_general x1, matrix products, local(): jnp.einsum('rd,dgf->rgf', normed_ffn, w_gate_up, preferred_element_type=j...  5.64 us
    ppermute x4, starting transfers between devices, across_chip(): return lax.ppermute(value, 'tp', [(i, i ^ 2) for i in range(4)])  5.19 us
  transfers between devices with their start and end apart: 22, of which 9 were waited for; matrix products, arithmetic and copies ran while one was open for 19% of the time, Pallas kernels for 28%

profile of v8, /device:TPU:0, one launch (start us, length us, event | category | flops | bytes accessed | tf_op | source)
XLA Modules:
  0.0 130.8 jit_solution(3638722354568981695)
XLA Ops:
  0.6 3.0 %collective-permute-start.1 = (bf16[512,512]{1,0:T(8,128)(2,1)}, bf16[512,512]{1,0:T(8,128)(2,1)S(1)}, u32[]{:S(2)}, u32[]{:S(2)}) collective-permute-start(bf16[512,512]{1,0:T(8,128)(2,1)} %own_ref.1), channel_id=1, source_target_pairs={{0,2},{1,3},{2,0},{3,1},{4,6},{5,7},{6,4},{7,5},{8,10},{9,11},{10,... | collective-permute-start | bytes 1572872 | tf_op jit(solution)/shard_map/ppermute | solution.py:358
  3.7 1.1 dynamic-slice_bitcast_fusion.refs_0_
  4.8 2.6 %collective-permute-start.3 = (bf16[2,320,384]{2,1,0:T(8,128)(2,1)S(1)}, bf16[2,320,384]{2,1,0:T(8,128)(2,1)S(1)}, u32[]{:S(2)}, u32[]{:S(2)}) collective-permute-start(bf16[2,320,384]{2,1,0:T(8,128)(2,1)S(1)} %dynamic-slice_bitcast_fusion.refs_0_), channel_id=1, source_target_pairs={{0,16},{4,20},{16,24},{20,28},{24,8},{28,12},{8,0},{12,4},{1,17},{... | collective-permute-start | bytes 1474568 | tf_op jit(solution)/shard_map/ppermute | solution.py:376
  7.4 1.5 %collective-permute-start.2 = (bf16[2,320,384]{2,1,0:T(8,128)(2,1)S(1)}, bf16[2,320,384]{2,1,0:T(8,128)(2,1)S(1)}, u32[]{:S(2)}, u32[]{:S(2)}) collective-permute-start(bf16[2,320,384]{2,1,0:T(8,128)(2,1)S(1)} %dynamic-slice_bitcast_fusion.refs_0_), channel_id=1, source_target_pairs={{0,4},{4,0},{8,12},{12,8},{16,20},{20,16},{24,28},{28,24},{1,5},{5... | collective-permute-start | bytes 1474568 | tf_op jit(solution)/shard_map/ppermute | solution.py:379
  8.9 0.7 add_convert_fusion.3
  9.6 0.3 multiply_sine_fusion
  9.9 7.7 %collective-permute-done.3.refs_2_ = bf16[2,320,384]{2,1,0:T(8,128)(2,1)S(1)} collective-permute-done((bf16[2,320,384]{2,1,0:T(8,128)(2,1)S(1)}, bf16[2,320,384]{2,1,0:T(8,128)(2,1)S(1)}, u32[]{:S(2)}, u32[]{:S(2)}) %collective-permute-start.3) | collective-permute-done | bytes 491552 | tf_op jit(solution)/shard_map/ppermute | solution.py:376
  17.6 2.2 %collective-permute-done.2.refs_1_ = bf16[2,320,384]{2,1,0:T(8,128)(2,1)S(1)} collective-permute-done((bf16[2,320,384]{2,1,0:T(8,128)(2,1)S(1)}, bf16[2,320,384]{2,1,0:T(8,128)(2,1)S(1)}, u32[]{:S(2)}, u32[]{:S(2)}) %collective-permute-start.2) | collective-permute-done | bytes 491552 | tf_op jit(solution)/shard_map/ppermute | solution.py:379
  19.8 0.8 copy-done.19
  20.6 1.6 %collective-permute-start.5 = (bf16[2,320,384]{2,1,0:T(8,128)(2,1)}, bf16[2,320,384]{2,1,0:T(8,128)(2,1)}, u32[]{:S(2)}, u32[]{:S(2)}) collective-permute-start(bf16[2,320,384]{2,1,0:T(8,128)(2,1)} %copy-done.18), channel_id=1, source_target_pairs={{0,16},{4,20},{16,24},{20,28},{24,8},{28,12},{8,0},{12,4},{1,17},{... | collective-permute-start | bytes 1474568 | tf_op jit(solution)/shard_map/ppermute | solution.py:376
  22.2 1.5 %collective-permute-start.8 = (bf16[2,320,384]{2,1,0:T(8,128)(2,1)}, bf16[2,320,384]{2,1,0:T(8,128)(2,1)}, u32[]{:S(2)}, u32[]{:S(2)}) collective-permute-start(bf16[2,320,384]{2,1,0:T(8,128)(2,1)} %copy-done.18), channel_id=1, source_target_pairs={{0,4},{4,0},{8,12},{12,8},{16,20},{20,16},{24,28},{28,24},{1,5},{5... | collective-permute-start | bytes 1474568 | tf_op jit(solution)/shard_map/ppermute | solution.py:379
  23.7 0.7 collective-permute-start.16
  24.4 4.7 %gather_norm.1 = (bf16[512,2048]{1,0:T(8,128)(2,1)}, bf16[512,2048]{1,0:T(8,128)(2,1)}) custom-call(s32[1]{0:T(128)} %bitcast.rank_ref, bf16[512,512]{1,0:T(8,128)(2,1)} %own_ref.1, bf16[512,512]{1,0:T(8,128)(2,1)} %collective-permute-done.core_ref, bf16[512,512]{1,0:T(8,128)(2,1)} %copy-done.9, bf16[512,512]{1,0:T(8,128)(2,1)} %collective-permute-done.4.both_ref, ...), custom_call_target="tpu_custom_call" | custom-call | tf_op jit(solution)/shard_map/gather_norm/pallas_call | solution.py:73
  29.2 3.0 %fusion.12 = f32[512,320]{0,1:T(8,128)S(1)} fusion(bf16[512,2048]{1,0:T(8,128)(2,1)} %get-tuple-element.36, bf16[2048,320]{0,1:T(8,128)(2,1)} %param.20), kind=kOutput, calls=%fused_computation.48 | convolution fusion | flops 671088640 | bytes 4063232 | tf_op jit(solution)/shard_map/dot_general | solution.py:394
  32.2 1.6 %fusion.13 = f32[512,640]{0,1:T(8,128)S(1)} fusion(bf16[512,2048]{1,0:T(8,128)(2,1)S(1)} %copy-done.17, bf16[2048,640]{1,0:T(8,128)(2,1)S(1)} %copy-done), kind=kOutput, calls=%fused_computation.49 | convolution fusion | flops 1342177280 | bytes 6029312 | tf_op jit(solution)/shard_map/dot_general | solution.py:397
  33.8 0.8 collective-permute-done.5.refs_4_
  34.6 2.5 %collective-permute-start.6 = (bf16[2,320,384]{2,1,0:T(8,128)(2,1)}, bf16[2,320,384]{2,1,0:T(8,128)(2,1)S(1)}, u32[]{:S(2)}, u32[]{:S(2)}) collective-permute-start(bf16[2,320,384]{2,1,0:T(8,128)(2,1)} %collective-permute-done.5.refs_4_), channel_id=1, source_target_pairs={{0,16},{4,20},{16,24},{20,28},{24,8},{28,12},{8,0},{12,4},{1,17},{... | collective-permute-start | bytes 1474568 | tf_op jit(solution)/shard_map/ppermute | solution.py:376
  37.1 1.5 %collective-permute-start.9 = (bf16[2,320,384]{2,1,0:T(8,128)(2,1)}, bf16[2,320,384]{2,1,0:T(8,128)(2,1)S(1)}, u32[]{:S(2)}, u32[]{:S(2)}) collective-permute-start(bf16[2,320,384]{2,1,0:T(8,128)(2,1)} %collective-permute-done.5.refs_4_), channel_id=1, source_target_pairs={{0,4},{4,0},{8,12},{12,8},{16,20},{20,16},{24,28},{28,24},{1,5},{5... | collective-permute-start | bytes 1474568 | tf_op jit(solution)/shard_map/ppermute | solution.py:379
  38.6 0.1 multiply_reduce_fusion.1
  38.7 0.2 fusion.10
  39.0 0.1 subtract_convert_fusion
  39.1 0.1 maximum_multiply_fusion
  39.1 0.1 collective-permute-start.7
  39.2 0.1 fusion.11
  39.3 0.8 slice.70
  40.1 0.1 multiply_subtract_fusion
  40.2 0.8 maximum_convert_fusion
  41.0 5.2 %suffix_attend.1 = (f32[320,512]{1,0:T(8,128)}, f32[8,512]{1,0:T(8,128)}) custom-call(s32[1,2]{1,0:T(1,128)} %lengths_ref.1, bf16[320,512]{1,0:T(8,128)(2,1)} %bitcast.72, bf16[320,512]{1,0:T(8,128)(2,1)} %bitcast.69, bf16[320,512]{1,0:T(8,128)(2,1)} %bitcast.67), custom_call_target="tpu_custom_call" | custom-call | flops 335544320 | bytes 3145728 | tf_op jit(solution)/shard_map/suffix_attend/pallas_call | solution.py:115
  46.1 1.6 %collective-permute-done.6.refs_6_ = bf16[2,320,384]{2,1,0:T(8,128)(2,1)S(1)} collective-permute-done((bf16[2,320,384]{2,1,0:T(8,128)(2,1)}, bf16[2,320,384]{2,1,0:T(8,128)(2,1)S(1)}, u32[]{:S(2)}, u32[]{:S(2)}) %collective-permute-start.6) | collective-permute-done | bytes 491552 | tf_op jit(solution)/shard_map/ppermute | solution.py:376
  47.7 2.1 %collective-permute-done.9.refs_5_ = bf16[2,320,384]{2,1,0:T(8,128)(2,1)S(1)} collective-permute-done((bf16[2,320,384]{2,1,0:T(8,128)(2,1)}, bf16[2,320,384]{2,1,0:T(8,128)(2,1)S(1)}, u32[]{:S(2)}, u32[]{:S(2)}) %collective-permute-start.9) | collective-permute-done | bytes 491552 | tf_op jit(solution)/shard_map/ppermute | solution.py:379
  49.8 1.5 %collective-permute-start.10 = (bf16[1,320,384]{2,1,0:T(8,128)(2,1)S(1)}, bf16[1,320,384]{2,1,0:T(8,128)(2,1)S(1)}, u32[]{:S(2)}, u32[]{:S(2)}) collective-permute-start(bf16[1,320,384]{2,1,0:T(8,128)(2,1)S(1)} %slice.40), channel_id=1, source_target_pairs={{0,4},{4,0},{8,12},{12,8},{16,20},{20,16},{24,28},{28,24},{1,5},{5... | collective-permute-start | bytes 737288 | tf_op jit(solution)/shard_map/ppermute | solution.py:379
  51.3 1.4 %collective-permute-start.11 = (bf16[1,320,384]{2,1,0:T(8,128)(2,1)S(1)}, bf16[1,320,384]{2,1,0:T(8,128)(2,1)S(1)}, u32[]{:S(2)}, u32[]{:S(2)}) collective-permute-start(bf16[1,320,384]{2,1,0:T(8,128)(2,1)S(1)} %slice.48), channel_id=1, source_target_pairs={{0,16},{4,20},{16,24},{20,28},{24,8},{28,12},{8,0},{12,4},{1,17},{... | collective-permute-start | bytes 737288 | tf_op jit(solution)/shard_map/ppermute | solution.py:376
  52.7 5.0 %constant_dynamic-slice_fusion = (bf16[1280,512]{1,0:T(8,128)(2,1)}, bf16[1280,512]{1,0:T(8,128)(2,1)}, bf16[1280,512]{1,0:T(8,128)(2,1)}, bf16[1280,512]{1,0:T(8,128)(2,1)}) fusion(bf16[1280,2048]{1,0:T(8,128)(2,1)} %param.27, s32[]{:T(128)S(6)} %select_n.28, s32[]{:T(128)S(6)} %select_n.27, s32[]{:T(128)S(6)} %select_n.26, s32[]{:T(128)S(6)} %select_n.25), kind=kLoop, calls=%fused_computation.43 | loop fusion | bytes 10485776 | tf_op jit(solution)/shard_map/dynamic_slice | solution.py:425
  57.7 0.6 collective-permute-done.11.refs_8_
  58.3 0.1 copy-done.20
  58.4 0.1 copy-done.21
  58.5 0.5 copy-done.22
  59.0 24.8 %prefix_attend.1 = (f32[320,512]{1,0:T(8,128)}, f32[8,512]{1,0:T(8,128)}, bf16[352,512]{1,0:T(8,128)(2,1)}) custom-call(s32[8]{0:T(128)} %owners_ref.1, s32[1,2]{1,0:T(1,128)} %groups_ref.1, s32[1,2]{1,0:T(1,128)} %lengths_ref.1, s32[1]{0:T(128)} %bitcast.6.me_ref, bf16[320,512]{1,0:T(8,128)(2,1)} %bitcast.73, bf16[320,512]{1,0:T(8,128)(2,1)} %copy-done.20, ...), custom_call_target="tpu_custom_call" | custom-call | flops 2013265920 | bytes 6291456 | tf_op jit(solution)/shard_map/prefix_attend/pallas_call | solution.py:271
  83.8 0.1 collective-permute-start.12
  83.9 0.5 collective-permute-start.18
  84.4 1.4 %collective-permute-done.12.got_ref = bf16[352,512]{1,0:T(8,128)(2,1)S(1)} collective-permute-done((bf16[352,512]{1,0:T(8,128)(2,1)}, bf16[352,512]{1,0:T(8,128)(2,1)S(1)}, u32[]{:S(2)}, u32[]{:S(2)}) %collective-permute-start.12) | collective-permute-done | bytes 360480 | tf_op jit(solution)/shard_map/ppermute | solution.py:361
  85.8 0.7 copy-done.11
  86.5 2.2 %merge.1 = bf16[320,512]{1,0:T(8,128)(2,1)} custom-call(f32[320,512]{1,0:T(8,128)} %get-tuple-element.48.own_ref, f32[8,512]{1,0:T(8,128)} %get-tuple-element.49.own_lse_ref, bf16[352,512]{1,0:T(8,128)(2,1)} %copy-done.11, f32[320,512]{1,0:T(8,128)} %get-tuple-element.51.suffix_ref, f32[8,512]{1,0:T(8,128)} %get-tuple-element.52.suffix_lse_ref), custom_call_target="tpu_custom_call" | custom-call | flops 1310720 | bytes 1048576 | tf_op jit(solution)/shard_map/merge/pallas_call | solution.py:316
  88.7 0.1 collective-permute-start.13
  88.8 0.7 collective-permute-start.15
  89.5 2.7 %fusion.14 = f32[512,2048]{1,0:T(8,128)S(1)} fusion(bf16[320,512]{1,0:T(8,128)(2,1)} %merge.1, bf16[320,2048]{1,0:T(8,128)(2,1)} %param.24), kind=kOutput, calls=%fused_computation.50 | convolution fusion | flops 671088640 | bytes 5832704 | tf_op jit(solution)/shard_map/dot_general | solution.py:46
  92.3 2.8 %add_add_fusion.1 = f32[512,2048]{1,0:T(8,128)S(1)} fusion(f32[512,2048]{1,0:T(8,128)S(1)} %fusion.14, bf16[512,2048]{1,0:T(8,128)(2,1)S(1)} %copy-done.2, bf16[320,512]{1,0:T(8,128)(2,1)S(1)} %collective-permute-done.13, bf16[320,2048]{1,0:T(8,128)(2,1)} %collective-permute-done.14), kind=kOutput, calls=%fused_computation.5 | convolution fusion | flops 674234368 | bytes 12124160 | tf_op jit(solution)/shard_map/dot_general | solution.py:46
  95.1 3.9 %collective-permute-done.15 = bf16[320,512]{1,0:T(8,128)(2,1)S(1)} collective-permute-done((bf16[320,512]{1,0:T(8,128)(2,1)}, bf16[320,512]{1,0:T(8,128)(2,1)S(1)}, u32[]{:S(2)}, u32[]{:S(2)}) %collective-permute-start.15) | collective-permute-done | bytes 327712 | tf_op jit(solution)/shard_map/ppermute | solution.py:358
  99.0 2.6 %fusion.15 = f32[512,2048]{1,0:T(8,128)S(1)} fusion(bf16[320,512]{1,0:T(8,128)(2,1)S(1)} %collective-permute-done.15, bf16[320,2048]{1,0:T(8,128)(2,1)} %collective-permute-done.16), kind=kOutput, calls=%fused_computation.51 | convolution fusion | flops 671088640 | bytes 5832704 | tf_op jit(solution)/shard_map/dot_general | solution.py:46
  101.7 3.2 %multiply_reduce_fusion = (f32[512]{0:T(512)S(1)}, f32[512,2048]{1,0:T(8,128)S(1)}) fusion(bf16[320,512]{1,0:T(8,128)(2,1)S(1)} %collective-permute-done.17, bf16[320,2048]{1,0:T(8,128)(2,1)} %collective-permute-done.18, f32[512,2048]{1,0:T(8,128)S(1)} %add_add_fusion.1, f32[512,2048]{1,0:T(8,128)S(1)} %fusion.15), kind=kOutput, calls=%fused_computation.3 | convolution fusion | flops 675282432 | bytes 14223360 | tf_op jit(solution)/shard_map/dot_general | solution.py:46
  105.0 5.6 %fusion = f32[512,2,1280]{2,0,1:T(8,128)S(1)} fusion(bf16[2048,2,1280]{2,1,0:T(2,128)(2,1)S(1)} %bitcast.77, f32[512,2048]{1,0:T(8,128)S(1)} %get-tuple-element.75, f32[2048]{0:T(1024)S(1)} %copy-done.23, f32[512]{0:T(512)S(1)} %add_rsqrt_fusion.2), kind=kOutput, calls=%fused_computation | convolution fusion | flops 5371854848 | bytes 19933184 | tf_op jit(solution)/shard_map/rd,dgf->rgf/dot_general | solution.py:439
  110.6 0.8 fusion.3
  111.4 0.5 copy-done.8
  111.9 0.8 convolution_convert_fusion.2
  112.8 0.6 collective-permute-start.19
  113.4 0.8 convolution_convert_fusion.1
  114.2 0.8 fusion.8
  115.1 0.2 add_convert_fusion.1
  115.3 0.8 collective-permute-start.21
  116.0 0.2 collective-permute-start.20
  116.2 0.9 pad_maximum_fusion
  117.1 0.8 fusion.9
  118.0 11.7 %collective-permute-done.21 = bf16[512,512]{1,0:T(8,128)(2,1)S(1)} collective-permute-done((bf16[512,512]{1,0:T(8,128)(2,1)S(1)}, bf16[512,512]{1,0:T(8,128)(2,1)S(1)}, u32[]{:S(2)}, u32[]{:S(2)}) %collective-permute-start.21) | collective-permute-done | bytes 524320 | tf_op jit(solution)/shard_map/ppermute | solution.py:358
  129.6 1.1 add_convert_fusion
  (72 shorter events, 0.2 us)
Async XLA Ops:
  0.6 31.5 %copy-start = (bf16[2048,640]{1,0:T(8,128)(2,1)S(1)}, bf16[2048,640]{1,0:T(8,128)(2,1)}, u32[]{:S(2)}) copy-start(bf16[2048,640]{1,0:T(8,128)(2,1)} %param.21) | copy-start | bytes 7864324
  0.6 19.2 %collective-permute-start.1 = (bf16[512,512]{1,0:T(8,128)(2,1)}, bf16[512,512]{1,0:T(8,128)(2,1)S(1)}, u32[]{:S(2)}, u32[]{:S(2)}) collective-permute-start(bf16[512,512]{1,0:T(8,128)(2,1)} %own_ref.1), channel_id=1, source_target_pairs={{0,2},{1,3},{2,0},{3,1},{4,6},{5,7},{6,4},{7,5},{8,10},{9,11},{10,... | collective-permute-start | bytes 1572872 | tf_op jit(solution)/shard_map/ppermute | solution.py:358
  4.8 15.1 %copy-start.10 = (bf16[2,320,384]{2,1,0:T(8,128)(2,1)}, bf16[2,320,384]{2,1,0:T(8,128)(2,1)S(1)}, u32[]{:S(2)}) copy-start(bf16[2,320,384]{2,1,0:T(8,128)(2,1)S(1)} %dynamic-slice_bitcast_fusion.refs_0_) | copy-start | bytes 1474564
  4.8 12.8 %collective-permute-start.3 = (bf16[2,320,384]{2,1,0:T(8,128)(2,1)S(1)}, bf16[2,320,384]{2,1,0:T(8,128)(2,1)S(1)}, u32[]{:S(2)}, u32[]{:S(2)}) collective-permute-start(bf16[2,320,384]{2,1,0:T(8,128)(2,1)S(1)} %dynamic-slice_bitcast_fusion.refs_0_), channel_id=1, source_target_pairs={{0,16},{4,20},{16,24},{20,28},{24,8},{28,12},{8,0},{12,4},{1,17},{... | collective-permute-start | bytes 1474568 | tf_op jit(solution)/shard_map/ppermute | solution.py:376
  7.4 12.4 %collective-permute-start.2 = (bf16[2,320,384]{2,1,0:T(8,128)(2,1)S(1)}, bf16[2,320,384]{2,1,0:T(8,128)(2,1)S(1)}, u32[]{:S(2)}, u32[]{:S(2)}) collective-permute-start(bf16[2,320,384]{2,1,0:T(8,128)(2,1)S(1)} %dynamic-slice_bitcast_fusion.refs_0_), channel_id=1, source_target_pairs={{0,4},{4,0},{8,12},{12,8},{16,20},{20,16},{24,28},{28,24},{1,5},{5... | collective-permute-start | bytes 1474568 | tf_op jit(solution)/shard_map/ppermute | solution.py:379
  8.9 15.5 %collective-permute-start = (bf16[512,512]{1,0:T(8,128)(2,1)}, bf16[512,512]{1,0:T(8,128)(2,1)}, u32[]{:S(2)}, u32[]{:S(2)}) collective-permute-start(bf16[512,512]{1,0:T(8,128)(2,1)} %own_ref.1), channel_id=1, source_target_pairs={{0,1},{1,0},{2,3},{3,2},{4,5},{5,4},{6,7},{7,6},{8,9},{9,8},{10,11... | collective-permute-start | bytes 1572872 | tf_op jit(solution)/shard_map/ppermute | solution.py:361
  17.6 2.2 %copy-start.18 = (bf16[2,320,384]{2,1,0:T(8,128)(2,1)}, bf16[2,320,384]{2,1,0:T(8,128)(2,1)S(1)}, u32[]{:S(2)}) copy-start(bf16[2,320,384]{2,1,0:T(8,128)(2,1)S(1)} %collective-permute-done.3.refs_2_) | copy-start | bytes 1474564
  19.8 0.8 copy-start.19
  20.6 3.8 %copy-start.9 = (bf16[512,512]{1,0:T(8,128)(2,1)}, bf16[512,512]{1,0:T(8,128)(2,1)S(1)}, u32[]{:S(2)}) copy-start(bf16[512,512]{1,0:T(8,128)(2,1)S(1)} %collective-permute-done.1.chip_ref) | copy-start | bytes 1572868
  20.6 3.8 %collective-permute-start.4 = (bf16[512,512]{1,0:T(8,128)(2,1)S(1)}, bf16[512,512]{1,0:T(8,128)(2,1)}, u32[]{:S(2)}, u32[]{:S(2)}) collective-permute-start(bf16[512,512]{1,0:T(8,128)(2,1)S(1)} %collective-permute-done.1.chip_ref), channel_id=1, source_target_pairs={{0,1},{1,0},{2,3},{3,2},{4,5},{5,4},{6,7},{7,6},{8,9},{9,8},{10,11... | collective-permute-start | bytes 1572872 | tf_op jit(solution)/shard_map/ppermute | solution.py:361
  20.6 13.9 %collective-permute-start.5 = (bf16[2,320,384]{2,1,0:T(8,128)(2,1)}, bf16[2,320,384]{2,1,0:T(8,128)(2,1)}, u32[]{:S(2)}, u32[]{:S(2)}) collective-permute-start(bf16[2,320,384]{2,1,0:T(8,128)(2,1)} %copy-done.18), channel_id=1, source_target_pairs={{0,16},{4,20},{16,24},{20,28},{24,8},{28,12},{8,0},{12,4},{1,17},{... | collective-permute-start | bytes 1474568 | tf_op jit(solution)/shard_map/ppermute | solution.py:376
  22.2 29.1 %collective-permute-start.8 = (bf16[2,320,384]{2,1,0:T(8,128)(2,1)}, bf16[2,320,384]{2,1,0:T(8,128)(2,1)}, u32[]{:S(2)}, u32[]{:S(2)}) collective-permute-start(bf16[2,320,384]{2,1,0:T(8,128)(2,1)} %copy-done.18), channel_id=1, source_target_pairs={{0,4},{4,0},{8,12},{12,8},{16,20},{20,16},{24,28},{28,24},{1,5},{5... | collective-permute-start | bytes 1474568 | tf_op jit(solution)/shard_map/ppermute | solution.py:379
  23.7 60.2 %collective-permute-start.16 = (bf16[320,2048]{1,0:T(8,128)(2,1)}, bf16[320,2048]{1,0:T(8,128)(2,1)}, u32[]{:S(2)}, u32[]{:S(2)}) collective-permute-start(bf16[320,2048]{1,0:T(8,128)(2,1)} %param.24), channel_id=1, source_target_pairs={{0,2},{1,3},{2,0},{3,1},{4,6},{5,7},{6,4},{7,5},{8,10},{9,11},{10,... | collective-permute-start | bytes 3932168 | tf_op jit(solution)/shard_map/ppermute | solution.py:358
  29.2 3.0 %copy-start.17 = (bf16[512,2048]{1,0:T(8,128)(2,1)S(1)}, bf16[512,2048]{1,0:T(8,128)(2,1)}, u32[]{:S(2)}) copy-start(bf16[512,2048]{1,0:T(8,128)(2,1)} %get-tuple-element.36) | copy-start | bytes 6291460
  32.2 6.5 %copy-start.16 = (f32[64]{0:T(128)S(1)}, f32[64]{0:T(128)}, u32[]{:S(2)}) copy-start(f32[64]{0:T(128)} %param.22) | copy-start | bytes 772
  34.6 4.6 %copy-start.15 = (f32[64]{0:T(128)S(1)}, f32[64]{0:T(128)}, u32[]{:S(2)}) copy-start(f32[64]{0:T(128)} %param.23) | copy-start | bytes 772
  34.6 13.1 %collective-permute-start.6 = (bf16[2,320,384]{2,1,0:T(8,128)(2,1)}, bf16[2,320,384]{2,1,0:T(8,128)(2,1)S(1)}, u32[]{:S(2)}, u32[]{:S(2)}) collective-permute-start(bf16[2,320,384]{2,1,0:T(8,128)(2,1)} %collective-permute-done.5.refs_4_), channel_id=1, source_target_pairs={{0,16},{4,20},{16,24},{20,28},{24,8},{28,12},{8,0},{12,4},{1,17},{... | collective-permute-start | bytes 1474568 | tf_op jit(solution)/shard_map/ppermute | solution.py:376
  37.1 12.7 %collective-permute-start.9 = (bf16[2,320,384]{2,1,0:T(8,128)(2,1)}, bf16[2,320,384]{2,1,0:T(8,128)(2,1)S(1)}, u32[]{:S(2)}, u32[]{:S(2)}) collective-permute-start(bf16[2,320,384]{2,1,0:T(8,128)(2,1)} %collective-permute-done.5.refs_4_), channel_id=1, source_target_pairs={{0,4},{4,0},{8,12},{12,8},{16,20},{20,16},{24,28},{28,24},{1,5},{5... | collective-permute-start | bytes 1474568 | tf_op jit(solution)/shard_map/ppermute | solution.py:379
  39.1 1.8 %copy-start.12 = (bf16[512,5,64]{0,2,1:T(8,128)(2,1)}, bf16[512,5,64]{0,2,1:T(8,128)(2,1)S(1)}, u32[]{:S(2)}) copy-start(bf16[512,5,64]{0,2,1:T(8,128)(2,1)S(1)} %maximum_multiply_fusion) | copy-start | bytes 983044
  39.1 18.5 %collective-permute-start.7 = (bf16[320,512]{1,0:T(8,128)(2,1)S(1)}, bf16[320,512]{1,0:T(8,128)(2,1)S(1)}, u32[]{:S(2)}, u32[]{:S(2)}) collective-permute-start(bf16[320,512]{1,0:T(8,128)(2,1)S(1)} %bitcast.71), channel_id=1, source_target_pairs={{0,1},{1,0},{2,3},{3,2},{4,5},{5,4},{6,7},{7,6},{8,9},{9,8},{10,11... | collective-permute-start | bytes 983048 | tf_op jit(solution)/shard_map/ppermute | solution.py:361
  47.7 10.0 %copy-start.13 = (bf16[2,320,384]{2,1,0:T(8,128)(2,1)}, bf16[2,320,384]{2,1,0:T(8,128)(2,1)S(1)}, u32[]{:S(2)}) copy-start(bf16[2,320,384]{2,1,0:T(8,128)(2,1)S(1)} %collective-permute-done.6.refs_6_) | copy-start | bytes 1474564
  47.7 44.6 %collective-permute-start.14 = (bf16[320,2048]{1,0:T(8,128)(2,1)}, bf16[320,2048]{1,0:T(8,128)(2,1)}, u32[]{:S(2)}, u32[]{:S(2)}) collective-permute-start(bf16[320,2048]{1,0:T(8,128)(2,1)} %param.24), channel_id=1, source_target_pairs={{0,1},{1,0},{2,3},{3,2},{4,5},{5,4},{6,7},{7,6},{8,9},{9,8},{10,11... | collective-permute-start | bytes 3932168 | tf_op jit(solution)/shard_map/ppermute | solution.py:361
  49.8 7.9 %copy-start.14 = (bf16[2,320,384]{2,1,0:T(8,128)(2,1)}, bf16[2,320,384]{2,1,0:T(8,128)(2,1)S(1)}, u32[]{:S(2)}) copy-start(bf16[2,320,384]{2,1,0:T(8,128)(2,1)S(1)} %collective-permute-done.9.refs_5_) | copy-start | bytes 1474564
  49.8 7.9 %collective-permute-start.10 = (bf16[1,320,384]{2,1,0:T(8,128)(2,1)S(1)}, bf16[1,320,384]{2,1,0:T(8,128)(2,1)S(1)}, u32[]{:S(2)}, u32[]{:S(2)}) collective-permute-start(bf16[1,320,384]{2,1,0:T(8,128)(2,1)S(1)} %slice.40), channel_id=1, source_target_pairs={{0,4},{4,0},{8,12},{12,8},{16,20},{20,16},{24,28},{28,24},{1,5},{5... | collective-permute-start | bytes 737288 | tf_op jit(solution)/shard_map/ppermute | solution.py:379
  51.3 7.0 %collective-permute-start.11 = (bf16[1,320,384]{2,1,0:T(8,128)(2,1)S(1)}, bf16[1,320,384]{2,1,0:T(8,128)(2,1)S(1)}, u32[]{:S(2)}, u32[]{:S(2)}) collective-permute-start(bf16[1,320,384]{2,1,0:T(8,128)(2,1)S(1)} %slice.48), channel_id=1, source_target_pairs={{0,16},{4,20},{16,24},{20,28},{24,8},{28,12},{8,0},{12,4},{1,17},{... | collective-permute-start | bytes 737288 | tf_op jit(solution)/shard_map/ppermute | solution.py:376
  57.7 0.7 copy-start.20
  57.7 0.8 copy-start.21
  58.3 0.7 copy-start.22
  83.8 2.0 %collective-permute-start.12 = (bf16[352,512]{1,0:T(8,128)(2,1)}, bf16[352,512]{1,0:T(8,128)(2,1)S(1)}, u32[]{:S(2)}, u32[]{:S(2)}) collective-permute-start(bf16[352,512]{1,0:T(8,128)(2,1)} %get-tuple-element.50), channel_id=1, source_target_pairs={{0,1},{1,0},{2,3},{3,2},{4,5},{5,4},{6,7},{7,6},{8,9},{9,8},{10,11... | collective-permute-start | bytes 1081352 | tf_op jit(solution)/shard_map/ppermute | solution.py:361
  83.9 17.8 %collective-permute-start.18 = (bf16[320,2048]{1,0:T(8,128)(2,1)}, bf16[320,2048]{1,0:T(8,128)(2,1)}, u32[]{:S(2)}, u32[]{:S(2)}) collective-permute-start(bf16[320,2048]{1,0:T(8,128)(2,1)} %collective-permute-done.16), channel_id=1, source_target_pairs={{0,1},{1,0},{2,3},{3,2},{4,5},{5,4},{6,7},{7,6},{8,9},{9,8},{10,11... | collective-permute-start | bytes 3932168 | tf_op jit(solution)/shard_map/ppermute | solution.py:361
  85.8 0.7 copy-start.11
  88.7 3.6 %copy-start.2 = (bf16[512,2048]{1,0:T(8,128)(2,1)S(1)}, bf16[512,2048]{1,0:T(8,128)(2,1)}, u32[]{:S(2)}) copy-start(bf16[512,2048]{1,0:T(8,128)(2,1)} %get-tuple-element.35) | copy-start | bytes 6291460
  88.7 3.5 %collective-permute-start.13 = (bf16[320,512]{1,0:T(8,128)(2,1)}, bf16[320,512]{1,0:T(8,128)(2,1)S(1)}, u32[]{:S(2)}, u32[]{:S(2)}) collective-permute-start(bf16[320,512]{1,0:T(8,128)(2,1)} %merge.1), channel_id=1, source_target_pairs={{0,1},{1,0},{2,3},{3,2},{4,5},{5,4},{6,7},{7,6},{8,9},{9,8},{10,11... | collective-permute-start | bytes 983048 | tf_op jit(solution)/shard_map/ppermute | solution.py:361
  88.8 10.2 %collective-permute-start.15 = (bf16[320,512]{1,0:T(8,128)(2,1)}, bf16[320,512]{1,0:T(8,128)(2,1)S(1)}, u32[]{:S(2)}, u32[]{:S(2)}) collective-permute-start(bf16[320,512]{1,0:T(8,128)(2,1)} %merge.1), channel_id=1, source_target_pairs={{0,2},{1,3},{2,0},{3,1},{4,6},{5,7},{6,4},{7,5},{8,10},{9,11},{10,... | collective-permute-start | bytes 983048 | tf_op jit(solution)/shard_map/ppermute | solution.py:358
  92.3 12.7 %slice-start = ((s8[10485760]{0:T(1024)(128)(4,1)}), s8[4194304]{0:T(1024)(128)(4,1)S(1)}, s32[]{:S(2)}) async-start(s8[10485760]{0:T(1024)(128)(4,1)} %bitcast.76), calls=%async_computation | async-start | bytes 8388608
  92.3 12.7 %slice-start.1 = ((s8[10485760]{0:T(1024)(128)(4,1)}), s8[4194304]{0:T(1024)(128)(4,1)S(1)}, s32[]{:S(2)}) async-start(s8[10485760]{0:T(1024)(128)(4,1)} %bitcast.76), calls=%async_computation.1 | async-start | bytes 8388608
  99.0 2.6 %collective-permute-start.17 = (bf16[320,512]{1,0:T(8,128)(2,1)S(1)}, bf16[320,512]{1,0:T(8,128)(2,1)S(1)}, u32[]{:S(2)}, u32[]{:S(2)}) collective-permute-start(bf16[320,512]{1,0:T(8,128)(2,1)S(1)} %collective-permute-done.15), channel_id=1, source_target_pairs={{0,1},{1,0},{2,3},{3,2},{4,5},{5,4},{6,7},{7,6},{8,9},{9,8},{10,11... | collective-permute-start | bytes 983048 | tf_op jit(solution)/shard_map/ppermute | solution.py:361
  101.6 3.3 %slice-start.2 = ((s8[10485760]{0:T(1024)(128)(4,1)}), s8[2097152]{0:T(1024)(128)(4,1)S(1)}, s32[]{:S(2)}) async-start(s8[10485760]{0:T(1024)(128)(4,1)} %bitcast.76), calls=%async_computation.2 | async-start | bytes 4194304
  101.7 3.3 %copy-start.23 = (f32[2048]{0:T(1024)S(1)}, f32[2048]{0:T(1024)}, u32[]{:S(2)}) copy-start(f32[2048]{0:T(1024)} %param.25) | copy-start | bytes 24580
  110.6 1.3 %copy-start.8 = (bf16[1280,512]{1,0:T(8,128)(2,1)S(1)}, bf16[1280,512]{1,0:T(8,128)(2,1)}, u32[]{:S(2)}) copy-start(bf16[1280,512]{1,0:T(8,128)(2,1)} %get-tuple-element.58) | copy-start | bytes 3932164
  111.9 1.4 %copy-start.7 = (bf16[1280,512]{1,0:T(8,128)(2,1)S(1)}, bf16[1280,512]{1,0:T(8,128)(2,1)}, u32[]{:S(2)}) copy-start(bf16[1280,512]{1,0:T(8,128)(2,1)} %get-tuple-element.59) | copy-start | bytes 3932164
  112.8 1.4 %copy-start.6 = (bf16[1280,512]{1,0:T(8,128)(2,1)S(1)}, bf16[1280,512]{1,0:T(8,128)(2,1)}, u32[]{:S(2)}) copy-start(bf16[1280,512]{1,0:T(8,128)(2,1)} %get-tuple-element.57) | copy-start | bytes 3932164
  112.8 2.3 %collective-permute-start.19 = (bf16[512,512]{1,0:T(8,128)(2,1)S(1)}, bf16[512,512]{1,0:T(8,128)(2,1)S(1)}, u32[]{:S(2)}, u32[]{:S(2)}) collective-permute-start(bf16[512,512]{1,0:T(8,128)(2,1)S(1)} %convolution_convert_fusion.2), channel_id=1, source_target_pairs={{0,1},{1,0},{2,3},{3,2},{4,5},{5,4},{6,7},{7,6},{8,9},{9,8},{10,11... | collective-permute-start | bytes 1572872 | tf_op jit(solution)/shard_map/ppermute | solution.py:361
  115.1 1.2 copy-start.3
  115.1 1.2 copy-start.4
  115.1 2.1 %copy-start.5 = (bf16[1280,512]{1,0:T(8,128)(2,1)S(1)}, bf16[1280,512]{1,0:T(8,128)(2,1)}, u32[]{:S(2)}) copy-start(bf16[1280,512]{1,0:T(8,128)(2,1)} %get-tuple-element.62) | copy-start | bytes 3932164
  115.3 14.4 %collective-permute-start.21 = (bf16[512,512]{1,0:T(8,128)(2,1)S(1)}, bf16[512,512]{1,0:T(8,128)(2,1)S(1)}, u32[]{:S(2)}, u32[]{:S(2)}) collective-permute-start(bf16[512,512]{1,0:T(8,128)(2,1)S(1)} %add_convert_fusion.1), channel_id=1, source_target_pairs={{0,2},{1,3},{2,0},{3,1},{4,6},{5,7},{6,4},{7,5},{8,10},{9,11},{10,... | collective-permute-start | bytes 1572872 | tf_op jit(solution)/shard_map/ppermute | solution.py:358
  116.0 13.6 %collective-permute-start.20 = (bf16[512,512]{1,0:T(8,128)(2,1)S(1)}, bf16[512,512]{1,0:T(8,128)(2,1)S(1)}, u32[]{:S(2)}, u32[]{:S(2)}) collective-permute-start(bf16[512,512]{1,0:T(8,128)(2,1)S(1)} %convolution_convert_fusion.1), channel_id=1, source_target_pairs={{0,1},{1,0},{2,3},{3,2},{4,5},{5,4},{6,7},{7,6},{8,9},{9,8},{10,11... | collective-permute-start | bytes 1572872 | tf_op jit(solution)/shard_map/ppermute | solution.py:361
  117.1 13.6 %copy-start.1 = (bf16[2048,640]{1,0:T(8,128)(2,1)S(1)}, bf16[2048,640]{1,0:T(8,128)(2,1)}, u32[]{:S(2)}) copy-start(bf16[2048,640]{1,0:T(8,128)(2,1)} %param.21) | copy-start | bytes 7864324

commit v9 on v8

--- a/solution.py
+++ b/solution.py
@@ -439,16 +439,27 @@
     gate_up = jnp.einsum("rd,dgf->rgf", normed_ffn, w_gate_up, preferred_element_type=jnp.float32)
     activated = (jax.nn.silu(gate_up[:, 0]) * gate_up[:, 1]).astype(jnp.bfloat16)
 
-    def down(flip):
-        return jnp.dot(activated, down_blocks[flip], preferred_element_type=jnp.float32).astype(jnp.bfloat16)
-
-    got_far, near = lax.optimization_barrier((across_core(down(3)), down(1)))
-    far_sum = (down(2).astype(jnp.float32) + got_far.astype(jnp.float32)).astype(jnp.bfloat16)
-    from_far = across_chip(far_sum)
-    activated, far_sum = lax.optimization_barrier((activated, far_sum))
+    def down(flip, rows=slice(None)):
+        return jnp.dot(activated[rows], down_blocks[flip], preferred_element_type=jnp.float32).astype(jnp.bfloat16)
+
+    first, second = slice(0, row_count // 2), slice(row_count // 2, row_count)
+    got_first, far_second, near = lax.optimization_barrier(
+        (across_core(down(3, first)), down(3, second), down(1))
+    )
+    sum_first = (down(2, first).astype(jnp.float32) + got_first.astype(jnp.float32)).astype(jnp.bfloat16)
+    sum_first, got_second = lax.optimization_barrier((sum_first, across_core(far_second)))
+    from_first = across_chip(sum_first)
+    sum_second = (down(2, second).astype(jnp.float32) + got_second.astype(jnp.float32)).astype(jnp.bfloat16)
+    from_second = across_chip(sum_second)
+    activated, sum_second = lax.optimization_barrier((activated, sum_second))
     own_mixed = lax.dynamic_slice_in_dim(mixed, rank * width, width, 1)
     near_sum = own_mixed + down(0).astype(jnp.float32) + across_core(near).astype(jnp.float32)
-    return ((near_sum + from_far.astype(jnp.float32)).astype(jnp.bfloat16), cache_rows)
+    near_sum, from_first = lax.optimization_barrier((near_sum, from_first))
+    done = (near_sum[first] + from_first.astype(jnp.float32)).astype(jnp.bfloat16)
+    hidden = jnp.pad(done, ((0, row_count // 2), (0, 0)))
+    hidden, from_second = lax.optimization_barrier((hidden, from_second))
+    last = (near_sum[second] + from_second.astype(jnp.float32)).astype(jnp.bfloat16)
+    return (lax.dynamic_update_slice(hidden, last, (row_count // 2, 0)), cache_rows)
 
 
 def solution(mesh):

time: 131 us -> 134 us (1.023)
  local copies, waits for them, and re-layouts: 9.72 us -> 12.2 us
  starting transfers between devices: 20.9 us -> 22.6 us
    unnamed x54 -> x56, local copies, waits for them, and re-layouts: 2.84 us -> 5.26 us
    ppermute x4 -> x5, starting transfers between devices: 5.19 us -> 6.52 us  [across_chip(): return lax.ppermute(value, 'tp', [(i, i ^ 2) for i in range(4)])]
    ppermute x4 -> x5, waiting for transfers between devices: 15.6 us -> 14.8 us  [across_chip(): return lax.ppermute(value, 'tp', [(i, i ^ 2) for i in range(4)])]
    dot_general x4 -> x6, matrix products: 3.35 us -> 3.66 us  [down(): jnp.dot(activated[rows], down_blocks[flip], preferred_element_type=jnp.fl...]
  transfers between devices with their start and end apart: 22 -> 24, of which waited for: 9 -> 11; matrix products, arithmetic and copies ran while one was open for 19% -> 19% of each run, Pallas kernels for 28% -> 28%
where the time goes in v9:
time: 134 us
  Pallas kernels  36.9 us (28%)
  waiting for transfers between devices  30.9 us (23%)
  matrix products  25.4 us (19%)
  starting transfers between devices  22.6 us (17%)
  local copies, waits for them, and re-layouts  12.2 us (9%)
  other arithmetic  4.68 us (3%)
    pallas_call x1, Pallas kernels, prefix_attend(): pl.pallas_call(functools.partial(prefix_kernel, block, 256, len(units) -...  24.9 us
    ppermute x5, waiting for transfers between devices, across_chip(): return lax.ppermute(value, 'tp', [(i, i ^ 2) for i in range(4)])  14.8 us
    dot_general x4, matrix products, tn_dot(): lax.dot_general(lhs, rhs, (((0,), (0,)), ((), ())), preferred_element_typ...  11.5 us
    ppermute x4, waiting for transfers between devices, ring(): lax.ppermute(value, 'req', [(2 * a + b, 2 * c + b) for a, c in steps for...  10.3 us
    ppermute x4, starting transfers between devices, ring(): lax.ppermute(value, 'req', [(2 * a + b, 2 * c + b) for a, c in steps for...  8.04 us
    ppermute x5, starting transfers between devices, across_chip(): return lax.ppermute(value, 'tp', [(i, i ^ 2) for i in range(4)])  6.52 us
    ppermute x4, starting transfers between devices, aside(): return lax.ppermute(value, 'req', [(r, r ^ 1) for r in range(n_req)])  6.08 us
    dot_general x1, matrix products, local(): jnp.einsum('rd,dgf->rgf', normed_ffn, w_gate_up, preferred_element_type=j...  5.64 us
  transfers between devices with their start and end apart: 24, of which 11 were waited for; matrix products, arithmetic and copies ran while one was open for 19% of the time, Pallas kernels for 28%

profile of v9, /device:TPU:0, one launch (start us, length us, event | category | flops | bytes accessed | tf_op | source)
XLA Modules:
  0.0 133.7 jit_solution(2229530892496194800)
XLA Ops:
  0.6 3.0 %collective-permute-start.1 = (bf16[512,512]{1,0:T(8,128)(2,1)}, bf16[512,512]{1,0:T(8,128)(2,1)S(1)}, u32[]{:S(2)}, u32[]{:S(2)}) collective-permute-start(bf16[512,512]{1,0:T(8,128)(2,1)} %own_ref.1), channel_id=1, source_target_pairs={{0,2},{1,3},{2,0},{3,1},{4,6},{5,7},{6,4},{7,5},{8,10},{9,11},{10,... | collective-permute-start | bytes 1572872 | tf_op jit(solution)/shard_map/ppermute | solution.py:358
  3.7 1.1 dynamic-slice_bitcast_fusion.refs_0_
  4.8 2.6 %collective-permute-start.3 = (bf16[2,320,384]{2,1,0:T(8,128)(2,1)S(1)}, bf16[2,320,384]{2,1,0:T(8,128)(2,1)S(1)}, u32[]{:S(2)}, u32[]{:S(2)}) collective-permute-start(bf16[2,320,384]{2,1,0:T(8,128)(2,1)S(1)} %dynamic-slice_bitcast_fusion.refs_0_), channel_id=1, source_target_pairs={{0,16},{4,20},{16,24},{20,28},{24,8},{28,12},{8,0},{12,4},{1,17},{... | collective-permute-start | bytes 1474568 | tf_op jit(solution)/shard_map/ppermute | solution.py:376
  7.4 1.5 %collective-permute-start.2 = (bf16[2,320,384]{2,1,0:T(8,128)(2,1)S(1)}, bf16[2,320,384]{2,1,0:T(8,128)(2,1)S(1)}, u32[]{:S(2)}, u32[]{:S(2)}) collective-permute-start(bf16[2,320,384]{2,1,0:T(8,128)(2,1)S(1)} %dynamic-slice_bitcast_fusion.refs_0_), channel_id=1, source_target_pairs={{0,4},{4,0},{8,12},{12,8},{16,20},{20,16},{24,28},{28,24},{1,5},{5... | collective-permute-start | bytes 1474568 | tf_op jit(solution)/shard_map/ppermute | solution.py:379
  8.9 0.7 add_convert_fusion.5
  9.6 0.3 multiply_sine_fusion
  9.9 7.7 %collective-permute-done.3.refs_2_ = bf16[2,320,384]{2,1,0:T(8,128)(2,1)S(1)} collective-permute-done((bf16[2,320,384]{2,1,0:T(8,128)(2,1)S(1)}, bf16[2,320,384]{2,1,0:T(8,128)(2,1)S(1)}, u32[]{:S(2)}, u32[]{:S(2)}) %collective-permute-start.3) | collective-permute-done | bytes 491552 | tf_op jit(solution)/shard_map/ppermute | solution.py:376
  17.6 2.2 %collective-permute-done.2.refs_1_ = bf16[2,320,384]{2,1,0:T(8,128)(2,1)S(1)} collective-permute-done((bf16[2,320,384]{2,1,0:T(8,128)(2,1)S(1)}, bf16[2,320,384]{2,1,0:T(8,128)(2,1)S(1)}, u32[]{:S(2)}, u32[]{:S(2)}) %collective-permute-start.2) | collective-permute-done | bytes 491552 | tf_op jit(solution)/shard_map/ppermute | solution.py:379
  19.8 0.7 copy-done.20
  20.6 1.6 %collective-permute-start.5 = (bf16[2,320,384]{2,1,0:T(8,128)(2,1)}, bf16[2,320,384]{2,1,0:T(8,128)(2,1)}, u32[]{:S(2)}, u32[]{:S(2)}) collective-permute-start(bf16[2,320,384]{2,1,0:T(8,128)(2,1)} %copy-done.19), channel_id=1, source_target_pairs={{0,16},{4,20},{16,24},{20,28},{24,8},{28,12},{8,0},{12,4},{1,17},{... | collective-permute-start | bytes 1474568 | tf_op jit(solution)/shard_map/ppermute | solution.py:376
  22.2 1.5 %collective-permute-start.8 = (bf16[2,320,384]{2,1,0:T(8,128)(2,1)}, bf16[2,320,384]{2,1,0:T(8,128)(2,1)}, u32[]{:S(2)}, u32[]{:S(2)}) collective-permute-start(bf16[2,320,384]{2,1,0:T(8,128)(2,1)} %copy-done.19), channel_id=1, source_target_pairs={{0,4},{4,0},{8,12},{12,8},{16,20},{20,16},{24,28},{28,24},{1,5},{5... | collective-permute-start | bytes 1474568 | tf_op jit(solution)/shard_map/ppermute | solution.py:379
  23.7 0.7 collective-permute-start.16
  24.4 4.7 %gather_norm.1 = (bf16[512,2048]{1,0:T(8,128)(2,1)}, bf16[512,2048]{1,0:T(8,128)(2,1)}) custom-call(s32[1]{0:T(128)} %bitcast.rank_ref, bf16[512,512]{1,0:T(8,128)(2,1)} %own_ref.1, bf16[512,512]{1,0:T(8,128)(2,1)} %collective-permute-done.core_ref, bf16[512,512]{1,0:T(8,128)(2,1)} %copy-done.9, bf16[512,512]{1,0:T(8,128)(2,1)} %collective-permute-done.4.both_ref, ...), custom_call_target="tpu_custom_call" | custom-call | tf_op jit(solution)/shard_map/gather_norm/pallas_call | solution.py:73
  29.1 3.0 %fusion.18 = f32[512,320]{0,1:T(8,128)S(1)} fusion(bf16[512,2048]{1,0:T(8,128)(2,1)} %get-tuple-element.43, bf16[2048,320]{0,1:T(8,128)(2,1)} %param.20), kind=kOutput, calls=%fused_computation.59 | convolution fusion | flops 671088640 | bytes 4063232 | tf_op jit(solution)/shard_map/dot_general | solution.py:394
  32.1 1.6 %fusion.19 = f32[512,640]{0,1:T(8,128)S(1)} fusion(bf16[512,2048]{1,0:T(8,128)(2,1)S(1)} %copy-done.18, bf16[2048,640]{1,0:T(8,128)(2,1)S(1)} %copy-done), kind=kOutput, calls=%fused_computation.60 | convolution fusion | flops 1342177280 | bytes 6029312 | tf_op jit(solution)/shard_map/dot_general | solution.py:397
  33.7 0.8 collective-permute-done.5.refs_4_
  34.5 2.5 %collective-permute-start.6 = (bf16[2,320,384]{2,1,0:T(8,128)(2,1)}, bf16[2,320,384]{2,1,0:T(8,128)(2,1)S(1)}, u32[]{:S(2)}, u32[]{:S(2)}) collective-permute-start(bf16[2,320,384]{2,1,0:T(8,128)(2,1)} %collective-permute-done.5.refs_4_), channel_id=1, source_target_pairs={{0,16},{4,20},{16,24},{20,28},{24,8},{28,12},{8,0},{12,4},{1,17},{... | collective-permute-start | bytes 1474568 | tf_op jit(solution)/shard_map/ppermute | solution.py:376
  37.0 1.5 %collective-permute-start.9 = (bf16[2,320,384]{2,1,0:T(8,128)(2,1)}, bf16[2,320,384]{2,1,0:T(8,128)(2,1)S(1)}, u32[]{:S(2)}, u32[]{:S(2)}) collective-permute-start(bf16[2,320,384]{2,1,0:T(8,128)(2,1)} %collective-permute-done.5.refs_4_), channel_id=1, source_target_pairs={{0,4},{4,0},{8,12},{12,8},{16,20},{20,16},{24,28},{28,24},{1,5},{5... | collective-permute-start | bytes 1474568 | tf_op jit(solution)/shard_map/ppermute | solution.py:379
  38.6 0.2 fusion.11
  39.2 0.4 copy-done.16
  39.7 0.8 slice.102
  40.5 0.8 maximum_convert_fusion
  41.3 5.1 %suffix_attend.1 = (f32[320,512]{1,0:T(8,128)}, f32[8,512]{1,0:T(8,128)}) custom-call(s32[1,2]{1,0:T(1,128)} %lengths_ref.1, bf16[320,512]{1,0:T(8,128)(2,1)} %bitcast.72, bf16[320,512]{1,0:T(8,128)(2,1)} %bitcast.69, bf16[320,512]{1,0:T(8,128)(2,1)} %bitcast.67), custom_call_target="tpu_custom_call" | custom-call | flops 335544320 | bytes 3145728 | tf_op jit(solution)/shard_map/suffix_attend/pallas_call | solution.py:115
  46.4 1.2 collective-permute-done.6.refs_6_
  47.7 2.1 %collective-permute-done.9.refs_5_ = bf16[2,320,384]{2,1,0:T(8,128)(2,1)S(1)} collective-permute-done((bf16[2,320,384]{2,1,0:T(8,128)(2,1)}, bf16[2,320,384]{2,1,0:T(8,128)(2,1)S(1)}, u32[]{:S(2)}, u32[]{:S(2)}) %collective-permute-start.9) | collective-permute-done | bytes 491552 | tf_op jit(solution)/shard_map/ppermute | solution.py:379
  49.7 1.5 %collective-permute-start.10 = (bf16[1,320,384]{2,1,0:T(8,128)(2,1)S(1)}, bf16[1,320,384]{2,1,0:T(8,128)(2,1)S(1)}, u32[]{:S(2)}, u32[]{:S(2)}) collective-permute-start(bf16[1,320,384]{2,1,0:T(8,128)(2,1)S(1)} %slice.54), channel_id=1, source_target_pairs={{0,4},{4,0},{8,12},{12,8},{16,20},{20,16},{24,28},{28,24},{1,5},{5... | collective-permute-start | bytes 737288 | tf_op jit(solution)/shard_map/ppermute | solution.py:379
  51.3 1.4 %collective-permute-start.11 = (bf16[1,320,384]{2,1,0:T(8,128)(2,1)S(1)}, bf16[1,320,384]{2,1,0:T(8,128)(2,1)S(1)}, u32[]{:S(2)}, u32[]{:S(2)}) collective-permute-start(bf16[1,320,384]{2,1,0:T(8,128)(2,1)S(1)} %slice.66), channel_id=1, source_target_pairs={{0,16},{4,20},{16,24},{20,28},{24,8},{28,12},{8,0},{12,4},{1,17},{... | collective-permute-start | bytes 737288 | tf_op jit(solution)/shard_map/ppermute | solution.py:376
  52.6 5.0 %constant_dynamic-slice_fusion = (bf16[1280,512]{1,0:T(8,128)(2,1)}, bf16[1280,512]{1,0:T(8,128)(2,1)}, bf16[1280,512]{1,0:T(8,128)(2,1)}, bf16[1280,512]{1,0:T(8,128)(2,1)}) fusion(bf16[1280,2048]{1,0:T(8,128)(2,1)} %param.27, s32[]{:T(128)S(6)} %select_n.28, s32[]{:T(128)S(6)} %select_n.27, s32[]{:T(128)S(6)} %select_n.26, s32[]{:T(128)S(6)} %select_n.25), kind=kLoop, calls=%fused_computation.54 | loop fusion | bytes 10485776 | tf_op jit(solution)/shard_map/dynamic_slice | solution.py:425
  57.7 0.6 collective-permute-done.11.refs_8_
  58.5 0.5 copy-done.23
  59.0 24.9 %prefix_attend.1 = (f32[320,512]{1,0:T(8,128)}, f32[8,512]{1,0:T(8,128)}, bf16[352,512]{1,0:T(8,128)(2,1)}) custom-call(s32[8]{0:T(128)} %owners_ref.1, s32[1,2]{1,0:T(1,128)} %groups_ref.1, s32[1,2]{1,0:T(1,128)} %lengths_ref.1, s32[1]{0:T(128)} %bitcast.6.me_ref, bf16[320,512]{1,0:T(8,128)(2,1)} %bitcast.73, bf16[320,512]{1,0:T(8,128)(2,1)} %copy-done.21, ...), custom_call_target="tpu_custom_call" | custom-call | flops 2013265920 | bytes 6291456 | tf_op jit(solution)/shard_map/prefix_attend/pallas_call | solution.py:271
  83.9 0.5 collective-permute-start.18
  84.4 0.9 pad_maximum_fusion
  85.3 0.5 collective-permute-done.12.got_ref
  85.8 0.7 copy-done.12
  86.5 2.2 %merge.1 = bf16[320,512]{1,0:T(8,128)(2,1)} custom-call(f32[320,512]{1,0:T(8,128)} %get-tuple-element.55.own_ref, f32[8,512]{1,0:T(8,128)} %get-tuple-element.56.own_lse_ref, bf16[352,512]{1,0:T(8,128)(2,1)} %copy-done.12, f32[320,512]{1,0:T(8,128)} %get-tuple-element.58.suffix_ref, f32[8,512]{1,0:T(8,128)} %get-tuple-element.59.suffix_lse_ref), custom_call_target="tpu_custom_call" | custom-call | flops 1310720 | bytes 1048576 | tf_op jit(solution)/shard_map/merge/pallas_call | solution.py:316
  88.7 0.1 collective-permute-start.13
  88.9 0.7 collective-permute-start.15
  89.6 2.8 %fusion.20 = f32[512,2048]{1,0:T(8,128)S(1)} fusion(bf16[320,512]{1,0:T(8,128)(2,1)} %merge.1, bf16[320,2048]{1,0:T(8,128)(2,1)} %param.24), kind=kOutput, calls=%fused_computation.61 | convolution fusion | flops 671088640 | bytes 5832704 | tf_op jit(solution)/shard_map/dot_general | solution.py:46
  92.5 2.9 %add_add_fusion.1 = f32[512,2048]{1,0:T(8,128)S(1)} fusion(f32[512,2048]{1,0:T(8,128)S(1)} %fusion.20, bf16[512,2048]{1,0:T(8,128)(2,1)S(1)} %copy-done.2, bf16[320,512]{1,0:T(8,128)(2,1)S(1)} %collective-permute-done.13, bf16[320,2048]{1,0:T(8,128)(2,1)} %collective-permute-done.14), kind=kOutput, calls=%fused_computation.5 | convolution fusion | flops 674234368 | bytes 12124160 | tf_op jit(solution)/shard_map/dot_general | solution.py:46
  95.3 3.7 %collective-permute-done.15 = bf16[320,512]{1,0:T(8,128)(2,1)S(1)} collective-permute-done((bf16[320,512]{1,0:T(8,128)(2,1)}, bf16[320,512]{1,0:T(8,128)(2,1)S(1)}, u32[]{:S(2)}, u32[]{:S(2)}) %collective-permute-start.15) | collective-permute-done | bytes 327712 | tf_op jit(solution)/shard_map/ppermute | solution.py:358
  99.1 2.6 %fusion.21 = f32[512,2048]{1,0:T(8,128)S(1)} fusion(bf16[320,512]{1,0:T(8,128)(2,1)S(1)} %collective-permute-done.15, bf16[320,2048]{1,0:T(8,128)(2,1)} %collective-permute-done.16), kind=kOutput, calls=%fused_computation.62 | convolution fusion | flops 671088640 | bytes 5832704 | tf_op jit(solution)/shard_map/dot_general | solution.py:46
  101.7 3.2 %multiply_reduce_fusion = (f32[512]{0:T(512)S(1)}, f32[512,2048]{1,0:T(8,128)S(1)}) fusion(bf16[320,512]{1,0:T(8,128)(2,1)S(1)} %collective-permute-done.17, bf16[320,2048]{1,0:T(8,128)(2,1)} %collective-permute-done.18, f32[512,2048]{1,0:T(8,128)S(1)} %add_add_fusion.1, f32[512,2048]{1,0:T(8,128)S(1)} %fusion.21), kind=kOutput, calls=%fused_computation.3 | convolution fusion | flops 675282432 | bytes 14223360 | tf_op jit(solution)/shard_map/dot_general | solution.py:46
  105.0 5.6 %fusion = f32[512,2,1280]{2,0,1:T(8,128)S(1)} fusion(bf16[2048,2,1280]{2,1,0:T(2,128)(2,1)S(1)} %bitcast.77, f32[512,2048]{1,0:T(8,128)S(1)} %get-tuple-element.89, f32[2048]{0:T(1024)S(1)} %copy-done.24, f32[512]{0:T(512)S(1)} %add_rsqrt_fusion.2), kind=kOutput, calls=%fused_computation | convolution fusion | flops 5371854848 | bytes 19933184 | tf_op jit(solution)/shard_map/rd,dgf->rgf/dot_general | solution.py:439
  110.7 0.8 fusion.3
  111.4 0.5 copy-done.6
  112.0 0.5 fusion.10
  112.5 0.8 copy-done.8
  113.3 0.8 convolution_convert_fusion.1
  114.1 0.5 copy-done.7
  114.6 0.5 convolution_convert_fusion.3
  115.1 0.6 collective-permute-start.19
  115.7 0.5 convolution_convert_fusion.2
  116.2 0.7 collective-permute-done.19
  116.8 0.4 collective-permute-start.20
  117.2 0.5 fusion.9
  117.7 0.2 collective-permute-start.21
  118.0 0.4 collective-permute-done.20
  118.4 0.8 collective-permute-start.23
  119.2 1.3 collective-permute-start.22
  120.5 0.8 fusion.8
  121.4 0.3 convert_add_fusion
  121.7 11.0 %collective-permute-done.22 = bf16[256,512]{1,0:T(8,128)(2,1)S(1)} collective-permute-done((bf16[256,512]{1,0:T(8,128)(2,1)S(1)}, bf16[256,512]{1,0:T(8,128)(2,1)S(1)}, u32[]{:S(2)}, u32[]{:S(2)}) %collective-permute-start.22) | collective-permute-done | bytes 262176 | tf_op jit(solution)/shard_map/ppermute | solution.py:358
  132.9 0.8 copy-done.10
  (84 shorter events, 1.4 us)
Async XLA Ops:
  0.6 31.5 %copy-start = (bf16[2048,640]{1,0:T(8,128)(2,1)S(1)}, bf16[2048,640]{1,0:T(8,128)(2,1)}, u32[]{:S(2)}) copy-start(bf16[2048,640]{1,0:T(8,128)(2,1)} %param.21) | copy-start | bytes 7864324
  0.6 19.2 %collective-permute-start.1 = (bf16[512,512]{1,0:T(8,128)(2,1)}, bf16[512,512]{1,0:T(8,128)(2,1)S(1)}, u32[]{:S(2)}, u32[]{:S(2)}) collective-permute-start(bf16[512,512]{1,0:T(8,128)(2,1)} %own_ref.1), channel_id=1, source_target_pairs={{0,2},{1,3},{2,0},{3,1},{4,6},{5,7},{6,4},{7,5},{8,10},{9,11},{10,... | collective-permute-start | bytes 1572872 | tf_op jit(solution)/shard_map/ppermute | solution.py:358
  4.8 15.1 %copy-start.11 = (bf16[2,320,384]{2,1,0:T(8,128)(2,1)}, bf16[2,320,384]{2,1,0:T(8,128)(2,1)S(1)}, u32[]{:S(2)}) copy-start(bf16[2,320,384]{2,1,0:T(8,128)(2,1)S(1)} %dynamic-slice_bitcast_fusion.refs_0_) | copy-start | bytes 1474564
  4.8 12.8 %collective-permute-start.3 = (bf16[2,320,384]{2,1,0:T(8,128)(2,1)S(1)}, bf16[2,320,384]{2,1,0:T(8,128)(2,1)S(1)}, u32[]{:S(2)}, u32[]{:S(2)}) collective-permute-start(bf16[2,320,384]{2,1,0:T(8,128)(2,1)S(1)} %dynamic-slice_bitcast_fusion.refs_0_), channel_id=1, source_target_pairs={{0,16},{4,20},{16,24},{20,28},{24,8},{28,12},{8,0},{12,4},{1,17},{... | collective-permute-start | bytes 1474568 | tf_op jit(solution)/shard_map/ppermute | solution.py:376
  7.4 12.4 %collective-permute-start.2 = (bf16[2,320,384]{2,1,0:T(8,128)(2,1)S(1)}, bf16[2,320,384]{2,1,0:T(8,128)(2,1)S(1)}, u32[]{:S(2)}, u32[]{:S(2)}) collective-permute-start(bf16[2,320,384]{2,1,0:T(8,128)(2,1)S(1)} %dynamic-slice_bitcast_fusion.refs_0_), channel_id=1, source_target_pairs={{0,4},{4,0},{8,12},{12,8},{16,20},{20,16},{24,28},{28,24},{1,5},{5... | collective-permute-start | bytes 1474568 | tf_op jit(solution)/shard_map/ppermute | solution.py:379
  8.9 15.5 %collective-permute-start = (bf16[512,512]{1,0:T(8,128)(2,1)}, bf16[512,512]{1,0:T(8,128)(2,1)}, u32[]{:S(2)}, u32[]{:S(2)}) collective-permute-start(bf16[512,512]{1,0:T(8,128)(2,1)} %own_ref.1), channel_id=1, source_target_pairs={{0,1},{1,0},{2,3},{3,2},{4,5},{5,4},{6,7},{7,6},{8,9},{9,8},{10,11... | collective-permute-start | bytes 1572872 | tf_op jit(solution)/shard_map/ppermute | solution.py:361
  17.6 2.2 %copy-start.19 = (bf16[2,320,384]{2,1,0:T(8,128)(2,1)}, bf16[2,320,384]{2,1,0:T(8,128)(2,1)S(1)}, u32[]{:S(2)}) copy-start(bf16[2,320,384]{2,1,0:T(8,128)(2,1)S(1)} %collective-permute-done.3.refs_2_) | copy-start | bytes 1474564
  19.8 0.8 copy-start.20
  20.6 3.8 %copy-start.9 = (bf16[512,512]{1,0:T(8,128)(2,1)}, bf16[512,512]{1,0:T(8,128)(2,1)S(1)}, u32[]{:S(2)}) copy-start(bf16[512,512]{1,0:T(8,128)(2,1)S(1)} %collective-permute-done.1.chip_ref) | copy-start | bytes 1572868
  20.6 3.8 %collective-permute-start.4 = (bf16[512,512]{1,0:T(8,128)(2,1)S(1)}, bf16[512,512]{1,0:T(8,128)(2,1)}, u32[]{:S(2)}, u32[]{:S(2)}) collective-permute-start(bf16[512,512]{1,0:T(8,128)(2,1)S(1)} %collective-permute-done.1.chip_ref), channel_id=1, source_target_pairs={{0,1},{1,0},{2,3},{3,2},{4,5},{5,4},{6,7},{7,6},{8,9},{9,8},{10,11... | collective-permute-start | bytes 1572872 | tf_op jit(solution)/shard_map/ppermute | solution.py:361
  20.6 13.9 %collective-permute-start.5 = (bf16[2,320,384]{2,1,0:T(8,128)(2,1)}, bf16[2,320,384]{2,1,0:T(8,128)(2,1)}, u32[]{:S(2)}, u32[]{:S(2)}) collective-permute-start(bf16[2,320,384]{2,1,0:T(8,128)(2,1)} %copy-done.19), channel_id=1, source_target_pairs={{0,16},{4,20},{16,24},{20,28},{24,8},{28,12},{8,0},{12,4},{1,17},{... | collective-permute-start | bytes 1474568 | tf_op jit(solution)/shard_map/ppermute | solution.py:376
  22.2 29.1 %collective-permute-start.8 = (bf16[2,320,384]{2,1,0:T(8,128)(2,1)}, bf16[2,320,384]{2,1,0:T(8,128)(2,1)}, u32[]{:S(2)}, u32[]{:S(2)}) collective-permute-start(bf16[2,320,384]{2,1,0:T(8,128)(2,1)} %copy-done.19), channel_id=1, source_target_pairs={{0,4},{4,0},{8,12},{12,8},{16,20},{20,16},{24,28},{28,24},{1,5},{5... | collective-permute-start | bytes 1474568 | tf_op jit(solution)/shard_map/ppermute | solution.py:379
  23.7 60.2 %collective-permute-start.16 = (bf16[320,2048]{1,0:T(8,128)(2,1)}, bf16[320,2048]{1,0:T(8,128)(2,1)}, u32[]{:S(2)}, u32[]{:S(2)}) collective-permute-start(bf16[320,2048]{1,0:T(8,128)(2,1)} %param.24), channel_id=1, source_target_pairs={{0,2},{1,3},{2,0},{3,1},{4,6},{5,7},{6,4},{7,5},{8,10},{9,11},{10,... | collective-permute-start | bytes 3932168 | tf_op jit(solution)/shard_map/ppermute | solution.py:358
  29.1 3.0 %copy-start.18 = (bf16[512,2048]{1,0:T(8,128)(2,1)S(1)}, bf16[512,2048]{1,0:T(8,128)(2,1)}, u32[]{:S(2)}) copy-start(bf16[512,2048]{1,0:T(8,128)(2,1)} %get-tuple-element.43) | copy-start | bytes 6291460
  32.1 6.5 %copy-start.17 = (f32[64]{0:T(128)S(1)}, f32[64]{0:T(128)}, u32[]{:S(2)}) copy-start(f32[64]{0:T(128)} %param.22) | copy-start | bytes 772
  34.5 13.1 %collective-permute-start.6 = (bf16[2,320,384]{2,1,0:T(8,128)(2,1)}, bf16[2,320,384]{2,1,0:T(8,128)(2,1)S(1)}, u32[]{:S(2)}, u32[]{:S(2)}) collective-permute-start(bf16[2,320,384]{2,1,0:T(8,128)(2,1)} %collective-permute-done.5.refs_4_), channel_id=1, source_target_pairs={{0,16},{4,20},{16,24},{20,28},{24,8},{28,12},{8,0},{12,4},{1,17},{... | collective-permute-start | bytes 1474568 | tf_op jit(solution)/shard_map/ppermute | solution.py:376
  37.0 12.7 %collective-permute-start.9 = (bf16[2,320,384]{2,1,0:T(8,128)(2,1)}, bf16[2,320,384]{2,1,0:T(8,128)(2,1)S(1)}, u32[]{:S(2)}, u32[]{:S(2)}) collective-permute-start(bf16[2,320,384]{2,1,0:T(8,128)(2,1)} %collective-permute-done.5.refs_4_), channel_id=1, source_target_pairs={{0,4},{4,0},{8,12},{12,8},{16,20},{20,16},{24,28},{28,24},{1,5},{5... | collective-permute-start | bytes 1474568 | tf_op jit(solution)/shard_map/ppermute | solution.py:379
  38.9 0.7 copy-start.16
  39.1 1.4 %copy-start.13 = (bf16[512,5,64]{0,2,1:T(8,128)(2,1)}, bf16[512,5,64]{0,2,1:T(8,128)(2,1)S(1)}, u32[]{:S(2)}) copy-start(bf16[512,5,64]{0,2,1:T(8,128)(2,1)S(1)} %maximum_multiply_fusion) | copy-start | bytes 983044
  39.1 18.5 %collective-permute-start.7 = (bf16[320,512]{1,0:T(8,128)(2,1)S(1)}, bf16[320,512]{1,0:T(8,128)(2,1)S(1)}, u32[]{:S(2)}, u32[]{:S(2)}) collective-permute-start(bf16[320,512]{1,0:T(8,128)(2,1)S(1)} %bitcast.71), channel_id=1, source_target_pairs={{0,1},{1,0},{2,3},{3,2},{4,5},{5,4},{6,7},{7,6},{8,9},{9,8},{10,11... | collective-permute-start | bytes 983048 | tf_op jit(solution)/shard_map/ppermute | solution.py:361
  47.6 10.0 %copy-start.14 = (bf16[2,320,384]{2,1,0:T(8,128)(2,1)}, bf16[2,320,384]{2,1,0:T(8,128)(2,1)S(1)}, u32[]{:S(2)}) copy-start(bf16[2,320,384]{2,1,0:T(8,128)(2,1)S(1)} %collective-permute-done.6.refs_6_) | copy-start | bytes 1474564
  47.6 44.8 %collective-permute-start.14 = (bf16[320,2048]{1,0:T(8,128)(2,1)}, bf16[320,2048]{1,0:T(8,128)(2,1)}, u32[]{:S(2)}, u32[]{:S(2)}) collective-permute-start(bf16[320,2048]{1,0:T(8,128)(2,1)} %param.24), channel_id=1, source_target_pairs={{0,1},{1,0},{2,3},{3,2},{4,5},{5,4},{6,7},{7,6},{8,9},{9,8},{10,11... | collective-permute-start | bytes 3932168 | tf_op jit(solution)/shard_map/ppermute | solution.py:361
  49.7 7.9 %copy-start.15 = (bf16[2,320,384]{2,1,0:T(8,128)(2,1)}, bf16[2,320,384]{2,1,0:T(8,128)(2,1)S(1)}, u32[]{:S(2)}) copy-start(bf16[2,320,384]{2,1,0:T(8,128)(2,1)S(1)} %collective-permute-done.9.refs_5_) | copy-start | bytes 1474564
  49.7 7.9 %collective-permute-start.10 = (bf16[1,320,384]{2,1,0:T(8,128)(2,1)S(1)}, bf16[1,320,384]{2,1,0:T(8,128)(2,1)S(1)}, u32[]{:S(2)}, u32[]{:S(2)}) collective-permute-start(bf16[1,320,384]{2,1,0:T(8,128)(2,1)S(1)} %slice.54), channel_id=1, source_target_pairs={{0,4},{4,0},{8,12},{12,8},{16,20},{20,16},{24,28},{28,24},{1,5},{5... | collective-permute-start | bytes 737288 | tf_op jit(solution)/shard_map/ppermute | solution.py:379
  51.3 7.0 %collective-permute-start.11 = (bf16[1,320,384]{2,1,0:T(8,128)(2,1)S(1)}, bf16[1,320,384]{2,1,0:T(8,128)(2,1)S(1)}, u32[]{:S(2)}, u32[]{:S(2)}) collective-permute-start(bf16[1,320,384]{2,1,0:T(8,128)(2,1)S(1)} %slice.66), channel_id=1, source_target_pairs={{0,16},{4,20},{16,24},{20,28},{24,8},{28,12},{8,0},{12,4},{1,17},{... | collective-permute-start | bytes 737288 | tf_op jit(solution)/shard_map/ppermute | solution.py:376
  57.6 0.7 copy-start.21
  57.6 0.8 copy-start.22
  58.2 0.7 copy-start.23
  58.9 25.5 %copy-start.3 = (bf16[512,1,5,64]{0,3,2,1:T(8,128)(2,1)S(1)}, bf16[512,1,5,64]{0,3,2,1:T(8,128)(2,1)}, u32[]{:S(2)}) copy-start(bf16[512,1,5,64]{0,3,2,1:T(8,128)(2,1)} %slice.102) | copy-start | bytes 983044
  58.9 25.5 %copy-start.4 = (bf16[512,5,64]{0,2,1:T(8,128)(2,1)S(1)}, bf16[512,5,64]{0,2,1:T(8,128)(2,1)}, u32[]{:S(2)}) copy-start(bf16[512,5,64]{0,2,1:T(8,128)(2,1)} %maximum_convert_fusion) | copy-start | bytes 983044
  83.8 2.0 %collective-permute-start.12 = (bf16[352,512]{1,0:T(8,128)(2,1)}, bf16[352,512]{1,0:T(8,128)(2,1)S(1)}, u32[]{:S(2)}, u32[]{:S(2)}) collective-permute-start(bf16[352,512]{1,0:T(8,128)(2,1)} %get-tuple-element.57), channel_id=1, source_target_pairs={{0,1},{1,0},{2,3},{3,2},{4,5},{5,4},{6,7},{7,6},{8,9},{9,8},{10,11... | collective-permute-start | bytes 1081352 | tf_op jit(solution)/shard_map/ppermute | solution.py:361
  83.9 17.8 %collective-permute-start.18 = (bf16[320,2048]{1,0:T(8,128)(2,1)}, bf16[320,2048]{1,0:T(8,128)(2,1)}, u32[]{:S(2)}, u32[]{:S(2)}) collective-permute-start(bf16[320,2048]{1,0:T(8,128)(2,1)} %collective-permute-done.16), channel_id=1, source_target_pairs={{0,1},{1,0},{2,3},{3,2},{4,5},{5,4},{6,7},{7,6},{8,9},{9,8},{10,11... | collective-permute-start | bytes 3932168 | tf_op jit(solution)/shard_map/ppermute | solution.py:361
  85.8 0.7 copy-start.12
  88.7 3.7 %collective-permute-start.13 = (bf16[320,512]{1,0:T(8,128)(2,1)}, bf16[320,512]{1,0:T(8,128)(2,1)S(1)}, u32[]{:S(2)}, u32[]{:S(2)}) collective-permute-start(bf16[320,512]{1,0:T(8,128)(2,1)} %merge.1), channel_id=1, source_target_pairs={{0,1},{1,0},{2,3},{3,2},{4,5},{5,4},{6,7},{7,6},{8,9},{9,8},{10,11... | collective-permute-start | bytes 983048 | tf_op jit(solution)/shard_map/ppermute | solution.py:361
  88.9 10.2 %collective-permute-start.15 = (bf16[320,512]{1,0:T(8,128)(2,1)}, bf16[320,512]{1,0:T(8,128)(2,1)S(1)}, u32[]{:S(2)}, u32[]{:S(2)}) collective-permute-start(bf16[320,512]{1,0:T(8,128)(2,1)} %merge.1), channel_id=1, source_target_pairs={{0,2},{1,3},{2,0},{3,1},{4,6},{5,7},{6,4},{7,5},{8,10},{9,11},{10,... | collective-permute-start | bytes 983048 | tf_op jit(solution)/shard_map/ppermute | solution.py:358
  89.6 2.9 %copy-start.2 = (bf16[512,2048]{1,0:T(8,128)(2,1)S(1)}, bf16[512,2048]{1,0:T(8,128)(2,1)}, u32[]{:S(2)}) copy-start(bf16[512,2048]{1,0:T(8,128)(2,1)} %get-tuple-element.42) | copy-start | bytes 6291460
  92.4 12.5 %slice-start = ((s8[10485760]{0:T(1024)(128)(4,1)}), s8[4194304]{0:T(1024)(128)(4,1)S(1)}, s32[]{:S(2)}) async-start(s8[10485760]{0:T(1024)(128)(4,1)} %bitcast.76), calls=%async_computation | async-start | bytes 8388608
  92.4 12.5 %slice-start.1 = ((s8[10485760]{0:T(1024)(128)(4,1)}), s8[4194304]{0:T(1024)(128)(4,1)S(1)}, s32[]{:S(2)}) async-start(s8[10485760]{0:T(1024)(128)(4,1)} %bitcast.76), calls=%async_computation.1 | async-start | bytes 8388608
  99.1 2.6 %collective-permute-start.17 = (bf16[320,512]{1,0:T(8,128)(2,1)S(1)}, bf16[320,512]{1,0:T(8,128)(2,1)S(1)}, u32[]{:S(2)}, u32[]{:S(2)}) collective-permute-start(bf16[320,512]{1,0:T(8,128)(2,1)S(1)} %collective-permute-done.15), channel_id=1, source_target_pairs={{0,1},{1,0},{2,3},{3,2},{4,5},{5,4},{6,7},{7,6},{8,9},{9,8},{10,11... | collective-permute-start | bytes 983048 | tf_op jit(solution)/shard_map/ppermute | solution.py:361
  101.7 3.3 %slice-start.2 = ((s8[10485760]{0:T(1024)(128)(4,1)}), s8[2097152]{0:T(1024)(128)(4,1)S(1)}, s32[]{:S(2)}) async-start(s8[10485760]{0:T(1024)(128)(4,1)} %bitcast.76), calls=%async_computation.2 | async-start | bytes 4194304
  101.7 3.3 %copy-start.24 = (f32[2048]{0:T(1024)S(1)}, f32[2048]{0:T(1024)}, u32[]{:S(2)}) copy-start(f32[2048]{0:T(1024)} %param.25) | copy-start | bytes 24580
  110.6 1.3 copy-start.6
  112.0 1.3 copy-start.8
  113.3 1.3 copy-start.7
  115.1 1.7 %collective-permute-start.19 = (bf16[256,512]{1,0:T(8,128)(2,1)S(1)}, bf16[256,512]{1,0:T(8,128)(2,1)S(1)}, u32[]{:S(2)}, u32[]{:S(2)}) collective-permute-start(bf16[256,512]{1,0:T(8,128)(2,1)S(1)} %convolution_convert_fusion.3), channel_id=1, source_target_pairs={{0,1},{1,0},{2,3},{3,2},{4,5},{5,4},{6,7},{7,6},{8,9},{9,8},{10,11... | collective-permute-start | bytes 786440 | tf_op jit(solution)/shard_map/ppermute | solution.py:361
  116.8 1.5 %collective-permute-start.20 = (bf16[256,512]{1,0:T(8,128)(2,1)S(1)}, bf16[256,512]{1,0:T(8,128)(2,1)S(1)}, u32[]{:S(2)}, u32[]{:S(2)}) collective-permute-start(bf16[256,512]{1,0:T(8,128)(2,1)S(1)} %convolution_convert_fusion.2), channel_id=1, source_target_pairs={{0,1},{1,0},{2,3},{3,2},{4,5},{5,4},{6,7},{7,6},{8,9},{9,8},{10,11... | collective-permute-start | bytes 786440 | tf_op jit(solution)/shard_map/ppermute | solution.py:361
  117.7 2.8 %copy-start.5 = (bf16[1280,512]{1,0:T(8,128)(2,1)S(1)}, bf16[1280,512]{1,0:T(8,128)(2,1)}, u32[]{:S(2)}) copy-start(bf16[1280,512]{1,0:T(8,128)(2,1)} %get-tuple-element.71) | copy-start | bytes 3932164
  117.7 3.7 %collective-permute-start.21 = (bf16[512,512]{1,0:T(8,128)(2,1)S(1)}, bf16[512,512]{1,0:T(8,128)(2,1)S(1)}, u32[]{:S(2)}, u32[]{:S(2)}) collective-permute-start(bf16[512,512]{1,0:T(8,128)(2,1)S(1)} %convolution_convert_fusion.1), channel_id=1, source_target_pairs={{0,1},{1,0},{2,3},{3,2},{4,5},{5,4},{6,7},{7,6},{8,9},{9,8},{10,11... | collective-permute-start | bytes 1572872 | tf_op jit(solution)/shard_map/ppermute | solution.py:361
  118.4 14.4 %collective-permute-start.23 = (bf16[256,512]{1,0:T(8,128)(2,1)S(1)}, bf16[256,512]{1,0:T(8,128)(2,1)S(1)}, u32[]{:S(2)}, u32[]{:S(2)}) collective-permute-start(bf16[256,512]{1,0:T(8,128)(2,1)S(1)} %add_convert_fusion.2), channel_id=1, source_target_pairs={{0,2},{1,3},{2,0},{3,1},{4,6},{5,7},{6,4},{7,5},{8,10},{9,11},{10,... | collective-permute-start | bytes 786440 | tf_op jit(solution)/shard_map/ppermute | solution.py:358
  119.2 13.5 %collective-permute-start.22 = (bf16[256,512]{1,0:T(8,128)(2,1)S(1)}, bf16[256,512]{1,0:T(8,128)(2,1)S(1)}, u32[]{:S(2)}, u32[]{:S(2)}) collective-permute-start(bf16[256,512]{1,0:T(8,128)(2,1)S(1)} %add_convert_fusion.3), channel_id=1, source_target_pairs={{0,2},{1,3},{2,0},{3,1},{4,6},{5,7},{6,4},{7,5},{8,10},{9,11},{10,... | collective-permute-start | bytes 786440 | tf_op jit(solution)/shard_map/ppermute | solution.py:358
  121.4 12.3 %copy-start.1 = (bf16[2048,640]{1,0:T(8,128)(2,1)S(1)}, bf16[2048,640]{1,0:T(8,128)(2,1)}, u32[]{:S(2)}) copy-start(bf16[2048,640]{1,0:T(8,128)(2,1)} %param.21) | copy-start | bytes 7864324
  132.9 0.8 copy-start.10
